TPU v7x, 32 devices: a whole 2x2x4 slice. The times are simulated.
32 devices in a mesh: dp: 8 (over y, x, core), tensor: 4 (over z).
Axes of the slice: x: 2, y: 2, z: 4, core: 2. Of those that a mesh axis runs over, the one named last changes fastest.
Arguments:
- block_in: bfloat16 [2, 16384, 1024], P(None, ('dp', 'tensor')), may hold values from -6 to 6
- norm1_gain: bfloat16 [1024], P('dp'), may hold values from 0.5 to 1.5
- norm1_bias: bfloat16 [1024], P('dp'), may hold values from -3 to 3
- w_query: bfloat16 [1024, 1024], P('dp', 'tensor'), may hold values from -0.1875 to 0.1875
- w_key: bfloat16 [1024, 1024], P('dp', 'tensor'), may hold values from -0.1875 to 0.1875
- w_value: bfloat16 [1024, 1024], P('dp', 'tensor'), may hold values from -0.1875 to 0.1875
- w_out: bfloat16 [1024, 1024], P('tensor', 'dp'), may hold values from -1.5 to 1.5
- norm2_gain: bfloat16 [1024], P('dp'), may hold values from 0.5 to 1.5
- norm2_bias: bfloat16 [1024], P('dp'), may hold values from -3 to 3
- w_up: bfloat16 [1024, 4096], P('dp', 'tensor'), may hold values from -0.1875 to 0.1875
- up_bias: bfloat16 [4, 1024], P('tensor', 'dp'), may hold values from -3 to 3
- w_down: bfloat16 [4096, 1024], P('tensor', 'dp'), may hold values from -0.125 to 0.125
- down_bias: bfloat16 [1024], P('dp'), may hold values from -3 to 3
- segments: int32 [2, 16384], P(None, 'dp'), may hold values from 0 to 10, as said below
- rand_blocks: int32 [2, 8, 16, 32, 3], P(None, 'dp', 'tensor'), may hold values from 0 to 31
- glob_blocks: int32 [2, 8, 2], P(None, 'dp'), may hold values from 0 to 31
- cotangent: bfloat16 [2, 16384, 1024], P(None, ('dp', 'tensor')), may hold values from -6 to 6
Outputs:
- block_out: bfloat16 [2, 16384, 1024], P(None, ('dp', 'tensor'))
- grad_in: float32 [2, 16384, 1024], P(None, ('dp', 'tensor'))
- grad_norm1_gain: float32 [1024], P(('dp', 'tensor'))
- grad_norm1_bias: float32 [1024], P(('dp', 'tensor'))
- grad_query: float32 [1024, 1024], P('dp', 'tensor')
- grad_key: float32 [1024, 1024], P('dp', 'tensor')
- grad_value: float32 [1024, 1024], P('dp', 'tensor')
- grad_out: float32 [1024, 1024], P('tensor', 'dp')
- grad_norm2_gain: float32 [1024], P(('dp', 'tensor'))
- grad_norm2_bias: float32 [1024], P(('dp', 'tensor'))
- grad_up: float32 [1024, 4096], P('dp', 'tensor')
- grad_up_bias: float32 [4, 1024], P('tensor', 'dp')
- grad_down: float32 [4096, 1024], P('tensor', 'dp')
- grad_down_bias: float32 [1024], P(('dp', 'tensor'))
Inputs may be any that keep to these rules, and one draw needn't show every extreme that they name: `segments`: segment numbers start at 0 in every sequence and never fall along it; each document but a sequence's last holds between 204 and 2000 tokens; the largest number is reached in some sequence of every micro-batch.
All inputs are finite; a program needn't handle non-finite values.
Results may differ from a plain program's by a relative error of at most 0.019.
Values may be sent and summed in bfloat16 or wider, within the bound.
No kernel may reach another device: no remote copies, remote signals or barrier semaphores. Data moves between devices by JAX's collectives and lax.ppermute only.
A program may use at most 192 MiB of HBM per device.

v0:
```python
import jax
import jax.numpy as jnp
from jax import lax
from jax.sharding import PartitionSpec as P

HD = 64
BLOCK = 64


epsilon = 1e-05
masked_score = -1e30


def layer_norm(rows, gain, shift):
    center = rows - jnp.mean(rows, axis=-1, keepdims=True)
    spread = jnp.mean(center * center, axis=-1, keepdims=True)
    return center * lax.rsqrt(spread + epsilon) * gain + shift


def gelu_new(preact):
    inner = 0.7978845608028654 * (preact + 0.044715 * preact * preact * preact)
    return 0.5 * preact * (1.0 + jnp.tanh(inner))


def block_table(rand_heads, glob_row):
    block_index = jnp.arange(rand_heads.shape[1], dtype=jnp.int32)
    window = jnp.abs(block_index[:, None] - block_index[None, :]) <= 1
    chosen = jnp.any(rand_heads[:, :, :, None] == block_index[None, None, None, :], axis=2)
    glob_hit = jnp.any(glob_row[:, None] == block_index[None, :], axis=0)
    return window[None] | chosen | glob_hit[None, None, :] | glob_hit[None, :, None]


def block_mask(table, segment_row, start_row, block_len):
    table_rows = lax.dynamic_slice_in_dim(table, start_row // BLOCK, block_len // BLOCK, 1)
    expanded = jnp.repeat(jnp.repeat(table_rows, BLOCK, axis=1), BLOCK, axis=2)
    seg_rows = lax.dynamic_slice_in_dim(segment_row, start_row, block_len, 0)
    same_doc = seg_rows[:, None] == segment_row[None, :]
    return expanded & same_doc[None]


def split_heads(rows):
    return rows.reshape(rows.shape[0], rows.shape[1] // HD, HD)


def row_slice(rows, start_row, row_count):
    return lax.dynamic_slice_in_dim(rows, start_row, row_count, 0)


def block_scores(query_rows, key_heads, table, segment_row, start_row):
    scores = (
        jnp.einsum("qhd,khd->hqk", query_rows, key_heads, preferred_element_type=jnp.float32)
        * 0.125
    )
    allowed = block_mask(table, segment_row, start_row, query_rows.shape[0])
    return jnp.where(allowed, scores, masked_score)


def attend(query, key, value, table, segment_row):
    length = query.shape[0]
    block_len = min(512, length)
    query_heads = split_heads(query)
    key_heads = split_heads(key)
    value_heads = split_heads(value)

    def one_block(start_row):
        query_rows = row_slice(query_heads, start_row, block_len)
        scores = block_scores(query_rows, key_heads, table, segment_row, start_row)
        row_max = jnp.max(scores, axis=-1, keepdims=True)
        exponent = jnp.exp(scores - row_max)
        row_total = jnp.sum(exponent, axis=-1, keepdims=True)
        attn_probs = (exponent / row_total).astype(jnp.bfloat16)
        context = jnp.einsum(
            "hqk,khd->qhd", attn_probs, value_heads, preferred_element_type=jnp.float32
        )
        return (
            context.astype(jnp.bfloat16).reshape(block_len, -1),
            (row_max + jnp.log(row_total))[..., 0],
        )

    starts = jnp.arange(length // block_len, dtype=jnp.int32) * block_len
    blocks, logsum = lax.map(one_block, starts)
    return (blocks.reshape(length, -1), logsum)


def attend_back(query, key, value, grad_context, logsum, table, segment_row):
    length = query.shape[0]
    block_len = min(512, length)
    query_heads = split_heads(query)
    key_heads = split_heads(key)
    value_heads = split_heads(value)
    grad_heads = split_heads(grad_context)

    def one_block(running, block_item):
        start_row, block_logsum = block_item
        query_rows = row_slice(query_heads, start_row, block_len)
        grad_rows = row_slice(grad_heads, start_row, block_len)
        scores = block_scores(query_rows, key_heads, table, segment_row, start_row)
        attn_probs = jnp.exp(scores - block_logsum[..., None])
        grad_probs = jnp.einsum(
            "qhd,khd->hqk", grad_rows, value_heads, preferred_element_type=jnp.float32
        )
        row_delta = jnp.sum(attn_probs * grad_probs, axis=-1, keepdims=True)
        grad_scores = (attn_probs * (grad_probs - row_delta)).astype(jnp.bfloat16)
        grad_query = (
            jnp.einsum("hqk,khd->qhd", grad_scores, key_heads, preferred_element_type=jnp.float32)
            * 0.125
        )
        grad_key = (
            running[0]
            + jnp.einsum(
                "hqk,qhd->khd", grad_scores, query_rows, preferred_element_type=jnp.float32
            )
            * 0.125
        )
        grad_value = running[1] + jnp.einsum(
            "hqk,qhd->khd",
            attn_probs.astype(jnp.bfloat16),
            grad_rows,
            preferred_element_type=jnp.float32,
        )
        return ((grad_key, grad_value), grad_query.astype(jnp.bfloat16).reshape(block_len, -1))

    zero_heads = jnp.zeros(key_heads.shape, jnp.float32)
    starts = jnp.arange(length // block_len, dtype=jnp.int32) * block_len
    (grad_key, grad_value), grad_blocks = lax.scan(
        one_block, (zero_heads, zero_heads), (starts, logsum)
    )
    return (
        grad_blocks.reshape(length, -1),
        grad_key.astype(jnp.bfloat16).reshape(length, -1),
        grad_value.astype(jnp.bfloat16).reshape(length, -1),
    )


def unpack(gathered):
    small = tuple((member.astype(jnp.float32) for member in gathered[6:]))
    return gathered[:6] + small


def per_device(
    block_in,
    norm1_gain,
    norm1_bias,
    w_query,
    w_key,
    w_value,
    w_out,
    norm2_gain,
    norm2_bias,
    w_up,
    up_bias,
    w_down,
    down_bias,
    segments,
    rand_blocks,
    glob_blocks,
    cotangent,
):
    local_rows = block_in.shape[1]
    dp_count = lax.axis_size("dp")
    layout = (
        w_query,
        w_key,
        w_value,
        w_out,
        w_up,
        w_down,
        up_bias,
        norm1_gain,
        norm1_bias,
        norm2_gain,
        norm2_bias,
        down_bias,
    )

    def micro_step(running, micro_item):
        weight_sums, vector_sums = running
        rows_in, grad_given, segment_row, rand_seq, glob_seq = micro_item
        gathered = (
            lax.all_gather(layout[0], "dp", axis=0, tiled=True),
            lax.all_gather(layout[1], "dp", axis=0, tiled=True),
            lax.all_gather(layout[2], "dp", axis=0, tiled=True),
            lax.all_gather(layout[3], "dp", axis=1, tiled=True),
            lax.all_gather(layout[4], "dp", axis=0, tiled=True),
            lax.all_gather(layout[5], "dp", axis=1, tiled=True),
            lax.all_gather(layout[6], "dp", axis=1, tiled=True),
            lax.all_gather(layout[7], "dp", axis=0, tiled=True),
            lax.all_gather(layout[8], "dp", axis=0, tiled=True),
            lax.all_gather(layout[9], "dp", axis=0, tiled=True),
            lax.all_gather(layout[10], "dp", axis=0, tiled=True),
            lax.all_gather(layout[11], "dp", axis=0, tiled=True),
        )
        (
            all_query,
            all_key,
            all_value,
            all_out,
            all_up,
            all_down,
            up_shift,
            gain_one,
            shift_one,
            gain_two,
            shift_two,
            down_shift,
        ) = unpack(gathered)
        table = block_table(rand_seq[0], glob_seq[0])
        resid_in = rows_in.astype(jnp.float32)
        normed = layer_norm(resid_in, gain_one, shift_one).astype(jnp.bfloat16)
        normed_all = lax.all_gather(normed, "tensor", axis=0, tiled=True)
        query = jnp.dot(normed_all, all_query, preferred_element_type=jnp.float32).astype(
            jnp.bfloat16
        )
        key = jnp.dot(normed_all, all_key, preferred_element_type=jnp.float32).astype(jnp.bfloat16)
        value = jnp.dot(normed_all, all_value, preferred_element_type=jnp.float32).astype(
            jnp.bfloat16
        )
        context, logsum = attend(query, key, value, table, segment_row)
        attn_sum = lax.psum_scatter(
            jnp.dot(
                row_slice(context, jnp.int32(0), local_rows * lax.axis_size("tensor")),
                all_out,
                preferred_element_type=jnp.float32,
            ).astype(jnp.bfloat16),
            "tensor",
            scatter_dimension=0,
            tiled=True,
        ).astype(jnp.float32)
        resid = resid_in + attn_sum
        normed_two = layer_norm(resid, gain_two, shift_two).astype(jnp.bfloat16)
        normed_two_all = lax.all_gather(normed_two, "tensor", axis=0, tiled=True)
        up_val = jnp.dot(normed_two_all, all_up, preferred_element_type=jnp.float32) + up_shift[0]
        act = gelu_new(up_val).astype(jnp.bfloat16)
        ffn_sum = lax.psum_scatter(
            jnp.dot(
                row_slice(act, jnp.int32(0), local_rows * lax.axis_size("tensor")),
                all_down,
                preferred_element_type=jnp.float32,
            ).astype(jnp.bfloat16),
            "tensor",
            scatter_dimension=0,
            tiled=True,
        ).astype(jnp.float32)
        block_out = (resid + ffn_sum + down_shift).astype(jnp.bfloat16)
        gathered = (
            lax.all_gather(layout[0], "dp", axis=0, tiled=True),
            lax.all_gather(layout[1], "dp", axis=0, tiled=True),
            lax.all_gather(layout[2], "dp", axis=0, tiled=True),
            lax.all_gather(layout[3], "dp", axis=1, tiled=True),
            lax.all_gather(layout[4], "dp", axis=0, tiled=True),
            lax.all_gather(layout[5], "dp", axis=1, tiled=True),
            lax.all_gather(layout[6], "dp", axis=1, tiled=True),
            lax.all_gather(layout[7], "dp", axis=0, tiled=True),
            lax.all_gather(layout[8], "dp", axis=0, tiled=True),
            lax.all_gather(layout[9], "dp", axis=0, tiled=True),
            lax.all_gather(layout[10], "dp", axis=0, tiled=True),
            lax.all_gather(layout[11], "dp", axis=0, tiled=True),
        )
        (
            all_query,
            all_key,
            all_value,
            all_out,
            all_up,
            all_down,
            up_shift,
            gain_one,
            shift_one,
            gain_two,
            shift_two,
            down_shift,
        ) = unpack(gathered)
        grad_all = lax.all_gather(grad_given, "tensor", axis=0, tiled=True)
        grad_act = jnp.dot(grad_all, all_down.T, preferred_element_type=jnp.float32)
        grad_up_val = jax.vjp(gelu_new, up_val)[1](grad_act)[0].astype(jnp.bfloat16)
        grad_wdown = jnp.dot(act.T, grad_all, preferred_element_type=jnp.float32)
        grad_wup = jnp.dot(normed_two_all.T, grad_up_val, preferred_element_type=jnp.float32)
        grad_upbias = jnp.sum(grad_up_val.astype(jnp.float32), axis=0, keepdims=True)
        grad_normed_two = lax.psum_scatter(
            jnp.dot(
                row_slice(grad_up_val, jnp.int32(0), local_rows * lax.axis_size("tensor")),
                all_up.T,
                preferred_element_type=jnp.float32,
            ).astype(jnp.bfloat16),
            "tensor",
            scatter_dimension=0,
            tiled=True,
        ).astype(jnp.float32)
        grad_cot = grad_given.astype(jnp.float32)
        norm_pull_two = jax.vjp(layer_norm, resid, gain_two, shift_two)[1]
        grad_resid_norm, grad_gain_two, grad_shift_two = norm_pull_two(grad_normed_two)
        grad_resid = grad_cot + grad_resid_norm
        grad_resid_all = lax.all_gather(
            grad_resid.astype(jnp.bfloat16), "tensor", axis=0, tiled=True
        )
        grad_wout = jnp.dot(context.T, grad_resid_all, preferred_element_type=jnp.float32)
        grad_context = jnp.dot(
            grad_resid_all, all_out.T, preferred_element_type=jnp.float32
        ).astype(jnp.bfloat16)
        grad_q, grad_k, grad_v = attend_back(
            query, key, value, grad_context, logsum, table, segment_row
        )
        grad_wquery = jnp.dot(normed_all.T, grad_q, preferred_element_type=jnp.float32)
        grad_wkey = jnp.dot(normed_all.T, grad_k, preferred_element_type=jnp.float32)
        grad_wvalue = jnp.dot(normed_all.T, grad_v, preferred_element_type=jnp.float32)
        start_row = jnp.int32(0)
        from_query = jnp.dot(
            row_slice(grad_q, start_row, local_rows * lax.axis_size("tensor")),
            all_query.T,
            preferred_element_type=jnp.float32,
        )
        from_key = jnp.dot(
            row_slice(grad_k, start_row, local_rows * lax.axis_size("tensor")),
            all_key.T,
            preferred_element_type=jnp.float32,
        )
        from_value = jnp.dot(
            row_slice(grad_v, start_row, local_rows * lax.axis_size("tensor")),
            all_value.T,
            preferred_element_type=jnp.float32,
        )
        grad_normed = lax.psum_scatter(
            (from_query + from_key + from_value).astype(jnp.bfloat16),
            "tensor",
            scatter_dimension=0,
            tiled=True,
        ).astype(jnp.float32)
        norm_pull_one = jax.vjp(layer_norm, resid_in, gain_one, shift_one)[1]
        grad_in_norm, grad_gain_one, grad_shift_one = norm_pull_one(grad_normed)
        grad_in = grad_resid + grad_in_norm
        weight_terms = (
            grad_wquery,
            grad_wkey,
            grad_wvalue,
            grad_wout,
            grad_wup,
            grad_wdown,
            grad_upbias,
        )
        vector_terms = (
            grad_gain_one,
            grad_shift_one,
            grad_gain_two,
            grad_shift_two,
            jnp.sum(grad_cot, axis=0),
        )
        weight_terms = (
            lax.psum_scatter(weight_terms[0], "dp", scatter_dimension=0, tiled=True),
            lax.psum_scatter(weight_terms[1], "dp", scatter_dimension=0, tiled=True),
            lax.psum_scatter(weight_terms[2], "dp", scatter_dimension=0, tiled=True),
            lax.psum_scatter(weight_terms[3], "dp", scatter_dimension=1, tiled=True),
            lax.psum_scatter(weight_terms[4], "dp", scatter_dimension=0, tiled=True),
            lax.psum_scatter(weight_terms[5], "dp", scatter_dimension=1, tiled=True),
            lax.psum_scatter(weight_terms[6], "dp", scatter_dimension=1, tiled=True),
        )
        weight_sums = jax.tree.map(lambda left, right: left + right, weight_sums, weight_terms)
        vector_sums = jax.tree.map(lambda left, right: left + right, vector_sums, vector_terms)
        return ((weight_sums, vector_sums), (block_out, grad_in))

    weight_zero = tuple(
        (
            jnp.zeros(member.shape, jnp.float32)
            for member in (w_query, w_key, w_value, w_out, w_up, w_down, up_bias)
        )
    )
    width_full = norm1_gain.shape[0] * dp_count
    vector_zero = tuple((jnp.zeros((width_full,), jnp.float32) for member in range(5)))
    (weight_sums, vector_sums), (block_out, grad_in) = lax.scan(
        micro_step,
        (weight_zero, vector_zero),
        (block_in, cotangent, segments, rand_blocks, glob_blocks),
    )
    vector_grads = (
        lax.psum_scatter(vector_sums[0], ("dp", "tensor"), scatter_dimension=0, tiled=True),
        lax.psum_scatter(vector_sums[1], ("dp", "tensor"), scatter_dimension=0, tiled=True),
        lax.psum_scatter(vector_sums[2], ("dp", "tensor"), scatter_dimension=0, tiled=True),
        lax.psum_scatter(vector_sums[3], ("dp", "tensor"), scatter_dimension=0, tiled=True),
        lax.psum_scatter(vector_sums[4], ("dp", "tensor"), scatter_dimension=0, tiled=True),
    )
    return (
        block_out,
        grad_in,
        vector_grads[0],
        vector_grads[1],
        weight_sums[0],
        weight_sums[1],
        weight_sums[2],
        weight_sums[3],
        vector_grads[2],
        vector_grads[3],
        weight_sums[4],
        weight_sums[6],
        weight_sums[5],
        vector_grads[4],
    )


def solution(mesh):
    return jax.shard_map(
        per_device,
        mesh=mesh,
        in_specs=(
            P(None, ("dp", "tensor"), None),
            P("dp"),
            P("dp"),
            P("dp", "tensor"),
            P("dp", "tensor"),
            P("dp", "tensor"),
            P("tensor", "dp"),
            P("dp"),
            P("dp"),
            P("dp", "tensor"),
            P("tensor", "dp"),
            P("tensor", "dp"),
            P("dp"),
            P(None, "dp"),
            P(None, "dp", "tensor", None, None),
            P(None, "dp", None),
            P(None, ("dp", "tensor"), None),
        ),
        out_specs=(
            P(None, ("dp", "tensor"), None),
            P(None, ("dp", "tensor"), None),
            P(("dp", "tensor")),
            P(("dp", "tensor")),
            P("dp", "tensor"),
            P("dp", "tensor"),
            P("dp", "tensor"),
            P("tensor", "dp"),
            P(("dp", "tensor")),
            P(("dp", "tensor")),
            P("dp", "tensor"),
            P("tensor", "dp"),
            P("tensor", "dp"),
            P(("dp", "tensor")),
        ),
        check_vma=False,
    )
```

profile of v0, /device:TPU:0, one launch (start us, length us, event | category | flops | bytes accessed | tf_op | source)
XLA Modules:
  0.0 2618.8 jit_solution(6359592128269181894)
XLA Ops:
  7.3 2560.0 %while.102 = (s32[]{:T(128)}, f32[128,256]{1,0:T(8,128)}, f32[128,256]{1,0:T(8,128)}, f32[128,256]{1,0:T(8,128)}, f32[256,128]{1,0:T(8,128)}, /*index=5*/f32[128...) while((s32[]{:T(128)}, f32[128,256]{1,0:T(8,128)}, ...), condition=%wide.region_35.36_spmd.clone, body=%wide.region_0.35_spmd.clone.sunk | while | flops 42664108032 | bytes 880034816 | solution.py:368
  71.9 42.1 %all-gather.31.cloned.1.call-done = bf16[2048,1024]{1,0:T(8,128)(2,1)} async-done(((bf16[512,1024]{1,0:T(8,128)(2,1)}), bf16[2048,1024]{1,0:T(8,128)(2,1)}) %all-gather.31.cloned.1.call-update) | async-done | bytes 4194320 | tf_op jit(solution)/shard_map/while/body/eval_jaxpr/all_gather | solution.py:210
  123.2 176.1 %while.103 = (s32[]{:T(128)}, bf16[4,512,256]{2,1,0:T(8,128)(2,1)S(1)}, f32[4,4,512]{2,1,0:T(4,128)S(1)}, s32[4]{0:T(128)S(1)}, pred[4,32,32]{1,2,0:T(8,128)(4,1...) while((s32[]{:T(128)}, ...), condition=%wide.region_8.8_spmd, body=%wide.region_5.7_spmd.sunk | while | flops 1112668160 | bytes 73221512 | solution.py:81
  322.2 56.8 %reduce-scatter.16.cloned.1.call-done = bf16[512,1024]{1,0:T(8,128)(2,1)} async-done(((bf16[2048,1024]{1,0:T(8,128)(2,1)}), bf16[512,1024]{1,0:T(8,128)(2,1)}) %reduce-scatter.16.cloned.1.call-update) | async-done | bytes 1048592 | tf_op jit(solution)/shard_map/while/body/eval_jaxpr/reduce_scatter | solution.py:219
  409.5 82.3 %all-gather.33.cloned.1.call-done = bf16[2048,1024]{1,0:T(8,128)(2,1)} async-done(((bf16[512,1024]{1,0:T(8,128)(2,1)}), bf16[2048,1024]{1,0:T(8,128)(2,1)}) %all-gather.33.cloned.1.call-update) | async-done | bytes 4194320 | tf_op jit(solution)/shard_map/while/body/eval_jaxpr/all_gather | solution.py:231
  502.5 18.0 all-gather.37.cloned.1.call-done
  520.5 82.3 %all-gather.39.cloned.1.call-done = bf16[1,2048,1024]{2,1,0:T(8,128)(2,1)} async-done(((bf16[1,512,1024]{2,1,0:T(8,128)(2,1)}), bf16[1,2048,1024]{2,1,0:T(8,128)(2,1)}) %all-gather.39.cloned.1.call-update) | async-done | bytes 4194320 | tf_op jit(solution)/shard_map/while/body/eval_jaxpr/all_gather | solution.py:273
  602.8 15.1 convert_reduce_fusion.10
  626.3 75.2 %reduce-scatter.18.cloned.1.call-done = bf16[512,1024]{1,0:T(8,128)(2,1)} async-done(((bf16[2048,1024]{1,0:T(8,128)(2,1)}), bf16[512,1024]{1,0:T(8,128)(2,1)}) %reduce-scatter.18.cloned.1.call-update) | async-done | bytes 1048592 | tf_op jit(solution)/shard_map/while/body/eval_jaxpr/reduce_scatter | solution.py:279
  745.9 44.7 %all-gather.41.cloned.1.call-done = bf16[2048,1024]{1,0:T(8,128)(2,1)} async-done(((bf16[512,1024]{1,0:T(8,128)(2,1)}), bf16[2048,1024]{1,0:T(8,128)(2,1)}) %all-gather.41.cloned.1.call-update) | async-done | bytes 4194320 | tf_op jit(solution)/shard_map/while/body/eval_jaxpr/all_gather | solution.py:293
  800.7 281.0 %while.104 = (s32[]{:T(128)}, f32[2048,4,64]{0,2,1:T(8,128)}, f32[2048,4,64]{0,2,1:T(8,128)}, bf16[4,512,256]{2,1,0:T(8,128)(2,1)}, s32[4]{0:T(128)S(1)}, /*inde...) while((s32[]{:T(128)}, f32[2048,4,64]{0,2,1:T(8,128)}, ...), condition=%wide.region_17.17_spmd.clone, body=%wide.region_15.16_spmd.clone.sunk | while | flops 2730227712 | bytes 226026960 | solution.py:125
  827.2 14.3 multiply_reduce_fusion.5
  1038.0 14.0 multiply_reduce_fusion.5
  1127.6 33.4 %reduce-scatter.22.cloned.1.call-done = f32[128,256]{1,0:T(8,128)} async-done(((f32[1024,256]{1,0:T(8,128)}), f32[128,256]{1,0:T(8,128)}) %reduce-scatter.22.cloned.1.call-update) | async-done | bytes 131088 | tf_op jit(solution)/shard_map/while/body/eval_jaxpr/reduce_scatter | solution.py:349
  1162.0 38.1 %reduce-scatter.24.cloned.1.call-done = f32[128,256]{1,0:T(8,128)} async-done(((f32[1024,256]{1,0:T(8,128)}), f32[128,256]{1,0:T(8,128)}) %reduce-scatter.24.cloned.1.call-update) | async-done | bytes 131088 | tf_op jit(solution)/shard_map/while/body/eval_jaxpr/reduce_scatter | solution.py:350
  1201.1 78.1 %reduce-scatter.34.cloned.1.call-done = bf16[512,1024]{1,0:T(8,128)(2,1)} async-done(((bf16[2048,1024]{1,0:T(8,128)(2,1)}), bf16[512,1024]{1,0:T(8,128)(2,1)}) %reduce-scatter.34.cloned.1.call-update) | async-done | bytes 1048592 | tf_op jit(solution)/shard_map/while/body/eval_jaxpr/reduce_scatter | solution.py:322
  1349.8 41.4 %all-gather.31.cloned.1.call-done = bf16[2048,1024]{1,0:T(8,128)(2,1)} async-done(((bf16[512,1024]{1,0:T(8,128)(2,1)}), bf16[2048,1024]{1,0:T(8,128)(2,1)}) %all-gather.31.cloned.1.call-update) | async-done | bytes 4194320 | tf_op jit(solution)/shard_map/while/body/eval_jaxpr/all_gather | solution.py:210
  1400.4 176.4 %while.103 = (s32[]{:T(128)}, bf16[4,512,256]{2,1,0:T(8,128)(2,1)S(1)}, f32[4,4,512]{2,1,0:T(4,128)S(1)}, s32[4]{0:T(128)S(1)}, pred[4,32,32]{1,2,0:T(8,128)(4,1...) while((s32[]{:T(128)}, ...), condition=%wide.region_8.8_spmd, body=%wide.region_5.7_spmd.sunk | while | flops 1112668160 | bytes 73221512 | solution.py:81
  1599.4 57.2 %reduce-scatter.16.cloned.1.call-done = bf16[512,1024]{1,0:T(8,128)(2,1)} async-done(((bf16[2048,1024]{1,0:T(8,128)(2,1)}), bf16[512,1024]{1,0:T(8,128)(2,1)}) %reduce-scatter.16.cloned.1.call-update) | async-done | bytes 1048592 | tf_op jit(solution)/shard_map/while/body/eval_jaxpr/reduce_scatter | solution.py:219
  1686.9 82.5 %all-gather.33.cloned.1.call-done = bf16[2048,1024]{1,0:T(8,128)(2,1)} async-done(((bf16[512,1024]{1,0:T(8,128)(2,1)}), bf16[2048,1024]{1,0:T(8,128)(2,1)}) %all-gather.33.cloned.1.call-update) | async-done | bytes 4194320 | tf_op jit(solution)/shard_map/while/body/eval_jaxpr/all_gather | solution.py:231
  1780.0 18.1 all-gather.37.cloned.1.call-done
  1798.1 82.5 %all-gather.39.cloned.1.call-done = bf16[1,2048,1024]{2,1,0:T(8,128)(2,1)} async-done(((bf16[1,512,1024]{2,1,0:T(8,128)(2,1)}), bf16[1,2048,1024]{2,1,0:T(8,128)(2,1)}) %all-gather.39.cloned.1.call-update) | async-done | bytes 4194320 | tf_op jit(solution)/shard_map/while/body/eval_jaxpr/all_gather | solution.py:273
  1880.6 15.1 convert_reduce_fusion.10
  1904.1 75.2 %reduce-scatter.18.cloned.1.call-done = bf16[512,1024]{1,0:T(8,128)(2,1)} async-done(((bf16[2048,1024]{1,0:T(8,128)(2,1)}), bf16[512,1024]{1,0:T(8,128)(2,1)}) %reduce-scatter.18.cloned.1.call-update) | async-done | bytes 1048592 | tf_op jit(solution)/shard_map/while/body/eval_jaxpr/reduce_scatter | solution.py:279
  2023.7 44.7 %all-gather.41.cloned.1.call-done = bf16[2048,1024]{1,0:T(8,128)(2,1)} async-done(((bf16[512,1024]{1,0:T(8,128)(2,1)}), bf16[2048,1024]{1,0:T(8,128)(2,1)}) %all-gather.41.cloned.1.call-update) | async-done | bytes 4194320 | tf_op jit(solution)/shard_map/while/body/eval_jaxpr/all_gather | solution.py:293
  2078.5 280.9 %while.104 = (s32[]{:T(128)}, f32[2048,4,64]{0,2,1:T(8,128)}, f32[2048,4,64]{0,2,1:T(8,128)}, bf16[4,512,256]{2,1,0:T(8,128)(2,1)}, s32[4]{0:T(128)S(1)}, /*inde...) while((s32[]{:T(128)}, f32[2048,4,64]{0,2,1:T(8,128)}, ...), condition=%wide.region_17.17_spmd.clone, body=%wide.region_15.16_spmd.clone.sunk | while | flops 2730227712 | bytes 226026960 | solution.py:125
  2104.7 14.4 multiply_reduce_fusion.5
  2315.8 14.0 multiply_reduce_fusion.5
  2405.7 33.1 %reduce-scatter.22.cloned.1.call-done = f32[128,256]{1,0:T(8,128)} async-done(((f32[1024,256]{1,0:T(8,128)}), f32[128,256]{1,0:T(8,128)}) %reduce-scatter.22.cloned.1.call-update) | async-done | bytes 131088 | tf_op jit(solution)/shard_map/while/body/eval_jaxpr/reduce_scatter | solution.py:349
  2439.7 38.1 %reduce-scatter.24.cloned.1.call-done = f32[128,256]{1,0:T(8,128)} async-done(((f32[1024,256]{1,0:T(8,128)}), f32[128,256]{1,0:T(8,128)}) %reduce-scatter.24.cloned.1.call-update) | async-done | bytes 131088 | tf_op jit(solution)/shard_map/while/body/eval_jaxpr/reduce_scatter | solution.py:350
  2478.8 78.2 %reduce-scatter.34.cloned.1.call-done = bf16[512,1024]{1,0:T(8,128)(2,1)} async-done(((bf16[2048,1024]{1,0:T(8,128)(2,1)}), bf16[512,1024]{1,0:T(8,128)(2,1)}) %reduce-scatter.34.cloned.1.call-update) | async-done | bytes 1048592 | tf_op jit(solution)/shard_map/while/body/eval_jaxpr/reduce_scatter | solution.py:322
  2567.3 41.4 %all-reduce.5 = (f32[1024]{0:T(1024)S(1)}, f32[1024]{0:T(1024)S(1)}, f32[1024]{0:T(1024)S(1)}, f32[1024]{0:T(1024)S(1)}, f32[1024]{0:T(1024)S(1)}) all-reduce(f32[1024]{0:T(1024)} %get-tuple-element.806, f32[1024]{0:T(1024)} %get-tuple-element.807, ...), channel_id=14, replica_groups=mesh['dp'=8,'tensor'=4] {'dp','tensor'}, use_global_device_ids=true, to_apply=%region_36.37.clone | all-reduce | flops 5120 | bytes 40960
  (765 shorter events, 1304.6 us)
Async XLA Ops:
  7.9 106.0 %all-gather.31.cloned.1.call-start = ((), (), s32[]{:S(2)}) async-start(), calls=%async_computation.11 | async-start | bytes 5242880 | tf_op jit(solution)/shard_map/while/body/eval_jaxpr/all_gather | solution.py:210
  32.8 346.2 %reduce-scatter.16.cloned.1.call-start = ((), (), s32[]{:S(2)}) async-start(), calls=%async_computation.12 | async-start | bytes 5242880 | tf_op jit(solution)/shard_map/while/body/eval_jaxpr/reduce_scatter | solution.py:219
  303.6 105.9 %all-gather.35.cloned.1.call-start = ((), (), s32[]{:S(2)}) async-start(), calls=%async_computation.14 | async-start | bytes 2359296 | tf_op jit(solution)/shard_map/while/body/eval_jaxpr/all_gather | solution.py:184
  304.3 187.5 %all-gather.33.cloned.1.call-start = ((), (), s32[]{:S(2)}) async-start(), calls=%async_computation.13 | async-start | bytes 5242880 | tf_op jit(solution)/shard_map/while/body/eval_jaxpr/all_gather | solution.py:231
  383.9 136.5 %all-gather.37.cloned.1.call-start = ((), (), s32[]{:S(2)}) async-start(), calls=%async_computation.15 | async-start | bytes 2359296 | tf_op jit(solution)/shard_map/while/body/eval_jaxpr/all_gather | solution.py:251
  384.5 218.2 %all-gather.39.cloned.1.call-start = ((), (), s32[]{:S(2)}) async-start(), calls=%async_computation.16 | async-start | bytes 5242880 | tf_op jit(solution)/shard_map/while/body/eval_jaxpr/all_gather | solution.py:273
  387.6 313.9 %reduce-scatter.18.cloned.1.call-start = ((), (), s32[]{:S(2)}) async-start(), calls=%async_computation.17 | async-start | bytes 5242880 | tf_op jit(solution)/shard_map/while/body/eval_jaxpr/reduce_scatter | solution.py:279
  626.1 164.6 %all-gather.41.cloned.1.call-start = ((), (), s32[]{:S(2)}) async-start(), calls=%async_computation.18 | async-start | bytes 5242880 | tf_op jit(solution)/shard_map/while/body/eval_jaxpr/all_gather | solution.py:293
  709.3 406.2 %reduce-scatter.32.cloned.1.call-start = ((), (), s32[]{:S(2)}) async-start(), calls=%async_computation.25 | async-start | bytes 589824 | tf_op jit(solution)/shard_map/while
  710.4 406.0 %reduce-scatter.28.cloned.1.call-start = ((), (), s32[]{:S(2)}) async-start(), calls=%async_computation.23 | async-start | bytes 4718592 | tf_op jit(solution)/shard_map/while/body/eval_jaxpr/reduce_scatter | solution.py:352
  720.4 398.4 %reduce-scatter.30.cloned.1.call-start = ((), (), s32[]{:S(2)}) async-start(), calls=%async_computation.24 | async-start | bytes 4718592 | tf_op jit(solution)/shard_map/while/body/eval_jaxpr/reduce_scatter | solution.py:353
  733.0 389.0 %reduce-scatter.36.cloned.1.call-start = ((), (), s32[]{:S(2)}) async-start(), calls=%async_computation.27 | async-start | bytes 5242880 | tf_op jit(solution)/shard_map/while/body/eval_jaxpr/reduce_scatter | solution.py:234
  745.8 379.1 %reduce-scatter.26.cloned.1.call-start = ((), (), s32[]{:S(2)}) async-start(), calls=%async_computation.22 | async-start | bytes 1179648 | tf_op jit(solution)/shard_map/while/body/eval_jaxpr/reduce_scatter | solution.py:351
  795.2 330.8 %reduce-scatter.20.cloned.1.call-start = ((), (), s32[]{:S(2)}) async-start(), calls=%async_computation.19 | async-start | bytes 1179648 | tf_op jit(solution)/shard_map/while/body/eval_jaxpr/reduce_scatter | solution.py:348
  1092.9 107.2 %reduce-scatter.24.cloned.1.call-start = ((), (), s32[]{:S(2)}) async-start(), calls=%async_computation.21 | async-start | bytes 1179648 | tf_op jit(solution)/shard_map/while/body/eval_jaxpr/reduce_scatter | solution.py:350
  1098.8 180.3 %reduce-scatter.34.cloned.1.call-start = ((), (), s32[]{:S(2)}) async-start(), calls=%async_computation.26 | async-start | bytes 5242880 | tf_op jit(solution)/shard_map/while/body/eval_jaxpr/reduce_scatter | solution.py:322
  1287.4 103.8 %all-gather.31.cloned.1.call-start = ((), (), s32[]{:S(2)}) async-start(), calls=%async_computation.11 | async-start | bytes 5242880 | tf_op jit(solution)/shard_map/while/body/eval_jaxpr/all_gather | solution.py:210
  1310.7 345.9 %reduce-scatter.16.cloned.1.call-start = ((), (), s32[]{:S(2)}) async-start(), calls=%async_computation.12 | async-start | bytes 5242880 | tf_op jit(solution)/shard_map/while/body/eval_jaxpr/reduce_scatter | solution.py:219
  1581.1 105.8 %all-gather.35.cloned.1.call-start = ((), (), s32[]{:S(2)}) async-start(), calls=%async_computation.14 | async-start | bytes 2359296 | tf_op jit(solution)/shard_map/while/body/eval_jaxpr/all_gather | solution.py:184
  1581.7 187.6 %all-gather.33.cloned.1.call-start = ((), (), s32[]{:S(2)}) async-start(), calls=%async_computation.13 | async-start | bytes 5242880 | tf_op jit(solution)/shard_map/while/body/eval_jaxpr/all_gather | solution.py:231
  1661.5 136.6 %all-gather.37.cloned.1.call-start = ((), (), s32[]{:S(2)}) async-start(), calls=%async_computation.15 | async-start | bytes 2359296 | tf_op jit(solution)/shard_map/while/body/eval_jaxpr/all_gather | solution.py:251
  1662.2 218.3 %all-gather.39.cloned.1.call-start = ((), (), s32[]{:S(2)}) async-start(), calls=%async_computation.16 | async-start | bytes 5242880 | tf_op jit(solution)/shard_map/while/body/eval_jaxpr/all_gather | solution.py:273
  1665.3 314.1 %reduce-scatter.18.cloned.1.call-start = ((), (), s32[]{:S(2)}) async-start(), calls=%async_computation.17 | async-start | bytes 5242880 | tf_op jit(solution)/shard_map/while/body/eval_jaxpr/reduce_scatter | solution.py:279
  1903.9 164.6 %all-gather.41.cloned.1.call-start = ((), (), s32[]{:S(2)}) async-start(), calls=%async_computation.18 | async-start | bytes 5242880 | tf_op jit(solution)/shard_map/while/body/eval_jaxpr/all_gather | solution.py:293
  1987.1 406.1 %reduce-scatter.32.cloned.1.call-start = ((), (), s32[]{:S(2)}) async-start(), calls=%async_computation.25 | async-start | bytes 589824 | tf_op jit(solution)/shard_map/while
  1988.2 405.9 %reduce-scatter.28.cloned.1.call-start = ((), (), s32[]{:S(2)}) async-start(), calls=%async_computation.23 | async-start | bytes 4718592 | tf_op jit(solution)/shard_map/while/body/eval_jaxpr/reduce_scatter | solution.py:352
  1998.2 398.5 %reduce-scatter.30.cloned.1.call-start = ((), (), s32[]{:S(2)}) async-start(), calls=%async_computation.24 | async-start | bytes 4718592 | tf_op jit(solution)/shard_map/while/body/eval_jaxpr/reduce_scatter | solution.py:353
  2010.8 389.2 %reduce-scatter.36.cloned.1.call-start = ((), (), s32[]{:S(2)}) async-start(), calls=%async_computation.27 | async-start | bytes 5242880 | tf_op jit(solution)/shard_map/while/body/eval_jaxpr/reduce_scatter | solution.py:234
  2023.7 379.3 %reduce-scatter.26.cloned.1.call-start = ((), (), s32[]{:S(2)}) async-start(), calls=%async_computation.22 | async-start | bytes 1179648 | tf_op jit(solution)/shard_map/while/body/eval_jaxpr/reduce_scatter | solution.py:351
  2073.0 331.0 %reduce-scatter.20.cloned.1.call-start = ((), (), s32[]{:S(2)}) async-start(), calls=%async_computation.19 | async-start | bytes 1179648 | tf_op jit(solution)/shard_map/while/body/eval_jaxpr/reduce_scatter | solution.py:348
  2370.6 107.2 %reduce-scatter.24.cloned.1.call-start = ((), (), s32[]{:S(2)}) async-start(), calls=%async_computation.21 | async-start | bytes 1179648 | tf_op jit(solution)/shard_map/while/body/eval_jaxpr/reduce_scatter | solution.py:350
  2376.5 180.4 %reduce-scatter.34.cloned.1.call-start = ((), (), s32[]{:S(2)}) async-start(), calls=%async_computation.26 | async-start | bytes 5242880 | tf_op jit(solution)/shard_map/while/body/eval_jaxpr/reduce_scatter | solution.py:322
  (128 other events, 5006.4 us)
Sparse Core Ops, SparseCore 0:
  32.9 81.0 all-gather.30
  303.7 75.2 reduce-scatter.15
  381.1 28.4 all-gather.34
  411.0 80.7 all-gather.32
  522.0 80.7 all-gather.38
  626.2 75.2 reduce-scatter.17
  709.4 81.2 all-gather.40
  793.7 32.6 reduce-scatter.31
  829.6 51.3 reduce-scatter.27
  884.7 51.3 reduce-scatter.29
  938.2 76.7 reduce-scatter.35
  1018.2 36.5 reduce-scatter.25
  1086.6 35.3 reduce-scatter.19
  1125.0 35.9 reduce-scatter.21
  1164.1 36.0 reduce-scatter.23
  1202.4 76.7 reduce-scatter.33
  1310.8 80.3 all-gather.30
  1581.2 75.2 reduce-scatter.15
  1658.4 28.4 all-gather.34
  1688.5 80.7 all-gather.32
  1799.8 80.7 all-gather.38
  1904.0 75.2 reduce-scatter.17
  1987.2 81.2 all-gather.40
  2071.4 32.6 reduce-scatter.31
  2107.3 51.3 reduce-scatter.27
  2162.4 51.3 reduce-scatter.29
  2216.1 76.7 reduce-scatter.35
  2295.8 36.5 reduce-scatter.25
  2364.3 35.2 reduce-scatter.19
  2402.7 35.9 reduce-scatter.21
  2441.8 35.9 reduce-scatter.23
  2480.2 76.7 reduce-scatter.33
  (2 shorter events, 53.3 us)
where the time goes:
time: 2620 us
  waiting for transfers between devices  1130 us (43%)
  matrix products  662 us (25%)
  other arithmetic  258 us (10%)
  local copies, waits for them, and re-layouts  256 us (10%)
  blocking collectives  226 us (9%)
  loops' own time  69.5 us (3%)
    dot_general x16, matrix products, block_scores(): jnp.einsum('qhd,khd->hqk', query_rows, key_heads, preferred_element_type=...  204 us
    all_gather x2, waiting for transfers between devices, micro_step(): grad_all = lax.all_gather(grad_given, 'tensor', axis=0, tiled=True)  165 us
    all_gather x2, waiting for transfers between devices, micro_step(): normed_two_all = lax.all_gather(normed_two, 'tensor', axis=0, tiled=True)  165 us
    reshape x32, local copies, waits for them, and re-layouts, block_mask(): expanded = jnp.repeat(jnp.repeat(table_rows, BLOCK, axis=1), BLOCK, axis=2)  158 us
    reduce_scatter x2, waiting for transfers between devices, micro_step(): lax.psum_scatter((from_query + from_key + from_value).astype(jnp.bfloat16...  156 us
    reduce_scatter x2, waiting for transfers between devices, micro_step(): lax.psum_scatter(jnp.dot(row_slice(grad_up_val, jnp.int32(0), local_rows...  150 us
    reduce_scatter x2, waiting for transfers between devices, micro_step(): lax.psum_scatter(jnp.dot(row_slice(context, jnp.int32(0), local_rows * la...  114 us
    convert_element_type x8, other arithmetic, one_block(): grad_scores = (attn_probs * (grad_probs - row_delta)).astype(jnp.bfloat16)  94.7 us
  transfers between devices with their start and end apart: 34, of which 22 were waited for; matrix products, arithmetic and copies ran while one was open for 27% of the time, Pallas kernels for 0%

commit v1 on v0

v1 whole, which is shorter than its diff:
```python
import functools
import jax
import jax.numpy as jnp
from jax import lax
from jax.sharding import PartitionSpec as P
from jax.experimental import pallas as pl
from jax.experimental.pallas import tpu as pltpu

HD = 64
BLOCK = 64
COMMON = 5
RAND = 3
BIG = 1e30
bf16 = jnp.bfloat16
f32 = jnp.float32


def dot_nt(left, right):
    return lax.dot_general(left, right, (((1,), (1,)), ((), ())), preferred_element_type=f32)


def dot_tn(left, right):
    return lax.dot_general(left, right, (((0,), (0,)), ((), ())), preferred_element_type=f32)


def dot_nn(left, right):
    return lax.dot_general(left, right, (((1,), (0,)), ((), ())), preferred_element_type=f32)


def low_half(shape):
    return lax.broadcasted_iota(jnp.int32, shape, 1) % 128 < HD


def slot_offsets(tab, layout, pair, block):
    common_at, rand_at, blocks, heads = layout
    shared = [
        pl.multiple_of(tab[common_at + block * COMMON + slot], BLOCK) for slot in range(COMMON)
    ]
    first = rand_at + (2 * pair * blocks + block) * RAND
    second = first + blocks * RAND
    drawn = [
        (pl.multiple_of(tab[first + slot], BLOCK), pl.multiple_of(tab[second + slot], BLOCK))
        for slot in range(RAND)
    ]
    return shared, drawn


def gather_rows(ref, shared, drawn, width):
    keep = low_half((BLOCK, width))
    parts = [ref[pl.ds(start, BLOCK), :width] for start in shared]
    for left, right in drawn:
        parts.append(
            jnp.where(keep, ref[pl.ds(left, BLOCK), :width], ref[pl.ds(right, BLOCK), :width])
        )
    return jnp.concatenate(parts, axis=0)


def block_diag(rows):
    keep = low_half(rows.shape)
    zero = jnp.zeros_like(rows)
    return jnp.concatenate([jnp.where(keep, rows, zero), jnp.where(keep, zero, rows)], axis=0)


def fold_heads(rows):
    keep = low_half((BLOCK, 128))
    return jnp.where(keep, rows[:BLOCK], rows[BLOCK:])


def query_rows(qbuf, kaug, start):
    scaled = qbuf[pl.ds(start, BLOCK), :]
    hot = kaug[pl.ds(start, BLOCK), 128:]
    penalty = (hot - jnp.ones_like(hot)) * jnp.asarray(BIG, bf16)
    return block_diag(jnp.concatenate([scaled, penalty], axis=1))


def fill_keys(tab, layout, seg_ref, kaug, half, k_own, k_oth):
    blocks = layout[2]

    @pl.when(pl.program_id(0) == 0)
    def _():
        lane = lax.broadcasted_iota(jnp.int32, (BLOCK, 128), 1) % HD

        def one(block, carry):
            row = pl.multiple_of(tab[block], BLOCK)
            seg = seg_ref[pl.ds(pl.multiple_of(block * BLOCK, BLOCK), BLOCK), :]
            kaug[pl.ds(row, BLOCK), 128:] = jnp.where(seg == lane, 1.0, 0.0).astype(bf16)
            return carry

        lax.fori_loop(0, blocks, one, 0)
        kaug[2 * half :, :128] = jnp.zeros((BLOCK, 128), bf16)
        kaug[2 * half :, 128:] = jnp.where(lane == HD - 1, 1.0, 0.0).astype(bf16)

    kaug[:half, :128] = k_own[0]
    kaug[half : 2 * half, :128] = k_oth[0]


def attn_fwd_kernel(
    layout, unroll, tab, q_own, q_oth, k_own, k_oth, v_own, v_oth, seg_ref,
    out_own, out_oth, lse_ref, kaug, vbuf, qbuf, obuf, sbuf,
):
    pair = pl.program_id(0)
    half = q_own.shape[1]
    blocks = layout[2]
    fill_keys(tab, layout, seg_ref, kaug, half, k_own, k_oth)
    vbuf[:half, :] = v_own[0]
    vbuf[half : 2 * half, :] = v_oth[0]
    vbuf[2 * half :, :] = jnp.zeros((BLOCK, 128), bf16)
    scale = jnp.asarray(0.125, bf16)
    qbuf[:half, :] = q_own[0] * scale
    qbuf[half:, :] = q_oth[0] * scale

    def one_block(block):
        row = pl.multiple_of(tab[block], BLOCK)
        shared, drawn = slot_offsets(tab, layout, pair, block)
        scores = dot_nt(gather_rows(kaug, shared, drawn, 256), query_rows(qbuf, kaug, row))
        top = jnp.max(scores, axis=0, keepdims=True)
        weight = jnp.exp(scores - top)
        total = jnp.sum(weight, axis=0, keepdims=True)
        probs = (weight * (1.0 / total)).astype(bf16)
        context = dot_tn(probs, gather_rows(vbuf, shared, drawn, 128))
        obuf[pl.ds(row, BLOCK), :] = fold_heads(context).astype(bf16)
        lse_ref[0, pl.ds(block, 1), :] = top + jnp.log(total)

    def step(index, carry):
        for part in range(unroll):
            one_block(index * unroll + part)
        return carry

    lax.fori_loop(0, blocks // unroll, step, 0)

    def dense_block(block):
        row = pl.multiple_of(tab[block], BLOCK)
        query = query_rows(qbuf, kaug, row)
        chunk = 512
        count = 2 * half // chunk
        top = jnp.full((1, 128), -3e38, f32)
        for part in range(count):
            scores = dot_nt(kaug[part * chunk : (part + 1) * chunk, :], query)
            sbuf[part * chunk : (part + 1) * chunk, :] = scores
            top = jnp.maximum(top, jnp.max(scores, axis=0, keepdims=True))
        total = jnp.zeros((1, 128), f32)
        for part in range(count):
            weight = jnp.exp(sbuf[part * chunk : (part + 1) * chunk, :] - top)
            sbuf[part * chunk : (part + 1) * chunk, :] = weight
            total = total + jnp.sum(weight, axis=0, keepdims=True)
        inverse = 1.0 / total
        context = jnp.zeros((128, 128), f32)
        for part in range(count):
            probs = (sbuf[part * chunk : (part + 1) * chunk, :] * inverse).astype(bf16)
            context = context + dot_tn(probs, vbuf[part * chunk : (part + 1) * chunk, :])
        obuf[pl.ds(row, BLOCK), :] = fold_heads(context).astype(bf16)
        lse_ref[0, pl.ds(block, 1), :] = top + jnp.log(total)

    first, second = tab[blocks], tab[blocks + 1]

    def dense_step(index, carry):
        dense_block(jnp.where(index == 0, first, second))
        return carry

    lax.fori_loop(0, jnp.where(first == second, 1, 2), dense_step, 0)
    out_own[0] = obuf[:half, :]
    out_oth[0] = obuf[half:, :]


def attn_bwd_kernel(
    layout, unroll, tab, q_own, q_oth, k_own, k_oth, v_own, v_oth, g_own, g_oth, seg_ref, lse_ref,
    dq_own, dq_oth, dk_own, dk_oth, dv_own, dv_oth,
    kaug, vbuf, qbuf, gbuf, dqbuf, dkbuf, dvbuf, sbuf, tbuf,
):
    pair = pl.program_id(0)
    half = q_own.shape[1]
    blocks = layout[2]
    fill_keys(tab, layout, seg_ref, kaug, half, k_own, k_oth)
    vbuf[:half, :] = v_own[0]
    vbuf[half : 2 * half, :] = v_oth[0]
    vbuf[2 * half :, :] = jnp.zeros((BLOCK, 128), bf16)
    scale = jnp.asarray(0.125, bf16)
    qbuf[:half, :] = q_own[0] * scale
    qbuf[half:, :] = q_oth[0] * scale
    gbuf[:half, :] = g_own[0]
    gbuf[half:, :] = g_oth[0]
    dkbuf[...] = jnp.zeros_like(dkbuf)
    dvbuf[...] = jnp.zeros_like(dvbuf)
    keep = low_half((BLOCK, 128))

    def scatter(ref, update, shared, drawn):
        for slot, start in enumerate(shared):
            ref[pl.ds(start, BLOCK), :] += update[slot * BLOCK : (slot + 1) * BLOCK]
        for slot, (left, right) in enumerate(drawn):
            at = (COMMON + slot) * BLOCK
            piece = update[at : at + BLOCK]
            ref[pl.ds(left, BLOCK), :] += jnp.where(keep, piece, 0.0)
            ref[pl.ds(right, BLOCK), :] += jnp.where(keep, 0.0, piece)

    def one_block(block):
        row = pl.multiple_of(tab[block], BLOCK)
        shared, drawn = slot_offsets(tab, layout, pair, block)
        query = query_rows(qbuf, kaug, row)
        grad = block_diag(gbuf[pl.ds(row, BLOCK), :])
        keys = gather_rows(kaug, shared, drawn, 256)
        scores = dot_nt(keys, query)
        probs = jnp.exp(scores - lse_ref[0, pl.ds(block, 1), :])
        grad_probs = dot_nt(gather_rows(vbuf, shared, drawn, 128), grad)
        delta = jnp.sum(probs * grad_probs, axis=0, keepdims=True)
        grad_scores = (probs * (grad_probs - delta)).astype(bf16)
        grad_query = dot_tn(grad_scores, keys[:, :128])
        dqbuf[pl.ds(row, BLOCK), :] = (fold_heads(grad_query) * 0.125).astype(bf16)
        scatter(dkbuf, dot_nn(grad_scores, query[:, :128]), shared, drawn)
        scatter(dvbuf, dot_nn(probs.astype(bf16), grad), shared, drawn)

    def step(index, carry):
        for part in range(unroll):
            one_block(index * unroll + part)
        return carry

    lax.fori_loop(0, blocks // unroll, step, 0)

    def dense_block(block):
        row = pl.multiple_of(tab[block], BLOCK)
        query = query_rows(qbuf, kaug, row)
        grad = block_diag(gbuf[pl.ds(row, BLOCK), :])
        lse = lse_ref[0, pl.ds(block, 1), :]
        chunk = 512
        count = 2 * half // chunk
        delta = jnp.zeros((1, 128), f32)
        for part in range(count):
            here = slice(part * chunk, (part + 1) * chunk)
            probs = jnp.exp(dot_nt(kaug[here, :], query) - lse)
            grad_probs = dot_nt(vbuf[here, :], grad)
            delta = delta + jnp.sum(probs * grad_probs, axis=0, keepdims=True)
            sbuf[here, :] = probs
            tbuf[here, :] = grad_probs
        grad_query = jnp.zeros((128, 128), f32)
        for part in range(count):
            here = slice(part * chunk, (part + 1) * chunk)
            probs = sbuf[here, :]
            grad_scores = (probs * (tbuf[here, :] - delta)).astype(bf16)
            grad_query = grad_query + dot_tn(grad_scores, kaug[here, :128])
            dkbuf[here, :] += dot_nn(grad_scores, query[:, :128])
            dvbuf[here, :] += dot_nn(probs.astype(bf16), grad)
        dqbuf[pl.ds(row, BLOCK), :] = (fold_heads(grad_query) * 0.125).astype(bf16)

    first, second = tab[blocks], tab[blocks + 1]

    def dense_step(index, carry):
        dense_block(jnp.where(index == 0, first, second))
        return carry

    lax.fori_loop(0, jnp.where(first == second, 1, 2), dense_step, 0)
    dq_own[0] = dqbuf[:half, :]
    dq_oth[0] = dqbuf[half:, :]
    dk_own[0] = dkbuf[:half, :].astype(bf16)
    dk_oth[0] = dkbuf[half : 2 * half, :].astype(bf16)
    dv_own[0] = dvbuf[:half, :].astype(bf16)
    dv_oth[0] = dvbuf[half : 2 * half, :].astype(bf16)


def table_layout(blocks, heads):
    common_at = blocks + 2
    rand_at = common_at + blocks * COMMON
    return (common_at, rand_at, blocks, heads)


def attention_table(rand_heads, glob_row, row_of, dummy_row):
    heads, blocks, _ = rand_heads.shape
    index = jnp.arange(blocks, dtype=jnp.int32)
    g0, g1 = glob_row[0], glob_row[1]
    dense = (index == g0) | (index == g1)
    near0, near1 = jnp.abs(index - g0) <= 1, jnp.abs(index - g1) <= 1
    full = jnp.broadcast_to
    shared = jnp.stack([index - 1, index, index + 1, full(g0, (blocks,)), full(g1, (blocks,))], axis=1)
    valid = jnp.stack(
        [index > 0, index >= 0, index < blocks - 1, ~near0, ~near1 & (g1 != g0)], axis=1
    ) & ~dense[:, None]
    shared = jnp.where(valid, row_of(jnp.clip(shared, 0, blocks - 1)), dummy_row)
    far = jnp.abs(rand_heads - index[None, :, None]) > 1
    far = far & (rand_heads != g0) & (rand_heads != g1) & ~dense[None, :, None]
    r0, r1, r2 = rand_heads[..., 0], rand_heads[..., 1], rand_heads[..., 2]
    fresh = jnp.stack([r0 == r0, r1 != r0, (r2 != r0) & (r2 != r1)], axis=-1)
    drawn = jnp.where(far & fresh, row_of(rand_heads), dummy_row)
    return jnp.concatenate(
        [row_of(index), glob_row, shared.reshape(-1), drawn.reshape(-1)]
    ).astype(jnp.int32)


def lane_spec(half, column):
    return pl.BlockSpec((1, half, 128), lambda p, tab: (p // 2, 0, column * 2 + p % 2))


def attn_fwd(tab, qkv_own, qkv_oth, seg_abs, blocks, unroll=4):
    half = qkv_own.shape[1]
    slots = qkv_own.shape[0]
    pairs = 2 * slots
    layout = table_layout(blocks, 2 * pairs)
    rows = 2 * half + BLOCK
    shape = jax.ShapeDtypeStruct((slots, half, 256), bf16)
    return pl.pallas_call(
        functools.partial(attn_fwd_kernel, layout, unroll),
        out_shape=(shape, shape, jax.ShapeDtypeStruct((pairs, blocks, 128), f32)),
        grid_spec=pltpu.PrefetchScalarGridSpec(
            num_scalar_prefetch=1,
            grid=(pairs,),
            in_specs=[
                lane_spec(half, 0), lane_spec(half, 0), lane_spec(half, 1), lane_spec(half, 1),
                lane_spec(half, 2), lane_spec(half, 2),
                pl.BlockSpec((2 * half, 128), lambda p, tab: (0, 0)),
            ],
            out_specs=(
                lane_spec(half, 0), lane_spec(half, 0),
                pl.BlockSpec((1, blocks, 128), lambda p, tab: (p, 0, 0)),
            ),
            scratch_shapes=[
                pltpu.VMEM((rows, 256), bf16), pltpu.VMEM((rows, 128), bf16),
                pltpu.VMEM((2 * half, 128), bf16), pltpu.VMEM((2 * half, 128), bf16),
                pltpu.VMEM((2 * half, 128), f32),
            ],
        ),
        compiler_params=pltpu.CompilerParams(vmem_limit_bytes=40 << 20),
        cost_estimate=pl.CostEstimate(flops=4 * 10**9, bytes_accessed=8 * 10**6, transcendentals=10**7),
        name="attn_fwd",
    )(tab, qkv_own, qkv_oth, qkv_own, qkv_oth, qkv_own, qkv_oth, seg_abs)


def attn_bwd(tab, qkv_own, qkv_oth, grad_own, grad_oth, seg_abs, lse, blocks, unroll=4):
    half = qkv_own.shape[1]
    slots = qkv_own.shape[0]
    pairs = 2 * slots
    layout = table_layout(blocks, 2 * pairs)
    rows = 2 * half + BLOCK
    shape = jax.ShapeDtypeStruct((slots, half, 256), bf16)
    return pl.pallas_call(
        functools.partial(attn_bwd_kernel, layout, unroll),
        out_shape=(shape,) * 6,
        grid_spec=pltpu.PrefetchScalarGridSpec(
            num_scalar_prefetch=1,
            grid=(pairs,),
            in_specs=[
                lane_spec(half, 0), lane_spec(half, 0), lane_spec(half, 1), lane_spec(half, 1),
                lane_spec(half, 2), lane_spec(half, 2), lane_spec(half, 0), lane_spec(half, 0),
                pl.BlockSpec((2 * half, 128), lambda p, tab: (0, 0)),
                pl.BlockSpec((1, blocks, 128), lambda p, tab: (p, 0, 0)),
            ],
            out_specs=(lane_spec(half, 0),) * 6,
            scratch_shapes=[
                pltpu.VMEM((rows, 256), bf16), pltpu.VMEM((rows, 128), bf16),
                pltpu.VMEM((2 * half, 128), bf16), pltpu.VMEM((2 * half, 128), bf16),
                pltpu.VMEM((2 * half, 128), bf16),
                pltpu.VMEM((rows, 128), f32), pltpu.VMEM((rows, 128), f32),
                pltpu.VMEM((2 * half, 128), f32), pltpu.VMEM((2 * half, 128), f32),
            ],
        ),
        compiler_params=pltpu.CompilerParams(vmem_limit_bytes=48 << 20),
        cost_estimate=pl.CostEstimate(flops=10**10, bytes_accessed=16 * 10**6, transcendentals=10**7),
        name="attn_bwd",
    )(tab, qkv_own, qkv_oth, qkv_own, qkv_oth, qkv_own, qkv_oth, grad_own, grad_oth, seg_abs, lse)


EPS = 1e-05
BOTH = ("dp", "tensor")
ROWS = 256


def gelu_pair(u):
    c = 0.7978845608028654
    square = u * u
    bend = jnp.tanh(u * (c + (c * 0.044715) * square))
    half = 0.5 * (1.0 + bend)
    slope = half + (0.5 * u) * (1.0 - bend * bend) * (c + (3.0 * c * 0.044715) * square)
    return u * half, slope


def normalise(rows):
    center = rows - jnp.mean(rows, axis=-1, keepdims=True)
    inverse = lax.rsqrt(jnp.mean(center * center, axis=-1, keepdims=True) + EPS)
    return center * inverse, inverse


def norm_back(grad, unit, inverse, gain):
    scaled = grad * gain
    mean = jnp.mean(scaled, axis=-1, keepdims=True)
    along = jnp.mean(scaled * unit, axis=-1, keepdims=True)
    return inverse * (scaled - mean - unit * along)


def params(mib):
    return pltpu.CompilerParams(vmem_limit_bytes=mib << 20)


def project_kernel(core, x_ref, vec_ref, w_ref, send_ref, own_ref, n_ref, nbuf):
    slot, tile = pl.program_id(0), pl.program_id(1)
    here = pl.ds(pl.multiple_of(tile * ROWS, ROWS), ROWS)

    @pl.when(slot == 0)
    def _():
        unit, _ = normalise(x_ref[...].astype(f32))
        normed = (unit * vec_ref[0:1, :] + vec_ref[1:2, :]).astype(bf16)
        nbuf[here, :] = normed
        n_ref[...] = normed

    width = send_ref.shape[2]
    result = dot_nn(nbuf[here, :], w_ref[0, :, :width]).astype(bf16)

    @pl.when(slot < 2)
    def _():
        send_ref[0] = result

    @pl.when(slot >= 2)
    def _():
        own_ref[0] = result


def project(core, x, vecs, weights):
    rows, width = x.shape
    tiles = rows // ROWS
    out = width * 3 // 4
    shape = jax.ShapeDtypeStruct((2, rows, out), bf16)
    return pl.pallas_call(
        project_kernel,
        out_shape=(shape, shape, jax.ShapeDtypeStruct((rows, width), bf16)),
        grid_spec=pltpu.PrefetchScalarGridSpec(
            num_scalar_prefetch=1,
            grid=(4, tiles),
            in_specs=[
                pl.BlockSpec((ROWS, width), lambda s, i, c: (jnp.where(s == 0, i, tiles - 1), 0)),
                pl.BlockSpec(vecs.shape, lambda s, i, c: (0, 0)),
                pl.BlockSpec((1, width, width), lambda s, i, c: ((2 - 2 * c[0] + s) % 4, 0, 0)),
            ],
            out_specs=(
                pl.BlockSpec(
                    (1, ROWS, out),
                    lambda s, i, c: (jnp.minimum(s, 1), jnp.where(s < 2, i, tiles - 1), 0),
                ),
                pl.BlockSpec(
                    (1, ROWS, out),
                    lambda s, i, c: (jnp.maximum(s - 2, 0), jnp.where(s < 2, 0, i), 0),
                ),
                pl.BlockSpec((ROWS, width), lambda s, i, c: (jnp.where(s == 0, i, tiles - 1), 0)),
            ),
            scratch_shapes=[pltpu.VMEM((rows, width), bf16)],
        ),
        compiler_params=params(40),
        name="project",
    )(core, x, vecs, weights)


def out_kernel(core, x_ref, own_ref, oth_ref, w0, w1, w2, w3, vec_ref, resid_ref, n_ref):
    total = x_ref[...].astype(f32)
    total = total + dot_nt(own_ref[0], w0[0]) + dot_nt(own_ref[1], w1[0])
    total = total + dot_nt(oth_ref[0], w2[0]) + dot_nt(oth_ref[1], w3[0])
    resid_ref[...] = total
    unit, _ = normalise(total)
    n_ref[...] = (unit * vec_ref[2:3, :] + vec_ref[3:4, :]).astype(bf16)


def out_weight_specs(width):
    return [
        pl.BlockSpec((1, width, width // 4), lambda i, c, s=s: ((2 * c[0] + s) % 4, 0, 3))
        for s in range(4)
    ]


def out_project(core, x, ctx_own, ctx_oth, weights, vecs):
    rows, width = x.shape
    tile = pl.BlockSpec((ROWS, width), lambda i, c: (i, 0))
    part = pl.BlockSpec((2, ROWS, width // 4), lambda i, c: (0, i, 0))
    return pl.pallas_call(
        out_kernel,
        out_shape=(
            jax.ShapeDtypeStruct((rows, width), f32), jax.ShapeDtypeStruct((rows, width), bf16),
        ),
        grid_spec=pltpu.PrefetchScalarGridSpec(
            num_scalar_prefetch=1,
            grid=(rows // ROWS,),
            in_specs=[tile, part, part, *out_weight_specs(width),
                      pl.BlockSpec(vecs.shape, lambda i, c: (0, 0))],
            out_specs=(tile, tile),
        ),
        compiler_params=params(32),
        name="out_project",
    )(core, x, ctx_own, ctx_oth, weights, weights, weights, weights, vecs)


def ffn_kernel(n_ref, cot_ref, up_ref, down_ref, bias_ref,
               ffn_ref, gn_ref, gup_ref, gdown_ref, gbias_ref, nt, ct, act, gup):
    slot = pl.program_id(0)
    rows = n_ref.shape[0]

    @pl.when(slot == 0)
    def _():
        for at in range(0, rows, ROWS):
            nt[:, at : at + ROWS] = n_ref[at : at + ROWS, :].T
            ct[:, at : at + ROWS] = cot_ref[at : at + ROWS, :].T
        ffn_ref[...] = jnp.zeros_like(ffn_ref)
        gn_ref[...] = jnp.zeros_like(gn_ref)

    gbias_ref[...] = jnp.zeros_like(gbias_ref)

    def tile(index, carry):
        here = pl.ds(pl.multiple_of(index * ROWS, ROWS), ROWS)
        value = dot_nn(n_ref[here, :], up_ref[0]) + bias_ref[0]
        out, slope = gelu_pair(value)
        out = out.astype(bf16)
        act[here, :] = out
        back = (dot_nn(cot_ref[here, :], down_ref[0]) * slope).astype(bf16)
        gup[here, :] = back
        gbias_ref[0] += jnp.sum(back.astype(f32), axis=0, keepdims=True)
        ffn_ref[here, :] += dot_nt(out, down_ref[0])
        gn_ref[here, :] += dot_nt(back, up_ref[0])
        return carry

    lax.fori_loop(0, rows // ROWS, tile, 0)

    def grads(index, carry):
        here = pl.ds(pl.multiple_of(index * ROWS, ROWS), ROWS)
        gup_ref[0, here, :] = dot_nn(nt[here, :], gup[...]).astype(bf16)
        gdown_ref[0, here, :] = dot_nn(ct[here, :], act[...]).astype(bf16)
        return carry

    lax.fori_loop(0, gup_ref.shape[1] // ROWS, grads, 0)


def feed_forward(normed, cot, up, down, bias):
    rows, width = normed.shape
    slots, _, hidden = up.shape
    once = pl.Buffered(1)
    whole = pl.BlockSpec((rows, width), lambda s: (0, 0), pipeline_mode=once)
    weight = pl.BlockSpec((1, width, hidden), lambda s: (s, 0, 0))
    vector = pl.BlockSpec((1, 1, hidden), lambda s: (s, 0, 0))
    total = pl.BlockSpec((rows, width), lambda s: (0, 0))
    return pl.pallas_call(
        ffn_kernel,
        out_shape=(
            jax.ShapeDtypeStruct((rows, width), f32), jax.ShapeDtypeStruct((rows, width), f32),
            jax.ShapeDtypeStruct(up.shape, bf16), jax.ShapeDtypeStruct(up.shape, bf16),
            jax.ShapeDtypeStruct((slots, 1, hidden), f32),
        ),
        grid=(slots,),
        in_specs=[whole, whole, weight, weight, vector],
        out_specs=(total, total, weight, weight, vector),
        scratch_shapes=[
            pltpu.VMEM((width, rows), bf16), pltpu.VMEM((width, rows), bf16),
            pltpu.VMEM((rows, hidden), bf16), pltpu.VMEM((rows, hidden), bf16),
        ],
        compiler_params=params(58),
        name="feed_forward",
    )(normed, cot, up, down, bias)


def mid_kernel(core, resid_ref, ffn_ref, gn_ref, cot_ref, w0, w1, w2, w3, vec_ref,
               out_ref, gres_ref, low_ref, own_ref, send_ref, sums_ref):
    tile = pl.program_id(0)
    resid = resid_ref[...]
    cot = cot_ref[...].astype(f32)
    out_ref[...] = (resid + ffn_ref[...] + vec_ref[4:5, :]).astype(bf16)
    unit, inverse = normalise(resid)
    grad = gn_ref[...]
    gres = cot + norm_back(grad, unit, inverse, vec_ref[2:3, :])
    gres_ref[...] = gres
    low = gres.astype(bf16)
    low_ref[...] = low
    own_ref[0] = dot_nn(low, w0[0]).astype(bf16)
    own_ref[1] = dot_nn(low, w1[0]).astype(bf16)
    send_ref[0] = dot_nn(low, w2[0]).astype(bf16)
    send_ref[1] = dot_nn(low, w3[0]).astype(bf16)

    @pl.when(tile == 0)
    def _():
        sums_ref[...] = jnp.zeros_like(sums_ref)

    sums_ref[0:1, :] += jnp.sum(grad * unit, axis=0, keepdims=True)
    sums_ref[1:2, :] += jnp.sum(grad, axis=0, keepdims=True)
    sums_ref[2:3, :] += jnp.sum(cot, axis=0, keepdims=True)


def middle(core, resid, ffn, gn, cot, weights, vecs):
    rows, width = resid.shape
    tile = pl.BlockSpec((ROWS, width), lambda i, c: (i, 0))
    part = pl.BlockSpec((2, ROWS, width // 4), lambda i, c: (0, i, 0))
    piece = jax.ShapeDtypeStruct((2, rows, width // 4), bf16)
    return pl.pallas_call(
        mid_kernel,
        out_shape=(
            jax.ShapeDtypeStruct((rows, width), bf16), jax.ShapeDtypeStruct((rows, width), f32),
            jax.ShapeDtypeStruct((rows, width), bf16), piece, piece,
            jax.ShapeDtypeStruct((8, width), f32),
        ),
        grid_spec=pltpu.PrefetchScalarGridSpec(
            num_scalar_prefetch=1,
            grid=(rows // ROWS,),
            in_specs=[tile, tile, tile, tile, *out_weight_specs(width),
                      pl.BlockSpec(vecs.shape, lambda i, c: (0, 0))],
            out_specs=(tile, tile, tile, part, part, pl.BlockSpec((8, width), lambda i, c: (0, 0))),
        ),
        compiler_params=params(48),
        name="middle",
    )(core, resid, ffn, gn, cot, weights, weights, weights, weights, vecs)


def last_kernel(core, x_ref, n_ref, low_ref, gres_ref, dq0, dk0, dv0, c0, dq1, dk1, dv1, c1,
                w_ref, vec_ref, gin_ref, gw_ref, sums_ref, nt, lt, gn):
    slot = pl.program_id(0)
    rows, width = n_ref.shape
    quarter = width // 4

    @pl.when(slot == 0)
    def _():
        for at in range(0, rows, ROWS):
            nt[:, at : at + ROWS] = n_ref[at : at + ROWS, :].T
            lt[:, at : at + ROWS] = low_ref[at : at + ROWS, :].T
        gn[...] = jnp.zeros_like(gn)

    def work(refs):
        def tile(index, carry):
            here = pl.ds(pl.multiple_of(index * ROWS, ROWS), ROWS)
            total = gn[here, :]
            for part in range(3):
                columns = slice(part * quarter, (part + 1) * quarter)
                total = total + dot_nt(refs[part][0, here, :], w_ref[0, :, columns])
            gn[here, :] = total
            return carry

        lax.fori_loop(0, rows // ROWS, tile, 0)

        def grads(index, carry):
            here = pl.ds(pl.multiple_of(index * ROWS, ROWS), ROWS)
            for part in range(4):
                columns = slice(part * quarter, (part + 1) * quarter)
                left = lt if part == 3 else nt
                gw_ref[0, here, columns] = dot_nn(left[here, :], refs[part][0]).astype(bf16)
            return carry

        lax.fori_loop(0, width // ROWS, grads, 0)

    @pl.when(slot < 2)
    def _():
        work((dq0, dk0, dv0, c0))

    @pl.when(slot >= 2)
    def _():
        work((dq1, dk1, dv1, c1))

    @pl.when(slot == 3)
    def _():
        sums_ref[...] = jnp.zeros_like(sums_ref)

        def tile(index, carry):
            here = pl.ds(pl.multiple_of(index * ROWS, ROWS), ROWS)
            unit, inverse = normalise(x_ref[here, :].astype(f32))
            grad = gn[here, :]
            result = gres_ref[here, :] + norm_back(grad, unit, inverse, vec_ref[0:1, :])
            gin_ref[here, :] = result.astype(bf16)
            sums_ref[0:1, :] += jnp.sum(grad * unit, axis=0, keepdims=True)
            sums_ref[1:2, :] += jnp.sum(grad, axis=0, keepdims=True)
            return carry

        lax.fori_loop(0, rows // ROWS, tile, 0)


def last(core, x, normed, low, gres, own, oth, weights, vecs):
    rows, width = x.shape
    once = pl.Buffered(1)
    whole = pl.BlockSpec((rows, width), lambda s, c: (0, 0), pipeline_mode=once)
    first = pl.BlockSpec((1, rows, width // 4), lambda s, c: (jnp.minimum(s, 1), 0, 0))
    second = pl.BlockSpec((1, rows, width // 4), lambda s, c: (jnp.maximum(s - 2, 0), 0, 0))
    weight = pl.BlockSpec((1, width, width), lambda s, c: ((2 * c[0] + s) % 4, 0, 0))
    return pl.pallas_call(
        last_kernel,
        out_shape=(
            jax.ShapeDtypeStruct((rows, width), bf16),
            jax.ShapeDtypeStruct((4, width, width), bf16),
            jax.ShapeDtypeStruct((8, width), f32),
        ),
        grid_spec=pltpu.PrefetchScalarGridSpec(
            num_scalar_prefetch=1,
            grid=(4,),
            in_specs=[whole, whole, whole, whole, *[first] * 4, *[second] * 4, weight,
                      pl.BlockSpec(vecs.shape, lambda s, c: (0, 0))],
            out_specs=(
                pl.BlockSpec((rows, width), lambda s, c: (0, 0)), weight,
                pl.BlockSpec((8, width), lambda s, c: (0, 0)),
            ),
            scratch_shapes=[
                pltpu.VMEM((width, rows), bf16), pltpu.VMEM((width, rows), bf16),
                pltpu.VMEM((rows, width), f32),
            ],
        ),
        compiler_params=params(58),
        name="last",
    )(core, x, normed, low, gres, *own, *oth, weights, vecs)


def token_routes(dp_count, tensor_count, turn):
    routes = []
    for d in range(dp_count):
        for z in range(tensor_count):
            piece = z ^ turn
            target = (d - d % 2 + piece % 2) * tensor_count + 2 * (piece // 2) + d % 2
            routes.append((d * tensor_count + z, target))
    return routes


def per_device(
    block_in, norm1_gain, norm1_bias, w_query, w_key, w_value, w_out, norm2_gain, norm2_bias,
    w_up, up_bias, w_down, down_bias, segments, rand_blocks, glob_blocks, cotangent,
):
    dp_count, tensor_count = lax.axis_size("dp"), lax.axis_size("tensor")
    d, z = lax.axis_index("dp"), lax.axis_index("tensor")
    core = d % 2
    core_ref = core.astype(jnp.int32)[None]
    batches, local, width = block_in.shape
    share = local // 2
    blocks = segments.shape[1] // BLOCK
    swap = [
        (a * tensor_count + b, (a ^ 1) * tensor_count + b)
        for a in range(dp_count)
        for b in range(tensor_count)
    ]

    def other_core(value):
        return lax.ppermute(value, BOTH, swap)

    routes = [token_routes(dp_count, tensor_count, turn) for turn in range(tensor_count)]

    def bring(value):
        pieces = value.reshape(2 * batches, share, width)
        return jnp.concatenate(
            [
                lax.ppermute(
                    lax.dynamic_index_in_dim(pieces, z ^ turn, 0, keepdims=False), BOTH, routes[turn]
                )
                for turn in range(tensor_count)
            ],
            axis=0,
        )

    def give(value):
        back = [
            lax.ppermute(
                value[turn * share : (turn + 1) * share], BOTH, [(b, a) for a, b in routes[turn]]
            )
            for turn in range(tensor_count)
        ]
        low_bit, high_bit = z % 2 == 1, z // 2 == 1
        pairs = [jnp.where(low_bit, back[t ^ 1], back[t]) for t in range(4)]
        whole = [jnp.where(high_bit, pairs[t ^ 2], pairs[t]) for t in range(4)]
        return jnp.stack(whole).reshape(batches, local, width)

    ints = jnp.concatenate([rand_blocks.reshape(batches, -1), glob_blocks.reshape(batches, -1)], axis=1)
    ints = lax.all_gather(ints, "tensor", axis=0, tiled=False)
    head_count = rand_blocks.shape[2]
    mine = jnp.concatenate([ints.reshape(-1), segments.reshape(-1)])
    theirs = other_core(mine)
    mine = jnp.where(z % 2 == core, mine, theirs)
    ints = mine[: ints.size].reshape(ints.shape)[:, z // 2]
    segment_row = lax.dynamic_index_in_dim(
        mine[ints.size * batches :].reshape(segments.shape), z // 2, 0, keepdims=False
    )
    rand_size = head_count * blocks * RAND
    rand_heads = lax.dynamic_slice_in_dim(ints, 2 * core, 2, 0)[:, :rand_size]
    rand_heads = rand_heads.reshape(2 * head_count, blocks, RAND)
    glob_row = ints[0, rand_size:]
    segment_lanes = jnp.broadcast_to(segment_row[:, None], (segment_row.shape[0], 128))
    per_piece = share // BLOCK
    half = tensor_count * share

    def row_of(block):
        source, place = block // (2 * per_piece), block % (2 * per_piece)
        side = place // per_piece
        position = source ^ (2 * (z // 2) + side)
        return (
            jnp.where(side == core, 0, half) + position * share + (place % per_piece) * BLOCK
        )

    table = attention_table(rand_heads, glob_row, row_of, 2 * half)

    vectors = jnp.stack(
        [norm1_gain, norm1_bias, norm2_gain, norm2_bias, down_bias, up_bias[0]]
    )
    vectors = lax.all_gather(vectors, BOTH, axis=0, tiled=False)
    vectors = vectors.reshape(dp_count, tensor_count, 6, -1).astype(f32)
    vecs = vectors[:, 0, :5].transpose(1, 0, 2).reshape(5, width)
    vecs = jnp.concatenate([vecs, jnp.zeros((3, width), f32)])
    up_shift = vectors[:, :, 5].transpose(1, 0, 2).reshape(tensor_count, 1, -1)

    def gather(shard):
        whole = lax.all_gather(shard, ("tensor", "dp"), axis=0, tiled=True)
        return whole.reshape(tensor_count, width, -1)

    attn_weights = gather(jnp.concatenate([w_query, w_key, w_value, w_out.T], axis=1))
    x = bring(block_in)
    cot = bring(cotangent)
    up = gather(w_up)
    down = gather(w_down.T)

    send, own, normed = project(core_ref, x, vecs, attn_weights)
    oth = other_core(send)
    ctx_own, ctx_send, lse = attn_fwd(table, own, oth, segment_lanes, blocks)
    ctx_oth = other_core(ctx_send)
    resid, normed_two = out_project(core_ref, x, ctx_own, ctx_oth, attn_weights, vecs)
    ffn, grad_two, grad_up, grad_down, grad_bias = feed_forward(normed_two, cot, up, down, up_shift)
    out, grad_resid, low, gctx_own, gctx_send, sums_two = middle(
        core_ref, resid, ffn, grad_two, cot, attn_weights, vecs
    )
    gctx_oth = other_core(gctx_send)
    block_out = give(out)
    dq0, dq1, dk0, dk1, dv0, dv1 = attn_bwd(
        table, own, oth, gctx_own, gctx_oth, segment_lanes, lse, blocks
    )
    dq1, dk1, dv1 = other_core(dq1), other_core(dk1), other_core(dv1)
    grad_in, grad_attn, sums_one = last(
        core_ref, x, normed, low, grad_resid,
        (dq0, dk0, dv0, ctx_own), (dq1, dk1, dv1, ctx_oth), attn_weights, vecs,
    )
    grad_in = give(grad_in).astype(f32)

    def scatter(units):
        flat = units.reshape(-1, units.shape[-1])
        return lax.psum_scatter(flat, ("tensor", "dp"), scatter_dimension=0, tiled=True).astype(f32)

    g_up, g_down, g_attn = scatter(grad_up), scatter(grad_down), scatter(grad_attn)
    quarter = width // 4
    five = jnp.concatenate([sums_one[:2], sums_two[:3]]).reshape(5, dp_count, tensor_count, -1)
    five = five.transpose(1, 2, 0, 3).reshape(dp_count * tensor_count, -1)
    shift = grad_bias.reshape(tensor_count, dp_count, -1).transpose(1, 0, 2)
    small = jnp.concatenate([five, shift.reshape(dp_count * tensor_count, -1)], axis=1)
    small = lax.psum_scatter(small, BOTH, scatter_dimension=0, tiled=True)[0]
    piece = width // (dp_count * tensor_count)
    vector_grads = [small[i * piece : (i + 1) * piece] for i in range(5)]
    return (
        block_out, grad_in, vector_grads[0], vector_grads[1],
        g_attn[:, :quarter], g_attn[:, quarter : 2 * quarter], g_attn[:, 2 * quarter : 3 * quarter],
        g_attn[:, 3 * quarter :].T, vector_grads[2], vector_grads[3],
        g_up, small[5 * piece :][None], g_down.T, vector_grads[4],
    )


def solution(mesh):
    rows, both = P(None, BOTH, None), P(BOTH)
    dp, split, turned = P("dp"), P("dp", "tensor"), P("tensor", "dp")
    return jax.shard_map(
        per_device,
        mesh=mesh,
        in_specs=(
            rows, dp, dp, split, split, split, turned, dp, dp, split, turned, turned, dp,
            P(None, "dp"), P(None, "dp", "tensor", None, None), P(None, "dp", None), rows,
        ),
        out_specs=(
            rows, rows, both, both, split, split, split, turned, both, both, split, turned, turned,
            both,
        ),
        check_vma=False,
    )
```

time: 2620 us -> 923 us (0.35)
  waiting for transfers between devices: 1130 us -> 279 us
  matrix products: 662 us -> 0 us
  Pallas kernels: 0 us -> 284 us
  other arithmetic: 258 us -> 13.5 us
  local copies, waits for them, and re-layouts: 256 us -> 65.7 us
  loops' own time: 69.5 us -> 0 us
  starting transfers between devices: 2.98 us -> 34.9 us
    dot_general x92 -> x0, matrix products: 662 us -> none  [the longest x16 204 us: block_scores(): jnp.einsum('qhd,khd->hqk', query_rows, key_heads, preferred_element_type=...]
    all_gather x12 -> x3, waiting for transfers between devices: 564 us -> 0.01 us  [gather(): whole = lax.all_gather(shard, ('tensor', 'dp'), axis=0, tiled=True)]
    reduce_scatter x20 -> x1, waiting for transfers between devices: 564 us -> 0.01 us  [scatter(): lax.psum_scatter(flat, ('tensor', 'dp'), scatter_dimension=0, tiled=True)]
    pallas_call x0 -> x7, Pallas kernels: none -> 284 us  [the longest x1 76.3 us: attn_bwd(): pl.pallas_call(functools.partial(attn_bwd_kernel, layout, unroll), out_sh...]
    unnamed x0 -> x8, waiting for transfers between devices: none -> 168 us
    reshape x32 -> x9, local copies, waits for them, and re-layouts: 158 us -> 0.86 us  [the longest x2 0.21 us: per_device(): rand_heads = rand_heads.reshape(2 * head_count, blocks, RAND)]
    ppermute x0 -> x23, waiting for transfers between devices: none -> 110 us  [the longest x8 54.7 us: give(): lax.ppermute(value[turn * share:(turn + 1) * share], BOTH, [(b, a) for a,...]
    convert_element_type x28 -> x3, other arithmetic: 111 us -> 4.31 us  [the longest x1 2.48 us: per_device(): grad_in = give(grad_in).astype(f32)]
  transfers between devices with their start and end apart: 34 -> 29, of which waited for: 22 -> 12; matrix products, arithmetic and copies ran while one was open for 27% -> 6% of each run, Pallas kernels for 0% -> 23%
where the time goes in v1:
time: 923 us; the launch traced here: 921 us
  Pallas kernels  284 us (31%)
  waiting for transfers between devices  279 us (30%)
  blocking collectives  229 us (25%)
  local copies, waits for them, and re-layouts  65.7 us (7%)
  starting transfers between devices  34.9 us (4%)
  between operations  16.2 us (2%)
  other arithmetic  13.5 us (1%)
    unnamed x8, waiting for transfers between devices  168 us
    unnamed x1, blocking collectives  90.2 us
    pallas_call x1, Pallas kernels, attn_bwd(): pl.pallas_call(functools.partial(attn_bwd_kernel, layout, unroll), out_sh...  76.3 us
    pallas_call x1, Pallas kernels, feed_forward(): pl.pallas_call(ffn_kernel, out_shape=(jax.ShapeDtypeStruct((rows, width),...  71.6 us
    all_gather x1, blocking collectives, per_device(): vectors = lax.all_gather(vectors, BOTH, axis=0, tiled=False)  69.5 us
    all_gather x1, blocking collectives, per_device(): ints = lax.all_gather(ints, 'tensor', axis=0, tiled=False)  68.9 us
    pallas_call x1, Pallas kernels, attn_fwd(): pl.pallas_call(functools.partial(attn_fwd_kernel, layout, unroll), out_sh...  67.6 us
    ppermute x8, waiting for transfers between devices, give(): lax.ppermute(value[turn * share:(turn + 1) * share], BOTH, [(b, a) for a,...  54.7 us
  transfers between devices with their start and end apart: 29, of which 12 were waited for; matrix products, arithmetic and copies ran while one was open for 6% of the time, Pallas kernels for 23%

profile of v1, /device:TPU:0, one launch (start us, length us, event | category | flops | bytes accessed | tf_op | source)
XLA Modules:
  0.0 921.2 jit_solution(2062286064484071746)
XLA Ops:
  13.4 2.7 dynamic-slice_bitcast_fusion.4
  17.7 3.4 collective-permute-start.1
  21.1 2.6 collective-permute-start.2
  24.1 68.9 %all-gather.2 = s32[4,2,386]{2,1,0:T(2,128)S(1)} all-gather(s32[1,2,386]{2,1,0:T(2,128)S(1)} %add_bitcast_fusion), channel_id=2, replica_groups=mesh['dp'=8,'tensor'=4] {'tensor'}, dimensions={0}, use_global_device_ids=true | all-gather | bytes 15440 | tf_op jit(solution)/shard_map/all_gather | solution.py:749
  93.2 69.5 %all-gather.3 = bf16[32,6,128]{2,1,0:T(8,128)(2,1)S(1)} all-gather(bf16[1,6,128]{2,1,0:T(8,128)(2,1)S(1)} %bitcast.150), channel_id=3, replica_groups=mesh['dp'=8,'tensor'=4] {'dp','tensor'}, dimensions={0}, use_global_device_ids=true | all-gather | bytes 50688 | tf_op jit(solution)/shard_map/all_gather | solution.py:779
  164.4 12.0 %copy.87 = bf16[4096,1024]{1,0:T(8,128)(2,1)} copy(bf16[4096,1024]{0,1:T(8,128)(2,1)} %all-gather.8.cloned.1.call-done) | data formatting | bytes 16777216 | tf_op jit(solution)/shard_map/all_gather | solution.py:786
  177.9 17.2 %project.1 = (bf16[2,1024,768]{2,1,0:T(8,128)(2,1)}, bf16[2,1024,768]{2,1,0:T(8,128)(2,1)S(1)}, bf16[1024,1024]{1,0:T(8,128)(2,1)S(1)}) custom-call(s32[1]{0:T(128)} %bitcast.2.core, bf16[1024,1024]{1,0:T(8,128)(2,1)S(1)} %copy-done.3, f32[8,1024]{1,0:T(8,128)S(1)} %concatenate.31.vec_ref, bf16[4,1024,1024]{2,1,0:T(8,128)(2,1)} %bitcast.114), custom_call_target="tpu_custom_call" | custom-call | tf_op jit(solution)/shard_map/project/pallas_call | solution.py:417
  197.4 4.5 collective-permute-done.4
  211.4 67.6 %attn_fwd.1 = (bf16[2,1024,256]{2,1,0:T(8,128)(2,1)S(1)}, bf16[2,1024,256]{2,1,0:T(8,128)(2,1)}, f32[4,32,128]{2,1,0:T(8,128)S(1)}) custom-call(s32[962]{0:T(1024)S(1)} %pad_add_fusion.2.tab, bf16[2,1024,768]{2,1,0:T(8,128)(2,1)S(1)} %get-tuple-element.42.q_own.k_own.v_own, bf16[2,1024,768]{2,1,0:T(8,128)(2,1)} %collective-permute-done.5.q_oth.k_oth.v_oth, ...), custom_call_target="tpu_custom_call" | custom-call | flops 4000000000 | bytes 8000000 | tf_op jit(solution)/shard_map/attn_fwd/pallas_call | solution.py:297
  282.3 2.9 collective-permute-start.10
  286.7 24.9 %collective-permute-done.8 = bf16[256,1024]{1,0:T(8,128)(2,1)S(1)} collective-permute-done((bf16[256,1024]{1,0:T(8,128)(2,1)S(1)}, bf16[256,1024]{1,0:T(8,128)(2,1)S(1)}, u32[]{:S(2)}, u32[]{:S(2)}) %collective-permute-start.8) | collective-permute-done | bytes 524320 | tf_op jit(solution)/shard_map/ppermute | solution.py:728
  312.4 5.8 collective-permute-done.9
  319.1 12.9 %collective-permute-done.10 = bf16[256,1024]{1,0:T(8,128)(2,1)S(1)} collective-permute-done((bf16[256,1024]{1,0:T(8,128)(2,1)S(1)}, bf16[256,1024]{1,0:T(8,128)(2,1)S(1)}, u32[]{:S(2)}, u32[]{:S(2)}) %collective-permute-start.10) | collective-permute-done | bytes 524320 | tf_op jit(solution)/shard_map/ppermute | solution.py:728
  332.9 12.1 %copy.88 = bf16[4096,1024]{1,0:T(8,128)(2,1)} copy(bf16[4096,1024]{0,1:T(8,128)(2,1)} %all-gather.12.cloned.1.call-done) | data formatting | bytes 16777216 | tf_op jit(solution)/shard_map/all_gather | solution.py:786
  345.0 3.4 copy-done
  348.4 5.3 out_project.1
  353.7 2.0 copy-done.7
  357.0 71.6 %feed_forward.1 = (f32[1024,1024]{1,0:T(8,128)}, f32[1024,1024]{1,0:T(8,128)}, bf16[4,1024,1024]{2,1,0:T(8,128)(2,1)}, bf16[4,1024,1024]{2,1,0:T(8,128)(2,1)}, f32[4,1,1024]{2,1,0:T(1,128)}) custom-call(bf16[1024,1024]{1,0:T(8,128)(2,1)} %copy-done.10, bf16[1024,1024]{1,0:T(8,128)(2,1)} %constant_dynamic-update-slice_fusion.4.cot_ref, ...), custom_call_target="tpu_custom_call" | custom-call | tf_op jit(solution)/shard_map/feed_forward/pallas_call | solution.py:530
  429.5 11.2 %middle.1 = (bf16[1024,1024]{1,0:T(8,128)(2,1)S(1)}, f32[1024,1024]{1,0:T(8,128)}, bf16[1024,1024]{1,0:T(8,128)(2,1)}, bf16[2,1024,256]{2,1,0:T(8,128)(2,1)S(1)}...) custom-call(s32[1]{0:T(128)} %bitcast.2.core, f32[1024,1024]{1,0:T(8,128)} %copy-done.7, ...), custom_call_target="tpu_custom_call" | custom-call | tf_op jit(solution)/shard_map/middle/pallas_call | solution.py:580
  441.7 10.4 %collective-permute-start.15 = (bf16[2,1024,256]{2,1,0:T(8,128)(2,1)S(1)}, bf16[2,1024,256]{2,1,0:T(8,128)(2,1)S(1)}, u32[]{:S(2)}, u32[]{:S(2)}) collective-permute-start(bf16[2,1024,256]{2,1,0:T(8,128)(2,1)S(1)} %get-tuple-element.55), channel_id=1, source_target_pairs={{0,4},{1,5},{2,6},{3,7},{4,0},{5,1},{6,2},{7,3},{8,12},{9,13},{10,... | collective-permute-start | bytes 3145736 | tf_op jit(solution)/shard_map/ppermute | solution.py:720
  452.1 2.3 collective-permute-done.15.g_oth
  455.4 76.3 %attn_bwd.1 = (bf16[2,1024,256]{2,1,0:T(8,128)(2,1)S(1)}, bf16[2,1024,256]{2,1,0:T(8,128)(2,1)S(1)}, bf16[2,1024,256]{2,1,0:T(8,128)(2,1)S(1)}, bf16[2,1024,256]...) custom-call(s32[962]{0:T(1024)S(1)} %pad_add_fusion.2.tab, ...), custom_call_target="tpu_custom_call" | custom-call | flops 10000000000 | bytes 16000000 | tf_op jit(solution)/shard_map/attn_bwd/pallas_call | solution.py:331
  537.4 3.0 collective-permute-done.17.dk1
  541.8 34.4 %last.1 = (bf16[1024,1024]{1,0:T(8,128)(2,1)}, bf16[4,1024,1024]{2,1,0:T(8,128)(2,1)}, f32[8,1024]{1,0:T(8,128)}) custom-call(s32[1]{0:T(128)} %bitcast.2.core, bf16[1024,1024]{1,0:T(8,128)(2,1)} %copy-done.2, bf16[1024,1024]{1,0:T(8,128)(2,1)} %copy-done.9, bf16[1024,1024]{1,0:T(8,128)(2,1)} %get-tuple-element.52.low_ref, ...), custom_call_target="tpu_custom_call" | custom-call | tf_op jit(solution)/shard_map/last/pallas_call | solution.py:666
  577.5 1.8 collective-permute-start.11
  581.5 38.6 %collective-permute-done.11 = bf16[256,1024]{1,0:T(8,128)(2,1)S(1)} collective-permute-done((bf16[256,1024]{1,0:T(8,128)(2,1)}, bf16[256,1024]{1,0:T(8,128)(2,1)S(1)}, u32[]{:S(2)}, u32[]{:S(2)}) %collective-permute-start.11) | collective-permute-done | bytes 524320 | tf_op jit(solution)/shard_map/ppermute | solution.py:738
  620.1 16.1 %collective-permute-done.12 = bf16[256,1024]{1,0:T(8,128)(2,1)S(1)} collective-permute-done((bf16[256,1024]{1,0:T(8,128)(2,1)}, bf16[256,1024]{1,0:T(8,128)(2,1)S(1)}, u32[]{:S(2)}, u32[]{:S(2)}) %collective-permute-start.12) | collective-permute-done | bytes 524320 | tf_op jit(solution)/shard_map/ppermute | solution.py:738
  637.6 3.1 collective-permute-start.20
  645.6 90.2 %all-reduce.1 = f32[32,288]{1,0:T(8,128)S(1)} all-reduce(f32[32,288]{1,0:T(8,128)S(1)} %pad_maximum_fusion.3), channel_id=4, replica_groups=mesh['dp'=8,'tensor'=4] {'dp','tensor'}, use_global_device_ids=true, to_apply=%region_0.1.clone | all-reduce | flops 9216 | bytes 73728
  737.5 2.5 bitcast_convert_fusion
  741.8 8.0 reduce-scatter.12.cloned.1.call-done
  751.7 158.5 %reduce-scatter.10.cloned.1.call-done = bf16[128,1024]{1,0:T(8,128)(2,1)} async-done(((bf16[4096,1024]{1,0:T(8,128)(2,1)}), bf16[128,1024]{1,0:T(8,128)(2,1)}) %reduce-scatter.10.cloned.1.call-update) | async-done | bytes 262160
  (206 shorter events, 59.2 us)
Async XLA Ops:
  7.2 157.2 %all-gather.8.cloned.1.call-start = ((), (), s32[]{:S(2)}) async-start(), calls=%async_computation.3 | async-start | bytes 8650752 | tf_op jit(solution)/shard_map/all_gather | solution.py:786
  11.7 321.2 %all-gather.12.cloned.1.call-start = ((), (), s32[]{:S(2)}) async-start(), calls=%async_computation.5 | async-start | bytes 8650752 | tf_op jit(solution)/shard_map/all_gather | solution.py:786
  12.4 344.6 %all-gather.10.cloned.1.call-start = ((), (), s32[]{:S(2)}) async-start(), calls=%async_computation.4 | async-start | bytes 8650752 | tf_op jit(solution)/shard_map/all_gather | solution.py:786
  13.2 726.8 %reduce-scatter.8.cloned.1.call-start = ((), (), s32[]{:S(2)}) async-start(), calls=%async_computation.6 | async-start | bytes 8650752 | tf_op jit(solution)/shard_map/reduce_scatter | solution.py:818
  13.3 79.9 %copy-start.25 = (bf16[128]{0:T(256)(128)(2,1)S(1)}, bf16[128]{0:T(256)(128)(2,1)}, u32[]{:S(2)}) copy-start(bf16[128]{0:T(256)(128)(2,1)} %param.18) | copy-start | bytes 772
  16.0 146.8 %collective-permute-start = (bf16[256,1024]{1,0:T(8,128)(2,1)}, bf16[256,1024]{1,0:T(8,128)(2,1)S(1)}, u32[]{:S(2)}, u32[]{:S(2)}) collective-permute-start(bf16[256,1024]{1,0:T(8,128)(2,1)} %get-tuple-element.149), channel_id=1, source_target_pairs={{0,0},{1,4},{2,2},{3,6},{4,1},{5,5},{6,3},{7,7},{8,8},{9,12},{10,1... | collective-permute-start | bytes 1572872 | tf_op jit(solution)/shard_map/ppermute | solution.py:728
  17.7 145.1 %collective-permute-start.1 = (bf16[256,1024]{1,0:T(8,128)(2,1)}, bf16[256,1024]{1,0:T(8,128)(2,1)S(1)}, u32[]{:S(2)}, u32[]{:S(2)}) collective-permute-start(bf16[256,1024]{1,0:T(8,128)(2,1)} %get-tuple-element.148), channel_id=1, source_target_pairs={{0,4},{1,0},{2,6},{3,2},{4,5},{5,1},{6,7},{7,3},{8,12},{9,8},{10,1... | collective-permute-start | bytes 1572872 | tf_op jit(solution)/shard_map/ppermute | solution.py:728
  21.1 141.8 %collective-permute-start.2 = (bf16[256,1024]{1,0:T(8,128)(2,1)S(1)}, bf16[256,1024]{1,0:T(8,128)(2,1)S(1)}, u32[]{:S(2)}, u32[]{:S(2)}) collective-permute-start(bf16[256,1024]{1,0:T(8,128)(2,1)S(1)} %get-tuple-element.147), channel_id=1, source_target_pairs={{0,2},{1,6},{2,0},{3,4},{4,3},{5,7},{6,1},{7,5},{8,10},{9,14},{10,... | collective-permute-start | bytes 1572872 | tf_op jit(solution)/shard_map/ppermute | solution.py:728
  23.7 139.3 %collective-permute-start.3 = (bf16[256,1024]{1,0:T(8,128)(2,1)S(1)}, bf16[256,1024]{1,0:T(8,128)(2,1)S(1)}, u32[]{:S(2)}, u32[]{:S(2)}) collective-permute-start(bf16[256,1024]{1,0:T(8,128)(2,1)S(1)} %get-tuple-element.146), channel_id=1, source_target_pairs={{0,6},{1,2},{2,4},{3,0},{4,7},{5,3},{6,5},{7,1},{8,14},{9,10},{10,... | collective-permute-start | bytes 1572872 | tf_op jit(solution)/shard_map/ppermute | solution.py:728
  162.8 266.7 %copy-start.14 = (f32[8,1024]{1,0:T(8,128)}, f32[8,1024]{1,0:T(8,128)S(1)}, u32[]{:S(2)}) copy-start(f32[8,1024]{1,0:T(8,128)S(1)} %concatenate.31.vec_ref) | copy-start | bytes 98308
  196.5 82.4 %copy-start.1 = (bf16[2,1024,768]{2,1,0:T(8,128)(2,1)}, bf16[2,1024,768]{2,1,0:T(8,128)(2,1)S(1)}, u32[]{:S(2)}) copy-start(bf16[2,1024,768]{2,1,0:T(8,128)(2,1)S(1)} %get-tuple-element.42.q_own.k_own.v_own) | copy-start | bytes 9437188
  196.5 14.5 %collective-permute-start.5 = (bf16[2,1024,768]{2,1,0:T(8,128)(2,1)}, bf16[2,1024,768]{2,1,0:T(8,128)(2,1)}, u32[]{:S(2)}, u32[]{:S(2)}) collective-permute-start(bf16[2,1024,768]{2,1,0:T(8,128)(2,1)} %get-tuple-element.43), channel_id=1, source_target_pairs={{0,4},{1,5},{2,6},{3,7},{4,0},{5,1},{6,2},{7,3},{8,12},{9,13},{10,... | collective-permute-start | bytes 9437192 | tf_op jit(solution)/shard_map/ppermute | solution.py:720
  196.6 5.3 collective-permute-start.4
  279.0 66.0 %collective-permute-start.6 = (bf16[2,1024,256]{2,1,0:T(8,128)(2,1)}, bf16[2,1024,256]{2,1,0:T(8,128)(2,1)}, u32[]{:S(2)}, u32[]{:S(2)}) collective-permute-start(bf16[2,1024,256]{2,1,0:T(8,128)(2,1)} %get-tuple-element.45), channel_id=1, source_target_pairs={{0,4},{1,5},{2,6},{3,7},{4,0},{5,1},{6,2},{7,3},{8,12},{9,13},{10,... | collective-permute-start | bytes 3145736 | tf_op jit(solution)/shard_map/ppermute | solution.py:720
  280.0 5.9 collective-permute-start.7
  280.7 31.0 %collective-permute-start.8 = (bf16[256,1024]{1,0:T(8,128)(2,1)S(1)}, bf16[256,1024]{1,0:T(8,128)(2,1)S(1)}, u32[]{:S(2)}, u32[]{:S(2)}) collective-permute-start(bf16[256,1024]{1,0:T(8,128)(2,1)S(1)} %get-tuple-element.144), channel_id=1, source_target_pairs={{0,4},{1,0},{2,6},{3,2},{4,5},{5,1},{6,7},{7,3},{8,12},{9,8},{10,1... | collective-permute-start | bytes 1572872 | tf_op jit(solution)/shard_map/ppermute | solution.py:728
  282.3 35.9 %collective-permute-start.9 = (bf16[256,1024]{1,0:T(8,128)(2,1)S(1)}, bf16[256,1024]{1,0:T(8,128)(2,1)S(1)}, u32[]{:S(2)}, u32[]{:S(2)}) collective-permute-start(bf16[256,1024]{1,0:T(8,128)(2,1)S(1)} %get-tuple-element.143), channel_id=1, source_target_pairs={{0,2},{1,6},{2,0},{3,4},{4,3},{5,7},{6,1},{7,5},{8,10},{9,14},{10,... | collective-permute-start | bytes 1572872 | tf_op jit(solution)/shard_map/ppermute | solution.py:728
  282.3 49.7 %collective-permute-start.10 = (bf16[256,1024]{1,0:T(8,128)(2,1)S(1)}, bf16[256,1024]{1,0:T(8,128)(2,1)S(1)}, u32[]{:S(2)}, u32[]{:S(2)}) collective-permute-start(bf16[256,1024]{1,0:T(8,128)(2,1)S(1)} %get-tuple-element.142), channel_id=1, source_target_pairs={{0,6},{1,2},{2,4},{3,0},{4,7},{5,3},{6,5},{7,1},{8,14},{9,10},{10,... | collective-permute-start | bytes 1572872 | tf_op jit(solution)/shard_map/ppermute | solution.py:728
  428.6 321.1 %reduce-scatter.12.cloned.1.call-start = ((), (), s32[]{:S(2)}) async-start(), calls=%async_computation.8 | async-start | bytes 8650752
  429.2 481.0 %reduce-scatter.10.cloned.1.call-start = ((), (), s32[]{:S(2)}) async-start(), calls=%async_computation.7 | async-start | bytes 8650752
  441.7 12.7 %collective-permute-start.15 = (bf16[2,1024,256]{2,1,0:T(8,128)(2,1)S(1)}, bf16[2,1024,256]{2,1,0:T(8,128)(2,1)S(1)}, u32[]{:S(2)}, u32[]{:S(2)}) collective-permute-start(bf16[2,1024,256]{2,1,0:T(8,128)(2,1)S(1)} %get-tuple-element.55), channel_id=1, source_target_pairs={{0,4},{1,5},{2,6},{3,7},{4,0},{5,1},{6,2},{7,3},{8,12},{9,13},{10,... | collective-permute-start | bytes 3145736 | tf_op jit(solution)/shard_map/ppermute | solution.py:720
  534.7 2.7 collective-permute-start.16
  535.1 5.4 collective-permute-start.17
  535.2 5.4 collective-permute-start.18
  577.5 42.5 %collective-permute-start.11 = (bf16[256,1024]{1,0:T(8,128)(2,1)}, bf16[256,1024]{1,0:T(8,128)(2,1)S(1)}, u32[]{:S(2)}, u32[]{:S(2)}) collective-permute-start(bf16[256,1024]{1,0:T(8,128)(2,1)} %get-tuple-element.141), channel_id=1, source_target_pairs={{6,0},{2,1},{4,2},{0,3},{7,4},{3,5},{5,6},{1,7},{14,8},{10,9},{12,... | collective-permute-start | bytes 1572872 | tf_op jit(solution)/shard_map/ppermute | solution.py:738
  579.4 56.8 %collective-permute-start.12 = (bf16[256,1024]{1,0:T(8,128)(2,1)}, bf16[256,1024]{1,0:T(8,128)(2,1)S(1)}, u32[]{:S(2)}, u32[]{:S(2)}) collective-permute-start(bf16[256,1024]{1,0:T(8,128)(2,1)} %get-tuple-element.140), channel_id=1, source_target_pairs={{2,0},{6,1},{0,2},{4,3},{3,4},{7,5},{1,6},{5,7},{10,8},{14,9},{8,1... | collective-permute-start | bytes 1572872 | tf_op jit(solution)/shard_map/ppermute | solution.py:738
  579.7 56.5 %collective-permute-start.13 = (bf16[256,1024]{1,0:T(8,128)(2,1)S(1)}, bf16[256,1024]{1,0:T(8,128)(2,1)S(1)}, u32[]{:S(2)}, u32[]{:S(2)}) collective-permute-start(bf16[256,1024]{1,0:T(8,128)(2,1)S(1)} %get-tuple-element.138), channel_id=1, source_target_pairs={{4,0},{0,1},{6,2},{2,3},{5,4},{1,5},{7,6},{3,7},{12,8},{8,9},{14,1... | collective-permute-start | bytes 1572872 | tf_op jit(solution)/shard_map/ppermute | solution.py:738
  580.7 55.5 %collective-permute-start.14 = (bf16[256,1024]{1,0:T(8,128)(2,1)S(1)}, bf16[256,1024]{1,0:T(8,128)(2,1)S(1)}, u32[]{:S(2)}, u32[]{:S(2)}) collective-permute-start(bf16[256,1024]{1,0:T(8,128)(2,1)S(1)} %get-tuple-element.139), channel_id=1, source_target_pairs={{0,0},{4,1},{2,2},{6,3},{1,4},{5,5},{3,6},{7,7},{8,8},{12,9},{10,1... | collective-permute-start | bytes 1572872 | tf_op jit(solution)/shard_map/ppermute | solution.py:738
  637.6 99.4 %collective-permute-start.19 = (bf16[256,1024]{1,0:T(8,128)(2,1)}, bf16[256,1024]{1,0:T(8,128)(2,1)S(1)}, u32[]{:S(2)}, u32[]{:S(2)}) collective-permute-start(bf16[256,1024]{1,0:T(8,128)(2,1)} %get-tuple-element.133), channel_id=1, source_target_pairs={{6,0},{2,1},{4,2},{0,3},{7,4},{3,5},{5,6},{1,7},{14,8},{10,9},{12,... | collective-permute-start | bytes 1572872 | tf_op jit(solution)/shard_map/ppermute | solution.py:738
  637.6 99.4 %collective-permute-start.20 = (bf16[256,1024]{1,0:T(8,128)(2,1)}, bf16[256,1024]{1,0:T(8,128)(2,1)S(1)}, u32[]{:S(2)}, u32[]{:S(2)}) collective-permute-start(bf16[256,1024]{1,0:T(8,128)(2,1)} %get-tuple-element.132), channel_id=1, source_target_pairs={{2,0},{6,1},{0,2},{4,3},{3,4},{7,5},{1,6},{5,7},{10,8},{14,9},{8,1... | collective-permute-start | bytes 1572872 | tf_op jit(solution)/shard_map/ppermute | solution.py:738
  640.7 96.4 %collective-permute-start.21 = (bf16[256,1024]{1,0:T(8,128)(2,1)S(1)}, bf16[256,1024]{1,0:T(8,128)(2,1)S(1)}, u32[]{:S(2)}, u32[]{:S(2)}) collective-permute-start(bf16[256,1024]{1,0:T(8,128)(2,1)S(1)} %get-tuple-element.130), channel_id=1, source_target_pairs={{4,0},{0,1},{6,2},{2,3},{5,4},{1,5},{7,6},{3,7},{12,8},{8,9},{14,1... | collective-permute-start | bytes 1572872 | tf_op jit(solution)/shard_map/ppermute | solution.py:738
  642.0 95.1 %collective-permute-start.22 = (bf16[256,1024]{1,0:T(8,128)(2,1)S(1)}, bf16[256,1024]{1,0:T(8,128)(2,1)S(1)}, u32[]{:S(2)}, u32[]{:S(2)}) collective-permute-start(bf16[256,1024]{1,0:T(8,128)(2,1)S(1)} %get-tuple-element.131), channel_id=1, source_target_pairs={{0,0},{4,1},{2,2},{6,3},{1,4},{5,5},{3,6},{7,7},{8,8},{12,9},{10,1... | collective-permute-start | bytes 1572872 | tf_op jit(solution)/shard_map/ppermute | solution.py:738
  (29 other events, 673.4 us)
Sparse Core Ops, SparseCore 0:
  11.8 117.9 all-gather.7
  132.7 90.4 all-gather.11
  226.1 83.9 all-gather.9
  428.8 160.5 reduce-scatter.7
  591.5 158.2 reduce-scatter.11
  751.9 158.2 reduce-scatter.9

commit v2 on v1

v2 whole, which is shorter than its diff:
```python
import functools
import jax
import jax.numpy as jnp
from jax import lax
from jax.sharding import PartitionSpec as P
from jax.experimental import pallas as pl
from jax.experimental.pallas import tpu as pltpu

HD = 64
BLOCK = 64
COMMON = 5
RAND = 3
BIG = 1e30
bf16 = jnp.bfloat16
f32 = jnp.float32


def cost(micros):
    return pl.CostEstimate(flops=int(micros * 10**9), bytes_accessed=1000, transcendentals=0)


def dot_nt(left, right):
    return lax.dot_general(left, right, (((1,), (1,)), ((), ())), preferred_element_type=f32)


def dot_tn(left, right):
    return lax.dot_general(left, right, (((0,), (0,)), ((), ())), preferred_element_type=f32)


def dot_nn(left, right):
    return lax.dot_general(left, right, (((1,), (0,)), ((), ())), preferred_element_type=f32)


def low_half(shape):
    return lax.broadcasted_iota(jnp.int32, shape, 1) % 128 < HD


def slot_offsets(tab, layout, pair, block):
    common_at, rand_at, blocks, heads = layout
    shared = [
        pl.multiple_of(tab[common_at + block * COMMON + slot], BLOCK) for slot in range(COMMON)
    ]
    first = rand_at + (2 * pair * blocks + block) * RAND
    second = first + blocks * RAND
    drawn = [
        (pl.multiple_of(tab[first + slot], BLOCK), pl.multiple_of(tab[second + slot], BLOCK))
        for slot in range(RAND)
    ]
    return shared, drawn


def gather_rows(ref, shared, drawn, width):
    keep = low_half((BLOCK, width))
    parts = [ref[pl.ds(start, BLOCK), :width] for start in shared]
    for left, right in drawn:
        parts.append(
            jnp.where(keep, ref[pl.ds(left, BLOCK), :width], ref[pl.ds(right, BLOCK), :width])
        )
    return jnp.concatenate(parts, axis=0)


def block_diag(rows):
    keep = low_half(rows.shape)
    zero = jnp.zeros_like(rows)
    return jnp.concatenate([jnp.where(keep, rows, zero), jnp.where(keep, zero, rows)], axis=0)


def fold_heads(rows):
    keep = low_half((BLOCK, 128))
    return jnp.where(keep, rows[:BLOCK], rows[BLOCK:])


def query_rows(qbuf, kaug, start):
    scaled = qbuf[pl.ds(start, BLOCK), :]
    hot = kaug[pl.ds(start, BLOCK), 128:]
    penalty = (hot - jnp.ones_like(hot)) * jnp.asarray(BIG, bf16)
    return block_diag(jnp.concatenate([scaled, penalty], axis=1))


def fill_keys(tab, layout, seg_ref, kaug, half, k_own, k_oth):
    blocks = layout[2]

    @pl.when(pl.program_id(0) == 0)
    def _():
        lane = lax.broadcasted_iota(jnp.int32, (BLOCK, 128), 1) % HD

        def one(block, carry):
            row = pl.multiple_of(tab[block], BLOCK)
            seg = seg_ref[pl.ds(pl.multiple_of(block * BLOCK, BLOCK), BLOCK), :]
            kaug[pl.ds(row, BLOCK), 128:] = jnp.where(seg == lane, 1.0, 0.0).astype(bf16)
            return carry

        lax.fori_loop(0, blocks, one, 0)
        kaug[2 * half :, :128] = jnp.zeros((BLOCK, 128), bf16)
        kaug[2 * half :, 128:] = jnp.where(lane == HD - 1, 1.0, 0.0).astype(bf16)

    kaug[:half, :128] = k_own[0]
    kaug[half : 2 * half, :128] = k_oth[0]


def attn_fwd_kernel(
    layout, first_pair, unroll, tab, q_own, q_oth, k_own, k_oth, v_own, v_oth, seg_ref,
    out_own, out_oth, lse_ref, kaug, vbuf, qbuf, obuf, sbuf,
):
    pair = first_pair + pl.program_id(0)
    half = q_own.shape[1]
    blocks = layout[2]
    fill_keys(tab, layout, seg_ref, kaug, half, k_own, k_oth)
    vbuf[:half, :] = v_own[0]
    vbuf[half : 2 * half, :] = v_oth[0]
    vbuf[2 * half :, :] = jnp.zeros((BLOCK, 128), bf16)
    scale = jnp.asarray(0.125, bf16)
    qbuf[:half, :] = q_own[0] * scale
    qbuf[half:, :] = q_oth[0] * scale

    def one_block(block):
        row = pl.multiple_of(tab[block], BLOCK)
        shared, drawn = slot_offsets(tab, layout, pair, block)
        scores = dot_nt(gather_rows(kaug, shared, drawn, 256), query_rows(qbuf, kaug, row))
        top = jnp.max(scores, axis=0, keepdims=True)
        weight = jnp.exp(scores - top)
        total = jnp.sum(weight, axis=0, keepdims=True)
        probs = (weight * (1.0 / total)).astype(bf16)
        context = dot_tn(probs, gather_rows(vbuf, shared, drawn, 128))
        obuf[pl.ds(row, BLOCK), :] = fold_heads(context).astype(bf16)
        lse_ref[0, pl.ds(block, 1), :] = top + jnp.log(total)

    def step(index, carry):
        for part in range(unroll):
            one_block(index * unroll + part)
        return carry

    lax.fori_loop(0, blocks // unroll, step, 0)

    def dense_block(block):
        row = pl.multiple_of(tab[block], BLOCK)
        query = query_rows(qbuf, kaug, row)
        chunk = 512
        count = 2 * half // chunk
        top = jnp.full((1, 128), -3e38, f32)
        for part in range(count):
            scores = dot_nt(kaug[part * chunk : (part + 1) * chunk, :], query)
            sbuf[part * chunk : (part + 1) * chunk, :] = scores
            top = jnp.maximum(top, jnp.max(scores, axis=0, keepdims=True))
        total = jnp.zeros((1, 128), f32)
        for part in range(count):
            weight = jnp.exp(sbuf[part * chunk : (part + 1) * chunk, :] - top)
            sbuf[part * chunk : (part + 1) * chunk, :] = weight
            total = total + jnp.sum(weight, axis=0, keepdims=True)
        inverse = 1.0 / total
        context = jnp.zeros((128, 128), f32)
        for part in range(count):
            probs = (sbuf[part * chunk : (part + 1) * chunk, :] * inverse).astype(bf16)
            context = context + dot_tn(probs, vbuf[part * chunk : (part + 1) * chunk, :])
        obuf[pl.ds(row, BLOCK), :] = fold_heads(context).astype(bf16)
        lse_ref[0, pl.ds(block, 1), :] = top + jnp.log(total)

    first, second = tab[blocks], tab[blocks + 1]

    def dense_step(index, carry):
        dense_block(jnp.where(index == 0, first, second))
        return carry

    lax.fori_loop(0, jnp.where(first == second, 1, 2), dense_step, 0)
    out_own[0] = obuf[:half, :]
    out_oth[0] = obuf[half:, :]


def attn_bwd_kernel(
    layout, first_pair, unroll, tab, q_own, q_oth, k_own, k_oth, v_own, v_oth, g_own, g_oth, seg_ref, lse_ref,
    own_ref, oth_ref,
    kaug, vbuf, qbuf, gbuf, dqbuf, dkbuf, dvbuf, sbuf, tbuf,
):
    pair = first_pair + pl.program_id(0)
    half = q_own.shape[1]
    blocks = layout[2]
    fill_keys(tab, layout, seg_ref, kaug, half, k_own, k_oth)
    vbuf[:half, :] = v_own[0]
    vbuf[half : 2 * half, :] = v_oth[0]
    vbuf[2 * half :, :] = jnp.zeros((BLOCK, 128), bf16)
    scale = jnp.asarray(0.125, bf16)
    qbuf[:half, :] = q_own[0] * scale
    qbuf[half:, :] = q_oth[0] * scale
    gbuf[:half, :] = g_own[0]
    gbuf[half:, :] = g_oth[0]
    dkbuf[...] = jnp.zeros_like(dkbuf)
    dvbuf[...] = jnp.zeros_like(dvbuf)
    keep = low_half((BLOCK, 128))

    def scatter(ref, update, shared, drawn):
        for slot, start in enumerate(shared):
            ref[pl.ds(start, BLOCK), :] += update[slot * BLOCK : (slot + 1) * BLOCK]
        for slot, (left, right) in enumerate(drawn):
            at = (COMMON + slot) * BLOCK
            piece = update[at : at + BLOCK]
            ref[pl.ds(left, BLOCK), :] += jnp.where(keep, piece, 0.0)
            ref[pl.ds(right, BLOCK), :] += jnp.where(keep, 0.0, piece)

    def one_block(block):
        row = pl.multiple_of(tab[block], BLOCK)
        shared, drawn = slot_offsets(tab, layout, pair, block)
        query = query_rows(qbuf, kaug, row)
        grad = block_diag(gbuf[pl.ds(row, BLOCK), :])
        keys = gather_rows(kaug, shared, drawn, 256)
        scores = dot_nt(keys, query)
        probs = jnp.exp(scores - lse_ref[0, pl.ds(block, 1), :])
        grad_probs = dot_nt(gather_rows(vbuf, shared, drawn, 128), grad)
        delta = jnp.sum(probs * grad_probs, axis=0, keepdims=True)
        grad_scores = (probs * (grad_probs - delta)).astype(bf16)
        grad_query = dot_tn(grad_scores, keys[:, :128])
        dqbuf[pl.ds(row, BLOCK), :] = (fold_heads(grad_query) * 0.125).astype(bf16)
        scatter(dkbuf, dot_nn(grad_scores, query[:, :128]), shared, drawn)
        scatter(dvbuf, dot_nn(probs.astype(bf16), grad), shared, drawn)

    def step(index, carry):
        for part in range(unroll):
            one_block(index * unroll + part)
        return carry

    lax.fori_loop(0, blocks // unroll, step, 0)

    def dense_block(block):
        row = pl.multiple_of(tab[block], BLOCK)
        query = query_rows(qbuf, kaug, row)
        grad = block_diag(gbuf[pl.ds(row, BLOCK), :])
        lse = lse_ref[0, pl.ds(block, 1), :]
        chunk = 512
        count = 2 * half // chunk
        delta = jnp.zeros((1, 128), f32)
        for part in range(count):
            here = slice(part * chunk, (part + 1) * chunk)
            probs = jnp.exp(dot_nt(kaug[here, :], query) - lse)
            grad_probs = dot_nt(vbuf[here, :], grad)
            delta = delta + jnp.sum(probs * grad_probs, axis=0, keepdims=True)
            sbuf[here, :] = probs
            tbuf[here, :] = grad_probs
        grad_query = jnp.zeros((128, 128), f32)
        for part in range(count):
            here = slice(part * chunk, (part + 1) * chunk)
            probs = sbuf[here, :]
            grad_scores = (probs * (tbuf[here, :] - delta)).astype(bf16)
            grad_query = grad_query + dot_tn(grad_scores, kaug[here, :128])
            dkbuf[here, :] += dot_nn(grad_scores, query[:, :128])
            dvbuf[here, :] += dot_nn(probs.astype(bf16), grad)
        dqbuf[pl.ds(row, BLOCK), :] = (fold_heads(grad_query) * 0.125).astype(bf16)

    first, second = tab[blocks], tab[blocks + 1]

    def dense_step(index, carry):
        dense_block(jnp.where(index == 0, first, second))
        return carry

    lax.fori_loop(0, jnp.where(first == second, 1, 2), dense_step, 0)
    for part, buffer in enumerate((dqbuf, dkbuf, dvbuf)):
        lanes = pl.ds(pl.multiple_of((2 * part + pl.program_id(0)) * 128, 128), 128)
        own_ref[0, :, lanes] = buffer[:half, :].astype(bf16)
        oth_ref[0, :, lanes] = buffer[half : 2 * half, :].astype(bf16)


def table_layout(blocks, heads):
    common_at = blocks + 2
    rand_at = common_at + blocks * COMMON
    return (common_at, rand_at, blocks, heads)


def attention_table(rand_heads, glob_row, row_of, dummy_row):
    heads, blocks, _ = rand_heads.shape
    index = jnp.arange(blocks, dtype=jnp.int32)
    g0, g1 = glob_row[0], glob_row[1]
    dense = (index == g0) | (index == g1)
    near0, near1 = jnp.abs(index - g0) <= 1, jnp.abs(index - g1) <= 1
    full = jnp.broadcast_to
    shared = jnp.stack([index - 1, index, index + 1, full(g0, (blocks,)), full(g1, (blocks,))], axis=1)
    valid = jnp.stack(
        [index > 0, index >= 0, index < blocks - 1, ~near0, ~near1 & (g1 != g0)], axis=1
    ) & ~dense[:, None]
    shared = jnp.where(valid, row_of(jnp.clip(shared, 0, blocks - 1)), dummy_row)
    far = jnp.abs(rand_heads - index[None, :, None]) > 1
    far = far & (rand_heads != g0) & (rand_heads != g1) & ~dense[None, :, None]
    r0, r1, r2 = rand_heads[..., 0], rand_heads[..., 1], rand_heads[..., 2]
    fresh = jnp.stack([r0 == r0, r1 != r0, (r2 != r0) & (r2 != r1)], axis=-1)
    drawn = jnp.where(far & fresh, row_of(rand_heads), dummy_row)
    return jnp.concatenate(
        [row_of(index), glob_row, shared.reshape(-1), drawn.reshape(-1)]
    ).astype(jnp.int32)


def lane_spec(half, slot, column):
    return pl.BlockSpec((1, half, 128), lambda p, tab: (slot, 0, column * 2 + p))


def attn_fwd(tab, qkv_own, qkv_oth, seg_abs, blocks, slot, unroll=4):
    half = qkv_own.shape[1]
    layout = table_layout(blocks, 4 * qkv_own.shape[0])
    rows = 2 * half + BLOCK
    shape = jax.ShapeDtypeStruct((1, half, 256), bf16)
    result = pl.BlockSpec((1, half, 128), lambda p, tab: (0, 0, p))
    return pl.pallas_call(
        functools.partial(attn_fwd_kernel, layout, 2 * slot, unroll),
        out_shape=(shape, shape, jax.ShapeDtypeStruct((2, blocks, 128), f32)),
        grid_spec=pltpu.PrefetchScalarGridSpec(
            num_scalar_prefetch=1,
            grid=(2,),
            in_specs=[
                *[lane_spec(half, slot, column) for column in (0, 0, 1, 1, 2, 2)],
                pl.BlockSpec((2 * half, 128), lambda p, tab: (0, 0)),
            ],
            out_specs=(result, result, pl.BlockSpec((1, blocks, 128), lambda p, tab: (p, 0, 0))),
            scratch_shapes=[
                pltpu.VMEM((rows, 256), bf16), pltpu.VMEM((rows, 128), bf16),
                pltpu.VMEM((2 * half, 128), bf16), pltpu.VMEM((2 * half, 128), bf16),
                pltpu.VMEM((2 * half, 128), f32),
            ],
        ),
        compiler_params=pltpu.CompilerParams(vmem_limit_bytes=40 << 20),
        cost_estimate=cost(32),
        name="attn_fwd",
    )(tab, qkv_own, qkv_oth, qkv_own, qkv_oth, qkv_own, qkv_oth, seg_abs)


def attn_bwd(tab, qkv_own, qkv_oth, grad_own, grad_oth, seg_abs, lse, blocks, slot, unroll=4):
    half = qkv_own.shape[1]
    layout = table_layout(blocks, 4 * qkv_own.shape[0])
    rows = 2 * half + BLOCK
    shape = jax.ShapeDtypeStruct((1, half, 768), bf16)
    result = pl.BlockSpec((1, half, 768), lambda p, tab: (0, 0, 0))
    return pl.pallas_call(
        functools.partial(attn_bwd_kernel, layout, 2 * slot, unroll),
        out_shape=(shape, shape),
        grid_spec=pltpu.PrefetchScalarGridSpec(
            num_scalar_prefetch=1,
            grid=(2,),
            in_specs=[
                *[lane_spec(half, slot, column) for column in (0, 0, 1, 1, 2, 2, 0, 0)],
                pl.BlockSpec((2 * half, 128), lambda p, tab: (0, 0)),
                pl.BlockSpec((1, blocks, 128), lambda p, tab: (p, 0, 0)),
            ],
            out_specs=(result, result),
            scratch_shapes=[
                pltpu.VMEM((rows, 256), bf16), pltpu.VMEM((rows, 128), bf16),
                pltpu.VMEM((2 * half, 128), bf16), pltpu.VMEM((2 * half, 128), bf16),
                pltpu.VMEM((2 * half, 128), bf16),
                pltpu.VMEM((rows, 128), f32), pltpu.VMEM((rows, 128), f32),
                pltpu.VMEM((2 * half, 128), f32), pltpu.VMEM((2 * half, 128), f32),
            ],
        ),
        compiler_params=pltpu.CompilerParams(vmem_limit_bytes=48 << 20),
        cost_estimate=cost(37),
        name="attn_bwd",
    )(tab, qkv_own, qkv_oth, qkv_own, qkv_oth, qkv_own, qkv_oth, grad_own, grad_oth, seg_abs, lse)


EPS = 1e-05
BOTH = ("dp", "tensor")
ROWS = 256


def gelu_pair(u):
    c = 0.7978845608028654
    square = u * u
    bend = jnp.tanh(u * (c + (c * 0.044715) * square))
    half = 0.5 * (1.0 + bend)
    slope = half + (0.5 * u) * (1.0 - bend * bend) * (c + (3.0 * c * 0.044715) * square)
    return u * half, slope


def normalise(rows):
    center = rows - jnp.mean(rows, axis=-1, keepdims=True)
    inverse = lax.rsqrt(jnp.mean(center * center, axis=-1, keepdims=True) + EPS)
    return center * inverse, inverse


def norm_back(grad, unit, inverse, gain):
    scaled = grad * gain
    mean = jnp.mean(scaled, axis=-1, keepdims=True)
    along = jnp.mean(scaled * unit, axis=-1, keepdims=True)
    return inverse * (scaled - mean - unit * along)


def params(mib):
    return pltpu.CompilerParams(vmem_limit_bytes=mib << 20)


def prefetch(grid, in_specs, out_specs, scratch=()):
    return pltpu.PrefetchScalarGridSpec(
        num_scalar_prefetch=1, grid=grid, in_specs=in_specs, out_specs=out_specs,
        scratch_shapes=list(scratch),
    )


def struct(shape, dtype):
    return jax.ShapeDtypeStruct(shape, dtype)


def nn_halves(rows, low_ref, high_ref):
    split = rows.shape[1] // 2
    return dot_nn(rows[:, :split], low_ref) + dot_nn(rows[:, split:], high_ref)


def nt_halves(rows, low_ref, high_ref):
    return jnp.concatenate([dot_nt(rows, low_ref), dot_nt(rows, high_ref)], axis=1)


def chunk_at(d, place, count):
    return d ^ (2 * (place % (count // 2)) + place // (count // 2))


def restore_kernel(count, where, own_ref, oth_ref, out_ref):
    batches, rows, width = oth_ref.shape
    chunk = width // count
    core, d = where[0], where[1]
    for batch in range(batches):
        for place in range(count):
            lanes = slice(place * chunk, (place + 1) * chunk)
            here = pl.ds(pl.multiple_of(chunk_at(d, place, count) * chunk, chunk), chunk)
            out_ref[batch, core, :, here] = own_ref[2 * batch + core, :, lanes].astype(out_ref.dtype)
            there = pl.ds(pl.multiple_of(chunk_at(d ^ 1, place, count) * chunk, chunk), chunk)
            out_ref[batch, 1 - core, :, there] = oth_ref[batch, :, lanes].astype(out_ref.dtype)


def chunk_matrix(d, width, count):
    chunk = width // count
    index = jnp.arange(width, dtype=jnp.int32)
    source = chunk_at(d, index // chunk, count) * chunk + index % chunk
    return (index[:, None] == source[None, :]).astype(bf16)


def restore(where, own, oth, count, dtype):
    batches, rows, width = oth.shape
    core, d = where[0], where[1]
    if (width // count) % 128:
        mine = lax.dynamic_index_in_dim(own.reshape(batches, 2, rows, width), core, 1, False)
        pair = []
        for piece, owner in ((mine, d), (oth, d ^ 1)):
            matrix = chunk_matrix(owner, width, count).T
            pair.append(jnp.dot(piece, matrix, preferred_element_type=f32).astype(dtype))
        return jnp.where(core == 0, jnp.stack(pair, axis=1), jnp.stack(pair[::-1], axis=1))
    whole = lambda shape: pl.BlockSpec(shape, lambda i, w: (0,) * len(shape))
    shape = (batches, 2, rows, width)
    return pl.pallas_call(
        functools.partial(restore_kernel, count),
        out_shape=struct(shape, dtype),
        grid_spec=prefetch((1,), [whole(own.shape), whole(oth.shape)], whole(shape)),
        compiler_params=params(24),
        cost_estimate=cost(3),
        name="restore",
    )(where, own, oth)


def scatter_chunks(where, ref, rows, count):
    chunk = rows.shape[1] // count
    if chunk % 128:
        ref[...] = rows
        return
    for place in range(count):
        target = pl.ds(pl.multiple_of(chunk_at(where[1], place, count) * chunk, chunk), chunk)
        ref[:, target] = rows[:, place * chunk : (place + 1) * chunk]


def gather_chunks(where, ref, count):
    chunk = ref.shape[1] // count
    if chunk % 128:
        return ref[...]
    return jnp.concatenate(
        [
            ref[:, pl.ds(pl.multiple_of(chunk_at(where[1], place, count) * chunk, chunk), chunk)]
            for place in range(count)
        ],
        axis=1,
    )


def project_kernel(count, where, x_ref, vec_ref, wa_ref, wb_ref, out_ref, rel_ref, n_ref, nbuf):
    slot, tile = pl.program_id(0), pl.program_id(1)
    here = pl.ds(pl.multiple_of(tile * ROWS, ROWS), ROWS)

    @pl.when(slot == 0)
    def _():
        rows = gather_chunks(where, x_ref, count)
        rel_ref[...] = rows
        unit, _ = normalise(rows.astype(f32))
        normed = (unit * vec_ref[0:1, :] + vec_ref[1:2, :]).astype(bf16)
        nbuf[here, :] = normed
        n_ref[...] = normed

    out_ref[0] = nn_halves(nbuf[here, :], wa_ref[0], wb_ref[0]).astype(bf16)


def project_more_kernel(where, n_ref, wa_ref, wb_ref, out_ref):
    out_ref[0] = nn_halves(n_ref[...], wa_ref[0], wb_ref[0]).astype(bf16)


def project(where, x, vecs, weights, first, count):
    rows, width = x.shape
    tiles = rows // ROWS
    out = width * 3 // 4
    half = width // 2
    weight = pl.BlockSpec(
        (1, half, out), lambda s, i, w: (2 * (1 - w[0] if first else w[0]) + s, 0, 0)
    )
    outs = pl.BlockSpec((1, ROWS, out), lambda s, i, w: (s, i, 0))
    once = pl.BlockSpec((ROWS, width), lambda s, i, w: (jnp.where(s == 0, i, tiles - 1), 0))
    shape = struct((2, rows, out), bf16)
    if first:
        return pl.pallas_call(
            functools.partial(project_kernel, count),
            out_shape=(shape, struct((rows, width), bf16), struct((rows, width), bf16)),
            grid_spec=prefetch(
                (2, tiles),
                [once, pl.BlockSpec(vecs.shape, lambda s, i, w: (0, 0)), weight, weight],
                (outs, once, once),
                [pltpu.VMEM((rows, width), bf16)],
            ),
            compiler_params=params(32),
            cost_estimate=cost(9),
            name="project",
        )(where, x, vecs, *weights)
    return pl.pallas_call(
        project_more_kernel,
        out_shape=shape,
        grid_spec=prefetch(
            (2, tiles),
            [pl.BlockSpec((ROWS, width), lambda s, i, w: (i, 0)), weight, weight],
            outs,
        ),
        compiler_params=params(32),
        cost_estimate=cost(8),
        name="project_more",
    )(where, x, *weights)


def out_kernel(count, where, x_ref, c0, c1, c2, c3, a0, a1, a2, a3, b0, b1, b2, b3, vec_ref,
               resid_ref, n_ref):
    total = x_ref[...].astype(f32)
    for part, low, high in ((c0, a0, b0), (c1, a1, b1), (c2, a2, b2), (c3, a3, b3)):
        total = total + nt_halves(part[0], low[0], high[0])
    resid_ref[...] = total
    unit, _ = normalise(total)
    scatter_chunks(where, n_ref, (unit * vec_ref[2:3, :] + vec_ref[3:4, :]).astype(bf16), count)


def out_weight_specs(width):
    return [
        pl.BlockSpec((1, width // 2, width // 4), lambda i, w, s=s: ((2 * w[0] + s) % 4, 0, 3))
        for s in range(4)
    ]


def out_project(where, x, contexts, weights, vecs, count):
    rows, width = x.shape
    tile = pl.BlockSpec((ROWS, width), lambda i, w: (i, 0))
    part = pl.BlockSpec((1, ROWS, width // 4), lambda i, w: (0, i, 0))
    return pl.pallas_call(
        functools.partial(out_kernel, count),
        out_shape=(struct((rows, width), f32), struct((rows, width), bf16)),
        grid_spec=prefetch(
            (rows // ROWS,),
            [tile, *[part] * 4, *out_weight_specs(width) * 2,
             pl.BlockSpec(vecs.shape, lambda i, w: (0, 0))],
            (tile, tile),
        ),
        compiler_params=params(32),
        cost_estimate=cost(7),
        name="out_project",
    )(where, x, *contexts, *[weights[0]] * 4, *[weights[1]] * 4, vecs)


def ffn_kernel(first, where, n_ref, cot_ref, nt_in, ct_in, up_ref, down_ref, bias_ref,
               ffn_ref, gn_ref, own_ref, oth_ref, gbias_ref, nt_out, ct_out, nt, ct, act, gup):
    step = pl.program_id(0)
    rows, width = n_ref.shape
    hidden = act.shape[1]
    up = up_ref[...].reshape(width, hidden)
    down = down_ref[...].reshape(width, hidden)
    chunk = own_ref.shape[3]
    count = width // chunk

    @pl.when(step == 0)
    def _():
        if first:
            for index in range(count):
                place = (index % 2 ^ where[0]) * (count // 2) + index // 2
                target = pl.ds(pl.multiple_of(place * chunk, chunk), chunk)
                lanes = slice(index * chunk, (index + 1) * chunk)
                nt[target, :] = n_ref[:, lanes].T
                ct[target, :] = cot_ref[:, lanes].T
            nt_out[...] = nt[...]
            ct_out[...] = ct[...]
        else:
            nt[...] = nt_in[...]
            ct[...] = ct_in[...]
        ffn_ref[...] = jnp.zeros_like(ffn_ref)
        gn_ref[...] = jnp.zeros_like(gn_ref)

    gbias_ref[...] = jnp.zeros_like(gbias_ref)

    def tile(index, carry):
        here = pl.ds(pl.multiple_of(index * ROWS, ROWS), ROWS)
        value = dot_nn(n_ref[here, :], up) + bias_ref[0]
        out, slope = gelu_pair(value)
        out = out.astype(bf16)
        act[here, :] = out
        back = (dot_nn(cot_ref[here, :], down) * slope).astype(bf16)
        gup[here, :] = back
        gbias_ref[0] += jnp.sum(back.astype(f32), axis=0, keepdims=True)
        ffn_ref[here, :] += dot_nt(out, down)
        gn_ref[here, :] += dot_nt(back, up)
        return carry

    lax.fori_loop(0, rows // ROWS, tile, 0)
    many = ROWS // chunk

    for grad_ref, start in ((own_ref, 0), (oth_ref, width // 2)):

        def grads(index, carry, grad_ref=grad_ref, start=start):
            here = pl.ds(pl.multiple_of(start + index * ROWS, ROWS), ROWS)
            there = pl.ds(index * many, many)
            shape = (many, chunk, hidden)
            grad_ref[there, 0, 0] = dot_nn(nt[here, :], gup[...]).astype(bf16).reshape(shape)
            grad_ref[there, 0, 1] = dot_nn(ct[here, :], act[...]).astype(bf16).reshape(shape)
            return carry

        lax.fori_loop(0, width // 2 // ROWS, grads, 0)


def ffn_first_kernel(where, n_ref, cot_ref, up_ref, down_ref, bias_ref,
                     ffn_ref, gn_ref, own_ref, oth_ref, gbias_ref, nt_out, ct_out, *scratch):
    ffn_kernel(True, where, n_ref, cot_ref, None, None, up_ref, down_ref, bias_ref,
               ffn_ref, gn_ref, own_ref, oth_ref, gbias_ref, nt_out, ct_out, *scratch)


def ffn_second_kernel(where, n_ref, cot_ref, nt_in, ct_in, up_ref, down_ref, bias_ref,
                      ffn_ref, gn_ref, own_ref, oth_ref, gbias_ref, *scratch):
    ffn_kernel(False, where, n_ref, cot_ref, nt_in, ct_in, up_ref, down_ref, bias_ref,
               ffn_ref, gn_ref, own_ref, oth_ref, gbias_ref, None, None, *scratch)


def feed_forward(where, normed, cot, weights, bias, turned=None):
    rows, width = normed.shape
    count, slots, _, chunk, hidden = weights.shape
    offset = 0 if turned is None else 2
    once = pl.Buffered(1)
    fixed = lambda shape: pl.BlockSpec(shape, lambda s, w: (0, 0), pipeline_mode=once)
    whole, flipped = fixed((rows, width)), fixed((width, rows))
    slot = lambda s, w: (w[2] + offset + s) % slots
    weight = lambda k: pl.BlockSpec(
        (count, 1, 1, chunk, hidden), lambda s, w: (0, slot(s, w), k, 0, 0)
    )
    grad = pl.BlockSpec((count // 2, 1, 2, chunk, hidden), lambda s, w: (0, s, 0, 0, 0))
    total = pl.BlockSpec((rows, width), lambda s, w: (0, 0))
    shape = struct((count // 2, 2, 2, chunk, hidden), bf16)
    outs = (
        struct((rows, width), f32), struct((rows, width), f32), shape, shape,
        struct((2, 1, hidden), f32),
    )
    out_specs = (total, total, grad, grad, pl.BlockSpec((1, 1, hidden), lambda s, w: (s, 0, 0)))
    vector = pl.BlockSpec((1, 1, hidden), lambda s, w: (slot(s, w), 0, 0))
    if turned is None:
        outs += (struct((width, rows), bf16), struct((width, rows), bf16))
        out_specs += (pl.BlockSpec((width, rows), lambda s, w: (0, 0)),) * 2
    scratch = [
        pltpu.VMEM((width, rows), bf16), pltpu.VMEM((width, rows), bf16),
        pltpu.VMEM((rows, hidden), bf16), pltpu.VMEM((rows, hidden), bf16),
    ]
    return pl.pallas_call(
        ffn_first_kernel if turned is None else ffn_second_kernel,
        out_shape=outs,
        grid_spec=prefetch(
            (2,),
            [whole, whole, *([flipped, flipped] if turned else []), weight(0), weight(1), vector],
            out_specs,
            scratch,
        ),
        compiler_params=params(60),
        cost_estimate=cost(36),
        name="feed_forward",
    )(where, normed, cot, *(turned or ()), weights, weights, bias)


def mid_kernel(count, where, resid_ref, f0_ref, f1_ref, n0_ref, n1_ref, cot_ref, a0, a1, a2, a3, b0, b1, b2, b3, vec_ref,
               out_ref, gres_ref, low_ref, own_ref, send_ref, sums_ref):
    tile = pl.program_id(0)
    resid = resid_ref[...]
    cot = gather_chunks(where, cot_ref, count).astype(f32)
    result = resid + gather_chunks(where, f0_ref, count) + gather_chunks(where, f1_ref, count)
    out_ref[...] = (result + vec_ref[4:5, :]).astype(bf16)
    unit, inverse = normalise(resid)
    grad = gather_chunks(where, n0_ref, count) + gather_chunks(where, n1_ref, count)
    gres = cot + norm_back(grad, unit, inverse, vec_ref[2:3, :])
    gres_ref[...] = gres
    low = gres.astype(bf16)
    low_ref[...] = low
    own_ref[0] = nn_halves(low, a0[0], b0[0]).astype(bf16)
    own_ref[1] = nn_halves(low, a1[0], b1[0]).astype(bf16)
    send_ref[0] = nn_halves(low, a2[0], b2[0]).astype(bf16)
    send_ref[1] = nn_halves(low, a3[0], b3[0]).astype(bf16)

    @pl.when(tile == 0)
    def _():
        sums_ref[...] = jnp.zeros_like(sums_ref)

    sums_ref[0:1, :] += jnp.sum(grad * unit, axis=0, keepdims=True)
    sums_ref[1:2, :] += jnp.sum(grad, axis=0, keepdims=True)
    sums_ref[2:3, :] += jnp.sum(cot, axis=0, keepdims=True)


def middle(where, resid, ffn, gn, cot, weights, vecs, count):
    rows, width = resid.shape
    tile = pl.BlockSpec((ROWS, width), lambda i, w: (i, 0))
    part = pl.BlockSpec((2, ROWS, width // 4), lambda i, w: (0, i, 0))
    piece = struct((2, rows, width // 4), bf16)
    return pl.pallas_call(
        functools.partial(mid_kernel, count),
        out_shape=(
            struct((rows, width), bf16), struct((rows, width), f32), struct((rows, width), bf16),
            piece, piece, struct((8, width), f32),
        ),
        grid_spec=prefetch(
            (rows // ROWS,),
            [*[tile] * 6, *out_weight_specs(width) * 2,
             pl.BlockSpec(vecs.shape, lambda i, w: (0, 0))],
            (tile, tile, tile, part, part, pl.BlockSpec((8, width), lambda i, w: (0, 0))),
        ),
        compiler_params=params(48),
        cost_estimate=cost(12),
        name="middle",
    )(where, resid, *ffn, *gn, cot, *[weights[0]] * 4, *[weights[1]] * 4, vecs)


def qkv_back(nt, lt, refs, context, a_ref, b_ref, total, ga_ref, gb_ref):
    rows, width = total.shape
    quarter, half = width // 4, width // 2

    def tile(index, carry):
        here = pl.ds(pl.multiple_of(index * ROWS, ROWS), ROWS)
        inner = refs[0, here, :]
        total[here, :] += nt_halves(inner, a_ref[0, :, : 3 * quarter], b_ref[0, :, : 3 * quarter])
        return carry

    lax.fori_loop(0, rows // ROWS, tile, 0)

    for grad_ref, start in ((ga_ref, 0), (gb_ref, half)):

        def grads(index, carry, grad_ref=grad_ref, start=start):
            here = pl.ds(pl.multiple_of(index * ROWS, ROWS), ROWS)
            there = pl.ds(pl.multiple_of(start + index * ROWS, ROWS), ROWS)
            grad_ref[0, here, : 3 * quarter] = dot_nn(nt[there, :], refs[0]).astype(bf16)
            grad_ref[0, here, 3 * quarter :] = dot_nn(lt[there, :], context[0]).astype(bf16)
            return carry

        lax.fori_loop(0, half // ROWS, grads, 0)


def early_kernel(where, n_ref, low_ref, d0, c0, d1, c1, a_ref, b_ref,
                 total_ref, ga_ref, gb_ref, nt, lt):
    step = pl.program_id(0)
    rows = n_ref.shape[0]

    @pl.when(step == 0)
    def _():
        for at in range(0, rows, ROWS):
            nt[:, at : at + ROWS] = n_ref[at : at + ROWS, :].T
            lt[:, at : at + ROWS] = low_ref[at : at + ROWS, :].T
        total_ref[...] = jnp.zeros_like(total_ref)
        qkv_back(nt, lt, d0, c0, a_ref, b_ref, total_ref, ga_ref, gb_ref)

    @pl.when(step == 1)
    def _():
        qkv_back(nt, lt, d1, c1, a_ref, b_ref, total_ref, ga_ref, gb_ref)


def late_kernel(where, n_ref, low_ref, d0, c0, d1, c1, a_ref, b_ref, before_ref, x_ref, gres_ref,
                vec_ref, gin_ref, ga_ref, gb_ref, sums_ref, nt, lt, total):
    step = pl.program_id(0)
    rows = n_ref.shape[0]

    @pl.when(step == 0)
    def _():
        for at in range(0, rows, ROWS):
            nt[:, at : at + ROWS] = n_ref[at : at + ROWS, :].T
            lt[:, at : at + ROWS] = low_ref[at : at + ROWS, :].T
        total[...] = before_ref[...]
        qkv_back(nt, lt, d0, c0, a_ref, b_ref, total, ga_ref, gb_ref)

    @pl.when(step == 1)
    def _():
        qkv_back(nt, lt, d1, c1, a_ref, b_ref, total, ga_ref, gb_ref)
        sums_ref[...] = jnp.zeros_like(sums_ref)

        def tile(index, carry):
            here = pl.ds(pl.multiple_of(index * ROWS, ROWS), ROWS)
            unit, inverse = normalise(x_ref[here, :].astype(f32))
            grad = total[here, :]
            result = gres_ref[here, :] + norm_back(grad, unit, inverse, vec_ref[0:1, :])
            gin_ref[here, :] = result.astype(bf16)
            sums_ref[0:1, :] += jnp.sum(grad * unit, axis=0, keepdims=True)
            sums_ref[1:2, :] += jnp.sum(grad, axis=0, keepdims=True)
            return carry

        lax.fori_loop(0, rows // ROWS, tile, 0)


def project_back(where, normed, low, grads, contexts, weights, part, rest=None):
    rows, width = normed.shape
    once = pl.Buffered(1)
    whole = pl.BlockSpec((rows, width), lambda s, w: (0, 0), pipeline_mode=once)
    total = pl.BlockSpec((rows, width), lambda s, w: (0, 0))
    slice_of = lambda lanes: pl.BlockSpec((1, rows, lanes), lambda s, w: (0, 0, 0), pipeline_mode=once)
    side = lambda s, w: jnp.where(s == 0, w[0], 1 - w[0])
    weight = pl.BlockSpec((1, width // 2, width), lambda s, w: (2 * side(s, w) + part, 0, 0))
    grad = pl.BlockSpec((1, width // 2, width), lambda s, w: (side(s, w), 0, 0))
    inner, context = slice_of(width * 3 // 4), slice_of(width // 4)
    shape = struct((2, width // 2, width), bf16)
    specs = [whole, whole, inner, context, inner, context, weight, weight]
    args = (where, normed, low, grads[0], contexts[0], grads[1], contexts[1], *weights)
    turned = [pltpu.VMEM((width, rows), bf16), pltpu.VMEM((width, rows), bf16)]
    if rest is None:
        return pl.pallas_call(
            early_kernel,
            out_shape=(struct((rows, width), f32), shape, shape),
            grid_spec=prefetch((2,), specs, (total, grad, grad), turned),
            compiler_params=params(56),
            cost_estimate=cost(19),
            name="project_back",
        )(*args)
    before, x, gres, vecs = rest
    return pl.pallas_call(
        late_kernel,
        out_shape=(struct((rows, width), bf16), shape, shape, struct((8, width), f32)),
        grid_spec=prefetch(
            (2,),
            [*specs, whole, whole, whole, pl.BlockSpec(vecs.shape, lambda s, w: (0, 0))],
            (total, grad, grad, pl.BlockSpec((8, width), lambda s, w: (0, 0))),
            [*turned, pltpu.VMEM((rows, width), f32)],
        ),
        compiler_params=params(58),
        cost_estimate=cost(25),
        name="project_back_last",
    )(*args, before, x, gres, vecs)


def after(value, *others):
    return lax.optimization_barrier((value, others))[0]


def unpack_kernel(p0, p1, p2, p3, up_ref, down_ref):
    total = p0[...].astype(f32) + p1[...].astype(f32) + p2[...].astype(f32) + p3[...].astype(f32)
    up_ref[...] = total[0]
    down_ref[...] = total[1].T


def unpack_pair(*pairs):
    _, rows, width = pairs[0].shape
    return pl.pallas_call(
        unpack_kernel,
        out_shape=(struct((rows, width), f32), struct((width, rows), f32)),
        compiler_params=params(16),
        name="unpack_pair",
    )(*pairs)


def per_device(
    block_in, norm1_gain, norm1_bias, w_query, w_key, w_value, w_out, norm2_gain, norm2_bias,
    w_up, up_bias, w_down, down_bias, segments, rand_blocks, glob_blocks, cotangent,
):
    dp_count, tensor_count = lax.axis_size("dp"), lax.axis_size("tensor")
    d, z = lax.axis_index("dp").astype(jnp.int32), lax.axis_index("tensor").astype(jnp.int32)
    core = d % 2
    where = jnp.stack([core, d, z])
    batches, local, width = block_in.shape
    share = local // 2
    blocks = segments.shape[1] // BLOCK
    pairs = dp_count // 2

    def move(value, to):
        routes = [
            (a * tensor_count + b, to(a, b)[0] * tensor_count + to(a, b)[1] % tensor_count)
            for a in range(dp_count)
            for b in range(tensor_count)
        ]
        return lax.ppermute(value, BOTH, routes)

    def other_core(value):
        return move(value, lambda a, b: (a ^ 1, b))

    def along(value, step):
        return move(value, lambda a, b: (a, b + step + tensor_count))

    def across(value, r):
        return move(value, lambda a, b: (a ^ (2 * r), b))

    def exchange(value):
        return lax.all_to_all(value, "tensor", split_axis=0, concat_axis=0, tiled=True)

    def half_of(value, which):
        value = value.reshape(batches, 2, share, width)
        return lax.dynamic_index_in_dim(value, which, 1, keepdims=False)

    def both_halves(keep, come):
        both = jnp.where(core == 0, jnp.stack([keep, come], 1), jnp.stack([come, keep], 1))
        return both.reshape(2 * batches * share, width)

    def give(value):
        return exchange(value).reshape(2 * batches, share, width)

    def finish(own, dtype):
        pairs_of = own.reshape(batches, 2, share, width)
        oth = other_core(lax.dynamic_index_in_dim(pairs_of, 1 - core, 1, keepdims=False))
        return restore(where, own, oth, dp_count, dtype).reshape(batches, local, width)


    rand_size = rand_blocks.shape[2] * blocks * RAND
    chunk = norm1_gain.shape[0]
    small = jnp.concatenate(
        [norm1_gain, norm1_bias, norm2_gain, norm2_bias, down_bias, up_bias[0],
         rand_blocks.reshape(-1).astype(bf16), glob_blocks.reshape(-1).astype(bf16)]
    )
    devices = dp_count * tensor_count
    small = jnp.broadcast_to(small[None], (devices, small.shape[0]))
    small = lax.all_to_all(small, BOTH, split_axis=0, concat_axis=0, tiled=True)
    shard = jnp.concatenate([w_query, w_key, w_value, w_out.T], axis=1)
    attn_slots = [along(shard, -k) for k in range(1, tensor_count)]
    their_segments = other_core(segments)
    x_come, cot_come = other_core(half_of(block_in, 1 - core)), other_core(half_of(cotangent, 1 - core))
    small, attn_slots, their_segments, x_come, cot_come = lax.optimization_barrier(
        (small, attn_slots, their_segments, x_come, cot_come)
    )
    small = small.reshape(dp_count, tensor_count, -1)
    vectors = small[..., : 6 * chunk].reshape(dp_count, tensor_count, 6, chunk).astype(f32)
    up_shift = vectors[:, :, 5].transpose(1, 0, 2).reshape(tensor_count, 1, -1)
    places = jnp.arange(dp_count, dtype=jnp.int32)
    order = chunk_at(d, places, dp_count)
    vecs = jnp.take(vectors[:, 0, :5], order, axis=0).transpose(1, 0, 2).reshape(5, width)
    vecs = jnp.concatenate([vecs, jnp.zeros((3, width), f32)])
    ints = lax.dynamic_index_in_dim(small, d - core + z % 2, 0, keepdims=False)[:, 6 * chunk :]
    ints = ints.astype(jnp.int32)
    rand_heads = ints[:, : batches * rand_size].reshape(tensor_count, batches, -1)
    rand_heads = lax.dynamic_index_in_dim(rand_heads, z // 2, 1, keepdims=False)
    rand_heads = lax.dynamic_slice_in_dim(jnp.roll(rand_heads, -z, axis=0), 2 * core, 2, 0)
    rand_heads = rand_heads.reshape(2 * rand_blocks.shape[2], blocks, RAND)
    glob_row = lax.dynamic_index_in_dim(
        ints[0, batches * rand_size :].reshape(batches, -1), z // 2, 0, keepdims=False
    )
    segment_row = lax.dynamic_index_in_dim(
        jnp.where(z % 2 == core, segments, their_segments), z // 2, 0, keepdims=False
    )
    segment_lanes = jnp.broadcast_to(segment_row[:, None], (segment_row.shape[0], 128))
    per_piece = share // BLOCK
    half = tensor_count * share

    def row_of(block):
        source, place = block // (2 * per_piece), block % (2 * per_piece)
        side = place // per_piece
        return jnp.where(side == core, 0, half) + source * share + (place % per_piece) * BLOCK

    table = attention_table(rand_heads, glob_row, row_of, 2 * half)

    attn_slots = jnp.stack([shard, *attn_slots])
    x = exchange(both_halves(half_of(block_in, core), x_come))
    attn_own = [attn_slots] + [across(attn_slots, r) for r in range(1, pairs)]
    pair_shard = after(jnp.stack([w_up, w_down.T]), attn_slots)
    pair_weights = lax.all_gather(pair_shard, BOTH, axis=0, tiled=False)
    pair_weights = pair_weights.reshape(dp_count, tensor_count, 2, *w_up.shape)
    cot_half = both_halves(half_of(cotangent, core), cot_come)
    x, attn_own, table, segment_lanes, vecs, up_shift, cot_half = lax.optimization_barrier(
        (x, attn_own, table, segment_lanes, vecs, up_shift, cot_half)
    )
    attn_own = jnp.concatenate(attn_own, axis=-2)
    attn_weights = (attn_own, other_core(attn_own))
    aligned = chunk % 128 == 0
    own_features = chunk_matrix(d, width, dp_count)
    if not aligned:
        x = jnp.dot(x, own_features, preferred_element_type=f32).astype(bf16)

    send, x, normed = project(where, x, vecs, attn_weights, True, dp_count)
    oth = other_core(send)
    own = project(where, normed, vecs, attn_weights, False, dp_count)
    ctx_own0, ctx_send0, lse0 = attn_fwd(table, own, oth, segment_lanes, blocks, 0)
    ctx_oth0 = other_core(ctx_send0)
    ctx_own1, ctx_send1, lse1 = attn_fwd(table, own, oth, segment_lanes, blocks, 1)
    ctx_oth1 = other_core(ctx_send1)
    cot = exchange(after(cot_half, own))
    resid, normed_two = out_project(
        where, x, (ctx_own0, ctx_own1, ctx_oth0, ctx_oth1), attn_weights, vecs, dp_count
    )
    if not aligned:
        normed_two = jnp.dot(normed_two, own_features.T, preferred_element_type=f32).astype(bf16)
    ffn0, gn0, pair_own0, pair_oth0, bias0, *turned = feed_forward(
        where, normed_two, cot, pair_weights, up_shift
    )
    pair_come0 = other_core(pair_oth0)
    ffn1, gn1, pair_own1, pair_oth1, bias1 = feed_forward(
        where, normed_two, cot, pair_weights, up_shift, turned
    )
    grad_bias = jnp.concatenate([bias0, bias1])
    ffn, grad_two = (ffn0, ffn1), (gn0, gn1)
    if not aligned:
        reorder = lambda v: jnp.dot(
            v, own_features.astype(v.dtype), precision=lax.Precision.HIGHEST,
            preferred_element_type=f32,
        ).astype(v.dtype)
        ffn, grad_two = map(reorder, ffn), map(reorder, grad_two)
        cot = reorder(cot)

    groups = [
        [(2 * xy + c) * tensor_count + t for xy in range(pairs)]
        for c in range(2)
        for t in range(tensor_count)
    ]

    def add_low(left, right):
        return (left.astype(f32) + right.astype(f32)).astype(left.dtype)

    def reduce_groups(total):
        flat = total.reshape(-1, total.shape[-1])
        result = lax.psum_scatter(
            flat, BOTH, scatter_dimension=0, axis_index_groups=groups, tiled=True
        )
        return result.reshape(total.shape[1:])

    pair_come0, ffn1 = lax.optimization_barrier((pair_come0, ffn1))
    ffn = (ffn[0], ffn1) if aligned else tuple(ffn)
    pair_total0 = reduce_groups(add_low(pair_own0, pair_come0))
    pair_come1 = other_core(pair_oth1)
    def reduce_core(own_half, other_half):
        theirs = other_core(other_half)
        size = own_half.shape[-2] // pairs
        return [
            (
                own_half[..., r * size : (r + 1) * size, :].astype(f32)
                + theirs[..., r * size : (r + 1) * size, :].astype(f32)
            ).astype(own_half.dtype)
            for r in range(pairs)
        ]

    def reduce_across(parts):
        total = parts[0].astype(f32)
        for r in range(1, pairs):
            total = total + across(parts[r], r).astype(f32)
        return total.astype(parts[0].dtype)

    def reduce_along(total, slots):
        return sum(
            (along(total[i], k) if k else total[i]).astype(f32) for i, k in enumerate(slots)
        )

    out, grad_resid, low, gctx_own, gctx_send, sums_two = middle(
        where, resid, ffn, tuple(grad_two), cot, attn_weights, vecs, dp_count
    )
    gctx_oth = other_core(gctx_send)
    pair_come1, gctx_oth = lax.optimization_barrier((pair_come1, gctx_oth))
    pair_total1 = reduce_groups(add_low(pair_own1, pair_come1))
    out_back = give(out)
    d_own0, d_send0 = attn_bwd(
        table, own, oth, gctx_own, gctx_oth, segment_lanes, lse0, blocks, 0
    )
    d_send0, out_back = lax.optimization_barrier((d_send0, out_back))
    d_oth0 = other_core(d_send0)
    total_one, ga0, gb0 = project_back(
        where, normed, low, (d_own0, d_oth0), (ctx_own0, ctx_oth0), attn_weights, 0
    )
    attn_parts0 = reduce_core(ga0, gb0)
    out_other = other_core(half_of(out_back, 1 - core))
    lse1, attn_parts0, out_other = lax.optimization_barrier((lse1, attn_parts0, out_other))
    pair_next = [along(pair_total0[1], 1)]
    d_own1, d_send1 = attn_bwd(
        table, own, oth, gctx_own, gctx_oth, segment_lanes, lse1, blocks, 1
    )
    d_send1, pair_next = lax.optimization_barrier((d_send1, pair_next))
    d_oth1 = other_core(d_send1)
    attn_total0 = reduce_across(attn_parts0)
    pair_next += [along(pair_total1[0], 2), along(pair_total1[1], 3)]
    grad_in, ga1, gb1, sums_one = project_back(
        where, normed, low, (d_own1, d_oth1), (ctx_own1, ctx_oth1), attn_weights, 1,
        (total_one, x, grad_resid, vecs),
    )
    block_out = restore(where, out_back, out_other, dp_count, bf16).reshape(batches, local, width)
    attn_total1 = reduce_across(reduce_core(ga1, gb1))
    grad_in = finish(give(grad_in), f32)
    g_attn = reduce_along(attn_total0, (0, 2)) + reduce_along(attn_total1, (1, 3))
    g_up, g_down = unpack_pair(pair_total0[0], *pair_next)

    piece = width // devices
    five = jnp.concatenate([sums_one[:2], sums_two[:3]]).reshape(5, dp_count, chunk)
    relative = places ^ d
    back = (relative % 2) * pairs + relative // 2
    five = jnp.take(five, back, axis=1).reshape(5, devices, piece).transpose(1, 0, 2)
    shift = jnp.roll(grad_bias, z, axis=0)
    shift = shift.reshape(tensor_count, dp_count, -1).transpose(1, 0, 2)
    sums = jnp.concatenate([five.reshape(devices, -1), shift.reshape(devices, -1)], axis=1)
    sums = lax.all_to_all(sums, BOTH, split_axis=0, concat_axis=0, tiled=True)
    sums = jnp.sum(sums, axis=0)
    vector_grads = [sums[i * piece : (i + 1) * piece] for i in range(5)]
    quarter = width // 4
    return (
        block_out, grad_in, vector_grads[0], vector_grads[1],
        g_attn[:, :quarter], g_attn[:, quarter : 2 * quarter], g_attn[:, 2 * quarter : 3 * quarter],
        g_attn[:, 3 * quarter :].T, vector_grads[2], vector_grads[3],
        g_up, sums[5 * piece :][None], g_down, vector_grads[4],
    )


def solution(mesh):
    rows, both = P(None, BOTH, None), P(BOTH)
    dp, split, turned = P("dp"), P("dp", "tensor"), P("tensor", "dp")
    return jax.shard_map(
        per_device,
        mesh=mesh,
        in_specs=(
            rows, dp, dp, split, split, split, turned, dp, dp, split, turned, turned, dp,
            P(None, "dp"), P(None, "dp", "tensor", None, None), P(None, "dp", None), rows,
        ),
        out_specs=(
            rows, rows, both, both, split, split, split, turned, both, both, split, turned, turned,
            both,
        ),
        check_vma=False,
    )
```

time: 923 us -> 683 us (0.74)
  blocking collectives: 229 us -> 11.7 us
  waiting for transfers between devices: 279 us -> 152 us
  Pallas kernels: 284 us -> 323 us
  other arithmetic: 13.5 us -> 48.3 us
  starting transfers between devices: 34.9 us -> 68.2 us
  local copies, waits for them, and re-layouts: 65.7 us -> 54.4 us
    unnamed x8 -> x3, waiting for transfers between devices: 168 us -> 0.05 us
    all_gather x2 -> x0, blocking collectives: 138 us -> none  [the longest x1 69.5 us: per_device(): vectors = lax.all_gather(vectors, BOTH, axis=0, tiled=False)]
    unnamed x1 -> x0, blocking collectives: 90.2 us -> none
    all_to_all x0 -> x5, waiting for transfers between devices: none -> 42 us  [the longest x4 29.1 us: exchange(): lax.all_to_all(value, 'tensor', split_axis=0, concat_axis=0, tiled=True)]
    pallas_call x7 -> x15, Pallas kernels: 284 us -> 323 us  [the longest x2 86.6 us: feed_forward(): pl.pallas_call(ffn_first_kernel if turned is None else ffn_second_kernel,...]
    all_to_all x0 -> x5, starting transfers between devices: none -> 25.4 us  [the longest x4 20.4 us: exchange(): lax.all_to_all(value, 'tensor', split_axis=0, concat_axis=0, tiled=True)]
    all_gather x2 -> x0, local copies, waits for them, and re-layouts: 24.1 us -> none  [gather(): whole = lax.all_gather(shard, ('tensor', 'dp'), axis=0, tiled=True)]
    convert_element_type x3 -> x10, other arithmetic: 4.31 us -> 25.3 us  [the longest x2 14.1 us: add_low(): return (left.astype(f32) + right.astype(f32)).astype(left.dtype)]
  transfers between devices with their start and end apart: 29 -> 42, of which waited for: 12 -> 11; matrix products, arithmetic and copies ran while one was open for 6% -> 11% of each run, Pallas kernels for 23% -> 41%
where the time goes in v2:
time: 683 us; the launch traced here: 674 us
  Pallas kernels  323 us (47%)
  waiting for transfers between devices  152 us (22%)
  starting transfers between devices  68.2 us (10%)
  local copies, waits for them, and re-layouts  54.4 us (8%)
  other arithmetic  48.3 us (7%)
  between operations  16.6 us (2%)
  blocking collectives  11.7 us (2%)
    ppermute x34, waiting for transfers between devices, move(): return lax.ppermute(value, BOTH, routes)  110 us
    pallas_call x2, Pallas kernels, feed_forward(): pl.pallas_call(ffn_first_kernel if turned is None else ffn_second_kernel,...  86.6 us
    pallas_call x2, Pallas kernels, attn_bwd(): pl.pallas_call(functools.partial(attn_bwd_kernel, layout, 2 * slot, unrol...  78.9 us
    pallas_call x2, Pallas kernels, attn_fwd(): pl.pallas_call(functools.partial(attn_fwd_kernel, layout, 2 * slot, unrol...  69.4 us
    ppermute x34, starting transfers between devices, move(): return lax.ppermute(value, BOTH, routes)  42.6 us
    unnamed x135, local copies, waits for them, and re-layouts  31.1 us
    all_to_all x4, waiting for transfers between devices, exchange(): lax.all_to_all(value, 'tensor', split_axis=0, concat_axis=0, tiled=True)  29.1 us
    pallas_call x1, Pallas kernels, project_back(): pl.pallas_call(late_kernel, out_shape=(struct((rows, width), bf16), shape...  25.1 us
  transfers between devices with their start and end apart: 42, of which 11 were waited for; matrix products, arithmetic and copies ran while one was open for 11% of the time, Pallas kernels for 41%

profile of v2, /device:TPU:0, one launch (start us, length us, event | category | flops | bytes accessed | tf_op | source)
XLA Modules:
  0.0 674.3 jit_solution(11373330366018518788)
XLA Ops:
  13.4 4.6 collective-permute-start
  24.0 5.1 all-to-all-start
  32.0 12.9 %all-to-all-done = bf16[32,2,770]{2,1,0:T(2,128)(2,1)S(1)} async-done(((bf16[32,2,770]{2,1,0:T(2,128)(2,1)}), bf16[32,2,770]{2,1,0:T(2,128)(2,1)S(1)}, u32[]{:S(2)}, u32[]{:S(2)}) %all-to-all-start) | async-done | bytes 98592 | tf_op jit(solution)/shard_map/all_to_all | solution.py:920
  56.9 5.5 all-to-all-start.1
  80.4 15.0 %collective-permute-done.7 = bf16[4,128,1024]{2,1,0:T(8,128)(2,1)} collective-permute-done((bf16[4,128,1024]{2,1,0:T(8,128)(2,1)}, bf16[4,128,1024]{2,1,0:T(8,128)(2,1)}, u32[]{:S(2)}, u32[]{:S(2)}) %collective-permute-start.7) | collective-permute-done | bytes 1048608 | tf_op jit(solution)/shard_map/ppermute | solution.py:881
  95.5 15.3 %collective-permute-done.8 = bf16[4,128,1024]{2,1,0:T(8,128)(2,1)} collective-permute-done((bf16[4,128,1024]{2,1,0:T(8,128)(2,1)}, bf16[4,128,1024]{2,1,0:T(8,128)(2,1)}, u32[]{:S(2)}, u32[]{:S(2)}) %collective-permute-start.8) | collective-permute-done | bytes 1048608 | tf_op jit(solution)/shard_map/ppermute | solution.py:881
  110.7 29.1 %all-to-all-done.1 = bf16[4,256,1024]{2,1,0:T(8,128)(2,1)S(1)} async-done(((bf16[4,256,1024]{2,1,0:T(8,128)(2,1)}), bf16[4,256,1024]{2,1,0:T(8,128)(2,1)S(1)}, u32[]{:S(2)}, u32[]{:S(2)}) %all-to-all-start.1) | async-done | bytes 2097184 | tf_op jit(solution)/shard_map/all_to_all | solution.py:893
  147.2 8.3 %collective-permute-done.9.wb_ref.b0.b1.b2.b3.b_ref = bf16[4,512,1024]{2,1,0:T(8,128)(2,1)S(1)} collective-permute-done((bf16[4,512,1024]{2,1,0:T(8,128)(2,1)S(1)}, bf16[4,512,1024]{2,1,0:T(8,128)(2,1)S(1)}, u32[]{:S(2)}, u32[]{:S(2)}) %collective-permute-start.9) | collective-permute-done | bytes 4194336 | tf_op jit(solution)/shard_map/ppermute | solution.py:881
  155.5 8.5 %project.1 = (bf16[2,1024,768]{2,1,0:T(8,128)(2,1)}, bf16[1024,1024]{1,0:T(8,128)(2,1)S(1)}, bf16[1024,1024]{1,0:T(8,128)(2,1)S(1)}) custom-call(s32[3]{0:T(128)S(1)} %pad_add_fusion.2.where, bf16[1024,1024]{1,0:T(8,128)(2,1)S(1)} %bitcast.110, f32[8,1024]{1,0:T(8,128)S(1)} %concatenate.35.vec_ref, ...), custom_call_target="tpu_custom_call" | custom-call | flops 8999999488 | bytes 1000 | tf_op jit(solution)/shard_map/project/pallas_call | solution.py:505
  164.1 5.6 project_more.1.q_own.k_own.v_own
  171.3 5.4 all-to-all-start.2
  179.0 34.5 %attn_fwd.2 = (bf16[1,1024,256]{2,1,0:T(8,128)(2,1)S(1)}, bf16[1,1024,256]{2,1,0:T(8,128)(2,1)S(1)}, f32[2,32,128]{2,1,0:T(8,128)S(1)}) custom-call(s32[962]{0:T(1024)S(1)} %pad_add_fusion.1.tab, bf16[2,1024,768]{2,1,0:T(8,128)(2,1)S(1)} %copy-done.26, bf16[2,1024,768]{2,1,0:T(8,128)(2,1)} %collective-permute-done.10.q_oth.k_oth.v_oth, ...), custom_call_target="tpu_custom_call" | custom-call | flops 32000000000 | bytes 1000 | tf_op jit(solution)/shard_map/attn_fwd/pallas_call | solution.py:298
  213.7 34.9 %attn_fwd.3 = (bf16[1,1024,256]{2,1,0:T(8,128)(2,1)S(1)}, bf16[1,1024,256]{2,1,0:T(8,128)(2,1)S(1)}, f32[2,32,128]{2,1,0:T(8,128)S(1)}) custom-call(s32[962]{0:T(1024)S(1)} %pad_add_fusion.1.tab, bf16[2,1024,768]{2,1,0:T(8,128)(2,1)S(1)} %copy-done.27, bf16[2,1024,768]{2,1,0:T(8,128)(2,1)} %collective-permute-done.10.q_oth.k_oth.v_oth, ...), custom_call_target="tpu_custom_call" | custom-call | flops 32000000000 | bytes 1000 | tf_op jit(solution)/shard_map/attn_fwd/pallas_call | solution.py:298
  250.6 5.8 out_project.1
  262.1 44.1 %feed_forward.2 = (f32[1024,1024]{1,0:T(8,128)}, f32[1024,1024]{1,0:T(8,128)}, bf16[4,2,2,128,1024]{4,3,2,1,0:T(8,128)(2,1)}, bf16[4,2,2,128,1024]{4,3,2,1,0:T(8...) custom-call(s32[3]{0:T(128)} %copy-done.16, ...), custom_call_target="tpu_custom_call" | custom-call | flops 35999997952 | bytes 1000 | tf_op jit(solution)/shard_map/feed_forward/pallas_call | solution.py:665
  306.4 42.5 %feed_forward.3 = (f32[1024,1024]{1,0:T(8,128)}, f32[1024,1024]{1,0:T(8,128)}, bf16[4,2,2,128,1024]{4,3,2,1,0:T(8,128)(2,1)}, bf16[4,2,2,128,1024]{4,3,2,1,0:T(8,128)(2,1)}, f32[2,1,1024]{2,1,0:T(1,128)}) custom-call(s32[3]{0:T(128)} %copy-done.16, bf16[1024,1024]{1,0:T(8,128)(2,1)} %copy-done.19, bf16[1024,1024]{1,0:T(8,128)(2,1)} %bitcast.31.cot_ref, ...), custom_call_target="tpu_custom_call" | custom-call | flops 35999997952 | bytes 1000 | tf_op jit(solution)/shard_map/feed_forward/pallas_call | solution.py:665
  349.4 14.6 %middle.1 = (bf16[1024,1024]{1,0:T(8,128)(2,1)S(1)}, f32[1024,1024]{1,0:T(8,128)}, bf16[1024,1024]{1,0:T(8,128)(2,1)}, bf16[2,1024,256]{2,1,0:T(8,128)(2,1)S(1)}...) custom-call(s32[3]{0:T(128)S(1)} %copy-done.17, f32[1024,1024]{1,0:T(8,128)} %copy-done.4, ...), custom_call_target="tpu_custom_call" | custom-call | flops 12000000000 | bytes 1000 | tf_op jit(solution)/shard_map/middle/pallas_call | solution.py:712
  366.4 5.0 all-to-all-start.3
  371.3 7.7 %add_convert_fusion.1 = bf16[4,2,2,128,1024]{4,3,2,1,0:T(8,128)(2,1)} fusion(bf16[4,2,2,128,1024]{4,3,2,1,0:T(8,128)(2,1)} %collective-permute-done.13, bf16[4,2,2,128,1024]{4,3,2,1,0:T(8,128)(2,1)} %get-tuple-element.143), kind=kLoop, calls=%fused_computation.3 | loop fusion | flops 8388608 | bytes 12582912 | tf_op jit(solution)/shard_map/convert_element_type | solution.py:1012
  380.4 39.3 %attn_bwd.2 = (bf16[1,1024,768]{2,1,0:T(8,128)(2,1)S(1)}, bf16[1,1024,768]{2,1,0:T(8,128)(2,1)}) custom-call(s32[962]{0:T(1024)S(1)} %pad_add_fusion.1.tab, bf16[2,1024,768]{2,1,0:T(8,128)(2,1)} %copy-done.25, bf16[2,1024,768]{2,1,0:T(8,128)(2,1)} %collective-permute-done.10.q_oth.k_oth.v_oth, bf16[2,1024,768]{2,1,0:T(8,128)(2,1)} %copy-done.25, ...), custom_call_target="tpu_custom_call" | custom-call | flops 36999999488 | bytes 1000 | tf_op jit(solution)/shard_map/attn_bwd/pallas_call | solution.py:327
  425.7 20.1 %project_back.1 = (f32[1024,1024]{1,0:T(8,128)}, bf16[2,512,1024]{2,1,0:T(8,128)(2,1)}, bf16[2,512,1024]{2,1,0:T(8,128)(2,1)}) custom-call(s32[3]{0:T(128)} %copy-done.16, bf16[1024,1024]{1,0:T(8,128)(2,1)} %copy-done.28, bf16[1024,1024]{1,0:T(8,128)(2,1)} %get-tuple-element.134.low_ref, bf16[1,1024,768]{2,1,0:T(8,128)(2,1)} %copy-done.29, ...), custom_call_target="tpu_custom_call" | custom-call | flops 19000000512 | bytes 1000 | tf_op jit(solution)/shard_map/project_back/pallas_call | solution.py:818
  447.4 6.4 add_convert_fusion
  453.9 4.3 add_convert_fusion.8
  465.0 39.5 %attn_bwd.3 = (bf16[1,1024,768]{2,1,0:T(8,128)(2,1)S(1)}, bf16[1,1024,768]{2,1,0:T(8,128)(2,1)}) custom-call(s32[962]{0:T(1024)S(1)} %pad_add_fusion.1.tab, bf16[2,1024,768]{2,1,0:T(8,128)(2,1)} %copy-done.25, bf16[2,1024,768]{2,1,0:T(8,128)(2,1)} %collective-permute-done.10.q_oth.k_oth.v_oth, bf16[2,1024,768]{2,1,0:T(8,128)(2,1)} %copy-done.25, ...), custom_call_target="tpu_custom_call" | custom-call | flops 36999999488 | bytes 1000 | tf_op jit(solution)/shard_map/attn_bwd/pallas_call | solution.py:327
  509.6 25.1 %project_back_last.1 = (bf16[1024,1024]{1,0:T(8,128)(2,1)}, bf16[2,512,1024]{2,1,0:T(8,128)(2,1)}, bf16[2,512,1024]{2,1,0:T(8,128)(2,1)}, f32[8,1024]{1,0:T(8,128)}) custom-call(s32[3]{0:T(128)} %copy-done.16, bf16[1024,1024]{1,0:T(8,128)(2,1)} %copy-done.28, bf16[1024,1024]{1,0:T(8,128)(2,1)} %get-tuple-element.134.low_ref, ...), custom_call_target="tpu_custom_call" | custom-call | flops 24999999488 | bytes 1000 | tf_op jit(solution)/shard_map/project_back_last/pallas_call | solution.py:827
  536.6 11.7 %all_to_all.56 = f32[32,1,288]{2,1,0:T(1,128)S(1)} all-to-all(f32[32,1,288]{2,1,0:T(1,128)S(1)} %all_to_all.48), channel_id=1, replica_groups=mesh['dp'=8,'tensor'=4] {'dp','tensor'}, dimensions={0} | all-to-all | bytes 73728 | tf_op jit(solution)/shard_map/all_to_all | solution.py:1091
  548.3 4.6 all-to-all-start.4
  569.6 9.9 %collective-permute-done.23 = bf16[2,128,1024]{2,1,0:T(8,128)(2,1)} collective-permute-done((bf16[2,128,1024]{2,1,0:T(8,128)(2,1)}, bf16[2,128,1024]{2,1,0:T(8,128)(2,1)}, u32[]{:S(2)}, u32[]{:S(2)}) %collective-permute-start.23) | collective-permute-done | bytes 524320 | tf_op jit(solution)/shard_map/ppermute | solution.py:881
  583.1 41.6 %collective-permute-done.32.p2 = bf16[2,128,1024]{2,1,0:T(8,128)(2,1)S(1)} collective-permute-done((bf16[2,128,1024]{2,1,0:T(8,128)(2,1)S(1)}, bf16[2,128,1024]{2,1,0:T(8,128)(2,1)S(1)}, u32[]{:S(2)}, u32[]{:S(2)}) %collective-permute-start.32) | collective-permute-done | bytes 524320 | tf_op jit(solution)/shard_map/ppermute | solution.py:881
  629.5 17.3 %collective-permute-start.31 = (bf16[128,1024]{1,0:T(8,128)(2,1)S(1)}, bf16[128,1024]{1,0:T(8,128)(2,1)S(1)}, u32[]{:S(2)}, u32[]{:S(2)}) collective-permute-start(bf16[128,1024]{1,0:T(8,128)(2,1)S(1)} %get-tuple-element.268), channel_id=1, source_target_pairs={{0,3},{1,0},{2,1},{3,2},{4,7},{5,4},{6,5},{7,6},{8,11},{9,8},{10,9... | collective-permute-start | bytes 786440 | tf_op jit(solution)/shard_map/ppermute | solution.py:881
  648.7 11.3 %collective-permute-done.31 = bf16[128,1024]{1,0:T(8,128)(2,1)S(1)} collective-permute-done((bf16[128,1024]{1,0:T(8,128)(2,1)S(1)}, bf16[128,1024]{1,0:T(8,128)(2,1)S(1)}, u32[]{:S(2)}, u32[]{:S(2)}) %collective-permute-start.31) | collective-permute-done | bytes 262176 | tf_op jit(solution)/shard_map/ppermute | solution.py:881
  662.6 4.7 restore.3
  (313 shorter events, 117.7 us)
Async XLA Ops:
  10.1 35.0 %collective-permute-start.4 = (bf16[2,256,1024]{2,1,0:T(8,128)(2,1)}, bf16[2,256,1024]{2,1,0:T(8,128)(2,1)}, u32[]{:S(2)}, u32[]{:S(2)}) collective-permute-start(bf16[2,256,1024]{2,1,0:T(8,128)(2,1)} %get-tuple-element.258), channel_id=1, source_target_pairs={{0,4},{1,5},{2,6},{3,7},{4,0},{5,1},{6,2},{7,3},{8,12},{9,13},{10,... | collective-permute-start | bytes 3145736 | tf_op jit(solution)/shard_map/ppermute | solution.py:881
  11.9 33.3 %collective-permute-start.5 = (bf16[2,256,1024]{2,1,0:T(8,128)(2,1)}, bf16[2,256,1024]{2,1,0:T(8,128)(2,1)S(1)}, u32[]{:S(2)}, u32[]{:S(2)}) collective-permute-start(bf16[2,256,1024]{2,1,0:T(8,128)(2,1)} %get-tuple-element.256), channel_id=1, source_target_pairs={{0,4},{1,5},{2,6},{3,7},{4,0},{5,1},{6,2},{7,3},{8,12},{9,13},{10,... | collective-permute-start | bytes 3145736 | tf_op jit(solution)/shard_map/ppermute | solution.py:881
  13.4 31.7 %collective-permute-start = (bf16[128,1024]{1,0:T(8,128)(2,1)}, bf16[128,1024]{1,0:T(8,128)(2,1)}, u32[]{:S(2)}, u32[]{:S(2)}) collective-permute-start(bf16[128,1024]{1,0:T(8,128)(2,1)} %get-tuple-element.270), channel_id=1, source_target_pairs={{0,3},{1,0},{2,1},{3,2},{4,7},{5,4},{6,5},{7,6},{8,11},{9,8},{10,9... | collective-permute-start | bytes 786440 | tf_op jit(solution)/shard_map/ppermute | solution.py:881
  18.0 27.1 %collective-permute-start.1 = (bf16[128,1024]{1,0:T(8,128)(2,1)}, bf16[128,1024]{1,0:T(8,128)(2,1)}, u32[]{:S(2)}, u32[]{:S(2)}) collective-permute-start(bf16[128,1024]{1,0:T(8,128)(2,1)} %get-tuple-element.270), channel_id=1, source_target_pairs={{0,2},{1,3},{2,0},{3,1},{4,6},{5,7},{6,4},{7,5},{8,10},{9,11},{10,... | collective-permute-start | bytes 786440 | tf_op jit(solution)/shard_map/ppermute | solution.py:881
  18.4 26.7 %collective-permute-start.2 = (bf16[128,1024]{1,0:T(8,128)(2,1)}, bf16[128,1024]{1,0:T(8,128)(2,1)}, u32[]{:S(2)}, u32[]{:S(2)}) collective-permute-start(bf16[128,1024]{1,0:T(8,128)(2,1)} %get-tuple-element.270), channel_id=1, source_target_pairs={{0,1},{1,2},{2,3},{3,0},{4,5},{5,6},{6,7},{7,4},{8,9},{9,10},{10,1... | collective-permute-start | bytes 786440 | tf_op jit(solution)/shard_map/ppermute | solution.py:881
  24.0 20.9 %all-to-all-start = ((bf16[32,2,770]{2,1,0:T(2,128)(2,1)}), bf16[32,2,770]{2,1,0:T(2,128)(2,1)S(1)}, u32[]{:S(2)}, u32[]{:S(2)}) async-start(bf16[32,2,770]{2,1,0:T(2,128)(2,1)} %reshape.448), calls=%async_computation | async-start | bytes 229376 | tf_op jit(solution)/shard_map/all_to_all | solution.py:920
  29.1 233.0 %all-gather.3.cloned.1.call-start = ((), (), s32[]{:S(2)}) async-start(), calls=%async_computation.10 | async-start | bytes 17301504 | tf_op jit(solution)/shard_map/all_gather | solution.py:962
  50.2 30.2 %collective-permute-start.6 = (bf16[4,128,1024]{2,1,0:T(8,128)(2,1)}, bf16[4,128,1024]{2,1,0:T(8,128)(2,1)}, u32[]{:S(2)}, u32[]{:S(2)}) collective-permute-start(bf16[4,128,1024]{2,1,0:T(8,128)(2,1)} %pad_maximum_fusion), channel_id=1, source_target_pairs={{0,8},{1,9},{2,10},{3,11},{4,12},{5,13},{6,14},{7,15},{8,0},{9,1},... | collective-permute-start | bytes 3145736 | tf_op jit(solution)/shard_map/ppermute | solution.py:881
  51.1 44.4 %collective-permute-start.7 = (bf16[4,128,1024]{2,1,0:T(8,128)(2,1)}, bf16[4,128,1024]{2,1,0:T(8,128)(2,1)}, u32[]{:S(2)}, u32[]{:S(2)}) collective-permute-start(bf16[4,128,1024]{2,1,0:T(8,128)(2,1)} %pad_maximum_fusion), channel_id=1, source_target_pairs={{0,16},{1,17},{2,18},{3,19},{4,20},{5,21},{6,22},{7,23},{8,24},{9,... | collective-permute-start | bytes 3145736 | tf_op jit(solution)/shard_map/ppermute | solution.py:881
  51.7 59.1 %collective-permute-start.8 = (bf16[4,128,1024]{2,1,0:T(8,128)(2,1)}, bf16[4,128,1024]{2,1,0:T(8,128)(2,1)}, u32[]{:S(2)}, u32[]{:S(2)}) collective-permute-start(bf16[4,128,1024]{2,1,0:T(8,128)(2,1)} %pad_maximum_fusion), channel_id=1, source_target_pairs={{0,24},{1,25},{2,26},{3,27},{4,28},{5,29},{6,30},{7,31},{8,16},{9,... | collective-permute-start | bytes 3145736 | tf_op jit(solution)/shard_map/ppermute | solution.py:881
  56.9 83.0 %all-to-all-start.1 = ((bf16[4,256,1024]{2,1,0:T(8,128)(2,1)}), bf16[4,256,1024]{2,1,0:T(8,128)(2,1)S(1)}, u32[]{:S(2)}, u32[]{:S(2)}) async-start(bf16[4,256,1024]{2,1,0:T(8,128)(2,1)} %bitcast.115), calls=%async_computation.1 | async-start | bytes 4194304 | tf_op jit(solution)/shard_map/all_to_all | solution.py:893
  171.3 90.8 %all-to-all-start.2 = ((bf16[4,256,1024]{2,1,0:T(8,128)(2,1)}), bf16[4,256,1024]{2,1,0:T(8,128)(2,1)}, u32[]{:S(2)}, u32[]{:S(2)}) async-start(bf16[4,256,1024]{2,1,0:T(8,128)(2,1)} %bitcast.116), calls=%async_computation.2 | async-start | bytes 4194304 | tf_op jit(solution)/shard_map/all_to_all | solution.py:893
  213.6 35.2 %collective-permute-start.11 = (bf16[1,1024,256]{2,1,0:T(8,128)(2,1)S(1)}, bf16[1,1024,256]{2,1,0:T(8,128)(2,1)S(1)}, u32[]{:S(2)}, u32[]{:S(2)}) collective-permute-start(bf16[1,1024,256]{2,1,0:T(8,128)(2,1)S(1)} %get-tuple-element.109), channel_id=1, source_target_pairs={{0,4},{1,5},{2,6},{3,7},{4,0},{5,1},{6,2},{7,3},{8,12},{9,13},{10,... | collective-permute-start | bytes 1572872 | tf_op jit(solution)/shard_map/ppermute | solution.py:881
  306.2 43.1 %collective-permute-start.13 = (bf16[4,2,2,128,1024]{4,3,2,1,0:T(8,128)(2,1)}, bf16[4,2,2,128,1024]{4,3,2,1,0:T(8,128)(2,1)}, u32[]{:S(2)}, u32[]{:S(2)}) collective-permute-start(bf16[4,2,2,128,1024]{4,3,2,1,0:T(8,128)(2,1)} %get-tuple-element.118), channel_id=1, source_target_pairs={{0,4},{1,5},{2,6},{3,7},{4,0},{5,1},{6,2},{7,3},{8,12},{9,13},{10,... | collective-permute-start | bytes 12582920 | tf_op jit(solution)/shard_map/ppermute | solution.py:881
  348.9 30.2 %collective-permute-start.14 = (bf16[4,2,2,128,1024]{4,3,2,1,0:T(8,128)(2,1)}, bf16[4,2,2,128,1024]{4,3,2,1,0:T(8,128)(2,1)}, u32[]{:S(2)}, u32[]{:S(2)}) collective-permute-start(bf16[4,2,2,128,1024]{4,3,2,1,0:T(8,128)(2,1)} %get-tuple-element.126), channel_id=1, source_target_pairs={{0,4},{1,5},{2,6},{3,7},{4,0},{5,1},{6,2},{7,3},{8,12},{9,13},{10,... | collective-permute-start | bytes 12582920 | tf_op jit(solution)/shard_map/ppermute | solution.py:881
  366.4 54.6 %all-to-all-start.3 = ((bf16[4,256,1024]{2,1,0:T(8,128)(2,1)}), bf16[4,256,1024]{2,1,0:T(8,128)(2,1)S(1)}, u32[]{:S(2)}, u32[]{:S(2)}) async-start(bf16[4,256,1024]{2,1,0:T(8,128)(2,1)} %bitcast.111), calls=%async_computation.3 | async-start | bytes 4194304 | tf_op jit(solution)/shard_map/all_to_all | solution.py:893
  371.3 87.8 %reduce-scatter.3.cloned.1.call-start = ((), (), s32[]{:S(2)}) async-start(), calls=%async_computation.8 | async-start | bytes 5242880 | tf_op jit(solution)/shard_map/reduce_scatter | solution.py:1016
  379.1 180.9 %reduce-scatter.5.cloned.1.call-start = ((), (), s32[]{:S(2)}) async-start(), calls=%async_computation.9 | async-start | bytes 5242880 | tf_op jit(solution)/shard_map/reduce_scatter | solution.py:1016
  460.4 45.4 %collective-permute-start.19 = (bf16[2,128,1024]{2,1,0:T(8,128)(2,1)S(1)}, bf16[2,128,1024]{2,1,0:T(8,128)(2,1)S(1)}, u32[]{:S(2)}, u32[]{:S(2)}) collective-permute-start(bf16[2,128,1024]{2,1,0:T(8,128)(2,1)S(1)} %bitcast.124), channel_id=1, source_target_pairs={{0,1},{1,2},{2,3},{3,0},{4,5},{5,6},{6,7},{7,4},{8,9},{9,10},{10,1... | collective-permute-start | bytes 1572872 | tf_op jit(solution)/shard_map/ppermute | solution.py:881
  536.3 28.0 %collective-permute-start.26 = (bf16[2,512,1024]{2,1,0:T(8,128)(2,1)}, bf16[2,512,1024]{2,1,0:T(8,128)(2,1)}, u32[]{:S(2)}, u32[]{:S(2)}) collective-permute-start(bf16[2,512,1024]{2,1,0:T(8,128)(2,1)} %get-tuple-element.158), channel_id=1, source_target_pairs={{0,4},{1,5},{2,6},{3,7},{4,0},{5,1},{6,2},{7,3},{8,12},{9,13},{10,... | collective-permute-start | bytes 6291464 | tf_op jit(solution)/shard_map/ppermute | solution.py:881
  548.3 79.8 %all-to-all-start.4 = ((bf16[4,256,1024]{2,1,0:T(8,128)(2,1)}), bf16[4,256,1024]{2,1,0:T(8,128)(2,1)}, u32[]{:S(2)}, u32[]{:S(2)}) async-start(bf16[4,256,1024]{2,1,0:T(8,128)(2,1)} %bitcast.119), calls=%async_computation.5 | async-start | bytes 4194304 | tf_op jit(solution)/shard_map/all_to_all | solution.py:893
  552.9 16.2 %collective-permute-start.24 = (bf16[2,128,1024]{2,1,0:T(8,128)(2,1)}, bf16[2,128,1024]{2,1,0:T(8,128)(2,1)}, u32[]{:S(2)}, u32[]{:S(2)}) collective-permute-start(bf16[2,128,1024]{2,1,0:T(8,128)(2,1)} %get-tuple-element.156), channel_id=1, source_target_pairs={{0,24},{1,25},{2,26},{3,27},{4,28},{5,29},{6,30},{7,31},{8,16},{9,... | collective-permute-start | bytes 1572872 | tf_op jit(solution)/shard_map/ppermute | solution.py:881
  553.5 26.0 %collective-permute-start.23 = (bf16[2,128,1024]{2,1,0:T(8,128)(2,1)}, bf16[2,128,1024]{2,1,0:T(8,128)(2,1)}, u32[]{:S(2)}, u32[]{:S(2)}) collective-permute-start(bf16[2,128,1024]{2,1,0:T(8,128)(2,1)} %get-tuple-element.155), channel_id=1, source_target_pairs={{0,16},{1,17},{2,18},{3,19},{4,20},{5,21},{6,22},{7,23},{8,24},{9,... | collective-permute-start | bytes 1572872 | tf_op jit(solution)/shard_map/ppermute | solution.py:881
  555.0 25.8 %collective-permute-start.22 = (bf16[2,128,1024]{2,1,0:T(8,128)(2,1)}, bf16[2,128,1024]{2,1,0:T(8,128)(2,1)}, u32[]{:S(2)}, u32[]{:S(2)}) collective-permute-start(bf16[2,128,1024]{2,1,0:T(8,128)(2,1)} %get-tuple-element.154), channel_id=1, source_target_pairs={{0,8},{1,9},{2,10},{3,11},{4,12},{5,13},{6,14},{7,15},{8,0},{9,1},... | collective-permute-start | bytes 1572872 | tf_op jit(solution)/shard_map/ppermute | solution.py:881
  561.4 63.2 %collective-permute-start.32 = (bf16[2,128,1024]{2,1,0:T(8,128)(2,1)S(1)}, bf16[2,128,1024]{2,1,0:T(8,128)(2,1)S(1)}, u32[]{:S(2)}, u32[]{:S(2)}) collective-permute-start(bf16[2,128,1024]{2,1,0:T(8,128)(2,1)S(1)} %bitcast.123), channel_id=1, source_target_pairs={{0,2},{1,3},{2,0},{3,1},{4,6},{5,7},{6,4},{7,5},{8,10},{9,11},{10,... | collective-permute-start | bytes 1572872 | tf_op jit(solution)/shard_map/ppermute | solution.py:881
  564.3 60.3 %collective-permute-start.33 = (bf16[2,128,1024]{2,1,0:T(8,128)(2,1)S(1)}, bf16[2,128,1024]{2,1,0:T(8,128)(2,1)S(1)}, u32[]{:S(2)}, u32[]{:S(2)}) collective-permute-start(bf16[2,128,1024]{2,1,0:T(8,128)(2,1)S(1)} %bitcast.122), channel_id=1, source_target_pairs={{0,3},{1,0},{2,1},{3,2},{4,7},{5,4},{6,5},{7,6},{8,11},{9,8},{10,9... | collective-permute-start | bytes 1572872 | tf_op jit(solution)/shard_map/ppermute | solution.py:881
  569.0 56.9 %collective-permute-start.29 = (bf16[2,128,1024]{2,1,0:T(8,128)(2,1)}, bf16[2,128,1024]{2,1,0:T(8,128)(2,1)}, u32[]{:S(2)}, u32[]{:S(2)}) collective-permute-start(bf16[2,128,1024]{2,1,0:T(8,128)(2,1)} %get-tuple-element.249), channel_id=1, source_target_pairs={{0,24},{1,25},{2,26},{3,27},{4,28},{5,29},{6,30},{7,31},{8,16},{9,... | collective-permute-start | bytes 1572872 | tf_op jit(solution)/shard_map/ppermute | solution.py:881
  579.5 46.4 %collective-permute-start.28 = (bf16[2,128,1024]{2,1,0:T(8,128)(2,1)}, bf16[2,128,1024]{2,1,0:T(8,128)(2,1)}, u32[]{:S(2)}, u32[]{:S(2)}) collective-permute-start(bf16[2,128,1024]{2,1,0:T(8,128)(2,1)} %get-tuple-element.250), channel_id=1, source_target_pairs={{0,16},{1,17},{2,18},{3,19},{4,20},{5,21},{6,22},{7,23},{8,24},{9,... | collective-permute-start | bytes 1572872 | tf_op jit(solution)/shard_map/ppermute | solution.py:881
  580.8 45.2 %collective-permute-start.27 = (bf16[2,128,1024]{2,1,0:T(8,128)(2,1)}, bf16[2,128,1024]{2,1,0:T(8,128)(2,1)}, u32[]{:S(2)}, u32[]{:S(2)}) collective-permute-start(bf16[2,128,1024]{2,1,0:T(8,128)(2,1)} %get-tuple-element.248), channel_id=1, source_target_pairs={{0,8},{1,9},{2,10},{3,11},{4,12},{5,13},{6,14},{7,15},{8,0},{9,1},... | collective-permute-start | bytes 1572872 | tf_op jit(solution)/shard_map/ppermute | solution.py:881
  624.6 24.0 %collective-permute-start.25 = (bf16[128,1024]{1,0:T(8,128)(2,1)S(1)}, bf16[128,1024]{1,0:T(8,128)(2,1)}, u32[]{:S(2)}, u32[]{:S(2)}) collective-permute-start(bf16[128,1024]{1,0:T(8,128)(2,1)S(1)} %slice_bitcast_fusion.2), channel_id=1, source_target_pairs={{0,2},{1,3},{2,0},{3,1},{4,6},{5,7},{6,4},{7,5},{8,10},{9,11},{10,... | collective-permute-start | bytes 786440 | tf_op jit(solution)/shard_map/ppermute | solution.py:881
  629.4 33.2 %collective-permute-start.21 = (bf16[2,256,1024]{2,1,0:T(8,128)(2,1)S(1)}, bf16[2,256,1024]{2,1,0:T(8,128)(2,1)S(1)}, u32[]{:S(2)}, u32[]{:S(2)}) collective-permute-start(bf16[2,256,1024]{2,1,0:T(8,128)(2,1)S(1)} %dynamic-slice_bitcast_fusion), channel_id=1, source_target_pairs={{0,4},{1,5},{2,6},{3,7},{4,0},{5,1},{6,2},{7,3},{8,12},{9,13},{10,... | collective-permute-start | bytes 3145736 | tf_op jit(solution)/shard_map/ppermute | solution.py:881
  629.5 30.5 %collective-permute-start.31 = (bf16[128,1024]{1,0:T(8,128)(2,1)S(1)}, bf16[128,1024]{1,0:T(8,128)(2,1)S(1)}, u32[]{:S(2)}, u32[]{:S(2)}) collective-permute-start(bf16[128,1024]{1,0:T(8,128)(2,1)S(1)} %get-tuple-element.268), channel_id=1, source_target_pairs={{0,3},{1,0},{2,1},{3,2},{4,7},{5,4},{6,5},{7,6},{8,11},{9,8},{10,9... | collective-permute-start | bytes 786440 | tf_op jit(solution)/shard_map/ppermute | solution.py:881
  (69 other events, 1372.6 us)
Sparse Core Ops, SparseCore 0:
  48.0 168.5 all-gather.2
  379.2 54.0 reduce-scatter.2
  454.0 54.0 reduce-scatter.4

commit v3 on v2

--- a/solution.py
+++ b/solution.py
@@ -418,6 +418,20 @@
             out_ref[batch, 1 - core, :, there] = oth_ref[batch, :, lanes].astype(out_ref.dtype)
 
 
+def restore_direct_kernel(count, where, p0, p1, p2, p3, out_ref):
+    width = p0.shape[1]
+    chunk = width // count
+    core, d, z = where[0], where[1], where[2]
+    for turn, piece in enumerate((p0, p1, p2, p3)):
+        index = z ^ turn
+        sender = d - core + index % 2
+        for place in range(count):
+            target = pl.ds(pl.multiple_of(chunk_at(sender, place, count) * chunk, chunk), chunk)
+            out_ref[index, :, target] = piece[:, place * chunk : (place + 1) * chunk].astype(
+                out_ref.dtype
+            )
+
+
 def chunk_matrix(d, width, count):
     chunk = width // count
     index = jnp.arange(width, dtype=jnp.int32)
@@ -565,33 +579,27 @@
     )(where, x, *contexts, *[weights[0]] * 4, *[weights[1]] * 4, vecs)
 
 
-def ffn_kernel(first, where, n_ref, cot_ref, nt_in, ct_in, up_ref, down_ref, bias_ref,
-               ffn_ref, gn_ref, own_ref, oth_ref, gbias_ref, nt_out, ct_out, nt, ct, act, gup):
+def ffn_kernel(first, n_ref, cot_ref, nt_in, ct_in, up_ref, down_ref, bias_ref,
+               ffn_ref, gn_ref, grad_ref, gbias_ref, nt_out, ct_out, nt, ct, act, gup, total, back_total):
     step = pl.program_id(0)
     rows, width = n_ref.shape
     hidden = act.shape[1]
     up = up_ref[...].reshape(width, hidden)
     down = down_ref[...].reshape(width, hidden)
-    chunk = own_ref.shape[3]
-    count = width // chunk
 
     @pl.when(step == 0)
     def _():
         if first:
-            for index in range(count):
-                place = (index % 2 ^ where[0]) * (count // 2) + index // 2
-                target = pl.ds(pl.multiple_of(place * chunk, chunk), chunk)
-                lanes = slice(index * chunk, (index + 1) * chunk)
-                nt[target, :] = n_ref[:, lanes].T
-                ct[target, :] = cot_ref[:, lanes].T
+            for at in range(0, rows, ROWS):
+                nt[:, at : at + ROWS] = n_ref[at : at + ROWS, :].T
+                ct[:, at : at + ROWS] = cot_ref[at : at + ROWS, :].T
             nt_out[...] = nt[...]
             ct_out[...] = ct[...]
-        else:
-            nt[...] = nt_in[...]
-            ct[...] = ct_in[...]
-        ffn_ref[...] = jnp.zeros_like(ffn_ref)
-        gn_ref[...] = jnp.zeros_like(gn_ref)
-
+        total[...] = jnp.zeros_like(total)
+        back_total[...] = jnp.zeros_like(back_total)
+
+    if not first:
+        nt, ct = nt_in, ct_in
     gbias_ref[...] = jnp.zeros_like(gbias_ref)
 
     def tile(index, carry):
@@ -603,65 +611,68 @@
         back = (dot_nn(cot_ref[here, :], down) * slope).astype(bf16)
         gup[here, :] = back
         gbias_ref[0] += jnp.sum(back.astype(f32), axis=0, keepdims=True)
-        ffn_ref[here, :] += dot_nt(out, down)
-        gn_ref[here, :] += dot_nt(back, up)
+        total[here, :] += dot_nt(out, down)
+        back_total[here, :] += dot_nt(back, up)
         return carry
 
     lax.fori_loop(0, rows // ROWS, tile, 0)
+    chunk = grad_ref.shape[3]
     many = ROWS // chunk
 
-    for grad_ref, start in ((own_ref, 0), (oth_ref, width // 2)):
-
-        def grads(index, carry, grad_ref=grad_ref, start=start):
-            here = pl.ds(pl.multiple_of(start + index * ROWS, ROWS), ROWS)
-            there = pl.ds(index * many, many)
-            shape = (many, chunk, hidden)
-            grad_ref[there, 0, 0] = dot_nn(nt[here, :], gup[...]).astype(bf16).reshape(shape)
-            grad_ref[there, 0, 1] = dot_nn(ct[here, :], act[...]).astype(bf16).reshape(shape)
-            return carry
-
-        lax.fori_loop(0, width // 2 // ROWS, grads, 0)
+    def grads(index, carry):
+        here = pl.ds(pl.multiple_of(index * ROWS, ROWS), ROWS)
+        there = pl.ds(index * many, many)
+        shape = (many, chunk, hidden)
+        grad_ref[there, 0, 0] = dot_nn(nt[here, :], gup[...]).astype(bf16).reshape(shape)
+        grad_ref[there, 0, 1] = dot_nn(ct[here, :], act[...]).astype(bf16).reshape(shape)
+        return carry
+
+    lax.fori_loop(0, width // ROWS, grads, 0)
+
+    @pl.when(step == pl.num_programs(0) - 1)
+    def _():
+        ffn_ref[...] = total[...].astype(bf16)
+        gn_ref[...] = back_total[...].astype(bf16)
 
 
 def ffn_first_kernel(where, n_ref, cot_ref, up_ref, down_ref, bias_ref,
-                     ffn_ref, gn_ref, own_ref, oth_ref, gbias_ref, nt_out, ct_out, *scratch):
-    ffn_kernel(True, where, n_ref, cot_ref, None, None, up_ref, down_ref, bias_ref,
-               ffn_ref, gn_ref, own_ref, oth_ref, gbias_ref, nt_out, ct_out, *scratch)
+                     ffn_ref, gn_ref, grad_ref, gbias_ref, nt_out, ct_out, nt, ct, *scratch):
+    ffn_kernel(True, n_ref, cot_ref, None, None, up_ref, down_ref, bias_ref,
+               ffn_ref, gn_ref, grad_ref, gbias_ref, nt_out, ct_out, nt, ct, *scratch)
 
 
 def ffn_second_kernel(where, n_ref, cot_ref, nt_in, ct_in, up_ref, down_ref, bias_ref,
-                      ffn_ref, gn_ref, own_ref, oth_ref, gbias_ref, *scratch):
-    ffn_kernel(False, where, n_ref, cot_ref, nt_in, ct_in, up_ref, down_ref, bias_ref,
-               ffn_ref, gn_ref, own_ref, oth_ref, gbias_ref, None, None, *scratch)
-
-
-def feed_forward(where, normed, cot, weights, bias, turned=None):
+                      ffn_ref, gn_ref, grad_ref, gbias_ref, *scratch):
+    ffn_kernel(False, n_ref, cot_ref, nt_in, ct_in, up_ref, down_ref, bias_ref,
+               ffn_ref, gn_ref, grad_ref, gbias_ref, None, None, None, None, *scratch)
+
+
+def feed_forward(where, normed, cot, weights, bias, slots_at, turned=None):
     rows, width = normed.shape
     count, slots, _, chunk, hidden = weights.shape
-    offset = 0 if turned is None else 2
     once = pl.Buffered(1)
     fixed = lambda shape: pl.BlockSpec(shape, lambda s, w: (0, 0), pipeline_mode=once)
     whole, flipped = fixed((rows, width)), fixed((width, rows))
-    slot = lambda s, w: (w[2] + offset + s) % slots
+    slot = lambda s, w: (w[2] + slots_at + s) % slots
     weight = lambda k: pl.BlockSpec(
         (count, 1, 1, chunk, hidden), lambda s, w: (0, slot(s, w), k, 0, 0)
     )
-    grad = pl.BlockSpec((count // 2, 1, 2, chunk, hidden), lambda s, w: (0, s, 0, 0, 0))
+    grad = pl.BlockSpec((count, 1, 2, chunk, hidden), lambda s, w: (0, s, 0, 0, 0))
     total = pl.BlockSpec((rows, width), lambda s, w: (0, 0))
-    shape = struct((count // 2, 2, 2, chunk, hidden), bf16)
     outs = (
-        struct((rows, width), f32), struct((rows, width), f32), shape, shape,
-        struct((2, 1, hidden), f32),
-    )
-    out_specs = (total, total, grad, grad, pl.BlockSpec((1, 1, hidden), lambda s, w: (s, 0, 0)))
+        struct((rows, width), bf16), struct((rows, width), bf16),
+        struct((count, 2, 2, chunk, hidden), bf16), struct((2, 1, hidden), f32),
+    )
+    out_specs = (total, total, grad, pl.BlockSpec((1, 1, hidden), lambda s, w: (s, 0, 0)))
     vector = pl.BlockSpec((1, 1, hidden), lambda s, w: (slot(s, w), 0, 0))
+    scratch = [
+        pltpu.VMEM((rows, hidden), bf16), pltpu.VMEM((rows, hidden), bf16),
+        pltpu.VMEM((rows, width), f32), pltpu.VMEM((rows, width), f32),
+    ]
     if turned is None:
         outs += (struct((width, rows), bf16), struct((width, rows), bf16))
         out_specs += (pl.BlockSpec((width, rows), lambda s, w: (0, 0)),) * 2
-    scratch = [
-        pltpu.VMEM((width, rows), bf16), pltpu.VMEM((width, rows), bf16),
-        pltpu.VMEM((rows, hidden), bf16), pltpu.VMEM((rows, hidden), bf16),
-    ]
+        scratch = [pltpu.VMEM((width, rows), bf16), pltpu.VMEM((width, rows), bf16), *scratch]
     return pl.pallas_call(
         ffn_first_kernel if turned is None else ffn_second_kernel,
         out_shape=outs,
@@ -682,10 +693,12 @@
     tile = pl.program_id(0)
     resid = resid_ref[...]
     cot = gather_chunks(where, cot_ref, count).astype(f32)
-    result = resid + gather_chunks(where, f0_ref, count) + gather_chunks(where, f1_ref, count)
+    result = resid + gather_chunks(where, f0_ref, count).astype(f32)
+    result = result + gather_chunks(where, f1_ref, count).astype(f32)
     out_ref[...] = (result + vec_ref[4:5, :]).astype(bf16)
     unit, inverse = normalise(resid)
-    grad = gather_chunks(where, n0_ref, count) + gather_chunks(where, n1_ref, count)
+    grad = gather_chunks(where, n0_ref, count).astype(f32)
+    grad = grad + gather_chunks(where, n1_ref, count).astype(f32)
     gres = cot + norm_back(grad, unit, inverse, vec_ref[2:3, :])
     gres_ref[...] = gres
     low = gres.astype(bf16)
@@ -727,116 +740,183 @@
     )(where, resid, *ffn, *gn, cot, *[weights[0]] * 4, *[weights[1]] * 4, vecs)
 
 
-def qkv_back(nt, lt, refs, context, a_ref, b_ref, total, ga_ref, gb_ref):
-    rows, width = total.shape
-    quarter, half = width // 4, width // 2
+def token_part(inner, a_ref, b_ref, total):
+    lanes = inner.shape[2]
 
     def tile(index, carry):
         here = pl.ds(pl.multiple_of(index * ROWS, ROWS), ROWS)
-        inner = refs[0, here, :]
-        total[here, :] += nt_halves(inner, a_ref[0, :, : 3 * quarter], b_ref[0, :, : 3 * quarter])
+        total[here, :] += nt_halves(inner[0, here, :], a_ref[0, :, :lanes], b_ref[0, :, :lanes])
         return carry
 
-    lax.fori_loop(0, rows // ROWS, tile, 0)
-
+    lax.fori_loop(0, total.shape[0] // ROWS, tile, 0)
+
+
+def weight_part(nt, lt, inner, context, ga_ref, gb_ref):
+    lanes = inner.shape[2]
+    half = ga_ref.shape[1]
     for grad_ref, start in ((ga_ref, 0), (gb_ref, half)):
 
         def grads(index, carry, grad_ref=grad_ref, start=start):
             here = pl.ds(pl.multiple_of(index * ROWS, ROWS), ROWS)
             there = pl.ds(pl.multiple_of(start + index * ROWS, ROWS), ROWS)
-            grad_ref[0, here, : 3 * quarter] = dot_nn(nt[there, :], refs[0]).astype(bf16)
-            grad_ref[0, here, 3 * quarter :] = dot_nn(lt[there, :], context[0]).astype(bf16)
+            grad_ref[0, here, :lanes] = dot_nn(nt[there, :], inner[0]).astype(bf16)
+            grad_ref[0, here, lanes:] = dot_nn(lt[there, :], context[0]).astype(bf16)
             return carry
 
         lax.fori_loop(0, half // ROWS, grads, 0)
 
 
-def early_kernel(where, n_ref, low_ref, d0, c0, d1, c1, a_ref, b_ref,
-                 total_ref, ga_ref, gb_ref, nt, lt):
+def turn_rows(source, target):
+    for at in range(0, source.shape[0], ROWS):
+        target[:, at : at + ROWS] = source[at : at + ROWS, :].T
+
+
+def back_early_kernel(where, d0, d1, a_ref, b_ref, n_ref, low_ref, c0, c1,
+                      total_ref, ga_ref, gb_ref, nt_ref, lt_ref):
     step = pl.program_id(0)
-    rows = n_ref.shape[0]
 
     @pl.when(step == 0)
     def _():
-        for at in range(0, rows, ROWS):
-            nt[:, at : at + ROWS] = n_ref[at : at + ROWS, :].T
-            lt[:, at : at + ROWS] = low_ref[at : at + ROWS, :].T
+        turn_rows(n_ref, nt_ref)
+        turn_rows(low_ref, lt_ref)
         total_ref[...] = jnp.zeros_like(total_ref)
-        qkv_back(nt, lt, d0, c0, a_ref, b_ref, total_ref, ga_ref, gb_ref)
+        token_part(d0, a_ref, b_ref, total_ref)
+        weight_part(nt_ref, lt_ref, d0, c0, ga_ref, gb_ref)
 
     @pl.when(step == 1)
     def _():
-        qkv_back(nt, lt, d1, c1, a_ref, b_ref, total_ref, ga_ref, gb_ref)
-
-
-def late_kernel(where, n_ref, low_ref, d0, c0, d1, c1, a_ref, b_ref, before_ref, x_ref, gres_ref,
-                vec_ref, gin_ref, ga_ref, gb_ref, sums_ref, nt, lt, total):
+        token_part(d1, a_ref, b_ref, total_ref)
+        weight_part(nt_ref, lt_ref, d1, c1, ga_ref, gb_ref)
+
+
+def back_tokens_kernel(where, d0, d1, a0, b0, a1, b1, before_ref, x_ref, gres_ref, vec_ref,
+                       gin_ref, sums_ref):
+    lanes = d0.shape[2]
+    grad = before_ref[...] + nt_halves(d0[0], a0[0, :, :lanes], b0[0, :, :lanes])
+    grad = grad + nt_halves(d1[0], a1[0, :, :lanes], b1[0, :, :lanes])
+    unit, inverse = normalise(x_ref[...].astype(f32))
+    result = gres_ref[...] + norm_back(grad, unit, inverse, vec_ref[0:1, :])
+    gin_ref[...] = result.astype(bf16)
+
+    @pl.when(pl.program_id(0) == 0)
+    def _():
+        sums_ref[...] = jnp.zeros_like(sums_ref)
+
+    sums_ref[0:1, :] += jnp.sum(grad * unit, axis=0, keepdims=True)
+    sums_ref[1:2, :] += jnp.sum(grad, axis=0, keepdims=True)
+
+
+def back_weights_kernel(where, d0, d1, nt_ref, lt_ref, c0, c1, ga_ref, gb_ref):
     step = pl.program_id(0)
-    rows = n_ref.shape[0]
 
     @pl.when(step == 0)
     def _():
-        for at in range(0, rows, ROWS):
-            nt[:, at : at + ROWS] = n_ref[at : at + ROWS, :].T
-            lt[:, at : at + ROWS] = low_ref[at : at + ROWS, :].T
-        total[...] = before_ref[...]
-        qkv_back(nt, lt, d0, c0, a_ref, b_ref, total, ga_ref, gb_ref)
+        weight_part(nt_ref, lt_ref, d0, c0, ga_ref, gb_ref)
 
     @pl.when(step == 1)
     def _():
-        qkv_back(nt, lt, d1, c1, a_ref, b_ref, total, ga_ref, gb_ref)
-        sums_ref[...] = jnp.zeros_like(sums_ref)
-
-        def tile(index, carry):
-            here = pl.ds(pl.multiple_of(index * ROWS, ROWS), ROWS)
-            unit, inverse = normalise(x_ref[here, :].astype(f32))
-            grad = total[here, :]
-            result = gres_ref[here, :] + norm_back(grad, unit, inverse, vec_ref[0:1, :])
-            gin_ref[here, :] = result.astype(bf16)
-            sums_ref[0:1, :] += jnp.sum(grad * unit, axis=0, keepdims=True)
-            sums_ref[1:2, :] += jnp.sum(grad, axis=0, keepdims=True)
-            return carry
-
-        lax.fori_loop(0, rows // ROWS, tile, 0)
-
-
-def project_back(where, normed, low, grads, contexts, weights, part, rest=None):
+        weight_part(nt_ref, lt_ref, d1, c1, ga_ref, gb_ref)
+
+
+def side(s, w):
+    return jnp.where(s == 0, w[0], 1 - w[0])
+
+
+def fixed_spec(shape):
+    return pl.BlockSpec(shape, lambda s, w: (0,) * len(shape), pipeline_mode=pl.Buffered(1))
+
+
+def back_early(where, normed, low, grads, contexts, weights, part):
     rows, width = normed.shape
-    once = pl.Buffered(1)
-    whole = pl.BlockSpec((rows, width), lambda s, w: (0, 0), pipeline_mode=once)
-    total = pl.BlockSpec((rows, width), lambda s, w: (0, 0))
-    slice_of = lambda lanes: pl.BlockSpec((1, rows, lanes), lambda s, w: (0, 0, 0), pipeline_mode=once)
-    side = lambda s, w: jnp.where(s == 0, w[0], 1 - w[0])
+    whole, total = fixed_spec((rows, width)), pl.BlockSpec((rows, width), lambda s, w: (0, 0))
+    inner, context = fixed_spec((1, rows, width * 3 // 4)), fixed_spec((1, rows, width // 4))
     weight = pl.BlockSpec((1, width // 2, width), lambda s, w: (2 * side(s, w) + part, 0, 0))
     grad = pl.BlockSpec((1, width // 2, width), lambda s, w: (side(s, w), 0, 0))
-    inner, context = slice_of(width * 3 // 4), slice_of(width // 4)
     shape = struct((2, width // 2, width), bf16)
-    specs = [whole, whole, inner, context, inner, context, weight, weight]
-    args = (where, normed, low, grads[0], contexts[0], grads[1], contexts[1], *weights)
-    turned = [pltpu.VMEM((width, rows), bf16), pltpu.VMEM((width, rows), bf16)]
-    if rest is None:
-        return pl.pallas_call(
-            early_kernel,
-            out_shape=(struct((rows, width), f32), shape, shape),
-            grid_spec=prefetch((2,), specs, (total, grad, grad), turned),
-            compiler_params=params(56),
-            cost_estimate=cost(19),
-            name="project_back",
-        )(*args)
-    before, x, gres, vecs = rest
+    turned = struct((width, rows), bf16)
     return pl.pallas_call(
-        late_kernel,
-        out_shape=(struct((rows, width), bf16), shape, shape, struct((8, width), f32)),
+        back_early_kernel,
+        out_shape=(struct((rows, width), f32), shape, shape, turned, turned),
         grid_spec=prefetch(
-            (2,),
-            [*specs, whole, whole, whole, pl.BlockSpec(vecs.shape, lambda s, w: (0, 0))],
-            (total, grad, grad, pl.BlockSpec((8, width), lambda s, w: (0, 0))),
-            [*turned, pltpu.VMEM((rows, width), f32)],
+            (2,), [inner, inner, weight, weight, whole, whole, context, context],
+            (total, grad, grad, total, total),
         ),
-        compiler_params=params(58),
-        cost_estimate=cost(25),
-        name="project_back_last",
-    )(*args, before, x, gres, vecs)
+        compiler_params=params(56),
+        cost_estimate=cost(19),
+        name="back_early",
+    )(where, *grads, *weights, normed, low, *contexts)
+
+
+def back_tokens(where, grads, weights, part, before, x, gres, vecs):
+    rows, width = x.shape
+    tile = pl.BlockSpec((ROWS, width), lambda i, w: (i, 0))
+    inner = pl.BlockSpec((1, ROWS, width * 3 // 4), lambda i, w: (0, i, 0))
+    weight = lambda s: pl.BlockSpec(
+        (1, width // 2, width), lambda i, w: (2 * side(s, w) + part, 0, 0)
+    )
+    return pl.pallas_call(
+        back_tokens_kernel,
+        out_shape=(struct((rows, width), bf16), struct((8, width), f32)),
+        grid_spec=prefetch(
+            (rows // ROWS,),
+            [inner, inner, weight(0), weight(0), weight(1), weight(1), tile, tile, tile,
+             pl.BlockSpec(vecs.shape, lambda i, w: (0, 0))],
+            (
+                pl.BlockSpec((ROWS, width), lambda i, w: (i ^ (w[2] // 2 * 2 + w[0]), 0)),
+                pl.BlockSpec((8, width), lambda i, w: (0, 0)),
+            ),
+        ),
+        compiler_params=params(48),
+        cost_estimate=cost(11),
+        name="back_tokens",
+    )(where, *grads, *weights, *weights, before, x, gres, vecs)
+
+
+def back_weights(where, grads, contexts, turned):
+    width, rows = turned[0].shape
+    inner, context = fixed_spec((1, rows, width * 3 // 4)), fixed_spec((1, rows, width // 4))
+    grad = pl.BlockSpec((1, width // 2, width), lambda s, w: (side(s, w), 0, 0))
+    shape = struct((2, width // 2, width), bf16)
+    return pl.pallas_call(
+        back_weights_kernel,
+        out_shape=(shape, shape),
+        grid_spec=prefetch(
+            (2,), [inner, inner, *[fixed_spec((width, rows))] * 2, context, context], (grad, grad)
+        ),
+        compiler_params=params(40),
+        cost_estimate=cost(10),
+        name="back_weights",
+    )(where, *grads, *turned, *contexts)
+
+
+def restore_direct(where, pieces, count, dtype):
+    rows, width = pieces[0].shape
+    if (width // count) % 128:
+        core, d, z = where[0], where[1], where[2]
+        fixed = []
+        for turn, piece in enumerate(pieces):
+            matrix = chunk_matrix(d - core + (z ^ turn) % 2, width, count)
+            fixed.append(jnp.dot(piece, matrix.T, preferred_element_type=f32).astype(dtype))
+        fixed = jnp.stack(fixed)
+        return jnp.stack([lax.dynamic_index_in_dim(fixed, z ^ i, 0, False) for i in range(4)])
+    whole = lambda shape: pl.BlockSpec(shape, lambda i, w: (0,) * len(shape))
+    return pl.pallas_call(
+        functools.partial(restore_direct_kernel, count),
+        out_shape=struct((4, rows, width), dtype),
+        grid_spec=prefetch((1,), [whole((rows, width))] * 4, whole((4, rows, width))),
+        compiler_params=params(24),
+        cost_estimate=cost(4),
+        name="restore_direct",
+    )(where, *pieces)
+
+
+def token_routes(dp_count, tensor_count, turn):
+    routes = []
+    for d in range(dp_count):
+        for z in range(tensor_count):
+            source = (2 * (z // 2) + d % 2) ^ turn
+            routes.append((d * tensor_count + z, (d - d % 2 + z % 2) * tensor_count + source))
+    return routes
 
 
 def after(value, *others):
@@ -903,12 +983,6 @@
     def give(value):
         return exchange(value).reshape(2 * batches, share, width)
 
-    def finish(own, dtype):
-        pairs_of = own.reshape(batches, 2, share, width)
-        oth = other_core(lax.dynamic_index_in_dim(pairs_of, 1 - core, 1, keepdims=False))
-        return restore(where, own, oth, dp_count, dtype).reshape(batches, local, width)
-
-
     rand_size = rand_blocks.shape[2] * blocks * RAND
     chunk = norm1_gain.shape[0]
     small = jnp.concatenate(
@@ -917,14 +991,16 @@
     )
     devices = dp_count * tensor_count
     small = jnp.broadcast_to(small[None], (devices, small.shape[0]))
-    small = lax.all_to_all(small, BOTH, split_axis=0, concat_axis=0, tiled=True)
     shard = jnp.concatenate([w_query, w_key, w_value, w_out.T], axis=1)
     attn_slots = [along(shard, -k) for k in range(1, tensor_count)]
     their_segments = other_core(segments)
     x_come, cot_come = other_core(half_of(block_in, 1 - core)), other_core(half_of(cotangent, 1 - core))
-    small, attn_slots, their_segments, x_come, cot_come = lax.optimization_barrier(
-        (small, attn_slots, their_segments, x_come, cot_come)
-    )
+    x_half = both_halves(half_of(block_in, core), x_come)
+    small, x_half = lax.optimization_barrier((small, x_half))
+    small = lax.all_to_all(small, BOTH, split_axis=0, concat_axis=0, tiled=True)
+    attn_slots, small = lax.optimization_barrier((attn_slots, small))
+    attn_slots = jnp.stack([shard, *attn_slots])
+    x = exchange(x_half)
     small = small.reshape(dp_count, tensor_count, -1)
     vectors = small[..., : 6 * chunk].reshape(dp_count, tensor_count, 6, chunk).astype(f32)
     up_shift = vectors[:, :, 5].transpose(1, 0, 2).reshape(tensor_count, 1, -1)
@@ -955,8 +1031,6 @@
 
     table = attention_table(rand_heads, glob_row, row_of, 2 * half)
 
-    attn_slots = jnp.stack([shard, *attn_slots])
-    x = exchange(both_halves(half_of(block_in, core), x_come))
     attn_own = [attn_slots] + [across(attn_slots, r) for r in range(1, pairs)]
     pair_shard = after(jnp.stack([w_up, w_down.T]), attn_slots)
     pair_weights = lax.all_gather(pair_shard, BOTH, axis=0, tiled=False)
@@ -985,43 +1059,26 @@
     )
     if not aligned:
         normed_two = jnp.dot(normed_two, own_features.T, preferred_element_type=f32).astype(bf16)
-    ffn0, gn0, pair_own0, pair_oth0, bias0, *turned = feed_forward(
-        where, normed_two, cot, pair_weights, up_shift
-    )
-    pair_come0 = other_core(pair_oth0)
-    ffn1, gn1, pair_own1, pair_oth1, bias1 = feed_forward(
-        where, normed_two, cot, pair_weights, up_shift, turned
-    )
-    grad_bias = jnp.concatenate([bias0, bias1])
+    ffn0, gn0, pair0, bias0, *turned = feed_forward(
+        where, normed_two, cot, pair_weights, up_shift, 2
+    )
+
+    def reduce_rows(total):
+        flat = total.reshape(-1, total.shape[-1])
+        result = lax.psum_scatter(flat, "dp", scatter_dimension=0, tiled=True)
+        return result.reshape(total.shape[1:])
+
+    ffn1, gn1, pair1, bias1 = feed_forward(
+        where, normed_two, cot, pair_weights, up_shift, 0, turned
+    )
+    pair_total0 = reduce_rows(pair0)
+    pair_total1 = reduce_rows(pair1)
+    grad_bias = jnp.concatenate([bias1, bias0])
     ffn, grad_two = (ffn0, ffn1), (gn0, gn1)
     if not aligned:
-        reorder = lambda v: jnp.dot(
-            v, own_features.astype(v.dtype), precision=lax.Precision.HIGHEST,
-            preferred_element_type=f32,
-        ).astype(v.dtype)
-        ffn, grad_two = map(reorder, ffn), map(reorder, grad_two)
-        cot = reorder(cot)
-
-    groups = [
-        [(2 * xy + c) * tensor_count + t for xy in range(pairs)]
-        for c in range(2)
-        for t in range(tensor_count)
-    ]
-
-    def add_low(left, right):
-        return (left.astype(f32) + right.astype(f32)).astype(left.dtype)
-
-    def reduce_groups(total):
-        flat = total.reshape(-1, total.shape[-1])
-        result = lax.psum_scatter(
-            flat, BOTH, scatter_dimension=0, axis_index_groups=groups, tiled=True
-        )
-        return result.reshape(total.shape[1:])
-
-    pair_come0, ffn1 = lax.optimization_barrier((pair_come0, ffn1))
-    ffn = (ffn[0], ffn1) if aligned else tuple(ffn)
-    pair_total0 = reduce_groups(add_low(pair_own0, pair_come0))
-    pair_come1 = other_core(pair_oth1)
+        reorder = lambda v: jnp.dot(v, own_features, preferred_element_type=f32).astype(bf16)
+        ffn, grad_two, cot = map(reorder, ffn), map(reorder, grad_two), reorder(cot)
+
     def reduce_core(own_half, other_half):
         theirs = other_core(other_half)
         size = own_half.shape[-2] // pairs
@@ -1033,11 +1090,26 @@
             for r in range(pairs)
         ]
 
+    def add_parts(first, others):
+        total = first.astype(f32)
+        for part in others:
+            total = total + part.astype(f32)
+        return total.astype(first.dtype)
+
     def reduce_across(parts):
-        total = parts[0].astype(f32)
-        for r in range(1, pairs):
-            total = total + across(parts[r], r).astype(f32)
-        return total.astype(parts[0].dtype)
+        return add_parts(parts[0], [across(parts[r], r) for r in range(1, pairs)])
+
+    piece = width // devices
+
+    def exchange_sums(sums_one, sums_two, grad_bias):
+        five = jnp.concatenate([sums_one[:2], sums_two[:3]]).reshape(5, dp_count, chunk)
+        relative = places ^ d
+        back = (relative % 2) * pairs + relative // 2
+        five = jnp.take(five, back, axis=1).reshape(5, devices, piece).transpose(1, 0, 2)
+        shift = jnp.roll(grad_bias, z, axis=0)
+        shift = shift.reshape(tensor_count, dp_count, -1).transpose(1, 0, 2)
+        sums = jnp.concatenate([five.reshape(devices, -1), shift.reshape(devices, -1)], axis=1)
+        return lax.all_to_all(sums, BOTH, split_axis=0, concat_axis=0, tiled=True)
 
     def reduce_along(total, slots):
         return sum(
@@ -1045,50 +1117,52 @@
         )
 
     out, grad_resid, low, gctx_own, gctx_send, sums_two = middle(
-        where, resid, ffn, tuple(grad_two), cot, attn_weights, vecs, dp_count
+        where, resid, tuple(ffn), tuple(grad_two), cot, attn_weights, vecs, dp_count
     )
     gctx_oth = other_core(gctx_send)
-    pair_come1, gctx_oth = lax.optimization_barrier((pair_come1, gctx_oth))
-    pair_total1 = reduce_groups(add_low(pair_own1, pair_come1))
     out_back = give(out)
     d_own0, d_send0 = attn_bwd(
         table, own, oth, gctx_own, gctx_oth, segment_lanes, lse0, blocks, 0
     )
     d_send0, out_back = lax.optimization_barrier((d_send0, out_back))
     d_oth0 = other_core(d_send0)
-    total_one, ga0, gb0 = project_back(
+    total_one, ga0, gb0, *turned = back_early(
         where, normed, low, (d_own0, d_oth0), (ctx_own0, ctx_oth0), attn_weights, 0
     )
     attn_parts0 = reduce_core(ga0, gb0)
     out_other = other_core(half_of(out_back, 1 - core))
     lse1, attn_parts0, out_other = lax.optimization_barrier((lse1, attn_parts0, out_other))
-    pair_next = [along(pair_total0[1], 1)]
     d_own1, d_send1 = attn_bwd(
         table, own, oth, gctx_own, gctx_oth, segment_lanes, lse1, blocks, 1
     )
-    d_send1, pair_next = lax.optimization_barrier((d_send1, pair_next))
+    attn_total0 = reduce_across(attn_parts0)
+    pair_next = [along(pair_total0[0], 2), along(pair_total0[1], 3)]
+    d_send1, attn_total0, pair_next = lax.optimization_barrier((d_send1, attn_total0, pair_next))
     d_oth1 = other_core(d_send1)
-    attn_total0 = reduce_across(attn_parts0)
-    pair_next += [along(pair_total1[0], 2), along(pair_total1[1], 3)]
-    grad_in, ga1, gb1, sums_one = project_back(
-        where, normed, low, (d_own1, d_oth1), (ctx_own1, ctx_oth1), attn_weights, 1,
-        (total_one, x, grad_resid, vecs),
-    )
+    ga1, gb1 = back_weights(where, (d_own1, d_oth1), (ctx_own1, ctx_oth1), turned)
+    total_one, ga1, gb1 = lax.optimization_barrier((total_one, ga1, gb1))
+    grad_in, sums_one = back_tokens(
+        where, (d_own1, d_oth1), attn_weights, 1, total_one, x, grad_resid, vecs
+    )
+    grad_back = [
+        lax.ppermute(
+            grad_in[turn * share : (turn + 1) * share], BOTH,
+            token_routes(dp_count, tensor_count, turn),
+        )
+        for turn in range(tensor_count)
+    ]
+    attn_parts1 = reduce_core(ga1, gb1)
+    pair_next.append(along(pair_total1[1], 1))
+    sums_one, attn_parts1 = lax.optimization_barrier((sums_one, attn_parts1))
+    sums = exchange_sums(sums_one, sums_two, grad_bias)
+    attn_come1 = [across(attn_parts1[r], r) for r in range(1, pairs)]
+    sums, attn_come1 = lax.optimization_barrier((sums, attn_come1))
+    attn_total1 = add_parts(attn_parts1[0], attn_come1)
     block_out = restore(where, out_back, out_other, dp_count, bf16).reshape(batches, local, width)
-    attn_total1 = reduce_across(reduce_core(ga1, gb1))
-    grad_in = finish(give(grad_in), f32)
     g_attn = reduce_along(attn_total0, (0, 2)) + reduce_along(attn_total1, (1, 3))
-    g_up, g_down = unpack_pair(pair_total0[0], *pair_next)
-
-    piece = width // devices
-    five = jnp.concatenate([sums_one[:2], sums_two[:3]]).reshape(5, dp_count, chunk)
-    relative = places ^ d
-    back = (relative % 2) * pairs + relative // 2
-    five = jnp.take(five, back, axis=1).reshape(5, devices, piece).transpose(1, 0, 2)
-    shift = jnp.roll(grad_bias, z, axis=0)
-    shift = shift.reshape(tensor_count, dp_count, -1).transpose(1, 0, 2)
-    sums = jnp.concatenate([five.reshape(devices, -1), shift.reshape(devices, -1)], axis=1)
-    sums = lax.all_to_all(sums, BOTH, split_axis=0, concat_axis=0, tiled=True)
+    g_up, g_down = unpack_pair(pair_total1[0], *pair_next)
+    grad_in = restore_direct(where, grad_back, dp_count, f32).reshape(batches, local, width)
+
     sums = jnp.sum(sums, axis=0)
     vector_grads = [sums[i * piece : (i + 1) * piece] for i in range(5)]
     quarter = width // 4

time: 683 us -> 617 us (0.903)
  other arithmetic: 48.3 us -> 28.4 us
  waiting for transfers between devices: 152 us -> 134 us
  blocking collectives: 11.7 us -> 0 us
  Pallas kernels: 323 us -> 312 us
    ppermute x34 -> x31, waiting for transfers between devices: 110 us -> 67 us  [move(): return lax.ppermute(value, BOTH, routes)]
    ppermute x0 -> x4, waiting for transfers between devices: none -> 29.9 us  [per_device(): lax.ppermute(grad_in[turn * share:(turn + 1) * share], BOTH, token_routes...]
    ppermute x34 -> x31, starting transfers between devices: 42.6 us -> 23.9 us  [move(): return lax.ppermute(value, BOTH, routes)]
    convert_element_type x4 -> x2, other arithmetic: 18 us -> 4.87 us  [add_parts(): return total.astype(first.dtype)]
    all_to_all x0 -> x1, starting transfers between devices: none -> 12.7 us  [exchange_sums(): return lax.all_to_all(sums, BOTH, split_axis=0, concat_axis=0, tiled=True)]
    all_to_all x1 -> x0, blocking collectives: 11.7 us -> none  [per_device(): sums = lax.all_to_all(sums, BOTH, split_axis=0, concat_axis=0, tiled=True)]
    ppermute x0 -> x4, starting transfers between devices: none -> 7.68 us  [per_device(): lax.ppermute(grad_in[turn * share:(turn + 1) * share], BOTH, token_routes...]
    all_to_all x4 -> x3, starting transfers between devices: 20.4 us -> 14.7 us  [exchange(): lax.all_to_all(value, 'tensor', split_axis=0, concat_axis=0, tiled=True)]
  transfers between devices with their start and end apart: 42 -> 43, of which waited for: 11 -> 17; matrix products, arithmetic and copies ran while one was open for 11% -> 9% of each run, Pallas kernels for 41% -> 44%
where the time goes in v3:
time: 617 us; the launch traced here: 609 us
  Pallas kernels  312 us (51%)
  waiting for transfers between devices  134 us (22%)
  starting transfers between devices  64.6 us (10%)
  local copies, waits for them, and re-layouts  53.8 us (9%)
  other arithmetic  28.4 us (5%)
  between operations  16.5 us (3%)
    pallas_call x2, Pallas kernels, feed_forward(): pl.pallas_call(ffn_first_kernel if turned is None else ffn_second_kernel,...  84.4 us
    pallas_call x2, Pallas kernels, attn_bwd(): pl.pallas_call(functools.partial(attn_bwd_kernel, layout, 2 * slot, unrol...  78.9 us
    pallas_call x2, Pallas kernels, attn_fwd(): pl.pallas_call(functools.partial(attn_fwd_kernel, layout, 2 * slot, unrol...  69 us
    ppermute x31, waiting for transfers between devices, move(): return lax.ppermute(value, BOTH, routes)  67 us
    unnamed x128, local copies, waits for them, and re-layouts  34.6 us
    ppermute x4, waiting for transfers between devices, per_device(): lax.ppermute(grad_in[turn * share:(turn + 1) * share], BOTH, token_routes...  29.9 us
    all_to_all x3, waiting for transfers between devices, exchange(): lax.all_to_all(value, 'tensor', split_axis=0, concat_axis=0, tiled=True)  26.5 us
    ppermute x31, starting transfers between devices, move(): return lax.ppermute(value, BOTH, routes)  23.9 us
  transfers between devices with their start and end apart: 43, of which 17 were waited for; matrix products, arithmetic and copies ran while one was open for 9% of the time, Pallas kernels for 44%

profile of v3, /device:TPU:0, one launch (start us, length us, event | category | flops | bytes accessed | tf_op | source)
XLA Modules:
  0.0 609.0 jit_solution(12736508281226365535)
XLA Ops:
  11.3 4.6 collective-permute-start.1
  26.5 5.1 all-to-all-start.1
  33.7 9.1 %all-to-all-done.1 = bf16[32,2,770]{2,1,0:T(2,128)(2,1)S(1)} async-done(((bf16[32,2,770]{2,1,0:T(2,128)(2,1)}), bf16[32,2,770]{2,1,0:T(2,128)(2,1)S(1)}, u32[]{:S(2)}, u32[]{:S(2)}) %all-to-all-start.1) | async-done | bytes 98592 | tf_op jit(solution)/shard_map/all_to_all | solution.py:1000
  49.2 5.1 all-to-all-start
  71.5 12.4 %collective-permute-done.4 = bf16[4,128,1024]{2,1,0:T(8,128)(2,1)} collective-permute-done((bf16[4,128,1024]{2,1,0:T(8,128)(2,1)}, bf16[4,128,1024]{2,1,0:T(8,128)(2,1)}, u32[]{:S(2)}, u32[]{:S(2)}) %collective-permute-start.4) | collective-permute-done | bytes 1048608 | tf_op jit(solution)/shard_map/ppermute | solution.py:961
  83.9 22.6 %collective-permute-done.6 = bf16[4,128,1024]{2,1,0:T(8,128)(2,1)} collective-permute-done((bf16[4,128,1024]{2,1,0:T(8,128)(2,1)}, bf16[4,128,1024]{2,1,0:T(8,128)(2,1)}, u32[]{:S(2)}, u32[]{:S(2)}) %collective-permute-start.6) | collective-permute-done | bytes 1048608 | tf_op jit(solution)/shard_map/ppermute | solution.py:961
  106.5 20.6 %all-to-all-done = bf16[4,256,1024]{2,1,0:T(8,128)(2,1)S(1)} async-done(((bf16[4,256,1024]{2,1,0:T(8,128)(2,1)}), bf16[4,256,1024]{2,1,0:T(8,128)(2,1)S(1)}, u32[]{:S(2)}, u32[]{:S(2)}) %all-to-all-start) | async-done | bytes 2097184 | tf_op jit(solution)/shard_map/all_to_all | solution.py:973
  133.4 7.1 %collective-permute-done.9.wb_ref.b0.b1.b2.b3.b_ref = bf16[4,512,1024]{2,1,0:T(8,128)(2,1)S(1)} collective-permute-done((bf16[4,512,1024]{2,1,0:T(8,128)(2,1)S(1)}, bf16[4,512,1024]{2,1,0:T(8,128)(2,1)S(1)}, u32[]{:S(2)}, u32[]{:S(2)}) %collective-permute-start.9) | collective-permute-done | bytes 4194336 | tf_op jit(solution)/shard_map/ppermute | solution.py:961
  140.5 8.4 %project.1 = (bf16[2,1024,768]{2,1,0:T(8,128)(2,1)}, bf16[1024,1024]{1,0:T(8,128)(2,1)S(1)}, bf16[1024,1024]{1,0:T(8,128)(2,1)S(1)}) custom-call(s32[3]{0:T(128)S(1)} %pad_add_fusion.2.where, bf16[1024,1024]{1,0:T(8,128)(2,1)S(1)} %bitcast.107, f32[8,1024]{1,0:T(8,128)S(1)} %concatenate.35.vec_ref, ...), custom_call_target="tpu_custom_call" | custom-call | flops 8999999488 | bytes 1000 | tf_op jit(solution)/shard_map/project/pallas_call | solution.py:519
  149.1 5.6 project_more.1.q_own.k_own.v_own
  156.4 4.5 all-to-all-start.2
  163.3 34.5 %attn_fwd.2 = (bf16[1,1024,256]{2,1,0:T(8,128)(2,1)S(1)}, bf16[1,1024,256]{2,1,0:T(8,128)(2,1)S(1)}, f32[2,32,128]{2,1,0:T(8,128)S(1)}) custom-call(s32[962]{0:T(1024)S(1)} %pad_add_fusion.1.tab, bf16[2,1024,768]{2,1,0:T(8,128)(2,1)S(1)} %copy-done.34, bf16[2,1024,768]{2,1,0:T(8,128)(2,1)} %collective-permute-done.10.q_oth.k_oth.v_oth, ...), custom_call_target="tpu_custom_call" | custom-call | flops 32000000000 | bytes 1000 | tf_op jit(solution)/shard_map/attn_fwd/pallas_call | solution.py:298
  198.2 34.6 %attn_fwd.3 = (bf16[1,1024,256]{2,1,0:T(8,128)(2,1)S(1)}, bf16[1,1024,256]{2,1,0:T(8,128)(2,1)S(1)}, f32[2,32,128]{2,1,0:T(8,128)S(1)}) custom-call(s32[962]{0:T(1024)S(1)} %pad_add_fusion.1.tab, bf16[2,1024,768]{2,1,0:T(8,128)(2,1)S(1)} %copy-done.35, bf16[2,1024,768]{2,1,0:T(8,128)(2,1)} %collective-permute-done.10.q_oth.k_oth.v_oth, ...), custom_call_target="tpu_custom_call" | custom-call | flops 32000000000 | bytes 1000 | tf_op jit(solution)/shard_map/attn_fwd/pallas_call | solution.py:298
  234.8 5.8 out_project.1
  246.2 42.8 %feed_forward.2 = (bf16[1024,1024]{1,0:T(8,128)(2,1)}, bf16[1024,1024]{1,0:T(8,128)(2,1)}, bf16[8,2,2,128,1024]{4,3,2,1,0:T(8,128)(2,1)}, f32[2,1,1024]{2,1,0:T(...) custom-call(s32[3]{0:T(128)} %copy-done.21, bf16[1024,1024]{1,0:T(8,128)(2,1)} %copy-done.24, ...), custom_call_target="tpu_custom_call" | custom-call | flops 35999997952 | bytes 1000 | tf_op jit(solution)/shard_map/feed_forward/pallas_call | solution.py:676
  289.1 41.6 %feed_forward.3 = (bf16[1024,1024]{1,0:T(8,128)(2,1)}, bf16[1024,1024]{1,0:T(8,128)(2,1)}, bf16[8,2,2,128,1024]{4,3,2,1,0:T(8,128)(2,1)}, f32[2,1,1024]{2,1,0:T(1,128)}) custom-call(s32[3]{0:T(128)} %copy-done.21, bf16[1024,1024]{1,0:T(8,128)(2,1)} %copy-done.24, bf16[1024,1024]{1,0:T(8,128)(2,1)} %bitcast.33.cot_ref, ...), custom_call_target="tpu_custom_call" | custom-call | flops 35999997952 | bytes 1000 | tf_op jit(solution)/shard_map/feed_forward/pallas_call | solution.py:676
  330.7 13.1 %middle.1 = (bf16[1024,1024]{1,0:T(8,128)(2,1)S(1)}, f32[1024,1024]{1,0:T(8,128)}, bf16[1024,1024]{1,0:T(8,128)(2,1)}, bf16[2,1024,256]{2,1,0:T(8,128)(2,1)S(1)}...) custom-call(s32[3]{0:T(128)S(1)} %copy-done.22, f32[1024,1024]{1,0:T(8,128)} %copy-done.4, ...), custom_call_target="tpu_custom_call" | custom-call | flops 12000000000 | bytes 1000 | tf_op jit(solution)/shard_map/middle/pallas_call | solution.py:725
  346.1 5.2 all-to-all-start.3
  353.2 39.4 %attn_bwd.2 = (bf16[1,1024,768]{2,1,0:T(8,128)(2,1)S(1)}, bf16[1,1024,768]{2,1,0:T(8,128)(2,1)}) custom-call(s32[962]{0:T(1024)S(1)} %pad_add_fusion.1.tab, bf16[2,1024,768]{2,1,0:T(8,128)(2,1)} %copy-done.33, bf16[2,1024,768]{2,1,0:T(8,128)(2,1)} %collective-permute-done.10.q_oth.k_oth.v_oth, bf16[2,1024,768]{2,1,0:T(8,128)(2,1)} %copy-done.33, ...), custom_call_target="tpu_custom_call" | custom-call | flops 36999999488 | bytes 1000 | tf_op jit(solution)/shard_map/attn_bwd/pallas_call | solution.py:327
  393.8 5.8 all-to-all-done.3.own_ref
  399.6 3.6 collective-permute-done.14.d1
  404.4 20.8 %back_early.1 = (f32[1024,1024]{1,0:T(8,128)}, bf16[2,512,1024]{2,1,0:T(8,128)(2,1)}, bf16[2,512,1024]{2,1,0:T(8,128)(2,1)}, bf16[1024,1024]{1,0:T(8,128)(2,1)}, bf16[1024,1024]{1,0:T(8,128)(2,1)}) custom-call(s32[3]{0:T(128)} %copy-done.21, bf16[1,1024,768]{2,1,0:T(8,128)(2,1)} %copy-done.39, bf16[1,1024,768]{2,1,0:T(8,128)(2,1)} %copy-done.53, ...), custom_call_target="tpu_custom_call" | custom-call | flops 19000000512 | bytes 1000 | tf_op jit(solution)/shard_map/back_early/pallas_call | solution.py:837
  425.8 3.7 collective-permute-done.15
  440.8 39.5 %attn_bwd.3 = (bf16[1,1024,768]{2,1,0:T(8,128)(2,1)S(1)}, bf16[1,1024,768]{2,1,0:T(8,128)(2,1)}) custom-call(s32[962]{0:T(1024)S(1)} %pad_add_fusion.1.tab, bf16[2,1024,768]{2,1,0:T(8,128)(2,1)} %copy-done.33, bf16[2,1024,768]{2,1,0:T(8,128)(2,1)} %collective-permute-done.10.q_oth.k_oth.v_oth, bf16[2,1024,768]{2,1,0:T(8,128)(2,1)} %copy-done.33, ...), custom_call_target="tpu_custom_call" | custom-call | flops 36999999488 | bytes 1000 | tf_op jit(solution)/shard_map/attn_bwd/pallas_call | solution.py:327
  485.6 3.4 collective-permute-done.22.d1
  493.6 8.7 %back_weights.1 = (bf16[2,512,1024]{2,1,0:T(8,128)(2,1)S(1)}, bf16[2,512,1024]{2,1,0:T(8,128)(2,1)}) custom-call(s32[3]{0:T(128)S(1)} %copy-done.23, bf16[1,1024,768]{2,1,0:T(8,128)(2,1)S(1)} %copy-done.31, bf16[1,1024,768]{2,1,0:T(8,128)(2,1)} %collective-permute-done.22.d1, bf16[1024,1024]{1,0:T(8,128)(2,1)S(1)} %copy-done.37, ...), custom_call_target="tpu_custom_call" | custom-call | flops 10000000000 | bytes 1000 | tf_op jit(solution)/shard_map/back_weights/pallas_call | solution.py:880
  508.2 10.6 %back_tokens.1 = (bf16[1024,1024]{1,0:T(8,128)(2,1)S(1)}, f32[8,1024]{1,0:T(8,128)S(1)}) custom-call(s32[3]{0:T(128)S(1)} %copy-done.23, bf16[1,1024,768]{2,1,0:T(8,128)(2,1)S(1)} %copy-done.32, bf16[1,1024,768]{2,1,0:T(8,128)(2,1)} %collective-permute-done.22.d1, bf16[4,512,1024]{2,1,0:T(8,128)(2,1)} %copy-done, bf16[4,512,1024]{2,1,0:T(8,128)(2,1)} %copy-done.2, ...), custom_call_target="tpu_custom_call" | custom-call | flops 11000000512 | bytes 1000 | tf_op jit(solution)/shard_map/back_tokens/pallas_call | solution.py:857
  538.5 12.7 %all-to-all-start.4 = ((f32[32,1,288]{2,1,0:T(1,128)}), f32[32,1,288]{2,1,0:T(1,128)S(1)}, u32[]{:S(2)}, u32[]{:S(2)}) async-start(f32[32,1,288]{2,1,0:T(1,128)} %all_to_all.48), calls=%async_computation.5 | async-start | bytes 98304 | tf_op jit(solution)/shard_map/all_to_all | solution.py:1112
  551.2 14.1 %collective-permute-done.25.p2 = bf16[256,1024]{1,0:T(8,128)(2,1)S(1)} collective-permute-done((bf16[256,1024]{1,0:T(8,128)(2,1)}, bf16[256,1024]{1,0:T(8,128)(2,1)S(1)}, u32[]{:S(2)}, u32[]{:S(2)}) %collective-permute-start.25) | collective-permute-done | bytes 524320 | tf_op jit(solution)/shard_map/ppermute | solution.py:1148
  565.3 13.5 %collective-permute-done.26.p3 = bf16[256,1024]{1,0:T(8,128)(2,1)S(1)} collective-permute-done((bf16[256,1024]{1,0:T(8,128)(2,1)}, bf16[256,1024]{1,0:T(8,128)(2,1)S(1)}, u32[]{:S(2)}, u32[]{:S(2)}) %collective-permute-start.26) | collective-permute-done | bytes 524320 | tf_op jit(solution)/shard_map/ppermute | solution.py:1148
  588.9 4.1 collective-permute-done.33
  593.0 7.4 %collective-permute-done.32 = bf16[128,1024]{1,0:T(8,128)(2,1)S(1)} collective-permute-done((bf16[128,1024]{1,0:T(8,128)(2,1)S(1)}, bf16[128,1024]{1,0:T(8,128)(2,1)S(1)}, u32[]{:S(2)}, u32[]{:S(2)}) %collective-permute-start.32) | collective-permute-done | bytes 262176 | tf_op jit(solution)/shard_map/ppermute | solution.py:961
  (306 shorter events, 122.7 us)
Async XLA Ops:
  9.0 13.8 %collective-permute-start = (bf16[2,256,1024]{2,1,0:T(8,128)(2,1)S(1)}, bf16[2,256,1024]{2,1,0:T(8,128)(2,1)S(1)}, u32[]{:S(2)}, u32[]{:S(2)}) collective-permute-start(bf16[2,256,1024]{2,1,0:T(8,128)(2,1)S(1)} %get-tuple-element.295), channel_id=1, source_target_pairs={{0,4},{1,5},{2,6},{3,7},{4,0},{5,1},{6,2},{7,3},{8,12},{9,13},{10,... | collective-permute-start | bytes 3145736 | tf_op jit(solution)/shard_map/ppermute | solution.py:961
  11.3 31.7 %collective-permute-start.1 = (bf16[128,1024]{1,0:T(8,128)(2,1)}, bf16[128,1024]{1,0:T(8,128)(2,1)}, u32[]{:S(2)}, u32[]{:S(2)}) collective-permute-start(bf16[128,1024]{1,0:T(8,128)(2,1)} %get-tuple-element.307), channel_id=1, source_target_pairs={{0,3},{1,0},{2,1},{3,2},{4,7},{5,4},{6,5},{7,6},{8,11},{9,8},{10,9... | collective-permute-start | bytes 786440 | tf_op jit(solution)/shard_map/ppermute | solution.py:961
  15.9 27.1 %collective-permute-start.2 = (bf16[128,1024]{1,0:T(8,128)(2,1)}, bf16[128,1024]{1,0:T(8,128)(2,1)}, u32[]{:S(2)}, u32[]{:S(2)}) collective-permute-start(bf16[128,1024]{1,0:T(8,128)(2,1)} %get-tuple-element.307), channel_id=1, source_target_pairs={{0,2},{1,3},{2,0},{3,1},{4,6},{5,7},{6,4},{7,5},{8,10},{9,11},{10,... | collective-permute-start | bytes 786440 | tf_op jit(solution)/shard_map/ppermute | solution.py:961
  15.9 27.1 %collective-permute-start.3 = (bf16[128,1024]{1,0:T(8,128)(2,1)}, bf16[128,1024]{1,0:T(8,128)(2,1)}, u32[]{:S(2)}, u32[]{:S(2)}) collective-permute-start(bf16[128,1024]{1,0:T(8,128)(2,1)} %get-tuple-element.307), channel_id=1, source_target_pairs={{0,1},{1,2},{2,3},{3,0},{4,5},{5,6},{6,7},{7,4},{8,9},{9,10},{10,1... | collective-permute-start | bytes 786440 | tf_op jit(solution)/shard_map/ppermute | solution.py:961
  26.5 16.3 %all-to-all-start.1 = ((bf16[32,2,770]{2,1,0:T(2,128)(2,1)}), bf16[32,2,770]{2,1,0:T(2,128)(2,1)S(1)}, u32[]{:S(2)}, u32[]{:S(2)}) async-start(bf16[32,2,770]{2,1,0:T(2,128)(2,1)} %reshape.438), calls=%async_computation.1 | async-start | bytes 229376 | tf_op jit(solution)/shard_map/all_to_all | solution.py:1000
  31.6 214.7 %all-gather.3.cloned.1.call-start = ((), (), s32[]{:S(2)}) async-start(), calls=%async_computation.9 | async-start | bytes 17301504 | tf_op jit(solution)/shard_map/all_gather | solution.py:1036
  49.2 77.9 %all-to-all-start = ((bf16[4,256,1024]{2,1,0:T(8,128)(2,1)}), bf16[4,256,1024]{2,1,0:T(8,128)(2,1)S(1)}, u32[]{:S(2)}, u32[]{:S(2)}) async-start(bf16[4,256,1024]{2,1,0:T(8,128)(2,1)} %bitcast.112), calls=%async_computation | async-start | bytes 4194304 | tf_op jit(solution)/shard_map/all_to_all | solution.py:973
  57.6 26.3 %collective-permute-start.4 = (bf16[4,128,1024]{2,1,0:T(8,128)(2,1)}, bf16[4,128,1024]{2,1,0:T(8,128)(2,1)}, u32[]{:S(2)}, u32[]{:S(2)}) collective-permute-start(bf16[4,128,1024]{2,1,0:T(8,128)(2,1)} %pad_maximum_fusion), channel_id=1, source_target_pairs={{0,8},{1,9},{2,10},{3,11},{4,12},{5,13},{6,14},{7,15},{8,0},{9,1},... | collective-permute-start | bytes 3145736 | tf_op jit(solution)/shard_map/ppermute | solution.py:961
  58.3 25.6 %collective-permute-start.5 = (bf16[4,128,1024]{2,1,0:T(8,128)(2,1)}, bf16[4,128,1024]{2,1,0:T(8,128)(2,1)}, u32[]{:S(2)}, u32[]{:S(2)}) collective-permute-start(bf16[4,128,1024]{2,1,0:T(8,128)(2,1)} %pad_maximum_fusion), channel_id=1, source_target_pairs={{0,16},{1,17},{2,18},{3,19},{4,20},{5,21},{6,22},{7,23},{8,24},{9,... | collective-permute-start | bytes 3145736 | tf_op jit(solution)/shard_map/ppermute | solution.py:961
  58.8 47.7 %collective-permute-start.6 = (bf16[4,128,1024]{2,1,0:T(8,128)(2,1)}, bf16[4,128,1024]{2,1,0:T(8,128)(2,1)}, u32[]{:S(2)}, u32[]{:S(2)}) collective-permute-start(bf16[4,128,1024]{2,1,0:T(8,128)(2,1)} %pad_maximum_fusion), channel_id=1, source_target_pairs={{0,24},{1,25},{2,26},{3,27},{4,28},{5,29},{6,30},{7,31},{8,16},{9,... | collective-permute-start | bytes 3145736 | tf_op jit(solution)/shard_map/ppermute | solution.py:961
  156.4 89.9 %all-to-all-start.2 = ((bf16[4,256,1024]{2,1,0:T(8,128)(2,1)}), bf16[4,256,1024]{2,1,0:T(8,128)(2,1)}, u32[]{:S(2)}, u32[]{:S(2)}) async-start(bf16[4,256,1024]{2,1,0:T(8,128)(2,1)} %bitcast.113), calls=%async_computation.2 | async-start | bytes 4194304 | tf_op jit(solution)/shard_map/all_to_all | solution.py:973
  160.8 275.3 %reduce-scatter.3.cloned.1.call-start = ((), (), s32[]{:S(2)}) async-start(), calls=%async_computation.7 | async-start | bytes 9437184 | tf_op jit(solution)/shard_map/reduce_scatter | solution.py:1068
  197.8 35.2 %collective-permute-start.11 = (bf16[1,1024,256]{2,1,0:T(8,128)(2,1)S(1)}, bf16[1,1024,256]{2,1,0:T(8,128)(2,1)S(1)}, u32[]{:S(2)}, u32[]{:S(2)}) collective-permute-start(bf16[1,1024,256]{2,1,0:T(8,128)(2,1)S(1)} %get-tuple-element.117), channel_id=1, source_target_pairs={{0,4},{1,5},{2,6},{3,7},{4,0},{5,1},{6,2},{7,3},{8,12},{9,13},{10,... | collective-permute-start | bytes 1572872 | tf_op jit(solution)/shard_map/ppermute | solution.py:961
  346.1 53.5 %all-to-all-start.3 = ((bf16[4,256,1024]{2,1,0:T(8,128)(2,1)}), bf16[4,256,1024]{2,1,0:T(8,128)(2,1)S(1)}, u32[]{:S(2)}, u32[]{:S(2)}) async-start(bf16[4,256,1024]{2,1,0:T(8,128)(2,1)} %bitcast.108), calls=%async_computation.3 | async-start | bytes 4194304 | tf_op jit(solution)/shard_map/all_to_all | solution.py:973
  351.2 155.0 %reduce-scatter.5.cloned.1.call-start = ((), (), s32[]{:S(2)}) async-start(), calls=%async_computation.8 | async-start | bytes 9437184 | tf_op jit(solution)/shard_map/reduce_scatter | solution.py:1068
  432.6 47.8 %collective-permute-start.19 = (bf16[2,128,1024]{2,1,0:T(8,128)(2,1)}, bf16[2,128,1024]{2,1,0:T(8,128)(2,1)}, u32[]{:S(2)}, u32[]{:S(2)}) collective-permute-start(bf16[2,128,1024]{2,1,0:T(8,128)(2,1)} %get-tuple-element.150), channel_id=1, source_target_pairs={{0,24},{1,25},{2,26},{3,27},{4,28},{5,29},{6,30},{7,31},{8,16},{9,... | collective-permute-start | bytes 1572872 | tf_op jit(solution)/shard_map/ppermute | solution.py:961
  432.6 47.8 %collective-permute-start.18 = (bf16[2,128,1024]{2,1,0:T(8,128)(2,1)}, bf16[2,128,1024]{2,1,0:T(8,128)(2,1)}, u32[]{:S(2)}, u32[]{:S(2)}) collective-permute-start(bf16[2,128,1024]{2,1,0:T(8,128)(2,1)} %get-tuple-element.149), channel_id=1, source_target_pairs={{0,16},{1,17},{2,18},{3,19},{4,20},{5,21},{6,22},{7,23},{8,24},{9,... | collective-permute-start | bytes 1572872 | tf_op jit(solution)/shard_map/ppermute | solution.py:961
  434.4 46.1 %collective-permute-start.17 = (bf16[2,128,1024]{2,1,0:T(8,128)(2,1)}, bf16[2,128,1024]{2,1,0:T(8,128)(2,1)}, u32[]{:S(2)}, u32[]{:S(2)}) collective-permute-start(bf16[2,128,1024]{2,1,0:T(8,128)(2,1)} %get-tuple-element.148), channel_id=1, source_target_pairs={{0,8},{1,9},{2,10},{3,11},{4,12},{5,13},{6,14},{7,15},{8,0},{9,1},... | collective-permute-start | bytes 1572872 | tf_op jit(solution)/shard_map/ppermute | solution.py:961
  437.5 46.2 %collective-permute-start.20 = (bf16[2,128,1024]{2,1,0:T(8,128)(2,1)S(1)}, bf16[2,128,1024]{2,1,0:T(8,128)(2,1)S(1)}, u32[]{:S(2)}, u32[]{:S(2)}) collective-permute-start(bf16[2,128,1024]{2,1,0:T(8,128)(2,1)S(1)} %bitcast.119), channel_id=1, source_target_pairs={{0,2},{1,3},{2,0},{3,1},{4,6},{5,7},{6,4},{7,5},{8,10},{9,11},{10,... | collective-permute-start | bytes 1572872 | tf_op jit(solution)/shard_map/ppermute | solution.py:961
  437.6 46.9 %collective-permute-start.21 = (bf16[2,128,1024]{2,1,0:T(8,128)(2,1)S(1)}, bf16[2,128,1024]{2,1,0:T(8,128)(2,1)S(1)}, u32[]{:S(2)}, u32[]{:S(2)}) collective-permute-start(bf16[2,128,1024]{2,1,0:T(8,128)(2,1)S(1)} %bitcast.118), channel_id=1, source_target_pairs={{0,3},{1,0},{2,1},{3,2},{4,7},{5,4},{6,5},{7,6},{8,11},{9,8},{10,9... | collective-permute-start | bytes 1572872 | tf_op jit(solution)/shard_map/ppermute | solution.py:961
  503.7 26.2 %collective-permute-start.27 = (bf16[2,512,1024]{2,1,0:T(8,128)(2,1)}, bf16[2,512,1024]{2,1,0:T(8,128)(2,1)}, u32[]{:S(2)}, u32[]{:S(2)}) collective-permute-start(bf16[2,512,1024]{2,1,0:T(8,128)(2,1)} %get-tuple-element.163), channel_id=1, source_target_pairs={{0,4},{1,5},{2,6},{3,7},{4,0},{5,1},{6,2},{7,3},{8,12},{9,13},{10,... | collective-permute-start | bytes 6291464 | tf_op jit(solution)/shard_map/ppermute | solution.py:961
  507.6 17.5 %collective-permute-start.34 = (bf16[2,128,1024]{2,1,0:T(8,128)(2,1)S(1)}, bf16[2,128,1024]{2,1,0:T(8,128)(2,1)S(1)}, u32[]{:S(2)}, u32[]{:S(2)}) collective-permute-start(bf16[2,128,1024]{2,1,0:T(8,128)(2,1)S(1)} %bitcast.120), channel_id=1, source_target_pairs={{0,1},{1,2},{2,3},{3,0},{4,5},{5,6},{6,7},{7,4},{8,9},{9,10},{10,1... | collective-permute-start | bytes 1572872 | tf_op jit(solution)/shard_map/ppermute | solution.py:961
  520.2 13.8 %collective-permute-start.23 = (bf16[256,1024]{1,0:T(8,128)(2,1)}, bf16[256,1024]{1,0:T(8,128)(2,1)S(1)}, u32[]{:S(2)}, u32[]{:S(2)}) collective-permute-start(bf16[256,1024]{1,0:T(8,128)(2,1)} %get-tuple-element.291), channel_id=1, source_target_pairs={{0,0},{1,4},{2,2},{3,6},{4,1},{5,5},{6,3},{7,7},{8,8},{9,12},{10,1... | collective-permute-start | bytes 1572872 | tf_op jit(solution)/shard_map/ppermute | solution.py:1148
  522.0 14.9 %collective-permute-start.24 = (bf16[256,1024]{1,0:T(8,128)(2,1)}, bf16[256,1024]{1,0:T(8,128)(2,1)S(1)}, u32[]{:S(2)}, u32[]{:S(2)}) collective-permute-start(bf16[256,1024]{1,0:T(8,128)(2,1)} %get-tuple-element.290), channel_id=1, source_target_pairs={{0,1},{1,5},{2,3},{3,7},{4,0},{5,4},{6,2},{7,6},{8,9},{9,13},{10,1... | collective-permute-start | bytes 1572872 | tf_op jit(solution)/shard_map/ppermute | solution.py:1148
  526.3 39.0 %collective-permute-start.25 = (bf16[256,1024]{1,0:T(8,128)(2,1)}, bf16[256,1024]{1,0:T(8,128)(2,1)S(1)}, u32[]{:S(2)}, u32[]{:S(2)}) collective-permute-start(bf16[256,1024]{1,0:T(8,128)(2,1)} %get-tuple-element.289), channel_id=1, source_target_pairs={{0,2},{1,6},{2,0},{3,4},{4,3},{5,7},{6,1},{7,5},{8,10},{9,14},{10,... | collective-permute-start | bytes 1572872 | tf_op jit(solution)/shard_map/ppermute | solution.py:1148
  528.2 50.6 %collective-permute-start.26 = (bf16[256,1024]{1,0:T(8,128)(2,1)}, bf16[256,1024]{1,0:T(8,128)(2,1)S(1)}, u32[]{:S(2)}, u32[]{:S(2)}) collective-permute-start(bf16[256,1024]{1,0:T(8,128)(2,1)} %get-tuple-element.288), channel_id=1, source_target_pairs={{0,3},{1,7},{2,1},{3,5},{4,2},{5,6},{6,0},{7,4},{8,11},{9,15},{10,... | collective-permute-start | bytes 1572872 | tf_op jit(solution)/shard_map/ppermute | solution.py:1148
  533.9 48.4 %collective-permute-start.28 = (bf16[2,128,1024]{2,1,0:T(8,128)(2,1)}, bf16[2,128,1024]{2,1,0:T(8,128)(2,1)}, u32[]{:S(2)}, u32[]{:S(2)}) collective-permute-start(bf16[2,128,1024]{2,1,0:T(8,128)(2,1)} %get-tuple-element.168), channel_id=1, source_target_pairs={{0,8},{1,9},{2,10},{3,11},{4,12},{5,13},{6,14},{7,15},{8,0},{9,1},... | collective-permute-start | bytes 1572872 | tf_op jit(solution)/shard_map/ppermute | solution.py:961
  534.0 48.4 %collective-permute-start.29 = (bf16[2,128,1024]{2,1,0:T(8,128)(2,1)}, bf16[2,128,1024]{2,1,0:T(8,128)(2,1)}, u32[]{:S(2)}, u32[]{:S(2)}) collective-permute-start(bf16[2,128,1024]{2,1,0:T(8,128)(2,1)} %get-tuple-element.169), channel_id=1, source_target_pairs={{0,16},{1,17},{2,18},{3,19},{4,20},{5,21},{6,22},{7,23},{8,24},{9,... | collective-permute-start | bytes 1572872 | tf_op jit(solution)/shard_map/ppermute | solution.py:961
  536.9 45.5 %collective-permute-start.30 = (bf16[2,128,1024]{2,1,0:T(8,128)(2,1)}, bf16[2,128,1024]{2,1,0:T(8,128)(2,1)}, u32[]{:S(2)}, u32[]{:S(2)}) collective-permute-start(bf16[2,128,1024]{2,1,0:T(8,128)(2,1)} %get-tuple-element.170), channel_id=1, source_target_pairs={{0,24},{1,25},{2,26},{3,27},{4,28},{5,29},{6,30},{7,31},{8,16},{9,... | collective-permute-start | bytes 1572872 | tf_op jit(solution)/shard_map/ppermute | solution.py:961
  538.5 43.9 %all-to-all-start.4 = ((f32[32,1,288]{2,1,0:T(1,128)}), f32[32,1,288]{2,1,0:T(1,128)S(1)}, u32[]{:S(2)}, u32[]{:S(2)}) async-start(f32[32,1,288]{2,1,0:T(1,128)} %all_to_all.48), calls=%async_computation.5 | async-start | bytes 98304 | tf_op jit(solution)/shard_map/all_to_all | solution.py:1112
  565.3 23.6 %collective-permute-start.31 = (bf16[128,1024]{1,0:T(8,128)(2,1)}, bf16[128,1024]{1,0:T(8,128)(2,1)S(1)}, u32[]{:S(2)}, u32[]{:S(2)}) collective-permute-start(bf16[128,1024]{1,0:T(8,128)(2,1)} %slice_bitcast_fusion.2), channel_id=1, source_target_pairs={{0,2},{1,3},{2,0},{3,1},{4,6},{5,7},{6,4},{7,5},{8,10},{9,11},{10,... | collective-permute-start | bytes 786440 | tf_op jit(solution)/shard_map/ppermute | solution.py:961
  586.3 14.1 %collective-permute-start.32 = (bf16[128,1024]{1,0:T(8,128)(2,1)S(1)}, bf16[128,1024]{1,0:T(8,128)(2,1)S(1)}, u32[]{:S(2)}, u32[]{:S(2)}) collective-permute-start(bf16[128,1024]{1,0:T(8,128)(2,1)S(1)} %get-tuple-element.304), channel_id=1, source_target_pairs={{0,1},{1,2},{2,3},{3,0},{4,5},{5,6},{6,7},{7,4},{8,9},{9,10},{10,1... | collective-permute-start | bytes 786440 | tf_op jit(solution)/shard_map/ppermute | solution.py:961
  (66 other events, 695.3 us)
Sparse Core Ops, SparseCore 0:
  45.4 180.2 all-gather.2
  289.2 70.6 reduce-scatter.2
  363.7 71.2 reduce-scatter.4

commit v4 on v3

--- a/solution.py
+++ b/solution.py
@@ -113,55 +113,52 @@
     qbuf[:half, :] = q_own[0] * scale
     qbuf[half:, :] = q_oth[0] * scale
 
-    def one_block(block):
-        row = pl.multiple_of(tab[block], BLOCK)
-        shared, drawn = slot_offsets(tab, layout, pair, block)
-        scores = dot_nt(gather_rows(kaug, shared, drawn, 256), query_rows(qbuf, kaug, row))
-        top = jnp.max(scores, axis=0, keepdims=True)
-        weight = jnp.exp(scores - top)
-        total = jnp.sum(weight, axis=0, keepdims=True)
-        probs = (weight * (1.0 / total)).astype(bf16)
-        context = dot_tn(probs, gather_rows(vbuf, shared, drawn, 128))
-        obuf[pl.ds(row, BLOCK), :] = fold_heads(context).astype(bf16)
-        lse_ref[0, pl.ds(block, 1), :] = top + jnp.log(total)
-
     def step(index, carry):
-        for part in range(unroll):
-            one_block(index * unroll + part)
+        group = [index * unroll + part for part in range(unroll)]
+        rows = [pl.multiple_of(tab[block], BLOCK) for block in group]
+        slots = [slot_offsets(tab, layout, pair, block) for block in group]
+        scores = [
+            dot_nt(gather_rows(kaug, *slot, 256), query_rows(qbuf, kaug, row))
+            for slot, row in zip(slots, rows)
+        ]
+        top = [jnp.max(score, axis=0, keepdims=True) for score in scores]
+        weight = [jnp.exp(score - most) for score, most in zip(scores, top)]
+        total = [jnp.sum(part, axis=0, keepdims=True) for part in weight]
+        probs = [(part * (1.0 / whole)).astype(bf16) for part, whole in zip(weight, total)]
+        context = [
+            dot_tn(prob, gather_rows(vbuf, *slot, 128)) for prob, slot in zip(probs, slots)
+        ]
+        for block, row, part, most, whole in zip(group, rows, context, top, total):
+            obuf[pl.ds(row, BLOCK), :] = fold_heads(part).astype(bf16)
+            lse_ref[0, pl.ds(block, 1), :] = most + jnp.log(whole)
         return carry
 
     lax.fori_loop(0, blocks // unroll, step, 0)
 
-    def dense_block(block):
-        row = pl.multiple_of(tab[block], BLOCK)
-        query = query_rows(qbuf, kaug, row)
-        chunk = 512
-        count = 2 * half // chunk
-        top = jnp.full((1, 128), -3e38, f32)
-        for part in range(count):
-            scores = dot_nt(kaug[part * chunk : (part + 1) * chunk, :], query)
-            sbuf[part * chunk : (part + 1) * chunk, :] = scores
-            top = jnp.maximum(top, jnp.max(scores, axis=0, keepdims=True))
-        total = jnp.zeros((1, 128), f32)
-        for part in range(count):
-            weight = jnp.exp(sbuf[part * chunk : (part + 1) * chunk, :] - top)
-            sbuf[part * chunk : (part + 1) * chunk, :] = weight
-            total = total + jnp.sum(weight, axis=0, keepdims=True)
-        inverse = 1.0 / total
-        context = jnp.zeros((128, 128), f32)
-        for part in range(count):
-            probs = (sbuf[part * chunk : (part + 1) * chunk, :] * inverse).astype(bf16)
-            context = context + dot_tn(probs, vbuf[part * chunk : (part + 1) * chunk, :])
-        obuf[pl.ds(row, BLOCK), :] = fold_heads(context).astype(bf16)
-        lse_ref[0, pl.ds(block, 1), :] = top + jnp.log(total)
-
     first, second = tab[blocks], tab[blocks + 1]
-
-    def dense_step(index, carry):
-        dense_block(jnp.where(index == 0, first, second))
-        return carry
-
-    lax.fori_loop(0, jnp.where(first == second, 1, 2), dense_step, 0)
+    rows = [pl.multiple_of(tab[block], BLOCK) for block in (first, second)]
+    query = jnp.concatenate([query_rows(qbuf, kaug, row) for row in rows], axis=0)
+    chunk = 512
+    pieces = [slice(at, at + chunk) for at in range(0, 2 * half, chunk)]
+    top = jnp.full((1, 256), -3e38, f32)
+    for here in pieces:
+        scores = dot_nt(kaug[here, :], query)
+        sbuf[here, :] = scores
+        top = jnp.maximum(top, jnp.max(scores, axis=0, keepdims=True))
+    total = jnp.zeros((1, 256), f32)
+    for here in pieces:
+        weight = jnp.exp(sbuf[here, :] - top)
+        sbuf[here, :] = weight
+        total = total + jnp.sum(weight, axis=0, keepdims=True)
+    inverse = 1.0 / total
+    context = jnp.zeros((256, 128), f32)
+    for here in pieces:
+        context = context + dot_tn((sbuf[here, :] * inverse).astype(bf16), vbuf[here, :])
+    lse = top + jnp.log(total)
+    for index, (block, row) in enumerate(zip((first, second), rows)):
+        lanes = slice(index * 128, (index + 1) * 128)
+        obuf[pl.ds(row, BLOCK), :] = fold_heads(context[lanes]).astype(bf16)
+        lse_ref[0, pl.ds(block, 1), :] = lse[:, lanes]
     out_own[0] = obuf[:half, :]
     out_oth[0] = obuf[half:, :]
 
@@ -187,70 +184,81 @@
     dvbuf[...] = jnp.zeros_like(dvbuf)
     keep = low_half((BLOCK, 128))
 
-    def scatter(ref, update, shared, drawn):
-        for slot, start in enumerate(shared):
-            ref[pl.ds(start, BLOCK), :] += update[slot * BLOCK : (slot + 1) * BLOCK]
-        for slot, (left, right) in enumerate(drawn):
-            at = (COMMON + slot) * BLOCK
-            piece = update[at : at + BLOCK]
-            ref[pl.ds(left, BLOCK), :] += jnp.where(keep, piece, 0.0)
-            ref[pl.ds(right, BLOCK), :] += jnp.where(keep, 0.0, piece)
-
-    def one_block(block):
-        row = pl.multiple_of(tab[block], BLOCK)
-        shared, drawn = slot_offsets(tab, layout, pair, block)
-        query = query_rows(qbuf, kaug, row)
-        grad = block_diag(gbuf[pl.ds(row, BLOCK), :])
-        keys = gather_rows(kaug, shared, drawn, 256)
-        scores = dot_nt(keys, query)
-        probs = jnp.exp(scores - lse_ref[0, pl.ds(block, 1), :])
-        grad_probs = dot_nt(gather_rows(vbuf, shared, drawn, 128), grad)
-        delta = jnp.sum(probs * grad_probs, axis=0, keepdims=True)
-        grad_scores = (probs * (grad_probs - delta)).astype(bf16)
-        grad_query = dot_tn(grad_scores, keys[:, :128])
-        dqbuf[pl.ds(row, BLOCK), :] = (fold_heads(grad_query) * 0.125).astype(bf16)
-        scatter(dkbuf, dot_nn(grad_scores, query[:, :128]), shared, drawn)
-        scatter(dvbuf, dot_nn(probs.astype(bf16), grad), shared, drawn)
+    dummy = 2 * half
+    ends = [pl.multiple_of(tab[tab_block], BLOCK) for tab_block in (tab[blocks], tab[blocks + 1])]
+
+    def scatter(ref, updates, slots, base):
+        piece = lambda part, slot: updates[part][slot * BLOCK : (slot + 1) * BLOCK]
+        for shift in range(-1, unroll + 1):
+            block = base + shift
+            inside = (block >= 0) & (block < blocks)
+            row = jnp.where(inside, tab[jnp.clip(block, 0, blocks - 1)], dummy)
+            near = [piece(p, shift - p + 1) for p in range(unroll) if 0 <= shift - p + 1 <= 2]
+            ref[pl.ds(pl.multiple_of(row, BLOCK), BLOCK), :] += functools.reduce(jnp.add, near)
+        for slot, row in zip((3, 4), ends):
+            every = [piece(p, slot) for p in range(unroll)]
+            ref[pl.ds(row, BLOCK), :] += functools.reduce(jnp.add, every)
+        for part, (_, drawn) in enumerate(slots):
+            for slot, (left, right) in enumerate(drawn):
+                one = piece(part, COMMON + slot)
+                ref[pl.ds(left, BLOCK), :] += jnp.where(keep, one, 0.0)
+                ref[pl.ds(right, BLOCK), :] += jnp.where(keep, 0.0, one)
 
     def step(index, carry):
-        for part in range(unroll):
-            one_block(index * unroll + part)
+        group = [index * unroll + part for part in range(unroll)]
+        rows = [pl.multiple_of(tab[block], BLOCK) for block in group]
+        slots = [slot_offsets(tab, layout, pair, block) for block in group]
+        query = [query_rows(qbuf, kaug, row) for row in rows]
+        grad = [block_diag(gbuf[pl.ds(row, BLOCK), :]) for row in rows]
+        keys = [gather_rows(kaug, *slot, 256) for slot in slots]
+        scores = [dot_nt(key, one) for key, one in zip(keys, query)]
+        grad_probs = [
+            dot_nt(gather_rows(vbuf, *slot, 128), one) for slot, one in zip(slots, grad)
+        ]
+        probs = [
+            jnp.exp(score - lse_ref[0, pl.ds(block, 1), :]) for score, block in zip(scores, group)
+        ]
+        delta = [jnp.sum(p * g, axis=0, keepdims=True) for p, g in zip(probs, grad_probs)]
+        grad_scores = [
+            (p * (g - one)).astype(bf16) for p, g, one in zip(probs, grad_probs, delta)
+        ]
+        grad_query = [dot_tn(one, key[:, :128]) for one, key in zip(grad_scores, keys)]
+        grad_key = [dot_nn(one, q[:, :128]) for one, q in zip(grad_scores, query)]
+        grad_value = [dot_nn(p.astype(bf16), g) for p, g in zip(probs, grad)]
+        for row, one in zip(rows, grad_query):
+            dqbuf[pl.ds(row, BLOCK), :] = (fold_heads(one) * 0.125).astype(bf16)
+        scatter(dkbuf, grad_key, slots, index * unroll)
+        scatter(dvbuf, grad_value, slots, index * unroll)
         return carry
 
     lax.fori_loop(0, blocks // unroll, step, 0)
 
-    def dense_block(block):
-        row = pl.multiple_of(tab[block], BLOCK)
-        query = query_rows(qbuf, kaug, row)
-        grad = block_diag(gbuf[pl.ds(row, BLOCK), :])
-        lse = lse_ref[0, pl.ds(block, 1), :]
-        chunk = 512
-        count = 2 * half // chunk
-        delta = jnp.zeros((1, 128), f32)
-        for part in range(count):
-            here = slice(part * chunk, (part + 1) * chunk)
-            probs = jnp.exp(dot_nt(kaug[here, :], query) - lse)
-            grad_probs = dot_nt(vbuf[here, :], grad)
-            delta = delta + jnp.sum(probs * grad_probs, axis=0, keepdims=True)
-            sbuf[here, :] = probs
-            tbuf[here, :] = grad_probs
-        grad_query = jnp.zeros((128, 128), f32)
-        for part in range(count):
-            here = slice(part * chunk, (part + 1) * chunk)
-            probs = sbuf[here, :]
-            grad_scores = (probs * (tbuf[here, :] - delta)).astype(bf16)
-            grad_query = grad_query + dot_tn(grad_scores, kaug[here, :128])
-            dkbuf[here, :] += dot_nn(grad_scores, query[:, :128])
-            dvbuf[here, :] += dot_nn(probs.astype(bf16), grad)
-        dqbuf[pl.ds(row, BLOCK), :] = (fold_heads(grad_query) * 0.125).astype(bf16)
-
     first, second = tab[blocks], tab[blocks + 1]
-
-    def dense_step(index, carry):
-        dense_block(jnp.where(index == 0, first, second))
-        return carry
-
-    lax.fori_loop(0, jnp.where(first == second, 1, 2), dense_step, 0)
+    rows = [pl.multiple_of(tab[block], BLOCK) for block in (first, second)]
+    query = jnp.concatenate([query_rows(qbuf, kaug, row) for row in rows], axis=0)
+    grads = [block_diag(gbuf[pl.ds(row, BLOCK), :]) for row in rows]
+    grads[1] = jnp.where(first == second, jnp.zeros_like(grads[1]), grads[1])
+    grad = jnp.concatenate(grads, axis=0)
+    lse = jnp.concatenate([lse_ref[0, pl.ds(block, 1), :] for block in (first, second)], axis=1)
+    chunk = 512
+    pieces = [slice(at, at + chunk) for at in range(0, 2 * half, chunk)]
+    delta = jnp.zeros((1, 256), f32)
+    for here in pieces:
+        probs = jnp.exp(dot_nt(kaug[here, :], query) - lse)
+        grad_probs = dot_nt(vbuf[here, :], grad)
+        delta = delta + jnp.sum(probs * grad_probs, axis=0, keepdims=True)
+        sbuf[here, :] = probs
+        tbuf[here, :] = grad_probs
+    grad_query = jnp.zeros((256, 128), f32)
+    for here in pieces:
+        probs = sbuf[here, :]
+        grad_scores = (probs * (tbuf[here, :] - delta)).astype(bf16)
+        grad_query = grad_query + dot_tn(grad_scores, kaug[here, :128])
+        dkbuf[here, :] += dot_nn(grad_scores, query[:, :128])
+        dvbuf[here, :] += dot_nn(probs.astype(bf16), grad)
+    for index in (1, 0):
+        part = fold_heads(grad_query[index * 128 : (index + 1) * 128]) * 0.125
+        dqbuf[pl.ds(rows[index], BLOCK), :] = part.astype(bf16)
     for part, buffer in enumerate((dqbuf, dkbuf, dvbuf)):
         lanes = pl.ds(pl.multiple_of((2 * part + pl.program_id(0)) * 128, 128), 128)
         own_ref[0, :, lanes] = buffer[:half, :].astype(bf16)
@@ -289,7 +297,7 @@
     return pl.BlockSpec((1, half, 128), lambda p, tab: (slot, 0, column * 2 + p))
 
 
-def attn_fwd(tab, qkv_own, qkv_oth, seg_abs, blocks, slot, unroll=4):
+def attn_fwd(tab, qkv_own, qkv_oth, seg_abs, blocks, slot, unroll=8):
     half = qkv_own.shape[1]
     layout = table_layout(blocks, 4 * qkv_own.shape[0])
     rows = 2 * half + BLOCK
@@ -309,16 +317,16 @@
             scratch_shapes=[
                 pltpu.VMEM((rows, 256), bf16), pltpu.VMEM((rows, 128), bf16),
                 pltpu.VMEM((2 * half, 128), bf16), pltpu.VMEM((2 * half, 128), bf16),
-                pltpu.VMEM((2 * half, 128), f32),
+                pltpu.VMEM((2 * half, 256), f32),
             ],
         ),
         compiler_params=pltpu.CompilerParams(vmem_limit_bytes=40 << 20),
-        cost_estimate=cost(32),
+        cost_estimate=cost(17),
         name="attn_fwd",
     )(tab, qkv_own, qkv_oth, qkv_own, qkv_oth, qkv_own, qkv_oth, seg_abs)
 
 
-def attn_bwd(tab, qkv_own, qkv_oth, grad_own, grad_oth, seg_abs, lse, blocks, slot, unroll=4):
+def attn_bwd(tab, qkv_own, qkv_oth, grad_own, grad_oth, seg_abs, lse, blocks, slot, unroll=8):
     half = qkv_own.shape[1]
     layout = table_layout(blocks, 4 * qkv_own.shape[0])
     rows = 2 * half + BLOCK
@@ -341,11 +349,11 @@
                 pltpu.VMEM((2 * half, 128), bf16), pltpu.VMEM((2 * half, 128), bf16),
                 pltpu.VMEM((2 * half, 128), bf16),
                 pltpu.VMEM((rows, 128), f32), pltpu.VMEM((rows, 128), f32),
-                pltpu.VMEM((2 * half, 128), f32), pltpu.VMEM((2 * half, 128), f32),
+                pltpu.VMEM((2 * half, 256), f32), pltpu.VMEM((2 * half, 256), f32),
             ],
         ),
         compiler_params=pltpu.CompilerParams(vmem_limit_bytes=48 << 20),
-        cost_estimate=cost(37),
+        cost_estimate=cost(29),
         name="attn_bwd",
     )(tab, qkv_own, qkv_oth, qkv_own, qkv_oth, qkv_own, qkv_oth, grad_own, grad_oth, seg_abs, lse)
 
@@ -353,6 +361,7 @@
 EPS = 1e-05
 BOTH = ("dp", "tensor")
 ROWS = 256
+WIDE = 512
 
 
 def gelu_pair(u):
@@ -486,7 +495,7 @@
 
 def project_kernel(count, where, x_ref, vec_ref, wa_ref, wb_ref, out_ref, rel_ref, n_ref, nbuf):
     slot, tile = pl.program_id(0), pl.program_id(1)
-    here = pl.ds(pl.multiple_of(tile * ROWS, ROWS), ROWS)
+    here = pl.ds(pl.multiple_of(tile * WIDE, WIDE), WIDE)
 
     @pl.when(slot == 0)
     def _():
@@ -506,14 +515,14 @@
 
 def project(where, x, vecs, weights, first, count):
     rows, width = x.shape
-    tiles = rows // ROWS
+    tiles = rows // WIDE
     out = width * 3 // 4
     half = width // 2
     weight = pl.BlockSpec(
         (1, half, out), lambda s, i, w: (2 * (1 - w[0] if first else w[0]) + s, 0, 0)
     )
-    outs = pl.BlockSpec((1, ROWS, out), lambda s, i, w: (s, i, 0))
-    once = pl.BlockSpec((ROWS, width), lambda s, i, w: (jnp.where(s == 0, i, tiles - 1), 0))
+    outs = pl.BlockSpec((1, WIDE, out), lambda s, i, w: (s, i, 0))
+    once = pl.BlockSpec((WIDE, width), lambda s, i, w: (jnp.where(s == 0, i, tiles - 1), 0))
     shape = struct((2, rows, out), bf16)
     if first:
         return pl.pallas_call(
@@ -534,7 +543,7 @@
         out_shape=shape,
         grid_spec=prefetch(
             (2, tiles),
-            [pl.BlockSpec((ROWS, width), lambda s, i, w: (i, 0)), weight, weight],
+            [pl.BlockSpec((WIDE, width), lambda s, i, w: (i, 0)), weight, weight],
             outs,
         ),
         compiler_params=params(32),
@@ -579,8 +588,8 @@
     )(where, x, *contexts, *[weights[0]] * 4, *[weights[1]] * 4, vecs)
 
 
-def ffn_kernel(first, n_ref, cot_ref, nt_in, ct_in, up_ref, down_ref, bias_ref,
-               ffn_ref, gn_ref, grad_ref, gbias_ref, nt_out, ct_out, nt, ct, act, gup, total, back_total):
+def ffn_kernel(where, n_ref, cot_ref, up_ref, down_ref, bias_ref,
+               ffn_ref, gn_ref, grad_ref, gbias_ref, nt, ct, act, gup, total, back_total):
     step = pl.program_id(0)
     rows, width = n_ref.shape
     hidden = act.shape[1]
@@ -589,45 +598,23 @@
 
     @pl.when(step == 0)
     def _():
-        if first:
-            for at in range(0, rows, ROWS):
-                nt[:, at : at + ROWS] = n_ref[at : at + ROWS, :].T
-                ct[:, at : at + ROWS] = cot_ref[at : at + ROWS, :].T
-            nt_out[...] = nt[...]
-            ct_out[...] = ct[...]
+        turn_rows(n_ref, nt)
+        turn_rows(cot_ref, ct)
         total[...] = jnp.zeros_like(total)
         back_total[...] = jnp.zeros_like(back_total)
 
-    if not first:
-        nt, ct = nt_in, ct_in
-    gbias_ref[...] = jnp.zeros_like(gbias_ref)
-
-    def tile(index, carry):
-        here = pl.ds(pl.multiple_of(index * ROWS, ROWS), ROWS)
-        value = dot_nn(n_ref[here, :], up) + bias_ref[0]
-        out, slope = gelu_pair(value)
-        out = out.astype(bf16)
-        act[here, :] = out
-        back = (dot_nn(cot_ref[here, :], down) * slope).astype(bf16)
-        gup[here, :] = back
-        gbias_ref[0] += jnp.sum(back.astype(f32), axis=0, keepdims=True)
-        total[here, :] += dot_nt(out, down)
-        back_total[here, :] += dot_nt(back, up)
-        return carry
-
-    lax.fori_loop(0, rows // ROWS, tile, 0)
-    chunk = grad_ref.shape[3]
-    many = ROWS // chunk
-
-    def grads(index, carry):
-        here = pl.ds(pl.multiple_of(index * ROWS, ROWS), ROWS)
-        there = pl.ds(index * many, many)
-        shape = (many, chunk, hidden)
-        grad_ref[there, 0, 0] = dot_nn(nt[here, :], gup[...]).astype(bf16).reshape(shape)
-        grad_ref[there, 0, 1] = dot_nn(ct[here, :], act[...]).astype(bf16).reshape(shape)
-        return carry
-
-    lax.fori_loop(0, width // ROWS, grads, 0)
+    value = dot_nn(n_ref[...], up) + bias_ref[0]
+    out, slope = gelu_pair(value)
+    out = out.astype(bf16)
+    act[...] = out
+    back = (dot_nn(cot_ref[...], down) * slope).astype(bf16)
+    gup[...] = back
+    gbias_ref[0] = jnp.sum(back.astype(f32), axis=0, keepdims=True)
+    total[...] += dot_nt(out, down)
+    back_total[...] += dot_nt(back, up)
+    shape = grad_ref.shape[0], grad_ref.shape[3], hidden
+    grad_ref[:, 0, 0] = dot_nn(nt[...], gup[...]).astype(bf16).reshape(shape)
+    grad_ref[:, 0, 1] = dot_nn(ct[...], act[...]).astype(bf16).reshape(shape)
 
     @pl.when(step == pl.num_programs(0) - 1)
     def _():
@@ -635,57 +622,40 @@
         gn_ref[...] = back_total[...].astype(bf16)
 
 
-def ffn_first_kernel(where, n_ref, cot_ref, up_ref, down_ref, bias_ref,
-                     ffn_ref, gn_ref, grad_ref, gbias_ref, nt_out, ct_out, nt, ct, *scratch):
-    ffn_kernel(True, n_ref, cot_ref, None, None, up_ref, down_ref, bias_ref,
-               ffn_ref, gn_ref, grad_ref, gbias_ref, nt_out, ct_out, nt, ct, *scratch)
-
-
-def ffn_second_kernel(where, n_ref, cot_ref, nt_in, ct_in, up_ref, down_ref, bias_ref,
-                      ffn_ref, gn_ref, grad_ref, gbias_ref, *scratch):
-    ffn_kernel(False, n_ref, cot_ref, nt_in, ct_in, up_ref, down_ref, bias_ref,
-               ffn_ref, gn_ref, grad_ref, gbias_ref, None, None, None, None, *scratch)
-
-
-def feed_forward(where, normed, cot, weights, bias, slots_at, turned=None):
+def feed_forward(where, normed, cot, weights, bias, slots_at):
     rows, width = normed.shape
     count, slots, _, chunk, hidden = weights.shape
-    once = pl.Buffered(1)
-    fixed = lambda shape: pl.BlockSpec(shape, lambda s, w: (0, 0), pipeline_mode=once)
-    whole, flipped = fixed((rows, width)), fixed((width, rows))
+    whole = fixed_spec((rows, width))
     slot = lambda s, w: (w[2] + slots_at + s) % slots
     weight = lambda k: pl.BlockSpec(
         (count, 1, 1, chunk, hidden), lambda s, w: (0, slot(s, w), k, 0, 0)
     )
-    grad = pl.BlockSpec((count, 1, 2, chunk, hidden), lambda s, w: (0, s, 0, 0, 0))
     total = pl.BlockSpec((rows, width), lambda s, w: (0, 0))
-    outs = (
-        struct((rows, width), bf16), struct((rows, width), bf16),
-        struct((count, 2, 2, chunk, hidden), bf16), struct((2, 1, hidden), f32),
-    )
-    out_specs = (total, total, grad, pl.BlockSpec((1, 1, hidden), lambda s, w: (s, 0, 0)))
-    vector = pl.BlockSpec((1, 1, hidden), lambda s, w: (slot(s, w), 0, 0))
-    scratch = [
-        pltpu.VMEM((rows, hidden), bf16), pltpu.VMEM((rows, hidden), bf16),
-        pltpu.VMEM((rows, width), f32), pltpu.VMEM((rows, width), f32),
-    ]
-    if turned is None:
-        outs += (struct((width, rows), bf16), struct((width, rows), bf16))
-        out_specs += (pl.BlockSpec((width, rows), lambda s, w: (0, 0)),) * 2
-        scratch = [pltpu.VMEM((width, rows), bf16), pltpu.VMEM((width, rows), bf16), *scratch]
-    return pl.pallas_call(
-        ffn_first_kernel if turned is None else ffn_second_kernel,
-        out_shape=outs,
+    return pl.pallas_call(
+        ffn_kernel,
+        out_shape=(
+            struct((rows, width), bf16), struct((rows, width), bf16),
+            struct((count, 2, 2, chunk, hidden), bf16), struct((2, 1, hidden), f32),
+        ),
         grid_spec=prefetch(
             (2,),
-            [whole, whole, *([flipped, flipped] if turned else []), weight(0), weight(1), vector],
-            out_specs,
-            scratch,
+            [whole, whole, weight(0), weight(1),
+             pl.BlockSpec((1, 1, hidden), lambda s, w: (slot(s, w), 0, 0))],
+            (
+                total, total,
+                pl.BlockSpec((count, 1, 2, chunk, hidden), lambda s, w: (0, s, 0, 0, 0)),
+                pl.BlockSpec((1, 1, hidden), lambda s, w: (s, 0, 0)),
+            ),
+            [
+                pltpu.VMEM((width, rows), bf16), pltpu.VMEM((width, rows), bf16),
+                pltpu.VMEM((rows, hidden), bf16), pltpu.VMEM((rows, hidden), bf16),
+                pltpu.VMEM((rows, width), f32), pltpu.VMEM((rows, width), f32),
+            ],
         ),
         compiler_params=params(60),
-        cost_estimate=cost(36),
+        cost_estimate=cost(38),
         name="feed_forward",
-    )(where, normed, cot, *(turned or ()), weights, weights, bias)
+    )(where, normed, cot, weights, weights, bias)
 
 
 def mid_kernel(count, where, resid_ref, f0_ref, f1_ref, n0_ref, n1_ref, cot_ref, a0, a1, a2, a3, b0, b1, b2, b3, vec_ref,
@@ -744,11 +714,11 @@
     lanes = inner.shape[2]
 
     def tile(index, carry):
-        here = pl.ds(pl.multiple_of(index * ROWS, ROWS), ROWS)
+        here = pl.ds(pl.multiple_of(index * WIDE, WIDE), WIDE)
         total[here, :] += nt_halves(inner[0, here, :], a_ref[0, :, :lanes], b_ref[0, :, :lanes])
         return carry
 
-    lax.fori_loop(0, total.shape[0] // ROWS, tile, 0)
+    lax.fori_loop(0, total.shape[0] // WIDE, tile, 0)
 
 
 def weight_part(nt, lt, inner, context, ga_ref, gb_ref):
@@ -757,13 +727,13 @@
     for grad_ref, start in ((ga_ref, 0), (gb_ref, half)):
 
         def grads(index, carry, grad_ref=grad_ref, start=start):
-            here = pl.ds(pl.multiple_of(index * ROWS, ROWS), ROWS)
-            there = pl.ds(pl.multiple_of(start + index * ROWS, ROWS), ROWS)
+            here = pl.ds(pl.multiple_of(index * WIDE, WIDE), WIDE)
+            there = pl.ds(pl.multiple_of(start + index * WIDE, WIDE), WIDE)
             grad_ref[0, here, :lanes] = dot_nn(nt[there, :], inner[0]).astype(bf16)
             grad_ref[0, here, lanes:] = dot_nn(lt[there, :], context[0]).astype(bf16)
             return carry
 
-        lax.fori_loop(0, half // ROWS, grads, 0)
+        lax.fori_loop(0, half // WIDE, grads, 0)
 
 
 def turn_rows(source, target):
@@ -790,13 +760,19 @@
 
 
 def back_tokens_kernel(where, d0, d1, a0, b0, a1, b1, before_ref, x_ref, gres_ref, vec_ref,
-                       gin_ref, sums_ref):
+                       g0, g1, g2, g3, sums_ref):
     lanes = d0.shape[2]
     grad = before_ref[...] + nt_halves(d0[0], a0[0, :, :lanes], b0[0, :, :lanes])
     grad = grad + nt_halves(d1[0], a1[0, :, :lanes], b1[0, :, :lanes])
     unit, inverse = normalise(x_ref[...].astype(f32))
     result = gres_ref[...] + norm_back(grad, unit, inverse, vec_ref[0:1, :])
-    gin_ref[...] = result.astype(bf16)
+    result = result.astype(bf16)
+    turn = pl.program_id(0) ^ (where[2] // 2 * 2 + where[0])
+    for index, out_ref in enumerate((g0, g1, g2, g3)):
+
+        @pl.when(turn == index)
+        def _(out_ref=out_ref):
+            out_ref[...] = result
 
     @pl.when(pl.program_id(0) == 0)
     def _():
@@ -856,13 +832,13 @@
     )
     return pl.pallas_call(
         back_tokens_kernel,
-        out_shape=(struct((rows, width), bf16), struct((8, width), f32)),
+        out_shape=(*[struct((ROWS, width), bf16)] * 4, struct((8, width), f32)),
         grid_spec=prefetch(
             (rows // ROWS,),
             [inner, inner, weight(0), weight(0), weight(1), weight(1), tile, tile, tile,
              pl.BlockSpec(vecs.shape, lambda i, w: (0, 0))],
             (
-                pl.BlockSpec((ROWS, width), lambda i, w: (i ^ (w[2] // 2 * 2 + w[0]), 0)),
+                *[pl.BlockSpec((ROWS, width), lambda i, w: (0, 0))] * 4,
                 pl.BlockSpec((8, width), lambda i, w: (0, 0)),
             ),
         ),
@@ -917,6 +893,31 @@
             source = (2 * (z // 2) + d % 2) ^ turn
             routes.append((d * tensor_count + z, (d - d % 2 + z % 2) * tensor_count + source))
     return routes
+
+
+def pack_kernel(*refs):
+    *vectors, rand_ref, glob_ref, out_ref = refs
+    lanes = out_ref.shape[2]
+    out_ref[...] = jnp.zeros_like(out_ref)
+    copies = out_ref.shape[0]
+    spread = lambda row: jnp.broadcast_to(row.astype(f32)[None], (copies, *row.shape)).astype(bf16)
+    for index, vector in enumerate(vectors):
+        out_ref[:, index : index + 1, : vector.shape[1]] = spread(vector[...])
+    start = 8
+    out_ref[:, start : start + rand_ref.shape[0], :] = spread(rand_ref[...])
+    start += rand_ref.shape[0]
+    out_ref[:, start : start + 1, : glob_ref.shape[1]] = spread(glob_ref[...])
+
+
+def pack(vectors, rand, glob, copies):
+    rows = 8 + rand.shape[0] + 1
+    rows = -(-rows // 16) * 16
+    return pl.pallas_call(
+        pack_kernel,
+        out_shape=struct((copies, rows, rand.shape[1]), bf16),
+        compiler_params=params(8),
+        name="pack",
+    )(*vectors, rand, glob)
 
 
 def after(value, *others):
@@ -983,14 +984,14 @@
     def give(value):
         return exchange(value).reshape(2 * batches, share, width)
 
-    rand_size = rand_blocks.shape[2] * blocks * RAND
     chunk = norm1_gain.shape[0]
-    small = jnp.concatenate(
-        [norm1_gain, norm1_bias, norm2_gain, norm2_bias, down_bias, up_bias[0],
-         rand_blocks.reshape(-1).astype(bf16), glob_blocks.reshape(-1).astype(bf16)]
-    )
     devices = dp_count * tensor_count
-    small = jnp.broadcast_to(small[None], (devices, small.shape[0]))
+    rand_rows = rand_blocks.reshape(-1, 128)
+    rows_each = rand_rows.shape[0] // batches
+    small = pack(
+        [v.reshape(1, chunk) for v in (norm1_gain, norm1_bias, norm2_gain, norm2_bias, down_bias, up_bias)],
+        rand_rows, glob_blocks.reshape(1, -1), devices,
+    )
     shard = jnp.concatenate([w_query, w_key, w_value, w_out.T], axis=1)
     attn_slots = [along(shard, -k) for k in range(1, tensor_count)]
     their_segments = other_core(segments)
@@ -1001,22 +1002,20 @@
     attn_slots, small = lax.optimization_barrier((attn_slots, small))
     attn_slots = jnp.stack([shard, *attn_slots])
     x = exchange(x_half)
-    small = small.reshape(dp_count, tensor_count, -1)
-    vectors = small[..., : 6 * chunk].reshape(dp_count, tensor_count, 6, chunk).astype(f32)
+    small = small.reshape(dp_count, tensor_count, *small.shape[1:])
+    vectors = small[:, :, :6, :chunk].astype(f32)
     up_shift = vectors[:, :, 5].transpose(1, 0, 2).reshape(tensor_count, 1, -1)
     places = jnp.arange(dp_count, dtype=jnp.int32)
     order = chunk_at(d, places, dp_count)
     vecs = jnp.take(vectors[:, 0, :5], order, axis=0).transpose(1, 0, 2).reshape(5, width)
     vecs = jnp.concatenate([vecs, jnp.zeros((3, width), f32)])
-    ints = lax.dynamic_index_in_dim(small, d - core + z % 2, 0, keepdims=False)[:, 6 * chunk :]
-    ints = ints.astype(jnp.int32)
-    rand_heads = ints[:, : batches * rand_size].reshape(tensor_count, batches, -1)
+    ints = lax.dynamic_index_in_dim(small, d - core + z % 2, 0, keepdims=False).astype(jnp.int32)
+    rand_heads = ints[:, 8 : 8 + rand_rows.shape[0]].reshape(tensor_count, batches, rows_each, 128)
     rand_heads = lax.dynamic_index_in_dim(rand_heads, z // 2, 1, keepdims=False)
     rand_heads = lax.dynamic_slice_in_dim(jnp.roll(rand_heads, -z, axis=0), 2 * core, 2, 0)
     rand_heads = rand_heads.reshape(2 * rand_blocks.shape[2], blocks, RAND)
-    glob_row = lax.dynamic_index_in_dim(
-        ints[0, batches * rand_size :].reshape(batches, -1), z // 2, 0, keepdims=False
-    )
+    glob_row = ints[0, 8 + rand_rows.shape[0], : glob_blocks.size].reshape(batches, -1)
+    glob_row = lax.dynamic_index_in_dim(glob_row, z // 2, 0, keepdims=False)
     segment_row = lax.dynamic_index_in_dim(
         jnp.where(z % 2 == core, segments, their_segments), z // 2, 0, keepdims=False
     )
@@ -1032,7 +1031,7 @@
     table = attention_table(rand_heads, glob_row, row_of, 2 * half)
 
     attn_own = [attn_slots] + [across(attn_slots, r) for r in range(1, pairs)]
-    pair_shard = after(jnp.stack([w_up, w_down.T]), attn_slots)
+    pair_shard = jnp.stack([w_up, w_down.T])
     pair_weights = lax.all_gather(pair_shard, BOTH, axis=0, tiled=False)
     pair_weights = pair_weights.reshape(dp_count, tensor_count, 2, *w_up.shape)
     cot_half = both_halves(half_of(cotangent, core), cot_come)
@@ -1053,13 +1052,13 @@
     ctx_oth0 = other_core(ctx_send0)
     ctx_own1, ctx_send1, lse1 = attn_fwd(table, own, oth, segment_lanes, blocks, 1)
     ctx_oth1 = other_core(ctx_send1)
-    cot = exchange(after(cot_half, own))
+    cot = exchange(cot_half)
     resid, normed_two = out_project(
         where, x, (ctx_own0, ctx_own1, ctx_oth0, ctx_oth1), attn_weights, vecs, dp_count
     )
     if not aligned:
         normed_two = jnp.dot(normed_two, own_features.T, preferred_element_type=f32).astype(bf16)
-    ffn0, gn0, pair0, bias0, *turned = feed_forward(
+    ffn0, gn0, pair0, bias0 = feed_forward(
         where, normed_two, cot, pair_weights, up_shift, 2
     )
 
@@ -1069,7 +1068,7 @@
         return result.reshape(total.shape[1:])
 
     ffn1, gn1, pair1, bias1 = feed_forward(
-        where, normed_two, cot, pair_weights, up_shift, 0, turned
+        where, normed_two, cot, pair_weights, up_shift, 0
     )
     pair_total0 = reduce_rows(pair0)
     pair_total1 = reduce_rows(pair1)
@@ -1141,15 +1140,15 @@
     d_oth1 = other_core(d_send1)
     ga1, gb1 = back_weights(where, (d_own1, d_oth1), (ctx_own1, ctx_oth1), turned)
     total_one, ga1, gb1 = lax.optimization_barrier((total_one, ga1, gb1))
-    grad_in, sums_one = back_tokens(
+    *grad_in, sums_one = back_tokens(
         where, (d_own1, d_oth1), attn_weights, 1, total_one, x, grad_resid, vecs
     )
+    grad_in, out_back, out_other, pair_total1 = lax.optimization_barrier(
+        (grad_in, out_back, out_other, pair_total1)
+    )
     grad_back = [
-        lax.ppermute(
-            grad_in[turn * share : (turn + 1) * share], BOTH,
-            token_routes(dp_count, tensor_count, turn),
-        )
-        for turn in range(tensor_count)
+        lax.ppermute(piece, BOTH, token_routes(dp_count, tensor_count, turn))
+        for turn, piece in enumerate(grad_in)
     ]
     attn_parts1 = reduce_core(ga1, gb1)
     pair_next.append(along(pair_total1[1], 1))

time: 617 us -> 575 us (0.932)
  Pallas kernels: 312 us -> 244 us
  waiting for transfers between devices: 134 us -> 163 us
    pallas_call x2, Pallas kernels: 69 us -> 33.7 us  [attn_fwd(): pl.pallas_call(functools.partial(attn_fwd_kernel, layout, 2 * slot, unrol...]
    pallas_call x2, Pallas kernels: 78.9 us -> 56.6 us  [attn_bwd(): pl.pallas_call(functools.partial(attn_bwd_kernel, layout, 2 * slot, unrol...]
    ppermute x31, waiting for transfers between devices: 67 us -> 77.4 us  [move(): return lax.ppermute(value, BOTH, routes)]
    all_to_all x1, starting transfers between devices: 12.7 us -> 2.57 us  [exchange_sums(): return lax.all_to_all(sums, BOTH, split_axis=0, concat_axis=0, tiled=True)]
    ppermute x4, waiting for transfers between devices: 29.9 us -> 37.9 us  [per_device(): lax.ppermute(piece, BOTH, token_routes(dp_count, tensor_count, turn))]
    pallas_call x3 -> x4, Pallas kernels: 95 us -> 87.7 us  [the longest x2 76.4 us: feed_forward(): pl.pallas_call(ffn_kernel, out_shape=(struct((rows, width), bf16), struct...]
    all_to_all x1, waiting for transfers between devices: 9.06 us -> 16.2 us  [per_device(): small = lax.all_to_all(small, BOTH, split_axis=0, concat_axis=0, tiled=True)]
    unnamed x128 -> x145, local copies, waits for them, and re-layouts: 34.6 us -> 37.4 us
  transfers between devices with their start and end apart: 43 -> 43, of which waited for: 17 -> 17; matrix products, arithmetic and copies ran while one was open for 9% -> 9% of each run, Pallas kernels for 44% -> 36%
where the time goes in v4:
time: 575 us; the launch traced here: 568 us
  Pallas kernels  244 us (42%)
  waiting for transfers between devices  163 us (28%)
  starting transfers between devices  59.1 us (10%)
  local copies, waits for them, and re-layouts  58.9 us (10%)
  other arithmetic  26.8 us (5%)
  between operations  16.4 us (3%)
    ppermute x31, waiting for transfers between devices, move(): return lax.ppermute(value, BOTH, routes)  77.4 us
    pallas_call x2, Pallas kernels, feed_forward(): pl.pallas_call(ffn_kernel, out_shape=(struct((rows, width), bf16), struct...  76.4 us
    pallas_call x2, Pallas kernels, attn_bwd(): pl.pallas_call(functools.partial(attn_bwd_kernel, layout, 2 * slot, unrol...  56.6 us
    ppermute x4, waiting for transfers between devices, per_device(): lax.ppermute(piece, BOTH, token_routes(dp_count, tensor_count, turn))  37.9 us
    unnamed x145, local copies, waits for them, and re-layouts  37.4 us
    pallas_call x2, Pallas kernels, attn_fwd(): pl.pallas_call(functools.partial(attn_fwd_kernel, layout, 2 * slot, unrol...  33.7 us
    all_to_all x3, waiting for transfers between devices, exchange(): lax.all_to_all(value, 'tensor', split_axis=0, concat_axis=0, tiled=True)  31.3 us
    ppermute x31, starting transfers between devices, move(): return lax.ppermute(value, BOTH, routes)  29.5 us
  transfers between devices with their start and end apart: 43, of which 17 were waited for; matrix products, arithmetic and copies ran while one was open for 9% of the time, Pallas kernels for 36%

profile of v4, /device:TPU:0, one launch (start us, length us, event | category | flops | bytes accessed | tf_op | source)
XLA Modules:
  0.0 567.8 jit_solution(3192851358413915846)
XLA Ops:
  13.8 4.6 collective-permute-start.1
  31.4 5.1 all-to-all-start.1
  39.7 16.2 %all-to-all-done.1 = bf16[32,16,128]{2,1,0:T(8,128)(2,1)S(1)} async-done(((bf16[32,16,128]{2,1,0:T(8,128)(2,1)}), bf16[32,16,128]{2,1,0:T(8,128)(2,1)S(1)}, u32[]{:S(2)}, u32[]{:S(2)}) %all-to-all-start.1) | async-done | bytes 131104 | tf_op jit(solution)/shard_map/all_to_all | solution.py:1001
  56.6 6.3 %all-to-all-start = ((bf16[4,256,1024]{2,1,0:T(8,128)(2,1)}), bf16[4,256,1024]{2,1,0:T(8,128)(2,1)S(1)}, u32[]{:S(2)}, u32[]{:S(2)}) async-start(bf16[4,256,1024]{2,1,0:T(8,128)(2,1)} %bitcast.122), calls=%async_computation | async-start | bytes 4194304 | tf_op jit(solution)/shard_map/all_to_all | solution.py:974
  79.5 20.4 %collective-permute-done.4 = bf16[4,128,1024]{2,1,0:T(8,128)(2,1)} collective-permute-done((bf16[4,128,1024]{2,1,0:T(8,128)(2,1)S(1)}, bf16[4,128,1024]{2,1,0:T(8,128)(2,1)}, u32[]{:S(2)}, u32[]{:S(2)}) %collective-permute-start.4) | collective-permute-done | bytes 1048608 | tf_op jit(solution)/shard_map/ppermute | solution.py:962
  99.9 22.8 %collective-permute-done.6 = bf16[4,128,1024]{2,1,0:T(8,128)(2,1)} collective-permute-done((bf16[4,128,1024]{2,1,0:T(8,128)(2,1)S(1)}, bf16[4,128,1024]{2,1,0:T(8,128)(2,1)}, u32[]{:S(2)}, u32[]{:S(2)}) %collective-permute-start.6) | collective-permute-done | bytes 1048608 | tf_op jit(solution)/shard_map/ppermute | solution.py:962
  122.7 7.7 %all-to-all-done = bf16[4,256,1024]{2,1,0:T(8,128)(2,1)S(1)} async-done(((bf16[4,256,1024]{2,1,0:T(8,128)(2,1)}), bf16[4,256,1024]{2,1,0:T(8,128)(2,1)S(1)}, u32[]{:S(2)}, u32[]{:S(2)}) %all-to-all-start) | async-done | bytes 2097184 | tf_op jit(solution)/shard_map/all_to_all | solution.py:974
  136.7 7.3 %collective-permute-done.9.wb_ref.b0.b1.b2.b3.b_ref = bf16[4,512,1024]{2,1,0:T(8,128)(2,1)S(1)} collective-permute-done((bf16[4,512,1024]{2,1,0:T(8,128)(2,1)S(1)}, bf16[4,512,1024]{2,1,0:T(8,128)(2,1)S(1)}, u32[]{:S(2)}, u32[]{:S(2)}) %collective-permute-start.9) | collective-permute-done | bytes 4194336 | tf_op jit(solution)/shard_map/ppermute | solution.py:962
  144.0 7.5 %project.1 = (bf16[2,1024,768]{2,1,0:T(8,128)(2,1)}, bf16[1024,1024]{1,0:T(8,128)(2,1)S(1)}, bf16[1024,1024]{1,0:T(8,128)(2,1)S(1)}) custom-call(s32[3]{0:T(128)S(1)} %pad_add_fusion.2.where, bf16[1024,1024]{1,0:T(8,128)(2,1)S(1)} %bitcast.112, f32[8,1024]{1,0:T(8,128)S(1)} %concatenate.31.vec_ref, ...), custom_call_target="tpu_custom_call" | custom-call | flops 8999999488 | bytes 1000 | tf_op jit(solution)/shard_map/project/pallas_call | solution.py:528
  153.0 4.5 all-to-all-start.2
  164.1 4.8 project_more.1.q_own.k_own.v_own
  169.0 16.9 %attn_fwd.2 = (bf16[1,1024,256]{2,1,0:T(8,128)(2,1)S(1)}, bf16[1,1024,256]{2,1,0:T(8,128)(2,1)S(1)}, f32[2,32,128]{2,1,0:T(8,128)S(1)}) custom-call(s32[962]{0:T(1024)S(1)} %pad_add_fusion.1.tab, bf16[2,1024,768]{2,1,0:T(8,128)(2,1)S(1)} %project_more.1.q_own.k_own.v_own, bf16[2,1024,768]{2,1,0:T(8,128)(2,1)} %collective-permute-done.10.q_oth.k_oth.v_oth, ...), custom_call_target="tpu_custom_call" | custom-call | flops 16999999488 | bytes 1000 | tf_op jit(solution)/shard_map/attn_fwd/pallas_call | solution.py:306
  186.1 16.8 %attn_fwd.3 = (bf16[1,1024,256]{2,1,0:T(8,128)(2,1)S(1)}, bf16[1,1024,256]{2,1,0:T(8,128)(2,1)S(1)}, f32[2,32,128]{2,1,0:T(8,128)S(1)}) custom-call(s32[962]{0:T(1024)S(1)} %pad_add_fusion.1.tab, bf16[2,1024,768]{2,1,0:T(8,128)(2,1)S(1)} %project_more.1.q_own.k_own.v_own, bf16[2,1024,768]{2,1,0:T(8,128)(2,1)} %collective-permute-done.10.q_oth.k_oth.v_oth, ...), custom_call_target="tpu_custom_call" | custom-call | flops 16999999488 | bytes 1000 | tf_op jit(solution)/shard_map/attn_fwd/pallas_call | solution.py:306
  204.9 5.8 %out_project.1 = (f32[1024,1024]{1,0:T(8,128)S(1)}, bf16[1024,1024]{1,0:T(8,128)(2,1)S(1)}) custom-call(s32[3]{0:T(128)S(1)} %pad_add_fusion.2.where, bf16[1024,1024]{1,0:T(8,128)(2,1)S(1)} %get-tuple-element.119.x_ref, bf16[1,1024,256]{2,1,0:T(8,128)(2,1)S(1)} %get-tuple-element.121.c0, bf16[1,1024,256]{2,1,0:T(8,128)(2,1)S(1)} %get-tuple-element.122.c1.c0, ...), custom_call_target="tpu_custom_call" | custom-call | flops 7000000000 | bytes 1000 | tf_op jit(solution)/shard_map/out_project/pallas_call | solution.py:576
  216.5 5.1 all-to-all-done.2
  221.6 38.0 %feed_forward.2 = (bf16[1024,1024]{1,0:T(8,128)(2,1)}, bf16[1024,1024]{1,0:T(8,128)(2,1)}, bf16[8,2,2,128,1024]{4,3,2,1,0:T(8,128)(2,1)}, f32[2,1,1024]{2,1,0:T(1,128)}) custom-call(s32[3]{0:T(128)} %copy-done.23, bf16[1024,1024]{1,0:T(8,128)(2,1)} %copy-done.32, bf16[1024,1024]{1,0:T(8,128)(2,1)} %bitcast.40.cot_ref, ...), custom_call_target="tpu_custom_call" | custom-call | flops 38000001024 | bytes 1000 | tf_op jit(solution)/shard_map/feed_forward/pallas_call | solution.py:634
  259.6 38.4 %feed_forward.3 = (bf16[1024,1024]{1,0:T(8,128)(2,1)}, bf16[1024,1024]{1,0:T(8,128)(2,1)}, bf16[8,2,2,128,1024]{4,3,2,1,0:T(8,128)(2,1)}, f32[2,1,1024]{2,1,0:T(1,128)}) custom-call(s32[3]{0:T(128)} %copy-done.23, bf16[1024,1024]{1,0:T(8,128)(2,1)} %copy-done.32, bf16[1024,1024]{1,0:T(8,128)(2,1)} %bitcast.40.cot_ref, ...), custom_call_target="tpu_custom_call" | custom-call | flops 38000001024 | bytes 1000 | tf_op jit(solution)/shard_map/feed_forward/pallas_call | solution.py:634
  298.0 13.0 %middle.1 = (bf16[1024,1024]{1,0:T(8,128)(2,1)S(1)}, f32[1024,1024]{1,0:T(8,128)}, bf16[1024,1024]{1,0:T(8,128)(2,1)}, bf16[2,1024,256]{2,1,0:T(8,128)(2,1)S(1)}...) custom-call(s32[3]{0:T(128)S(1)} %copy-done.24, f32[1024,1024]{1,0:T(8,128)} %copy-done.6, ...), custom_call_target="tpu_custom_call" | custom-call | flops 12000000000 | bytes 1000 | tf_op jit(solution)/shard_map/middle/pallas_call | solution.py:695
  318.3 28.2 %attn_bwd.2 = (bf16[1,1024,768]{2,1,0:T(8,128)(2,1)S(1)}, bf16[1,1024,768]{2,1,0:T(8,128)(2,1)}) custom-call(s32[962]{0:T(1024)S(1)} %pad_add_fusion.1.tab, bf16[2,1024,768]{2,1,0:T(8,128)(2,1)} %copy-done.45, bf16[2,1024,768]{2,1,0:T(8,128)(2,1)} %collective-permute-done.10.q_oth.k_oth.v_oth, bf16[2,1024,768]{2,1,0:T(8,128)(2,1)} %copy-done.45, ...), custom_call_target="tpu_custom_call" | custom-call | flops 28999999488 | bytes 1000 | tf_op jit(solution)/shard_map/attn_bwd/pallas_call | solution.py:335
  347.6 18.5 %all-to-all-done.3.own_ref = bf16[4,256,1024]{2,1,0:T(8,128)(2,1)S(1)} async-done(((bf16[4,256,1024]{2,1,0:T(8,128)(2,1)}), bf16[4,256,1024]{2,1,0:T(8,128)(2,1)S(1)}, u32[]{:S(2)}, u32[]{:S(2)}) %all-to-all-start.3) | async-done | bytes 2097184 | tf_op jit(solution)/shard_map/all_to_all | solution.py:974
  366.1 3.7 collective-permute-done.14.d1
  369.9 20.3 %back_early.1 = (f32[1024,1024]{1,0:T(8,128)}, bf16[2,512,1024]{2,1,0:T(8,128)(2,1)}, bf16[2,512,1024]{2,1,0:T(8,128)(2,1)}, bf16[1024,1024]{1,0:T(8,128)(2,1)}, bf16[1024,1024]{1,0:T(8,128)(2,1)}) custom-call(s32[3]{0:T(128)} %copy-done.23, bf16[1,1024,768]{2,1,0:T(8,128)(2,1)} %copy-done.50, bf16[1,1024,768]{2,1,0:T(8,128)(2,1)} %collective-permute-done.14.d1, ...), custom_call_target="tpu_custom_call" | custom-call | flops 19000000512 | bytes 1000 | tf_op jit(solution)/shard_map/back_early/pallas_call | solution.py:813
  390.9 3.7 collective-permute-done.15
  404.0 28.4 %attn_bwd.3 = (bf16[1,1024,768]{2,1,0:T(8,128)(2,1)S(1)}, bf16[1,1024,768]{2,1,0:T(8,128)(2,1)}) custom-call(s32[962]{0:T(1024)S(1)} %pad_add_fusion.1.tab, bf16[2,1024,768]{2,1,0:T(8,128)(2,1)} %copy-done.45, bf16[2,1024,768]{2,1,0:T(8,128)(2,1)} %collective-permute-done.10.q_oth.k_oth.v_oth, bf16[2,1024,768]{2,1,0:T(8,128)(2,1)} %copy-done.45, ...), custom_call_target="tpu_custom_call" | custom-call | flops 28999999488 | bytes 1000 | tf_op jit(solution)/shard_map/attn_bwd/pallas_call | solution.py:335
  432.5 4.1 collective-permute-done.18
  445.3 6.3 %back_weights.1 = (bf16[2,512,1024]{2,1,0:T(8,128)(2,1)S(1)}, bf16[2,512,1024]{2,1,0:T(8,128)(2,1)}) custom-call(s32[3]{0:T(128)S(1)} %copy-done.25, bf16[1,1024,768]{2,1,0:T(8,128)(2,1)S(1)} %get-tuple-element.146.d0, bf16[1,1024,768]{2,1,0:T(8,128)(2,1)S(1)} %collective-permute-done.22.d1, bf16[1024,1024]{1,0:T(8,128)(2,1)S(1)} %copy-done.48, ...), custom_call_target="tpu_custom_call" | custom-call | flops 10000000000 | bytes 1000 | tf_op jit(solution)/shard_map/back_weights/pallas_call | solution.py:856
  457.9 10.6 %back_tokens.1 = (bf16[256,1024]{1,0:T(8,128)(2,1)S(1)}, bf16[256,1024]{1,0:T(8,128)(2,1)S(1)}, bf16[256,1024]{1,0:T(8,128)(2,1)S(1)}, bf16[256,1024]{1,0:T(8,128)(2,1)S(1)}, f32[8,1024]{1,0:T(8,128)S(1)}) custom-call(s32[3]{0:T(128)S(1)} %copy-done.25, bf16[1,1024,768]{2,1,0:T(8,128)(2,1)S(1)} %copy-done.44, bf16[1,1024,768]{2,1,0:T(8,128)(2,1)S(1)} %copy-done.34, ...), custom_call_target="tpu_custom_call" | custom-call | flops 11000000512 | bytes 1000 | tf_op jit(solution)/shard_map/back_tokens/pallas_call | solution.py:833
  489.8 34.8 %collective-permute-done.25.p2 = bf16[256,1024]{1,0:T(8,128)(2,1)} collective-permute-done((bf16[256,1024]{1,0:T(8,128)(2,1)}, bf16[256,1024]{1,0:T(8,128)(2,1)}, u32[]{:S(2)}, u32[]{:S(2)}) %collective-permute-start.25) | collective-permute-done | bytes 524320 | tf_op jit(solution)/shard_map/ppermute | solution.py:1150
  535.2 4.4 restore_direct.1
  542.8 6.2 %collective-permute-start.33 = (bf16[128,1024]{1,0:T(8,128)(2,1)S(1)}, bf16[128,1024]{1,0:T(8,128)(2,1)S(1)}, u32[]{:S(2)}, u32[]{:S(2)}) collective-permute-start(bf16[128,1024]{1,0:T(8,128)(2,1)S(1)} %get-tuple-element.285), channel_id=1, source_target_pairs={{0,3},{1,0},{2,1},{3,2},{4,7},{5,4},{6,5},{7,6},{8,11},{9,8},{10,9... | collective-permute-start | bytes 786440 | tf_op jit(solution)/shard_map/ppermute | solution.py:962
  550.1 5.5 collective-permute-done.33
  555.6 3.7 collective-permute-done.32
  (313 shorter events, 132.0 us)
Async XLA Ops:
  7.2 214.4 %all-gather.3.cloned.1.call-start = ((), (), s32[]{:S(2)}) async-start(), calls=%async_computation.9 | async-start | bytes 17301504 | tf_op jit(solution)/shard_map/all_gather | solution.py:1035
  11.6 17.6 %collective-permute-start = (bf16[2,256,1024]{2,1,0:T(8,128)(2,1)}, bf16[2,256,1024]{2,1,0:T(8,128)(2,1)S(1)}, u32[]{:S(2)}, u32[]{:S(2)}) collective-permute-start(bf16[2,256,1024]{2,1,0:T(8,128)(2,1)} %get-tuple-element.275), channel_id=1, source_target_pairs={{0,4},{1,5},{2,6},{3,7},{4,0},{5,1},{6,2},{7,3},{8,12},{9,13},{10,... | collective-permute-start | bytes 3145736 | tf_op jit(solution)/shard_map/ppermute | solution.py:962
  13.8 49.1 %collective-permute-start.1 = (bf16[128,1024]{1,0:T(8,128)(2,1)}, bf16[128,1024]{1,0:T(8,128)(2,1)}, u32[]{:S(2)}, u32[]{:S(2)}) collective-permute-start(bf16[128,1024]{1,0:T(8,128)(2,1)} %get-tuple-element.287), channel_id=1, source_target_pairs={{0,3},{1,0},{2,1},{3,2},{4,7},{5,4},{6,5},{7,6},{8,11},{9,8},{10,9... | collective-permute-start | bytes 786440 | tf_op jit(solution)/shard_map/ppermute | solution.py:962
  18.4 44.5 %collective-permute-start.2 = (bf16[128,1024]{1,0:T(8,128)(2,1)}, bf16[128,1024]{1,0:T(8,128)(2,1)}, u32[]{:S(2)}, u32[]{:S(2)}) collective-permute-start(bf16[128,1024]{1,0:T(8,128)(2,1)} %get-tuple-element.287), channel_id=1, source_target_pairs={{0,2},{1,3},{2,0},{3,1},{4,6},{5,7},{6,4},{7,5},{8,10},{9,11},{10,... | collective-permute-start | bytes 786440 | tf_op jit(solution)/shard_map/ppermute | solution.py:962
  18.4 44.5 %collective-permute-start.3 = (bf16[128,1024]{1,0:T(8,128)(2,1)}, bf16[128,1024]{1,0:T(8,128)(2,1)}, u32[]{:S(2)}, u32[]{:S(2)}) collective-permute-start(bf16[128,1024]{1,0:T(8,128)(2,1)} %get-tuple-element.287), channel_id=1, source_target_pairs={{0,1},{1,2},{2,3},{3,0},{4,5},{5,6},{6,7},{7,4},{8,9},{9,10},{10,1... | collective-permute-start | bytes 786440 | tf_op jit(solution)/shard_map/ppermute | solution.py:962
  22.3 14.3 %collective-permute-start.8 = (bf16[2,256,1024]{2,1,0:T(8,128)(2,1)}, bf16[2,256,1024]{2,1,0:T(8,128)(2,1)}, u32[]{:S(2)}, u32[]{:S(2)}) collective-permute-start(bf16[2,256,1024]{2,1,0:T(8,128)(2,1)} %get-tuple-element.273), channel_id=1, source_target_pairs={{0,4},{1,5},{2,6},{3,7},{4,0},{5,1},{6,2},{7,3},{8,12},{9,13},{10,... | collective-permute-start | bytes 3145736 | tf_op jit(solution)/shard_map/ppermute | solution.py:962
  31.4 24.5 %all-to-all-start.1 = ((bf16[32,16,128]{2,1,0:T(8,128)(2,1)}), bf16[32,16,128]{2,1,0:T(8,128)(2,1)S(1)}, u32[]{:S(2)}, u32[]{:S(2)}) async-start(bf16[32,16,128]{2,1,0:T(8,128)(2,1)} %pack.1), calls=%async_computation.1 | async-start | bytes 262144 | tf_op jit(solution)/shard_map/all_to_all | solution.py:1001
  56.6 73.8 %all-to-all-start = ((bf16[4,256,1024]{2,1,0:T(8,128)(2,1)}), bf16[4,256,1024]{2,1,0:T(8,128)(2,1)S(1)}, u32[]{:S(2)}, u32[]{:S(2)}) async-start(bf16[4,256,1024]{2,1,0:T(8,128)(2,1)} %bitcast.122), calls=%async_computation | async-start | bytes 4194304 | tf_op jit(solution)/shard_map/all_to_all | solution.py:974
  64.1 35.8 %collective-permute-start.4 = (bf16[4,128,1024]{2,1,0:T(8,128)(2,1)S(1)}, bf16[4,128,1024]{2,1,0:T(8,128)(2,1)}, u32[]{:S(2)}, u32[]{:S(2)}) collective-permute-start(bf16[4,128,1024]{2,1,0:T(8,128)(2,1)S(1)} %pad_maximum_fusion), channel_id=1, source_target_pairs={{0,8},{1,9},{2,10},{3,11},{4,12},{5,13},{6,14},{7,15},{8,0},{9,1},... | collective-permute-start | bytes 3145736 | tf_op jit(solution)/shard_map/ppermute | solution.py:962
  64.9 35.0 %collective-permute-start.5 = (bf16[4,128,1024]{2,1,0:T(8,128)(2,1)S(1)}, bf16[4,128,1024]{2,1,0:T(8,128)(2,1)}, u32[]{:S(2)}, u32[]{:S(2)}) collective-permute-start(bf16[4,128,1024]{2,1,0:T(8,128)(2,1)S(1)} %pad_maximum_fusion), channel_id=1, source_target_pairs={{0,16},{1,17},{2,18},{3,19},{4,20},{5,21},{6,22},{7,23},{8,24},{9,... | collective-permute-start | bytes 3145736 | tf_op jit(solution)/shard_map/ppermute | solution.py:962
  65.4 57.3 %collective-permute-start.6 = (bf16[4,128,1024]{2,1,0:T(8,128)(2,1)S(1)}, bf16[4,128,1024]{2,1,0:T(8,128)(2,1)}, u32[]{:S(2)}, u32[]{:S(2)}) collective-permute-start(bf16[4,128,1024]{2,1,0:T(8,128)(2,1)S(1)} %pad_maximum_fusion), channel_id=1, source_target_pairs={{0,24},{1,25},{2,26},{3,27},{4,28},{5,29},{6,30},{7,31},{8,16},{9,... | collective-permute-start | bytes 3145736 | tf_op jit(solution)/shard_map/ppermute | solution.py:962
  152.9 16.0 %collective-permute-start.10 = (bf16[2,1024,768]{2,1,0:T(8,128)(2,1)}, bf16[2,1024,768]{2,1,0:T(8,128)(2,1)}, u32[]{:S(2)}, u32[]{:S(2)}) collective-permute-start(bf16[2,1024,768]{2,1,0:T(8,128)(2,1)} %get-tuple-element.118), channel_id=1, source_target_pairs={{0,4},{1,5},{2,6},{3,7},{4,0},{5,1},{6,2},{7,3},{8,12},{9,13},{10,... | collective-permute-start | bytes 9437192 | tf_op jit(solution)/shard_map/ppermute | solution.py:962
  153.0 68.6 %all-to-all-start.2 = ((bf16[4,256,1024]{2,1,0:T(8,128)(2,1)}), bf16[4,256,1024]{2,1,0:T(8,128)(2,1)}, u32[]{:S(2)}, u32[]{:S(2)}) async-start(bf16[4,256,1024]{2,1,0:T(8,128)(2,1)} %bitcast.121), calls=%async_computation.2 | async-start | bytes 4194304 | tf_op jit(solution)/shard_map/all_to_all | solution.py:974
  157.5 243.6 %reduce-scatter.3.cloned.1.call-start = ((), (), s32[]{:S(2)}) async-start(), calls=%async_computation.7 | async-start | bytes 9437184 | tf_op jit(solution)/shard_map/reduce_scatter | solution.py:1067
  185.9 17.5 %collective-permute-start.11 = (bf16[1,1024,256]{2,1,0:T(8,128)(2,1)S(1)}, bf16[1,1024,256]{2,1,0:T(8,128)(2,1)S(1)}, u32[]{:S(2)}, u32[]{:S(2)}) collective-permute-start(bf16[1,1024,256]{2,1,0:T(8,128)(2,1)S(1)} %get-tuple-element.123), channel_id=1, source_target_pairs={{0,4},{1,5},{2,6},{3,7},{4,0},{5,1},{6,2},{7,3},{8,12},{9,13},{10,... | collective-permute-start | bytes 1572872 | tf_op jit(solution)/shard_map/ppermute | solution.py:962
  313.4 52.7 %all-to-all-start.3 = ((bf16[4,256,1024]{2,1,0:T(8,128)(2,1)}), bf16[4,256,1024]{2,1,0:T(8,128)(2,1)S(1)}, u32[]{:S(2)}, u32[]{:S(2)}) async-start(bf16[4,256,1024]{2,1,0:T(8,128)(2,1)} %bitcast.113), calls=%async_computation.3 | async-start | bytes 4194304 | tf_op jit(solution)/shard_map/all_to_all | solution.py:974
  317.0 153.9 %reduce-scatter.5.cloned.1.call-start = ((), (), s32[]{:S(2)}) async-start(), calls=%async_computation.8 | async-start | bytes 9437184 | tf_op jit(solution)/shard_map/reduce_scatter | solution.py:1067
  397.6 34.9 %collective-permute-start.19 = (bf16[2,128,1024]{2,1,0:T(8,128)(2,1)}, bf16[2,128,1024]{2,1,0:T(8,128)(2,1)}, u32[]{:S(2)}, u32[]{:S(2)}) collective-permute-start(bf16[2,128,1024]{2,1,0:T(8,128)(2,1)} %get-tuple-element.151), channel_id=1, source_target_pairs={{0,24},{1,25},{2,26},{3,27},{4,28},{5,29},{6,30},{7,31},{8,16},{9,... | collective-permute-start | bytes 1572872 | tf_op jit(solution)/shard_map/ppermute | solution.py:962
  400.3 36.2 %collective-permute-start.18 = (bf16[2,128,1024]{2,1,0:T(8,128)(2,1)}, bf16[2,128,1024]{2,1,0:T(8,128)(2,1)}, u32[]{:S(2)}, u32[]{:S(2)}) collective-permute-start(bf16[2,128,1024]{2,1,0:T(8,128)(2,1)} %get-tuple-element.150), channel_id=1, source_target_pairs={{0,16},{1,17},{2,18},{3,19},{4,20},{5,21},{6,22},{7,23},{8,24},{9,... | collective-permute-start | bytes 1572872 | tf_op jit(solution)/shard_map/ppermute | solution.py:962
  401.1 36.6 %collective-permute-start.17 = (bf16[2,128,1024]{2,1,0:T(8,128)(2,1)}, bf16[2,128,1024]{2,1,0:T(8,128)(2,1)}, u32[]{:S(2)}, u32[]{:S(2)}) collective-permute-start(bf16[2,128,1024]{2,1,0:T(8,128)(2,1)} %get-tuple-element.149), channel_id=1, source_target_pairs={{0,8},{1,9},{2,10},{3,11},{4,12},{5,13},{6,14},{7,15},{8,0},{9,1},... | collective-permute-start | bytes 1572872 | tf_op jit(solution)/shard_map/ppermute | solution.py:962
  402.5 37.7 %collective-permute-start.20 = (bf16[2,128,1024]{2,1,0:T(8,128)(2,1)S(1)}, bf16[2,128,1024]{2,1,0:T(8,128)(2,1)S(1)}, u32[]{:S(2)}, u32[]{:S(2)}) collective-permute-start(bf16[2,128,1024]{2,1,0:T(8,128)(2,1)S(1)} %bitcast.129), channel_id=1, source_target_pairs={{0,2},{1,3},{2,0},{3,1},{4,6},{5,7},{6,4},{7,5},{8,10},{9,11},{10,... | collective-permute-start | bytes 1572872 | tf_op jit(solution)/shard_map/ppermute | solution.py:962
  402.6 38.5 %collective-permute-start.21 = (bf16[2,128,1024]{2,1,0:T(8,128)(2,1)S(1)}, bf16[2,128,1024]{2,1,0:T(8,128)(2,1)S(1)}, u32[]{:S(2)}, u32[]{:S(2)}) collective-permute-start(bf16[2,128,1024]{2,1,0:T(8,128)(2,1)S(1)} %bitcast.128), channel_id=1, source_target_pairs={{0,3},{1,0},{2,1},{3,2},{4,7},{5,4},{6,5},{7,6},{8,11},{9,8},{10,9... | collective-permute-start | bytes 1572872 | tf_op jit(solution)/shard_map/ppermute | solution.py:962
  452.9 29.7 %collective-permute-start.27 = (bf16[2,512,1024]{2,1,0:T(8,128)(2,1)}, bf16[2,512,1024]{2,1,0:T(8,128)(2,1)}, u32[]{:S(2)}, u32[]{:S(2)}) collective-permute-start(bf16[2,512,1024]{2,1,0:T(8,128)(2,1)} %get-tuple-element.175), channel_id=1, source_target_pairs={{0,4},{1,5},{2,6},{3,7},{4,0},{5,1},{6,2},{7,3},{8,12},{9,13},{10,... | collective-permute-start | bytes 6291464 | tf_op jit(solution)/shard_map/ppermute | solution.py:962
  470.9 16.8 %collective-permute-start.23 = (bf16[256,1024]{1,0:T(8,128)(2,1)}, bf16[256,1024]{1,0:T(8,128)(2,1)S(1)}, u32[]{:S(2)}, u32[]{:S(2)}) collective-permute-start(bf16[256,1024]{1,0:T(8,128)(2,1)} %copy-done.42), channel_id=1, source_target_pairs={{0,0},{1,4},{2,2},{3,6},{4,1},{5,5},{6,3},{7,7},{8,8},{9,12},{10,1... | collective-permute-start | bytes 1572872 | tf_op jit(solution)/shard_map/ppermute | solution.py:1150
  472.6 15.8 %collective-permute-start.24 = (bf16[256,1024]{1,0:T(8,128)(2,1)}, bf16[256,1024]{1,0:T(8,128)(2,1)}, u32[]{:S(2)}, u32[]{:S(2)}) collective-permute-start(bf16[256,1024]{1,0:T(8,128)(2,1)} %copy-done.41), channel_id=1, source_target_pairs={{0,1},{1,5},{2,3},{3,7},{4,0},{5,4},{6,2},{7,6},{8,9},{9,13},{10,1... | collective-permute-start | bytes 1572872 | tf_op jit(solution)/shard_map/ppermute | solution.py:1150
  474.8 49.8 %collective-permute-start.25 = (bf16[256,1024]{1,0:T(8,128)(2,1)}, bf16[256,1024]{1,0:T(8,128)(2,1)}, u32[]{:S(2)}, u32[]{:S(2)}) collective-permute-start(bf16[256,1024]{1,0:T(8,128)(2,1)} %copy-done.40), channel_id=1, source_target_pairs={{0,2},{1,6},{2,0},{3,4},{4,3},{5,7},{6,1},{7,5},{8,10},{9,14},{10,... | collective-permute-start | bytes 1572872 | tf_op jit(solution)/shard_map/ppermute | solution.py:1150
  477.2 55.6 %collective-permute-start.26 = (bf16[256,1024]{1,0:T(8,128)(2,1)S(1)}, bf16[256,1024]{1,0:T(8,128)(2,1)}, u32[]{:S(2)}, u32[]{:S(2)}) collective-permute-start(bf16[256,1024]{1,0:T(8,128)(2,1)S(1)} %get-tuple-element.172), channel_id=1, source_target_pairs={{0,3},{1,7},{2,1},{3,5},{4,2},{5,6},{6,0},{7,4},{8,11},{9,15},{10,... | collective-permute-start | bytes 1572872 | tf_op jit(solution)/shard_map/ppermute | solution.py:1150
  482.6 57.0 %collective-permute-start.34 = (bf16[2,128,1024]{2,1,0:T(8,128)(2,1)}, bf16[2,128,1024]{2,1,0:T(8,128)(2,1)S(1)}, u32[]{:S(2)}, u32[]{:S(2)}) collective-permute-start(bf16[2,128,1024]{2,1,0:T(8,128)(2,1)} %get-tuple-element.276), channel_id=1, source_target_pairs={{0,1},{1,2},{2,3},{3,0},{4,5},{5,6},{6,7},{7,4},{8,9},{9,10},{10,1... | collective-permute-start | bytes 1572872 | tf_op jit(solution)/shard_map/ppermute | solution.py:962
  487.7 53.2 %collective-permute-start.28 = (bf16[2,128,1024]{2,1,0:T(8,128)(2,1)}, bf16[2,128,1024]{2,1,0:T(8,128)(2,1)}, u32[]{:S(2)}, u32[]{:S(2)}) collective-permute-start(bf16[2,128,1024]{2,1,0:T(8,128)(2,1)} %get-tuple-element.180), channel_id=1, source_target_pairs={{0,8},{1,9},{2,10},{3,11},{4,12},{5,13},{6,14},{7,15},{8,0},{9,1},... | collective-permute-start | bytes 1572872 | tf_op jit(solution)/shard_map/ppermute | solution.py:962
  488.4 52.5 %collective-permute-start.29 = (bf16[2,128,1024]{2,1,0:T(8,128)(2,1)}, bf16[2,128,1024]{2,1,0:T(8,128)(2,1)}, u32[]{:S(2)}, u32[]{:S(2)}) collective-permute-start(bf16[2,128,1024]{2,1,0:T(8,128)(2,1)} %get-tuple-element.181), channel_id=1, source_target_pairs={{0,16},{1,17},{2,18},{3,19},{4,20},{5,21},{6,22},{7,23},{8,24},{9,... | collective-permute-start | bytes 1572872 | tf_op jit(solution)/shard_map/ppermute | solution.py:962
  524.6 16.3 %collective-permute-start.30 = (bf16[2,128,1024]{2,1,0:T(8,128)(2,1)S(1)}, bf16[2,128,1024]{2,1,0:T(8,128)(2,1)}, u32[]{:S(2)}, u32[]{:S(2)}) collective-permute-start(bf16[2,128,1024]{2,1,0:T(8,128)(2,1)S(1)} %get-tuple-element.182), channel_id=1, source_target_pairs={{0,24},{1,25},{2,26},{3,27},{4,28},{5,29},{6,30},{7,31},{8,16},{9,... | collective-permute-start | bytes 1572872 | tf_op jit(solution)/shard_map/ppermute | solution.py:962
  532.8 17.3 %collective-permute-start.31 = (bf16[128,1024]{1,0:T(8,128)(2,1)}, bf16[128,1024]{1,0:T(8,128)(2,1)S(1)}, u32[]{:S(2)}, u32[]{:S(2)}) collective-permute-start(bf16[128,1024]{1,0:T(8,128)(2,1)} %slice_bitcast_fusion.4), channel_id=1, source_target_pairs={{0,2},{1,3},{2,0},{3,1},{4,6},{5,7},{6,4},{7,5},{8,10},{9,11},{10,... | collective-permute-start | bytes 786440 | tf_op jit(solution)/shard_map/ppermute | solution.py:962
  (79 other events, 783.2 us)
Sparse Core Ops, SparseCore 0:
  11.6 187.2 all-gather.2
  259.7 70.3 reduce-scatter.2
  366.3 92.8 reduce-scatter.4

commit v5 on v4

--- a/solution.py
+++ b/solution.py
@@ -320,7 +320,7 @@
                 pltpu.VMEM((2 * half, 256), f32),
             ],
         ),
-        compiler_params=pltpu.CompilerParams(vmem_limit_bytes=40 << 20),
+        compiler_params=pltpu.CompilerParams(vmem_limit_bytes=60 << 20),
         cost_estimate=cost(17),
         name="attn_fwd",
     )(tab, qkv_own, qkv_oth, qkv_own, qkv_oth, qkv_own, qkv_oth, seg_abs)
@@ -352,7 +352,7 @@
                 pltpu.VMEM((2 * half, 256), f32), pltpu.VMEM((2 * half, 256), f32),
             ],
         ),
-        compiler_params=pltpu.CompilerParams(vmem_limit_bytes=48 << 20),
+        compiler_params=pltpu.CompilerParams(vmem_limit_bytes=60 << 20),
         cost_estimate=cost(29),
         name="attn_bwd",
     )(tab, qkv_own, qkv_oth, qkv_own, qkv_oth, qkv_own, qkv_oth, grad_own, grad_oth, seg_abs, lse)
@@ -412,19 +412,6 @@
 
 def chunk_at(d, place, count):
     return d ^ (2 * (place % (count // 2)) + place // (count // 2))
-
-
-def restore_kernel(count, where, own_ref, oth_ref, out_ref):
-    batches, rows, width = oth_ref.shape
-    chunk = width // count
-    core, d = where[0], where[1]
-    for batch in range(batches):
-        for place in range(count):
-            lanes = slice(place * chunk, (place + 1) * chunk)
-            here = pl.ds(pl.multiple_of(chunk_at(d, place, count) * chunk, chunk), chunk)
-            out_ref[batch, core, :, here] = own_ref[2 * batch + core, :, lanes].astype(out_ref.dtype)
-            there = pl.ds(pl.multiple_of(chunk_at(d ^ 1, place, count) * chunk, chunk), chunk)
-            out_ref[batch, 1 - core, :, there] = oth_ref[batch, :, lanes].astype(out_ref.dtype)
 
 
 def restore_direct_kernel(count, where, p0, p1, p2, p3, out_ref):
@@ -446,28 +433,6 @@
     index = jnp.arange(width, dtype=jnp.int32)
     source = chunk_at(d, index // chunk, count) * chunk + index % chunk
     return (index[:, None] == source[None, :]).astype(bf16)
-
-
-def restore(where, own, oth, count, dtype):
-    batches, rows, width = oth.shape
-    core, d = where[0], where[1]
-    if (width // count) % 128:
-        mine = lax.dynamic_index_in_dim(own.reshape(batches, 2, rows, width), core, 1, False)
-        pair = []
-        for piece, owner in ((mine, d), (oth, d ^ 1)):
-            matrix = chunk_matrix(owner, width, count).T
-            pair.append(jnp.dot(piece, matrix, preferred_element_type=f32).astype(dtype))
-        return jnp.where(core == 0, jnp.stack(pair, axis=1), jnp.stack(pair[::-1], axis=1))
-    whole = lambda shape: pl.BlockSpec(shape, lambda i, w: (0,) * len(shape))
-    shape = (batches, 2, rows, width)
-    return pl.pallas_call(
-        functools.partial(restore_kernel, count),
-        out_shape=struct(shape, dtype),
-        grid_spec=prefetch((1,), [whole(own.shape), whole(oth.shape)], whole(shape)),
-        compiler_params=params(24),
-        cost_estimate=cost(3),
-        name="restore",
-    )(where, own, oth)
 
 
 def scatter_chunks(where, ref, rows, count):
@@ -582,7 +547,7 @@
              pl.BlockSpec(vecs.shape, lambda i, w: (0, 0))],
             (tile, tile),
         ),
-        compiler_params=params(32),
+        compiler_params=params(60),
         cost_estimate=cost(7),
         name="out_project",
     )(where, x, *contexts, *[weights[0]] * 4, *[weights[1]] * 4, vecs)
@@ -658,14 +623,23 @@
     )(where, normed, cot, weights, weights, bias)
 
 
+def write_piece(where, tile, refs, rows):
+    turn = tile ^ (where[2] // 2 * 2 + where[0])
+    for index, ref in enumerate(refs):
+
+        @pl.when(turn == index)
+        def _(ref=ref):
+            ref[...] = rows
+
+
 def mid_kernel(count, where, resid_ref, f0_ref, f1_ref, n0_ref, n1_ref, cot_ref, a0, a1, a2, a3, b0, b1, b2, b3, vec_ref,
-               out_ref, gres_ref, low_ref, own_ref, send_ref, sums_ref):
+               o0, o1, o2, o3, gres_ref, low_ref, own_ref, send_ref, sums_ref):
     tile = pl.program_id(0)
     resid = resid_ref[...]
     cot = gather_chunks(where, cot_ref, count).astype(f32)
     result = resid + gather_chunks(where, f0_ref, count).astype(f32)
     result = result + gather_chunks(where, f1_ref, count).astype(f32)
-    out_ref[...] = (result + vec_ref[4:5, :]).astype(bf16)
+    write_piece(where, tile, (o0, o1, o2, o3), (result + vec_ref[4:5, :]).astype(bf16))
     unit, inverse = normalise(resid)
     grad = gather_chunks(where, n0_ref, count).astype(f32)
     grad = grad + gather_chunks(where, n1_ref, count).astype(f32)
@@ -695,16 +669,17 @@
     return pl.pallas_call(
         functools.partial(mid_kernel, count),
         out_shape=(
-            struct((rows, width), bf16), struct((rows, width), f32), struct((rows, width), bf16),
+            *[struct((ROWS, width), bf16)] * 4,
+            struct((rows, width), f32), struct((rows, width), bf16),
             piece, piece, struct((8, width), f32),
         ),
         grid_spec=prefetch(
             (rows // ROWS,),
             [*[tile] * 6, *out_weight_specs(width) * 2,
              pl.BlockSpec(vecs.shape, lambda i, w: (0, 0))],
-            (tile, tile, tile, part, part, pl.BlockSpec((8, width), lambda i, w: (0, 0))),
-        ),
-        compiler_params=params(48),
+            (*[pl.BlockSpec((ROWS, width), lambda i, w: (0, 0))] * 4, tile, tile, part, part, pl.BlockSpec((8, width), lambda i, w: (0, 0))),
+        ),
+        compiler_params=params(60),
         cost_estimate=cost(12),
         name="middle",
     )(where, resid, *ffn, *gn, cot, *[weights[0]] * 4, *[weights[1]] * 4, vecs)
@@ -767,12 +742,7 @@
     unit, inverse = normalise(x_ref[...].astype(f32))
     result = gres_ref[...] + norm_back(grad, unit, inverse, vec_ref[0:1, :])
     result = result.astype(bf16)
-    turn = pl.program_id(0) ^ (where[2] // 2 * 2 + where[0])
-    for index, out_ref in enumerate((g0, g1, g2, g3)):
-
-        @pl.when(turn == index)
-        def _(out_ref=out_ref):
-            out_ref[...] = result
+    write_piece(where, pl.program_id(0), (g0, g1, g2, g3), result)
 
     @pl.when(pl.program_id(0) == 0)
     def _():
@@ -817,7 +787,7 @@
             (2,), [inner, inner, weight, weight, whole, whole, context, context],
             (total, grad, grad, total, total),
         ),
-        compiler_params=params(56),
+        compiler_params=params(60),
         cost_estimate=cost(19),
         name="back_early",
     )(where, *grads, *weights, normed, low, *contexts)
@@ -842,7 +812,7 @@
                 pl.BlockSpec((8, width), lambda i, w: (0, 0)),
             ),
         ),
-        compiler_params=params(48),
+        compiler_params=params(60),
         cost_estimate=cost(11),
         name="back_tokens",
     )(where, *grads, *weights, *weights, before, x, gres, vecs)
@@ -859,7 +829,7 @@
         grid_spec=prefetch(
             (2,), [inner, inner, *[fixed_spec((width, rows))] * 2, context, context], (grad, grad)
         ),
-        compiler_params=params(40),
+        compiler_params=params(60),
         cost_estimate=cost(10),
         name="back_weights",
     )(where, *grads, *turned, *contexts)
@@ -980,9 +950,6 @@
     def both_halves(keep, come):
         both = jnp.where(core == 0, jnp.stack([keep, come], 1), jnp.stack([come, keep], 1))
         return both.reshape(2 * batches * share, width)
-
-    def give(value):
-        return exchange(value).reshape(2 * batches, share, width)
 
     chunk = norm1_gain.shape[0]
     devices = dp_count * tensor_count
@@ -1115,22 +1082,31 @@
             (along(total[i], k) if k else total[i]).astype(f32) for i, k in enumerate(slots)
         )
 
-    out, grad_resid, low, gctx_own, gctx_send, sums_two = middle(
+    *out, grad_resid, low, gctx_own, gctx_send, sums_two = middle(
         where, resid, tuple(ffn), tuple(grad_two), cot, attn_weights, vecs, dp_count
     )
     gctx_oth = other_core(gctx_send)
-    out_back = give(out)
+    out_back = [None] * tensor_count
+
+    def give(piece, turn):
+        return lax.ppermute(piece, BOTH, token_routes(dp_count, tensor_count, turn))
+
+    out_back[0], out_back[2] = give(out[0], 0), give(out[2], 2)
     d_own0, d_send0 = attn_bwd(
         table, own, oth, gctx_own, gctx_oth, segment_lanes, lse0, blocks, 0
     )
-    d_send0, out_back = lax.optimization_barrier((d_send0, out_back))
+    d_send0, out_back[0], out_back[2] = lax.optimization_barrier(
+        (d_send0, out_back[0], out_back[2])
+    )
     d_oth0 = other_core(d_send0)
     total_one, ga0, gb0, *turned = back_early(
         where, normed, low, (d_own0, d_oth0), (ctx_own0, ctx_oth0), attn_weights, 0
     )
+    out[1], out[3], d_oth0 = lax.optimization_barrier((out[1], out[3], d_oth0))
+    out_back[1], out_back[3] = give(out[1], 1), give(out[3], 3)
+    ga0, gb0, out_back = lax.optimization_barrier((ga0, gb0, out_back))
     attn_parts0 = reduce_core(ga0, gb0)
-    out_other = other_core(half_of(out_back, 1 - core))
-    lse1, attn_parts0, out_other = lax.optimization_barrier((lse1, attn_parts0, out_other))
+    lse1, attn_parts0 = lax.optimization_barrier((lse1, attn_parts0))
     d_own1, d_send1 = attn_bwd(
         table, own, oth, gctx_own, gctx_oth, segment_lanes, lse1, blocks, 1
     )
@@ -1138,26 +1114,20 @@
     pair_next = [along(pair_total0[0], 2), along(pair_total0[1], 3)]
     d_send1, attn_total0, pair_next = lax.optimization_barrier((d_send1, attn_total0, pair_next))
     d_oth1 = other_core(d_send1)
-    ga1, gb1 = back_weights(where, (d_own1, d_oth1), (ctx_own1, ctx_oth1), turned)
-    total_one, ga1, gb1 = lax.optimization_barrier((total_one, ga1, gb1))
+    pair_next.append(along(pair_total1[1], 1))
     *grad_in, sums_one = back_tokens(
         where, (d_own1, d_oth1), attn_weights, 1, total_one, x, grad_resid, vecs
     )
-    grad_in, out_back, out_other, pair_total1 = lax.optimization_barrier(
-        (grad_in, out_back, out_other, pair_total1)
-    )
-    grad_back = [
-        lax.ppermute(piece, BOTH, token_routes(dp_count, tensor_count, turn))
-        for turn, piece in enumerate(grad_in)
-    ]
+    grad_in, out_back, turned = lax.optimization_barrier((grad_in, out_back, turned))
+    grad_back = [give(piece, turn) for turn, piece in enumerate(grad_in)]
+    ga1, gb1 = back_weights(where, (d_own1, d_oth1), (ctx_own1, ctx_oth1), turned)
+    ga1, gb1, pair_next = lax.optimization_barrier((ga1, gb1, pair_next))
     attn_parts1 = reduce_core(ga1, gb1)
-    pair_next.append(along(pair_total1[1], 1))
     sums_one, attn_parts1 = lax.optimization_barrier((sums_one, attn_parts1))
     sums = exchange_sums(sums_one, sums_two, grad_bias)
     attn_come1 = [across(attn_parts1[r], r) for r in range(1, pairs)]
-    sums, attn_come1 = lax.optimization_barrier((sums, attn_come1))
     attn_total1 = add_parts(attn_parts1[0], attn_come1)
-    block_out = restore(where, out_back, out_other, dp_count, bf16).reshape(batches, local, width)
+    block_out = restore_direct(where, out_back, dp_count, bf16).reshape(batches, local, width)
     g_attn = reduce_along(attn_total0, (0, 2)) + reduce_along(attn_total1, (1, 3))
     g_up, g_down = unpack_pair(pair_total1[0], *pair_next)
     grad_in = restore_direct(where, grad_back, dp_count, f32).reshape(batches, local, width)

time: 575 us -> 554 us (0.963)
  waiting for transfers between devices: 163 us -> 134 us
  local copies, waits for them, and re-layouts: 58.9 us -> 43.8 us
  Pallas kernels: 244 us -> 259 us
    all_to_all x3 -> x2, waiting for transfers between devices: 31.3 us -> 12.5 us  [exchange(): lax.all_to_all(value, 'tensor', split_axis=0, concat_axis=0, tiled=True)]
    unnamed x145 -> x86, local copies, waits for them, and re-layouts: 37.4 us -> 20.3 us
    ppermute x4 -> x8, starting transfers between devices: 7.26 us -> 14.7 us  [give(): return lax.ppermute(piece, BOTH, token_routes(dp_count, tensor_count, turn))]
    ppermute x4 -> x8, waiting for transfers between devices: 37.9 us -> 32.6 us  [give(): return lax.ppermute(piece, BOTH, token_routes(dp_count, tensor_count, turn))]
    ppermute x31 -> x30, waiting for transfers between devices: 77.4 us -> 72.6 us  [move(): return lax.ppermute(value, BOTH, routes)]
    all_to_all x3 -> x2, starting transfers between devices: 14.3 us -> 10.9 us  [exchange(): lax.all_to_all(value, 'tensor', split_axis=0, concat_axis=0, tiled=True)]
    ppermute x31 -> x30, starting transfers between devices: 29.5 us -> 26.4 us  [move(): return lax.ppermute(value, BOTH, routes)]
    pallas_call x2 -> x1, Pallas kernels: 15.4 us -> 15.8 us  [middle(): pl.pallas_call(functools.partial(mid_kernel, count), out_shape=(*[struct(...]
  transfers between devices with their start and end apart: 43 -> 45, of which waited for: 17 -> 16; matrix products, arithmetic and copies ran while one was open for 9% -> 10% of each run, Pallas kernels for 36% -> 40%
where the time goes in v5:
time: 554 us; the launch traced here: 547 us
  Pallas kernels  259 us (47%)
  waiting for transfers between devices  134 us (24%)
  starting transfers between devices  64.8 us (12%)
  local copies, waits for them, and re-layouts  43.8 us (8%)
  other arithmetic  28.7 us (5%)
  between operations  16.5 us (3%)
    pallas_call x2, Pallas kernels, feed_forward(): pl.pallas_call(ffn_kernel, out_shape=(struct((rows, width), bf16), struct...  76.1 us
    ppermute x30, waiting for transfers between devices, move(): return lax.ppermute(value, BOTH, routes)  72.6 us
    pallas_call x2, Pallas kernels, attn_bwd(): pl.pallas_call(functools.partial(attn_bwd_kernel, layout, 2 * slot, unrol...  59.4 us
    pallas_call x2, Pallas kernels, attn_fwd(): pl.pallas_call(functools.partial(attn_fwd_kernel, layout, 2 * slot, unrol...  36.2 us
    ppermute x8, waiting for transfers between devices, give(): return lax.ppermute(piece, BOTH, token_routes(dp_count, tensor_count, turn))  32.6 us
    ppermute x30, starting transfers between devices, move(): return lax.ppermute(value, BOTH, routes)  26.4 us
    unnamed x86, local copies, waits for them, and re-layouts  20.3 us
    pallas_call x1, Pallas kernels, back_early(): pl.pallas_call(back_early_kernel, out_shape=(struct((rows, width), f32),...  19.2 us
  transfers between devices with their start and end apart: 45, of which 16 were waited for; matrix products, arithmetic and copies ran while one was open for 10% of the time, Pallas kernels for 40%

profile of v5, /device:TPU:0, one launch (start us, length us, event | category | flops | bytes accessed | tf_op | source)
XLA Modules:
  0.0 546.7 jit_solution(13983425664324328698)
XLA Ops:
  13.8 4.6 collective-permute-start.1
  31.5 5.1 all-to-all-start.1
  39.8 16.2 %all-to-all-done.1 = bf16[32,16,128]{2,1,0:T(8,128)(2,1)S(1)} async-done(((bf16[32,16,128]{2,1,0:T(8,128)(2,1)}), bf16[32,16,128]{2,1,0:T(8,128)(2,1)S(1)}, u32[]{:S(2)}, u32[]{:S(2)}) %all-to-all-start.1) | async-done | bytes 131104 | tf_op jit(solution)/shard_map/all_to_all | solution.py:968
  56.6 6.3 %all-to-all-start = ((bf16[4,256,1024]{2,1,0:T(8,128)(2,1)}), bf16[4,256,1024]{2,1,0:T(8,128)(2,1)S(1)}, u32[]{:S(2)}, u32[]{:S(2)}) async-start(bf16[4,256,1024]{2,1,0:T(8,128)(2,1)} %bitcast.109), calls=%async_computation | async-start | bytes 4194304 | tf_op jit(solution)/shard_map/all_to_all | solution.py:944
  80.2 19.7 %collective-permute-done.4 = bf16[4,128,1024]{2,1,0:T(8,128)(2,1)} collective-permute-done((bf16[4,128,1024]{2,1,0:T(8,128)(2,1)S(1)}, bf16[4,128,1024]{2,1,0:T(8,128)(2,1)}, u32[]{:S(2)}, u32[]{:S(2)}) %collective-permute-start.4) | collective-permute-done | bytes 1048608 | tf_op jit(solution)/shard_map/ppermute | solution.py:932
  99.9 22.8 %collective-permute-done.6 = bf16[4,128,1024]{2,1,0:T(8,128)(2,1)} collective-permute-done((bf16[4,128,1024]{2,1,0:T(8,128)(2,1)S(1)}, bf16[4,128,1024]{2,1,0:T(8,128)(2,1)}, u32[]{:S(2)}, u32[]{:S(2)}) %collective-permute-start.6) | collective-permute-done | bytes 1048608 | tf_op jit(solution)/shard_map/ppermute | solution.py:932
  122.7 7.7 %all-to-all-done = bf16[4,256,1024]{2,1,0:T(8,128)(2,1)S(1)} async-done(((bf16[4,256,1024]{2,1,0:T(8,128)(2,1)}), bf16[4,256,1024]{2,1,0:T(8,128)(2,1)S(1)}, u32[]{:S(2)}, u32[]{:S(2)}) %all-to-all-start) | async-done | bytes 2097184 | tf_op jit(solution)/shard_map/all_to_all | solution.py:944
  135.9 7.1 %collective-permute-done.9.wb_ref.b0.b1.b2.b3.b_ref = bf16[4,512,1024]{2,1,0:T(8,128)(2,1)S(1)} collective-permute-done((bf16[4,512,1024]{2,1,0:T(8,128)(2,1)S(1)}, bf16[4,512,1024]{2,1,0:T(8,128)(2,1)S(1)}, u32[]{:S(2)}, u32[]{:S(2)}) %collective-permute-start.9) | collective-permute-done | bytes 4194336 | tf_op jit(solution)/shard_map/ppermute | solution.py:932
  143.0 7.5 %project.1 = (bf16[2,1024,768]{2,1,0:T(8,128)(2,1)}, bf16[1024,1024]{1,0:T(8,128)(2,1)S(1)}, bf16[1024,1024]{1,0:T(8,128)(2,1)S(1)}) custom-call(s32[3]{0:T(128)S(1)} %pad_add_fusion.2.where, bf16[1024,1024]{1,0:T(8,128)(2,1)S(1)} %bitcast.99, f32[8,1024]{1,0:T(8,128)S(1)} %concatenate.31.vec_ref, ...), custom_call_target="tpu_custom_call" | custom-call | flops 8999999488 | bytes 1000 | tf_op jit(solution)/shard_map/project/pallas_call | solution.py:493
  153.3 4.6 all-to-all-start.2
  162.7 4.8 project_more.1.q_own.k_own.v_own
  169.2 18.0 %attn_fwd.2 = (bf16[1,1024,256]{2,1,0:T(8,128)(2,1)}, bf16[1,1024,256]{2,1,0:T(8,128)(2,1)}, f32[2,32,128]{2,1,0:T(8,128)}) custom-call(s32[962]{0:T(1024)} %pad_add_fusion.1.tab, bf16[2,1024,768]{2,1,0:T(8,128)(2,1)} %copy-done.18, bf16[2,1024,768]{2,1,0:T(8,128)(2,1)} %collective-permute-done.10.q_oth.k_oth.v_oth, bf16[2,1024,768]{2,1,0:T(8,128)(2,1)} %copy-done.18, ...), custom_call_target="tpu_custom_call" | custom-call | flops 16999999488 | bytes 1000 | tf_op jit(solution)/shard_map/attn_fwd/pallas_call | solution.py:306
  187.6 18.2 %attn_fwd.3 = (bf16[1,1024,256]{2,1,0:T(8,128)(2,1)}, bf16[1,1024,256]{2,1,0:T(8,128)(2,1)}, f32[2,32,128]{2,1,0:T(8,128)}) custom-call(s32[962]{0:T(1024)} %pad_add_fusion.1.tab, bf16[2,1024,768]{2,1,0:T(8,128)(2,1)} %copy-done.18, bf16[2,1024,768]{2,1,0:T(8,128)(2,1)} %collective-permute-done.10.q_oth.k_oth.v_oth, bf16[2,1024,768]{2,1,0:T(8,128)(2,1)} %copy-done.18, ...), custom_call_target="tpu_custom_call" | custom-call | flops 16999999488 | bytes 1000 | tf_op jit(solution)/shard_map/attn_fwd/pallas_call | solution.py:306
  208.7 8.4 %out_project.1 = (f32[1024,1024]{1,0:T(8,128)}, bf16[1024,1024]{1,0:T(8,128)(2,1)}) custom-call(s32[3]{0:T(128)} %copy-done.6, bf16[1024,1024]{1,0:T(8,128)(2,1)} %copy-done.4, bf16[1,1024,256]{2,1,0:T(8,128)(2,1)} %get-tuple-element.133.c0, bf16[1,1024,256]{2,1,0:T(8,128)(2,1)} %get-tuple-element.134.c1.c0, bf16[1,1024,256]{2,1,0:T(8,128)(2,1)} %copy-done.25, ...), custom_call_target="tpu_custom_call" | custom-call | flops 7000000000 | bytes 1000 | tf_op jit(solution)/shard_map/out_project/pallas_call | solution.py:541
  217.2 4.8 all-to-all-done.2
  221.9 37.8 %feed_forward.2 = (bf16[1024,1024]{1,0:T(8,128)(2,1)}, bf16[1024,1024]{1,0:T(8,128)(2,1)}, bf16[8,2,2,128,1024]{4,3,2,1,0:T(8,128)(2,1)}, f32[2,1,1024]{2,1,0:T(1,128)}) custom-call(s32[3]{0:T(128)} %copy-done.6, bf16[1024,1024]{1,0:T(8,128)(2,1)} %get-tuple-element.138.n_ref, bf16[1024,1024]{1,0:T(8,128)(2,1)} %bitcast.40.cot_ref, ...), custom_call_target="tpu_custom_call" | custom-call | flops 38000001024 | bytes 1000 | tf_op jit(solution)/shard_map/feed_forward/pallas_call | solution.py:599
  259.8 38.3 %feed_forward.3 = (bf16[1024,1024]{1,0:T(8,128)(2,1)}, bf16[1024,1024]{1,0:T(8,128)(2,1)}, bf16[8,2,2,128,1024]{4,3,2,1,0:T(8,128)(2,1)}, f32[2,1,1024]{2,1,0:T(1,128)}) custom-call(s32[3]{0:T(128)} %copy-done.6, bf16[1024,1024]{1,0:T(8,128)(2,1)} %get-tuple-element.138.n_ref, bf16[1024,1024]{1,0:T(8,128)(2,1)} %bitcast.40.cot_ref, ...), custom_call_target="tpu_custom_call" | custom-call | flops 38000001024 | bytes 1000 | tf_op jit(solution)/shard_map/feed_forward/pallas_call | solution.py:599
  298.1 15.8 %middle.1 = (bf16[256,1024]{1,0:T(8,128)(2,1)}, bf16[256,1024]{1,0:T(8,128)(2,1)}, bf16[256,1024]{1,0:T(8,128)(2,1)}, bf16[256,1024]{1,0:T(8,128)(2,1)}, f32[102...) custom-call(s32[3]{0:T(128)} %copy-done.6, ...), custom_call_target="tpu_custom_call" | custom-call | flops 12000000000 | bytes 1000 | tf_op jit(solution)/shard_map/middle/pallas_call | solution.py:669
  317.8 29.6 %attn_bwd.2 = (bf16[1,1024,768]{2,1,0:T(8,128)(2,1)}, bf16[1,1024,768]{2,1,0:T(8,128)(2,1)}) custom-call(s32[962]{0:T(1024)} %pad_add_fusion.1.tab, bf16[2,1024,768]{2,1,0:T(8,128)(2,1)} %copy-done.18, bf16[2,1024,768]{2,1,0:T(8,128)(2,1)} %collective-permute-done.10.q_oth.k_oth.v_oth, bf16[2,1024,768]{2,1,0:T(8,128)(2,1)} %copy-done.18, ...), custom_call_target="tpu_custom_call" | custom-call | flops 28999999488 | bytes 1000 | tf_op jit(solution)/shard_map/attn_bwd/pallas_call | solution.py:335
  355.4 19.2 %back_early.1 = (f32[1024,1024]{1,0:T(8,128)}, bf16[2,512,1024]{2,1,0:T(8,128)(2,1)}, bf16[2,512,1024]{2,1,0:T(8,128)(2,1)}, bf16[1024,1024]{1,0:T(8,128)(2,1)}, bf16[1024,1024]{1,0:T(8,128)(2,1)}) custom-call(s32[3]{0:T(128)} %copy-done.6, bf16[1,1024,768]{2,1,0:T(8,128)(2,1)} %get-tuple-element.149.d0, bf16[1,1024,768]{2,1,0:T(8,128)(2,1)} %copy-done.36, ...), custom_call_target="tpu_custom_call" | custom-call | flops 19000000512 | bytes 1000 | tf_op jit(solution)/shard_map/back_early/pallas_call | solution.py:783
  374.6 3.8 collective-permute-done.18.p3
  378.5 4.4 collective-permute-done.19
  395.6 29.7 %attn_bwd.3 = (bf16[1,1024,768]{2,1,0:T(8,128)(2,1)}, bf16[1,1024,768]{2,1,0:T(8,128)(2,1)}) custom-call(s32[962]{0:T(1024)} %pad_add_fusion.1.tab, bf16[2,1024,768]{2,1,0:T(8,128)(2,1)} %copy-done.18, bf16[2,1024,768]{2,1,0:T(8,128)(2,1)} %collective-permute-done.10.q_oth.k_oth.v_oth, bf16[2,1024,768]{2,1,0:T(8,128)(2,1)} %copy-done.18, ...), custom_call_target="tpu_custom_call" | custom-call | flops 28999999488 | bytes 1000 | tf_op jit(solution)/shard_map/attn_bwd/pallas_call | solution.py:335
  431.6 12.4 %back_tokens.1 = (bf16[256,1024]{1,0:T(8,128)(2,1)}, bf16[256,1024]{1,0:T(8,128)(2,1)}, bf16[256,1024]{1,0:T(8,128)(2,1)}, bf16[256,1024]{1,0:T(8,128)(2,1)}, f32[8,1024]{1,0:T(8,128)}) custom-call(s32[3]{0:T(128)} %copy-done.6, bf16[1,1024,768]{2,1,0:T(8,128)(2,1)} %get-tuple-element.166.d0, bf16[1,1024,768]{2,1,0:T(8,128)(2,1)} %collective-permute-done.25.d1, ...), custom_call_target="tpu_custom_call" | custom-call | flops 11000000512 | bytes 1000 | tf_op jit(solution)/shard_map/back_tokens/pallas_call | solution.py:803
  444.1 10.3 %back_weights.1 = (bf16[2,512,1024]{2,1,0:T(8,128)(2,1)}, bf16[2,512,1024]{2,1,0:T(8,128)(2,1)}) custom-call(s32[3]{0:T(128)} %copy-done.6, bf16[1,1024,768]{2,1,0:T(8,128)(2,1)} %get-tuple-element.166.d0, bf16[1,1024,768]{2,1,0:T(8,128)(2,1)} %collective-permute-done.25.d1, bf16[1024,1024]{1,0:T(8,128)(2,1)} %get-tuple-element.195.nt_ref, ...), custom_call_target="tpu_custom_call" | custom-call | flops 10000000000 | bytes 1000 | tf_op jit(solution)/shard_map/back_weights/pallas_call | solution.py:826
  455.8 5.4 collective-permute-start.26
  461.5 3.9 collective-permute-start.29
  480.2 7.4 %all-to-all-start.3 = ((f32[32,1,288]{2,1,0:T(1,128)}), f32[32,1,288]{2,1,0:T(1,128)S(1)}, u32[]{:S(2)}, u32[]{:S(2)}) async-start(f32[32,1,288]{2,1,0:T(1,128)} %all_to_all.31), calls=%async_computation.5 | async-start | bytes 98304 | tf_op jit(solution)/shard_map/all_to_all | solution.py:1078
  487.7 12.5 %collective-permute-done.28.p2 = bf16[256,1024]{1,0:T(8,128)(2,1)} collective-permute-done((bf16[256,1024]{1,0:T(8,128)(2,1)}, bf16[256,1024]{1,0:T(8,128)(2,1)}, u32[]{:S(2)}, u32[]{:S(2)}) %collective-permute-start.28) | collective-permute-done | bytes 524320 | tf_op jit(solution)/shard_map/ppermute | solution.py:1092
  500.2 16.3 %collective-permute-done.29.p3 = bf16[256,1024]{1,0:T(8,128)(2,1)} collective-permute-done((bf16[256,1024]{1,0:T(8,128)(2,1)}, bf16[256,1024]{1,0:T(8,128)(2,1)}, u32[]{:S(2)}, u32[]{:S(2)}) %collective-permute-start.29) | collective-permute-done | bytes 524320 | tf_op jit(solution)/shard_map/ppermute | solution.py:1092
  516.4 4.6 restore_direct.3
  529.3 7.7 %collective-permute-done.36 = bf16[128,1024]{1,0:T(8,128)(2,1)S(1)} collective-permute-done((bf16[128,1024]{1,0:T(8,128)(2,1)S(1)}, bf16[128,1024]{1,0:T(8,128)(2,1)S(1)}, u32[]{:S(2)}, u32[]{:S(2)}) %collective-permute-start.36) | collective-permute-done | bytes 262176 | tf_op jit(solution)/shard_map/ppermute | solution.py:932
  (257 shorter events, 115.5 us)
Async XLA Ops:
  7.2 214.7 %all-gather.3.cloned.1.call-start = ((), (), s32[]{:S(2)}) async-start(), calls=%async_computation.8 | async-start | bytes 17301504 | tf_op jit(solution)/shard_map/all_gather | solution.py:1002
  11.6 17.7 %collective-permute-start = (bf16[2,256,1024]{2,1,0:T(8,128)(2,1)}, bf16[2,256,1024]{2,1,0:T(8,128)(2,1)S(1)}, u32[]{:S(2)}, u32[]{:S(2)}) collective-permute-start(bf16[2,256,1024]{2,1,0:T(8,128)(2,1)} %get-tuple-element.299), channel_id=1, source_target_pairs={{0,4},{1,5},{2,6},{3,7},{4,0},{5,1},{6,2},{7,3},{8,12},{9,13},{10,... | collective-permute-start | bytes 3145736 | tf_op jit(solution)/shard_map/ppermute | solution.py:932
  13.8 49.1 %collective-permute-start.1 = (bf16[128,1024]{1,0:T(8,128)(2,1)}, bf16[128,1024]{1,0:T(8,128)(2,1)}, u32[]{:S(2)}, u32[]{:S(2)}) collective-permute-start(bf16[128,1024]{1,0:T(8,128)(2,1)} %get-tuple-element.311), channel_id=1, source_target_pairs={{0,3},{1,0},{2,1},{3,2},{4,7},{5,4},{6,5},{7,6},{8,11},{9,8},{10,9... | collective-permute-start | bytes 786440 | tf_op jit(solution)/shard_map/ppermute | solution.py:932
  18.4 44.5 %collective-permute-start.2 = (bf16[128,1024]{1,0:T(8,128)(2,1)}, bf16[128,1024]{1,0:T(8,128)(2,1)}, u32[]{:S(2)}, u32[]{:S(2)}) collective-permute-start(bf16[128,1024]{1,0:T(8,128)(2,1)} %get-tuple-element.311), channel_id=1, source_target_pairs={{0,2},{1,3},{2,0},{3,1},{4,6},{5,7},{6,4},{7,5},{8,10},{9,11},{10,... | collective-permute-start | bytes 786440 | tf_op jit(solution)/shard_map/ppermute | solution.py:932
  18.4 44.5 %collective-permute-start.3 = (bf16[128,1024]{1,0:T(8,128)(2,1)}, bf16[128,1024]{1,0:T(8,128)(2,1)}, u32[]{:S(2)}, u32[]{:S(2)}) collective-permute-start(bf16[128,1024]{1,0:T(8,128)(2,1)} %get-tuple-element.311), channel_id=1, source_target_pairs={{0,1},{1,2},{2,3},{3,0},{4,5},{5,6},{6,7},{7,4},{8,9},{9,10},{10,1... | collective-permute-start | bytes 786440 | tf_op jit(solution)/shard_map/ppermute | solution.py:932
  31.5 24.5 %all-to-all-start.1 = ((bf16[32,16,128]{2,1,0:T(8,128)(2,1)}), bf16[32,16,128]{2,1,0:T(8,128)(2,1)S(1)}, u32[]{:S(2)}, u32[]{:S(2)}) async-start(bf16[32,16,128]{2,1,0:T(8,128)(2,1)} %pack.1), calls=%async_computation.1 | async-start | bytes 262144 | tf_op jit(solution)/shard_map/all_to_all | solution.py:968
  56.6 73.8 %all-to-all-start = ((bf16[4,256,1024]{2,1,0:T(8,128)(2,1)}), bf16[4,256,1024]{2,1,0:T(8,128)(2,1)S(1)}, u32[]{:S(2)}, u32[]{:S(2)}) async-start(bf16[4,256,1024]{2,1,0:T(8,128)(2,1)} %bitcast.109), calls=%async_computation | async-start | bytes 4194304 | tf_op jit(solution)/shard_map/all_to_all | solution.py:944
  64.2 35.8 %collective-permute-start.4 = (bf16[4,128,1024]{2,1,0:T(8,128)(2,1)S(1)}, bf16[4,128,1024]{2,1,0:T(8,128)(2,1)}, u32[]{:S(2)}, u32[]{:S(2)}) collective-permute-start(bf16[4,128,1024]{2,1,0:T(8,128)(2,1)S(1)} %pad_maximum_fusion), channel_id=1, source_target_pairs={{0,8},{1,9},{2,10},{3,11},{4,12},{5,13},{6,14},{7,15},{8,0},{9,1},... | collective-permute-start | bytes 3145736 | tf_op jit(solution)/shard_map/ppermute | solution.py:932
  65.0 35.0 %collective-permute-start.5 = (bf16[4,128,1024]{2,1,0:T(8,128)(2,1)S(1)}, bf16[4,128,1024]{2,1,0:T(8,128)(2,1)}, u32[]{:S(2)}, u32[]{:S(2)}) collective-permute-start(bf16[4,128,1024]{2,1,0:T(8,128)(2,1)S(1)} %pad_maximum_fusion), channel_id=1, source_target_pairs={{0,16},{1,17},{2,18},{3,19},{4,20},{5,21},{6,22},{7,23},{8,24},{9,... | collective-permute-start | bytes 3145736 | tf_op jit(solution)/shard_map/ppermute | solution.py:932
  65.5 57.3 %collective-permute-start.6 = (bf16[4,128,1024]{2,1,0:T(8,128)(2,1)S(1)}, bf16[4,128,1024]{2,1,0:T(8,128)(2,1)}, u32[]{:S(2)}, u32[]{:S(2)}) collective-permute-start(bf16[4,128,1024]{2,1,0:T(8,128)(2,1)S(1)} %pad_maximum_fusion), channel_id=1, source_target_pairs={{0,24},{1,25},{2,26},{3,27},{4,28},{5,29},{6,30},{7,31},{8,16},{9,... | collective-permute-start | bytes 3145736 | tf_op jit(solution)/shard_map/ppermute | solution.py:932
  153.3 68.7 %all-to-all-start.2 = ((bf16[4,256,1024]{2,1,0:T(8,128)(2,1)}), bf16[4,256,1024]{2,1,0:T(8,128)(2,1)}, u32[]{:S(2)}, u32[]{:S(2)}) async-start(bf16[4,256,1024]{2,1,0:T(8,128)(2,1)} %bitcast.108), calls=%async_computation.2 | async-start | bytes 4194304 | tf_op jit(solution)/shard_map/all_to_all | solution.py:944
  157.8 232.0 %reduce-scatter.3.cloned.1.call-start = ((), (), s32[]{:S(2)}) async-start(), calls=%async_computation.6 | async-start | bytes 9437184 | tf_op jit(solution)/shard_map/reduce_scatter | solution.py:1034
  187.2 18.8 %collective-permute-start.11 = (bf16[1,1024,256]{2,1,0:T(8,128)(2,1)}, bf16[1,1024,256]{2,1,0:T(8,128)(2,1)S(1)}, u32[]{:S(2)}, u32[]{:S(2)}) collective-permute-start(bf16[1,1024,256]{2,1,0:T(8,128)(2,1)} %get-tuple-element.135), channel_id=1, source_target_pairs={{0,4},{1,5},{2,6},{3,7},{4,0},{5,1},{6,2},{7,3},{8,12},{9,13},{10,... | collective-permute-start | bytes 1572872 | tf_op jit(solution)/shard_map/ppermute | solution.py:932
  259.7 168.2 %reduce-scatter.5.cloned.1.call-start = ((), (), s32[]{:S(2)}) async-start(), calls=%async_computation.7 | async-start | bytes 9437184 | tf_op jit(solution)/shard_map/reduce_scatter | solution.py:1034
  313.9 33.5 %collective-permute-start.14 = (bf16[256,1024]{1,0:T(8,128)(2,1)}, bf16[256,1024]{1,0:T(8,128)(2,1)S(1)}, u32[]{:S(2)}, u32[]{:S(2)}) collective-permute-start(bf16[256,1024]{1,0:T(8,128)(2,1)} %get-tuple-element.151), channel_id=1, source_target_pairs={{0,0},{1,4},{2,2},{3,6},{4,1},{5,5},{6,3},{7,7},{8,8},{9,12},{10,1... | collective-permute-start | bytes 1572872 | tf_op jit(solution)/shard_map/ppermute | solution.py:1092
  315.8 31.6 %collective-permute-start.15 = (bf16[256,1024]{1,0:T(8,128)(2,1)}, bf16[256,1024]{1,0:T(8,128)(2,1)S(1)}, u32[]{:S(2)}, u32[]{:S(2)}) collective-permute-start(bf16[256,1024]{1,0:T(8,128)(2,1)} %get-tuple-element.152), channel_id=1, source_target_pairs={{0,2},{1,6},{2,0},{3,4},{4,3},{5,7},{6,1},{7,5},{8,10},{9,14},{10,... | collective-permute-start | bytes 1572872 | tf_op jit(solution)/shard_map/ppermute | solution.py:1092
  352.1 22.6 %collective-permute-start.17 = (bf16[256,1024]{1,0:T(8,128)(2,1)}, bf16[256,1024]{1,0:T(8,128)(2,1)S(1)}, u32[]{:S(2)}, u32[]{:S(2)}) collective-permute-start(bf16[256,1024]{1,0:T(8,128)(2,1)} %get-tuple-element.160), channel_id=1, source_target_pairs={{0,1},{1,5},{2,3},{3,7},{4,0},{5,4},{6,2},{7,6},{8,9},{9,13},{10,1... | collective-permute-start | bytes 1572872 | tf_op jit(solution)/shard_map/ppermute | solution.py:1092
  352.7 25.8 %collective-permute-start.18 = (bf16[256,1024]{1,0:T(8,128)(2,1)}, bf16[256,1024]{1,0:T(8,128)(2,1)S(1)}, u32[]{:S(2)}, u32[]{:S(2)}) collective-permute-start(bf16[256,1024]{1,0:T(8,128)(2,1)} %get-tuple-element.162), channel_id=1, source_target_pairs={{0,3},{1,7},{2,1},{3,5},{4,2},{5,6},{6,0},{7,4},{8,11},{9,15},{10,... | collective-permute-start | bytes 1572872 | tf_op jit(solution)/shard_map/ppermute | solution.py:1092
  386.3 39.0 %collective-permute-start.22 = (bf16[2,128,1024]{2,1,0:T(8,128)(2,1)}, bf16[2,128,1024]{2,1,0:T(8,128)(2,1)}, u32[]{:S(2)}, u32[]{:S(2)}) collective-permute-start(bf16[2,128,1024]{2,1,0:T(8,128)(2,1)} %get-tuple-element.171), channel_id=1, source_target_pairs={{0,24},{1,25},{2,26},{3,27},{4,28},{5,29},{6,30},{7,31},{8,16},{9,... | collective-permute-start | bytes 1572872 | tf_op jit(solution)/shard_map/ppermute | solution.py:932
  388.8 36.6 %collective-permute-start.21 = (bf16[2,128,1024]{2,1,0:T(8,128)(2,1)}, bf16[2,128,1024]{2,1,0:T(8,128)(2,1)}, u32[]{:S(2)}, u32[]{:S(2)}) collective-permute-start(bf16[2,128,1024]{2,1,0:T(8,128)(2,1)} %get-tuple-element.170), channel_id=1, source_target_pairs={{0,16},{1,17},{2,18},{3,19},{4,20},{5,21},{6,22},{7,23},{8,24},{9,... | collective-permute-start | bytes 1572872 | tf_op jit(solution)/shard_map/ppermute | solution.py:932
  389.3 36.1 %collective-permute-start.20 = (bf16[2,128,1024]{2,1,0:T(8,128)(2,1)S(1)}, bf16[2,128,1024]{2,1,0:T(8,128)(2,1)}, u32[]{:S(2)}, u32[]{:S(2)}) collective-permute-start(bf16[2,128,1024]{2,1,0:T(8,128)(2,1)S(1)} %get-tuple-element.169), channel_id=1, source_target_pairs={{0,8},{1,9},{2,10},{3,11},{4,12},{5,13},{6,14},{7,15},{8,0},{9,1},... | collective-permute-start | bytes 1572872 | tf_op jit(solution)/shard_map/ppermute | solution.py:932
  391.9 36.0 %collective-permute-start.23 = (bf16[2,128,1024]{2,1,0:T(8,128)(2,1)}, bf16[2,128,1024]{2,1,0:T(8,128)(2,1)S(1)}, u32[]{:S(2)}, u32[]{:S(2)}) collective-permute-start(bf16[2,128,1024]{2,1,0:T(8,128)(2,1)} %bitcast.46), channel_id=1, source_target_pairs={{0,2},{1,3},{2,0},{3,1},{4,6},{5,7},{6,4},{7,5},{8,10},{9,11},{10,... | collective-permute-start | bytes 1572872 | tf_op jit(solution)/shard_map/ppermute | solution.py:932
  392.4 35.5 %collective-permute-start.24 = (bf16[2,128,1024]{2,1,0:T(8,128)(2,1)S(1)}, bf16[2,128,1024]{2,1,0:T(8,128)(2,1)S(1)}, u32[]{:S(2)}, u32[]{:S(2)}) collective-permute-start(bf16[2,128,1024]{2,1,0:T(8,128)(2,1)S(1)} %bitcast.114), channel_id=1, source_target_pairs={{0,3},{1,0},{2,1},{3,2},{4,7},{5,4},{6,5},{7,6},{8,11},{9,8},{10,9... | collective-permute-start | bytes 1572872 | tf_op jit(solution)/shard_map/ppermute | solution.py:932
  429.2 25.2 %collective-permute-start.30 = (bf16[2,128,1024]{2,1,0:T(8,128)(2,1)S(1)}, bf16[2,128,1024]{2,1,0:T(8,128)(2,1)S(1)}, u32[]{:S(2)}, u32[]{:S(2)}) collective-permute-start(bf16[2,128,1024]{2,1,0:T(8,128)(2,1)S(1)} %bitcast.115), channel_id=1, source_target_pairs={{0,1},{1,2},{2,3},{3,0},{4,5},{5,6},{6,7},{7,4},{8,9},{9,10},{10,1... | collective-permute-start | bytes 1572872 | tf_op jit(solution)/shard_map/ppermute | solution.py:932
  455.8 22.5 %collective-permute-start.26 = (bf16[256,1024]{1,0:T(8,128)(2,1)}, bf16[256,1024]{1,0:T(8,128)(2,1)}, u32[]{:S(2)}, u32[]{:S(2)}) collective-permute-start(bf16[256,1024]{1,0:T(8,128)(2,1)} %get-tuple-element.190), channel_id=1, source_target_pairs={{0,0},{1,4},{2,2},{3,6},{4,1},{5,5},{6,3},{7,7},{8,8},{9,12},{10,1... | collective-permute-start | bytes 1572872 | tf_op jit(solution)/shard_map/ppermute | solution.py:1092
  461.1 39.0 %collective-permute-start.28 = (bf16[256,1024]{1,0:T(8,128)(2,1)}, bf16[256,1024]{1,0:T(8,128)(2,1)}, u32[]{:S(2)}, u32[]{:S(2)}) collective-permute-start(bf16[256,1024]{1,0:T(8,128)(2,1)} %get-tuple-element.192), channel_id=1, source_target_pairs={{0,2},{1,6},{2,0},{3,4},{4,3},{5,7},{6,1},{7,5},{8,10},{9,14},{10,... | collective-permute-start | bytes 1572872 | tf_op jit(solution)/shard_map/ppermute | solution.py:1092
  461.5 54.9 %collective-permute-start.29 = (bf16[256,1024]{1,0:T(8,128)(2,1)}, bf16[256,1024]{1,0:T(8,128)(2,1)}, u32[]{:S(2)}, u32[]{:S(2)}) collective-permute-start(bf16[256,1024]{1,0:T(8,128)(2,1)} %get-tuple-element.193), channel_id=1, source_target_pairs={{0,3},{1,7},{2,1},{3,5},{4,2},{5,6},{6,0},{7,4},{8,11},{9,15},{10,... | collective-permute-start | bytes 1572872 | tf_op jit(solution)/shard_map/ppermute | solution.py:1092
  475.7 45.4 %collective-permute-start.35 = (bf16[2,128,1024]{2,1,0:T(8,128)(2,1)S(1)}, bf16[2,128,1024]{2,1,0:T(8,128)(2,1)S(1)}, u32[]{:S(2)}, u32[]{:S(2)}) collective-permute-start(bf16[2,128,1024]{2,1,0:T(8,128)(2,1)S(1)} %get-tuple-element.212), channel_id=1, source_target_pairs={{0,24},{1,25},{2,26},{3,27},{4,28},{5,29},{6,30},{7,31},{8,16},{9,... | collective-permute-start | bytes 1572872 | tf_op jit(solution)/shard_map/ppermute | solution.py:932
  478.3 42.8 %collective-permute-start.34 = (bf16[2,128,1024]{2,1,0:T(8,128)(2,1)S(1)}, bf16[2,128,1024]{2,1,0:T(8,128)(2,1)}, u32[]{:S(2)}, u32[]{:S(2)}) collective-permute-start(bf16[2,128,1024]{2,1,0:T(8,128)(2,1)S(1)} %get-tuple-element.211), channel_id=1, source_target_pairs={{0,16},{1,17},{2,18},{3,19},{4,20},{5,21},{6,22},{7,23},{8,24},{9,... | collective-permute-start | bytes 1572872 | tf_op jit(solution)/shard_map/ppermute | solution.py:932
  478.7 42.4 %collective-permute-start.33 = (bf16[2,128,1024]{2,1,0:T(8,128)(2,1)S(1)}, bf16[2,128,1024]{2,1,0:T(8,128)(2,1)}, u32[]{:S(2)}, u32[]{:S(2)}) collective-permute-start(bf16[2,128,1024]{2,1,0:T(8,128)(2,1)S(1)} %get-tuple-element.210), channel_id=1, source_target_pairs={{0,8},{1,9},{2,10},{3,11},{4,12},{5,13},{6,14},{7,15},{8,0},{9,1},... | collective-permute-start | bytes 1572872 | tf_op jit(solution)/shard_map/ppermute | solution.py:932
  480.2 40.8 %all-to-all-start.3 = ((f32[32,1,288]{2,1,0:T(1,128)}), f32[32,1,288]{2,1,0:T(1,128)S(1)}, u32[]{:S(2)}, u32[]{:S(2)}) async-start(f32[32,1,288]{2,1,0:T(1,128)} %all_to_all.31), calls=%async_computation.5 | async-start | bytes 98304 | tf_op jit(solution)/shard_map/all_to_all | solution.py:1078
  500.2 25.8 %collective-permute-start.32 = (bf16[128,1024]{1,0:T(8,128)(2,1)S(1)}, bf16[128,1024]{1,0:T(8,128)(2,1)}, u32[]{:S(2)}, u32[]{:S(2)}) collective-permute-start(bf16[128,1024]{1,0:T(8,128)(2,1)S(1)} %slice_bitcast_fusion.2), channel_id=1, source_target_pairs={{0,2},{1,3},{2,0},{3,1},{4,6},{5,7},{6,4},{7,5},{8,10},{9,11},{10,... | collective-permute-start | bytes 786440 | tf_op jit(solution)/shard_map/ppermute | solution.py:932
  (52 other events, 435.5 us)
Sparse Core Ops, SparseCore 0:
  11.0 188.1 all-gather.2
  259.8 70.2 reduce-scatter.2
  334.0 91.3 reduce-scatter.4

commit v6 on v5

--- a/solution.py
+++ b/solution.py
@@ -890,6 +890,28 @@
     )(*vectors, rand, glob)
 
 
+def join_kernel(*refs):
+    *pieces, out_ref = refs
+    size = pieces[0].shape[1]
+    for index, piece in enumerate(pieces):
+        out_ref[0, index * size : (index + 1) * size, :] = piece[0]
+
+
+def join(pieces):
+    slots, size, width = pieces[0].shape
+    rows = size * len(pieces)
+    return pl.pallas_call(
+        join_kernel,
+        out_shape=struct((slots, rows, width), pieces[0].dtype),
+        grid=(slots,),
+        in_specs=[pl.BlockSpec((1, size, width), lambda s: (s, 0, 0))] * len(pieces),
+        out_specs=pl.BlockSpec((1, rows, width), lambda s: (s, 0, 0)),
+        compiler_params=params(16),
+        cost_estimate=cost(4),
+        name="join",
+    )(*pieces)
+
+
 def after(value, *others):
     return lax.optimization_barrier((value, others))[0]
 
@@ -1005,7 +1027,7 @@
     x, attn_own, table, segment_lanes, vecs, up_shift, cot_half = lax.optimization_barrier(
         (x, attn_own, table, segment_lanes, vecs, up_shift, cot_half)
     )
-    attn_own = jnp.concatenate(attn_own, axis=-2)
+    attn_own = join(attn_own)
     attn_weights = (attn_own, other_core(attn_own))
     aligned = chunk % 128 == 0
     own_features = chunk_matrix(d, width, dp_count)
@@ -1091,19 +1113,19 @@
     def give(piece, turn):
         return lax.ppermute(piece, BOTH, token_routes(dp_count, tensor_count, turn))
 
-    out_back[0], out_back[2] = give(out[0], 0), give(out[2], 2)
+    out_back[0], out_back[1], out_back[2] = (give(out[turn], turn) for turn in range(3))
     d_own0, d_send0 = attn_bwd(
         table, own, oth, gctx_own, gctx_oth, segment_lanes, lse0, blocks, 0
     )
-    d_send0, out_back[0], out_back[2] = lax.optimization_barrier(
-        (d_send0, out_back[0], out_back[2])
+    d_send0, out_back[0], out_back[1], out_back[2] = lax.optimization_barrier(
+        (d_send0, *out_back[:3])
     )
     d_oth0 = other_core(d_send0)
     total_one, ga0, gb0, *turned = back_early(
         where, normed, low, (d_own0, d_oth0), (ctx_own0, ctx_oth0), attn_weights, 0
     )
-    out[1], out[3], d_oth0 = lax.optimization_barrier((out[1], out[3], d_oth0))
-    out_back[1], out_back[3] = give(out[1], 1), give(out[3], 3)
+    out[3], d_oth0 = lax.optimization_barrier((out[3], d_oth0))
+    out_back[3] = give(out[3], 3)
     ga0, gb0, out_back = lax.optimization_barrier((ga0, gb0, out_back))
     attn_parts0 = reduce_core(ga0, gb0)
     lse1, attn_parts0 = lax.optimization_barrier((lse1, attn_parts0))

time: 554 us -> 554 us (level)
    unnamed x86 -> x85, local copies, waits for them, and re-layouts: 20.3 us -> 18.8 us
  transfers between devices with their start and end apart: 45 -> 45, of which waited for: 16 -> 15; matrix products, arithmetic and copies ran while one was open for 10% -> 9% of each run, Pallas kernels for 40% -> 41%
where the time goes in v6:
time: 554 us; the launch traced here: 545 us
  Pallas kernels  262 us (47%)
  waiting for transfers between devices  132 us (24%)
  starting transfers between devices  65.4 us (12%)
  local copies, waits for them, and re-layouts  41 us (7%)
  other arithmetic  28.7 us (5%)
  between operations  16.5 us (3%)
    pallas_call x2, Pallas kernels, feed_forward(): pl.pallas_call(ffn_kernel, out_shape=(struct((rows, width), bf16), struct...  76.1 us
    ppermute x30, waiting for transfers between devices, move(): return lax.ppermute(value, BOTH, routes)  70.4 us
    pallas_call x2, Pallas kernels, attn_bwd(): pl.pallas_call(functools.partial(attn_bwd_kernel, layout, 2 * slot, unrol...  59.5 us
    pallas_call x2, Pallas kernels, attn_fwd(): pl.pallas_call(functools.partial(attn_fwd_kernel, layout, 2 * slot, unrol...  35.9 us
    ppermute x8, waiting for transfers between devices, give(): return lax.ppermute(piece, BOTH, token_routes(dp_count, tensor_count, turn))  32.9 us
    ppermute x30, starting transfers between devices, move(): return lax.ppermute(value, BOTH, routes)  25.4 us
    pallas_call x1, Pallas kernels, back_early(): pl.pallas_call(back_early_kernel, out_shape=(struct((rows, width), f32),...  19.2 us
    unnamed x85, local copies, waits for them, and re-layouts  18.8 us
  transfers between devices with their start and end apart: 45, of which 15 were waited for; matrix products, arithmetic and copies ran while one was open for 9% of the time, Pallas kernels for 41%

profile of v6, /device:TPU:0, one launch (start us, length us, event | category | flops | bytes accessed | tf_op | source)
XLA Modules:
  0.0 545.4 jit_solution(7274023180477879726)
XLA Ops:
  13.8 4.6 collective-permute-start.1
  31.5 5.0 all-to-all-start.1
  39.8 16.2 %all-to-all-done.1 = bf16[32,16,128]{2,1,0:T(8,128)(2,1)S(1)} async-done(((bf16[32,16,128]{2,1,0:T(8,128)(2,1)}), bf16[32,16,128]{2,1,0:T(8,128)(2,1)S(1)}, u32[]{:S(2)}, u32[]{:S(2)}) %all-to-all-start.1) | async-done | bytes 131104 | tf_op jit(solution)/shard_map/all_to_all | solution.py:990
  56.6 6.3 %all-to-all-start = ((bf16[4,256,1024]{2,1,0:T(8,128)(2,1)}), bf16[4,256,1024]{2,1,0:T(8,128)(2,1)S(1)}, u32[]{:S(2)}, u32[]{:S(2)}) async-start(bf16[4,256,1024]{2,1,0:T(8,128)(2,1)} %bitcast.109), calls=%async_computation | async-start | bytes 4194304 | tf_op jit(solution)/shard_map/all_to_all | solution.py:966
  80.2 19.7 %collective-permute-done.4.refs_1_ = bf16[4,128,1024]{2,1,0:T(8,128)(2,1)} collective-permute-done((bf16[4,128,1024]{2,1,0:T(8,128)(2,1)S(1)}, bf16[4,128,1024]{2,1,0:T(8,128)(2,1)}, u32[]{:S(2)}, u32[]{:S(2)}) %collective-permute-start.4) | collective-permute-done | bytes 1048608 | tf_op jit(solution)/shard_map/ppermute | solution.py:954
  99.9 22.8 %collective-permute-done.6.refs_3_ = bf16[4,128,1024]{2,1,0:T(8,128)(2,1)} collective-permute-done((bf16[4,128,1024]{2,1,0:T(8,128)(2,1)S(1)}, bf16[4,128,1024]{2,1,0:T(8,128)(2,1)}, u32[]{:S(2)}, u32[]{:S(2)}) %collective-permute-start.6) | collective-permute-done | bytes 1048608 | tf_op jit(solution)/shard_map/ppermute | solution.py:954
  122.7 7.7 %all-to-all-done = bf16[4,256,1024]{2,1,0:T(8,128)(2,1)S(1)} async-done(((bf16[4,256,1024]{2,1,0:T(8,128)(2,1)}), bf16[4,256,1024]{2,1,0:T(8,128)(2,1)S(1)}, u32[]{:S(2)}, u32[]{:S(2)}) %all-to-all-start) | async-done | bytes 2097184 | tf_op jit(solution)/shard_map/all_to_all | solution.py:966
  134.6 7.1 %collective-permute-done.9.wb_ref.b0.b1.b2.b3.b_ref = bf16[4,512,1024]{2,1,0:T(8,128)(2,1)S(1)} collective-permute-done((bf16[4,512,1024]{2,1,0:T(8,128)(2,1)S(1)}, bf16[4,512,1024]{2,1,0:T(8,128)(2,1)S(1)}, u32[]{:S(2)}, u32[]{:S(2)}) %collective-permute-start.9) | collective-permute-done | bytes 4194336 | tf_op jit(solution)/shard_map/ppermute | solution.py:954
  141.7 7.5 %project.1 = (bf16[2,1024,768]{2,1,0:T(8,128)(2,1)}, bf16[1024,1024]{1,0:T(8,128)(2,1)S(1)}, bf16[1024,1024]{1,0:T(8,128)(2,1)S(1)}) custom-call(s32[3]{0:T(128)S(1)} %pad_add_fusion.2.where, bf16[1024,1024]{1,0:T(8,128)(2,1)S(1)} %bitcast.99, f32[8,1024]{1,0:T(8,128)S(1)} %concatenate.28.vec_ref, bf16[4,512,1024]{2,1,0:T(8,128)(2,1)S(1)} %join.1.wa_ref.a0.a1.a2.a3.a_ref, ...), custom_call_target="tpu_custom_call" | custom-call | flops 8999999488 | bytes 1000 | tf_op jit(solution)/shard_map/project/pallas_call | solution.py:493
  152.0 4.6 all-to-all-start.2
  161.5 4.8 project_more.1.q_own.k_own.v_own
  167.9 18.0 %attn_fwd.2 = (bf16[1,1024,256]{2,1,0:T(8,128)(2,1)}, bf16[1,1024,256]{2,1,0:T(8,128)(2,1)}, f32[2,32,128]{2,1,0:T(8,128)}) custom-call(s32[962]{0:T(1024)} %pad_add_fusion.1.tab, bf16[2,1024,768]{2,1,0:T(8,128)(2,1)} %copy-done.18, bf16[2,1024,768]{2,1,0:T(8,128)(2,1)} %collective-permute-done.10.q_oth.k_oth.v_oth, bf16[2,1024,768]{2,1,0:T(8,128)(2,1)} %copy-done.18, ...), custom_call_target="tpu_custom_call" | custom-call | flops 16999999488 | bytes 1000 | tf_op jit(solution)/shard_map/attn_fwd/pallas_call | solution.py:306
  186.5 17.9 %attn_fwd.3 = (bf16[1,1024,256]{2,1,0:T(8,128)(2,1)}, bf16[1,1024,256]{2,1,0:T(8,128)(2,1)}, f32[2,32,128]{2,1,0:T(8,128)}) custom-call(s32[962]{0:T(1024)} %pad_add_fusion.1.tab, bf16[2,1024,768]{2,1,0:T(8,128)(2,1)} %copy-done.18, bf16[2,1024,768]{2,1,0:T(8,128)(2,1)} %collective-permute-done.10.q_oth.k_oth.v_oth, bf16[2,1024,768]{2,1,0:T(8,128)(2,1)} %copy-done.18, ...), custom_call_target="tpu_custom_call" | custom-call | flops 16999999488 | bytes 1000 | tf_op jit(solution)/shard_map/attn_fwd/pallas_call | solution.py:306
  207.4 8.4 %out_project.1 = (f32[1024,1024]{1,0:T(8,128)}, bf16[1024,1024]{1,0:T(8,128)(2,1)}) custom-call(s32[3]{0:T(128)} %copy-done.6, bf16[1024,1024]{1,0:T(8,128)(2,1)} %copy-done.4, bf16[1,1024,256]{2,1,0:T(8,128)(2,1)} %get-tuple-element.133.c0, bf16[1,1024,256]{2,1,0:T(8,128)(2,1)} %get-tuple-element.134.c1.c0, bf16[1,1024,256]{2,1,0:T(8,128)(2,1)} %copy-done.25, ...), custom_call_target="tpu_custom_call" | custom-call | flops 7000000000 | bytes 1000 | tf_op jit(solution)/shard_map/out_project/pallas_call | solution.py:541
  215.8 4.9 all-to-all-done.2
  220.7 37.8 %feed_forward.2 = (bf16[1024,1024]{1,0:T(8,128)(2,1)}, bf16[1024,1024]{1,0:T(8,128)(2,1)}, bf16[8,2,2,128,1024]{4,3,2,1,0:T(8,128)(2,1)}, f32[2,1,1024]{2,1,0:T(1,128)}) custom-call(s32[3]{0:T(128)} %copy-done.6, bf16[1024,1024]{1,0:T(8,128)(2,1)} %get-tuple-element.138.n_ref, bf16[1024,1024]{1,0:T(8,128)(2,1)} %bitcast.40.cot_ref, ...), custom_call_target="tpu_custom_call" | custom-call | flops 38000001024 | bytes 1000 | tf_op jit(solution)/shard_map/feed_forward/pallas_call | solution.py:599
  258.5 38.4 %feed_forward.3 = (bf16[1024,1024]{1,0:T(8,128)(2,1)}, bf16[1024,1024]{1,0:T(8,128)(2,1)}, bf16[8,2,2,128,1024]{4,3,2,1,0:T(8,128)(2,1)}, f32[2,1,1024]{2,1,0:T(1,128)}) custom-call(s32[3]{0:T(128)} %copy-done.6, bf16[1024,1024]{1,0:T(8,128)(2,1)} %get-tuple-element.138.n_ref, bf16[1024,1024]{1,0:T(8,128)(2,1)} %bitcast.40.cot_ref, ...), custom_call_target="tpu_custom_call" | custom-call | flops 38000001024 | bytes 1000 | tf_op jit(solution)/shard_map/feed_forward/pallas_call | solution.py:599
  296.9 15.7 %middle.1 = (bf16[256,1024]{1,0:T(8,128)(2,1)}, bf16[256,1024]{1,0:T(8,128)(2,1)}, bf16[256,1024]{1,0:T(8,128)(2,1)}, bf16[256,1024]{1,0:T(8,128)(2,1)}, f32[102...) custom-call(s32[3]{0:T(128)} %copy-done.6, ...), custom_call_target="tpu_custom_call" | custom-call | flops 12000000000 | bytes 1000 | tf_op jit(solution)/shard_map/middle/pallas_call | solution.py:669
  317.9 29.8 %attn_bwd.2 = (bf16[1,1024,768]{2,1,0:T(8,128)(2,1)}, bf16[1,1024,768]{2,1,0:T(8,128)(2,1)}) custom-call(s32[962]{0:T(1024)} %pad_add_fusion.1.tab, bf16[2,1024,768]{2,1,0:T(8,128)(2,1)} %copy-done.18, bf16[2,1024,768]{2,1,0:T(8,128)(2,1)} %collective-permute-done.10.q_oth.k_oth.v_oth, bf16[2,1024,768]{2,1,0:T(8,128)(2,1)} %copy-done.18, ...), custom_call_target="tpu_custom_call" | custom-call | flops 28999999488 | bytes 1000 | tf_op jit(solution)/shard_map/attn_bwd/pallas_call | solution.py:335
  354.4 19.2 %back_early.1 = (f32[1024,1024]{1,0:T(8,128)}, bf16[2,512,1024]{2,1,0:T(8,128)(2,1)}, bf16[2,512,1024]{2,1,0:T(8,128)(2,1)}, bf16[1024,1024]{1,0:T(8,128)(2,1)}, bf16[1024,1024]{1,0:T(8,128)(2,1)}) custom-call(s32[3]{0:T(128)} %copy-done.6, bf16[1,1024,768]{2,1,0:T(8,128)(2,1)} %get-tuple-element.149.d0, bf16[1,1024,768]{2,1,0:T(8,128)(2,1)} %copy-done.36, ...), custom_call_target="tpu_custom_call" | custom-call | flops 19000000512 | bytes 1000 | tf_op jit(solution)/shard_map/back_early/pallas_call | solution.py:783
  373.6 4.8 collective-permute-done.18.p3
  378.4 4.4 collective-permute-done.19
  395.3 29.8 %attn_bwd.3 = (bf16[1,1024,768]{2,1,0:T(8,128)(2,1)}, bf16[1,1024,768]{2,1,0:T(8,128)(2,1)}) custom-call(s32[962]{0:T(1024)} %pad_add_fusion.1.tab, bf16[2,1024,768]{2,1,0:T(8,128)(2,1)} %copy-done.18, bf16[2,1024,768]{2,1,0:T(8,128)(2,1)} %collective-permute-done.10.q_oth.k_oth.v_oth, bf16[2,1024,768]{2,1,0:T(8,128)(2,1)} %copy-done.18, ...), custom_call_target="tpu_custom_call" | custom-call | flops 28999999488 | bytes 1000 | tf_op jit(solution)/shard_map/attn_bwd/pallas_call | solution.py:335
  431.4 12.4 %back_tokens.1 = (bf16[256,1024]{1,0:T(8,128)(2,1)}, bf16[256,1024]{1,0:T(8,128)(2,1)}, bf16[256,1024]{1,0:T(8,128)(2,1)}, bf16[256,1024]{1,0:T(8,128)(2,1)}, f32[8,1024]{1,0:T(8,128)}) custom-call(s32[3]{0:T(128)} %copy-done.6, bf16[1,1024,768]{2,1,0:T(8,128)(2,1)} %get-tuple-element.166.d0, bf16[1,1024,768]{2,1,0:T(8,128)(2,1)} %collective-permute-done.25.d1, ...), custom_call_target="tpu_custom_call" | custom-call | flops 11000000512 | bytes 1000 | tf_op jit(solution)/shard_map/back_tokens/pallas_call | solution.py:803
  443.8 10.3 %back_weights.1 = (bf16[2,512,1024]{2,1,0:T(8,128)(2,1)}, bf16[2,512,1024]{2,1,0:T(8,128)(2,1)}) custom-call(s32[3]{0:T(128)} %copy-done.6, bf16[1,1024,768]{2,1,0:T(8,128)(2,1)} %get-tuple-element.166.d0, bf16[1,1024,768]{2,1,0:T(8,128)(2,1)} %collective-permute-done.25.d1, bf16[1024,1024]{1,0:T(8,128)(2,1)} %get-tuple-element.195.nt_ref, ...), custom_call_target="tpu_custom_call" | custom-call | flops 10000000000 | bytes 1000 | tf_op jit(solution)/shard_map/back_weights/pallas_call | solution.py:826
  455.5 5.4 collective-permute-start.26
  480.0 8.3 %all-to-all-start.3 = ((f32[32,1,288]{2,1,0:T(1,128)}), f32[32,1,288]{2,1,0:T(1,128)S(1)}, u32[]{:S(2)}, u32[]{:S(2)}) async-start(f32[32,1,288]{2,1,0:T(1,128)} %all_to_all.31), calls=%async_computation.5 | async-start | bytes 98304 | tf_op jit(solution)/shard_map/all_to_all | solution.py:1100
  488.3 11.6 %collective-permute-done.28.p2 = bf16[256,1024]{1,0:T(8,128)(2,1)} collective-permute-done((bf16[256,1024]{1,0:T(8,128)(2,1)}, bf16[256,1024]{1,0:T(8,128)(2,1)}, u32[]{:S(2)}, u32[]{:S(2)}) %collective-permute-start.28) | collective-permute-done | bytes 524320 | tf_op jit(solution)/shard_map/ppermute | solution.py:1114
  499.9 16.4 %collective-permute-done.29.p3 = bf16[256,1024]{1,0:T(8,128)(2,1)} collective-permute-done((bf16[256,1024]{1,0:T(8,128)(2,1)}, bf16[256,1024]{1,0:T(8,128)(2,1)}, u32[]{:S(2)}, u32[]{:S(2)}) %collective-permute-start.29) | collective-permute-done | bytes 524320 | tf_op jit(solution)/shard_map/ppermute | solution.py:1114
  516.4 4.6 restore_direct.3
  526.0 4.1 collective-permute-done.37
  530.1 5.7 %collective-permute-done.36 = bf16[128,1024]{1,0:T(8,128)(2,1)S(1)} collective-permute-done((bf16[128,1024]{1,0:T(8,128)(2,1)S(1)}, bf16[128,1024]{1,0:T(8,128)(2,1)S(1)}, u32[]{:S(2)}, u32[]{:S(2)}) %collective-permute-start.36) | collective-permute-done | bytes 262176 | tf_op jit(solution)/shard_map/ppermute | solution.py:954
  (256 shorter events, 114.8 us)
Async XLA Ops:
  7.2 213.5 %all-gather.3.cloned.1.call-start = ((), (), s32[]{:S(2)}) async-start(), calls=%async_computation.8 | async-start | bytes 17301504 | tf_op jit(solution)/shard_map/all_gather | solution.py:1024
  11.6 17.7 %collective-permute-start = (bf16[2,256,1024]{2,1,0:T(8,128)(2,1)}, bf16[2,256,1024]{2,1,0:T(8,128)(2,1)S(1)}, u32[]{:S(2)}, u32[]{:S(2)}) collective-permute-start(bf16[2,256,1024]{2,1,0:T(8,128)(2,1)} %get-tuple-element.299), channel_id=1, source_target_pairs={{0,4},{1,5},{2,6},{3,7},{4,0},{5,1},{6,2},{7,3},{8,12},{9,13},{10,... | collective-permute-start | bytes 3145736 | tf_op jit(solution)/shard_map/ppermute | solution.py:954
  13.8 49.1 %collective-permute-start.1 = (bf16[128,1024]{1,0:T(8,128)(2,1)}, bf16[128,1024]{1,0:T(8,128)(2,1)}, u32[]{:S(2)}, u32[]{:S(2)}) collective-permute-start(bf16[128,1024]{1,0:T(8,128)(2,1)} %get-tuple-element.311), channel_id=1, source_target_pairs={{0,3},{1,0},{2,1},{3,2},{4,7},{5,4},{6,5},{7,6},{8,11},{9,8},{10,9... | collective-permute-start | bytes 786440 | tf_op jit(solution)/shard_map/ppermute | solution.py:954
  18.4 44.5 %collective-permute-start.2 = (bf16[128,1024]{1,0:T(8,128)(2,1)}, bf16[128,1024]{1,0:T(8,128)(2,1)}, u32[]{:S(2)}, u32[]{:S(2)}) collective-permute-start(bf16[128,1024]{1,0:T(8,128)(2,1)} %get-tuple-element.311), channel_id=1, source_target_pairs={{0,2},{1,3},{2,0},{3,1},{4,6},{5,7},{6,4},{7,5},{8,10},{9,11},{10,... | collective-permute-start | bytes 786440 | tf_op jit(solution)/shard_map/ppermute | solution.py:954
  18.4 44.5 %collective-permute-start.3 = (bf16[128,1024]{1,0:T(8,128)(2,1)}, bf16[128,1024]{1,0:T(8,128)(2,1)}, u32[]{:S(2)}, u32[]{:S(2)}) collective-permute-start(bf16[128,1024]{1,0:T(8,128)(2,1)} %get-tuple-element.311), channel_id=1, source_target_pairs={{0,1},{1,2},{2,3},{3,0},{4,5},{5,6},{6,7},{7,4},{8,9},{9,10},{10,1... | collective-permute-start | bytes 786440 | tf_op jit(solution)/shard_map/ppermute | solution.py:954
  31.5 24.5 %all-to-all-start.1 = ((bf16[32,16,128]{2,1,0:T(8,128)(2,1)}), bf16[32,16,128]{2,1,0:T(8,128)(2,1)S(1)}, u32[]{:S(2)}, u32[]{:S(2)}) async-start(bf16[32,16,128]{2,1,0:T(8,128)(2,1)} %pack.1), calls=%async_computation.1 | async-start | bytes 262144 | tf_op jit(solution)/shard_map/all_to_all | solution.py:990
  56.6 73.8 %all-to-all-start = ((bf16[4,256,1024]{2,1,0:T(8,128)(2,1)}), bf16[4,256,1024]{2,1,0:T(8,128)(2,1)S(1)}, u32[]{:S(2)}, u32[]{:S(2)}) async-start(bf16[4,256,1024]{2,1,0:T(8,128)(2,1)} %bitcast.109), calls=%async_computation | async-start | bytes 4194304 | tf_op jit(solution)/shard_map/all_to_all | solution.py:966
  64.2 35.8 %collective-permute-start.4 = (bf16[4,128,1024]{2,1,0:T(8,128)(2,1)S(1)}, bf16[4,128,1024]{2,1,0:T(8,128)(2,1)}, u32[]{:S(2)}, u32[]{:S(2)}) collective-permute-start(bf16[4,128,1024]{2,1,0:T(8,128)(2,1)S(1)} %pad_maximum_fusion.refs_0_), channel_id=1, source_target_pairs={{0,8},{1,9},{2,10},{3,11},{4,12},{5,13},{6,14},{7,15},{8,0},{9,1},... | collective-permute-start | bytes 3145736 | tf_op jit(solution)/shard_map/ppermute | solution.py:954
  65.0 35.0 %collective-permute-start.5 = (bf16[4,128,1024]{2,1,0:T(8,128)(2,1)S(1)}, bf16[4,128,1024]{2,1,0:T(8,128)(2,1)}, u32[]{:S(2)}, u32[]{:S(2)}) collective-permute-start(bf16[4,128,1024]{2,1,0:T(8,128)(2,1)S(1)} %pad_maximum_fusion.refs_0_), channel_id=1, source_target_pairs={{0,16},{1,17},{2,18},{3,19},{4,20},{5,21},{6,22},{7,23},{8,24},{9,... | collective-permute-start | bytes 3145736 | tf_op jit(solution)/shard_map/ppermute | solution.py:954
  65.5 57.3 %collective-permute-start.6 = (bf16[4,128,1024]{2,1,0:T(8,128)(2,1)S(1)}, bf16[4,128,1024]{2,1,0:T(8,128)(2,1)}, u32[]{:S(2)}, u32[]{:S(2)}) collective-permute-start(bf16[4,128,1024]{2,1,0:T(8,128)(2,1)S(1)} %pad_maximum_fusion.refs_0_), channel_id=1, source_target_pairs={{0,24},{1,25},{2,26},{3,27},{4,28},{5,29},{6,30},{7,31},{8,16},{9,... | collective-permute-start | bytes 3145736 | tf_op jit(solution)/shard_map/ppermute | solution.py:954
  152.0 68.7 %all-to-all-start.2 = ((bf16[4,256,1024]{2,1,0:T(8,128)(2,1)}), bf16[4,256,1024]{2,1,0:T(8,128)(2,1)}, u32[]{:S(2)}, u32[]{:S(2)}) async-start(bf16[4,256,1024]{2,1,0:T(8,128)(2,1)} %bitcast.108), calls=%async_computation.2 | async-start | bytes 4194304 | tf_op jit(solution)/shard_map/all_to_all | solution.py:966
  156.5 233.2 %reduce-scatter.3.cloned.1.call-start = ((), (), s32[]{:S(2)}) async-start(), calls=%async_computation.6 | async-start | bytes 9437184 | tf_op jit(solution)/shard_map/reduce_scatter | solution.py:1056
  185.9 18.6 %collective-permute-start.11 = (bf16[1,1024,256]{2,1,0:T(8,128)(2,1)}, bf16[1,1024,256]{2,1,0:T(8,128)(2,1)S(1)}, u32[]{:S(2)}, u32[]{:S(2)}) collective-permute-start(bf16[1,1024,256]{2,1,0:T(8,128)(2,1)} %get-tuple-element.135), channel_id=1, source_target_pairs={{0,4},{1,5},{2,6},{3,7},{4,0},{5,1},{6,2},{7,3},{8,12},{9,13},{10,... | collective-permute-start | bytes 1572872 | tf_op jit(solution)/shard_map/ppermute | solution.py:954
  258.5 169.1 %reduce-scatter.5.cloned.1.call-start = ((), (), s32[]{:S(2)}) async-start(), calls=%async_computation.7 | async-start | bytes 9437184 | tf_op jit(solution)/shard_map/reduce_scatter | solution.py:1056
  312.7 34.9 %collective-permute-start.14 = (bf16[256,1024]{1,0:T(8,128)(2,1)}, bf16[256,1024]{1,0:T(8,128)(2,1)S(1)}, u32[]{:S(2)}, u32[]{:S(2)}) collective-permute-start(bf16[256,1024]{1,0:T(8,128)(2,1)} %get-tuple-element.151), channel_id=1, source_target_pairs={{0,0},{1,4},{2,2},{3,6},{4,1},{5,5},{6,3},{7,7},{8,8},{9,12},{10,1... | collective-permute-start | bytes 1572872 | tf_op jit(solution)/shard_map/ppermute | solution.py:1114
  314.6 33.1 %collective-permute-start.15 = (bf16[256,1024]{1,0:T(8,128)(2,1)}, bf16[256,1024]{1,0:T(8,128)(2,1)S(1)}, u32[]{:S(2)}, u32[]{:S(2)}) collective-permute-start(bf16[256,1024]{1,0:T(8,128)(2,1)} %get-tuple-element.152), channel_id=1, source_target_pairs={{0,1},{1,5},{2,3},{3,7},{4,0},{5,4},{6,2},{7,6},{8,9},{9,13},{10,1... | collective-permute-start | bytes 1572872 | tf_op jit(solution)/shard_map/ppermute | solution.py:1114
  316.8 30.8 %collective-permute-start.16 = (bf16[256,1024]{1,0:T(8,128)(2,1)}, bf16[256,1024]{1,0:T(8,128)(2,1)S(1)}, u32[]{:S(2)}, u32[]{:S(2)}) collective-permute-start(bf16[256,1024]{1,0:T(8,128)(2,1)} %get-tuple-element.153), channel_id=1, source_target_pairs={{0,2},{1,6},{2,0},{3,4},{4,3},{5,7},{6,1},{7,5},{8,10},{9,14},{10,... | collective-permute-start | bytes 1572872 | tf_op jit(solution)/shard_map/ppermute | solution.py:1114
  352.5 25.9 %collective-permute-start.18 = (bf16[256,1024]{1,0:T(8,128)(2,1)S(1)}, bf16[256,1024]{1,0:T(8,128)(2,1)S(1)}, u32[]{:S(2)}, u32[]{:S(2)}) collective-permute-start(bf16[256,1024]{1,0:T(8,128)(2,1)S(1)} %copy-done.38), channel_id=1, source_target_pairs={{0,3},{1,7},{2,1},{3,5},{4,2},{5,6},{6,0},{7,4},{8,11},{9,15},{10,... | collective-permute-start | bytes 1572872 | tf_op jit(solution)/shard_map/ppermute | solution.py:1114
  386.2 38.8 %collective-permute-start.22 = (bf16[2,128,1024]{2,1,0:T(8,128)(2,1)}, bf16[2,128,1024]{2,1,0:T(8,128)(2,1)}, u32[]{:S(2)}, u32[]{:S(2)}) collective-permute-start(bf16[2,128,1024]{2,1,0:T(8,128)(2,1)} %get-tuple-element.171), channel_id=1, source_target_pairs={{0,24},{1,25},{2,26},{3,27},{4,28},{5,29},{6,30},{7,31},{8,16},{9,... | collective-permute-start | bytes 1572872 | tf_op jit(solution)/shard_map/ppermute | solution.py:954
  388.6 36.4 %collective-permute-start.21 = (bf16[2,128,1024]{2,1,0:T(8,128)(2,1)}, bf16[2,128,1024]{2,1,0:T(8,128)(2,1)}, u32[]{:S(2)}, u32[]{:S(2)}) collective-permute-start(bf16[2,128,1024]{2,1,0:T(8,128)(2,1)} %get-tuple-element.170), channel_id=1, source_target_pairs={{0,16},{1,17},{2,18},{3,19},{4,20},{5,21},{6,22},{7,23},{8,24},{9,... | collective-permute-start | bytes 1572872 | tf_op jit(solution)/shard_map/ppermute | solution.py:954
  389.1 35.9 %collective-permute-start.20 = (bf16[2,128,1024]{2,1,0:T(8,128)(2,1)S(1)}, bf16[2,128,1024]{2,1,0:T(8,128)(2,1)}, u32[]{:S(2)}, u32[]{:S(2)}) collective-permute-start(bf16[2,128,1024]{2,1,0:T(8,128)(2,1)S(1)} %get-tuple-element.169), channel_id=1, source_target_pairs={{0,8},{1,9},{2,10},{3,11},{4,12},{5,13},{6,14},{7,15},{8,0},{9,1},... | collective-permute-start | bytes 1572872 | tf_op jit(solution)/shard_map/ppermute | solution.py:954
  391.8 35.8 %collective-permute-start.23 = (bf16[2,128,1024]{2,1,0:T(8,128)(2,1)}, bf16[2,128,1024]{2,1,0:T(8,128)(2,1)S(1)}, u32[]{:S(2)}, u32[]{:S(2)}) collective-permute-start(bf16[2,128,1024]{2,1,0:T(8,128)(2,1)} %bitcast.46), channel_id=1, source_target_pairs={{0,2},{1,3},{2,0},{3,1},{4,6},{5,7},{6,4},{7,5},{8,10},{9,11},{10,... | collective-permute-start | bytes 1572872 | tf_op jit(solution)/shard_map/ppermute | solution.py:954
  393.6 34.0 %collective-permute-start.24 = (bf16[2,128,1024]{2,1,0:T(8,128)(2,1)S(1)}, bf16[2,128,1024]{2,1,0:T(8,128)(2,1)S(1)}, u32[]{:S(2)}, u32[]{:S(2)}) collective-permute-start(bf16[2,128,1024]{2,1,0:T(8,128)(2,1)S(1)} %bitcast.114), channel_id=1, source_target_pairs={{0,3},{1,0},{2,1},{3,2},{4,7},{5,4},{6,5},{7,6},{8,11},{9,8},{10,9... | collective-permute-start | bytes 1572872 | tf_op jit(solution)/shard_map/ppermute | solution.py:954
  428.9 25.2 %collective-permute-start.30 = (bf16[2,128,1024]{2,1,0:T(8,128)(2,1)S(1)}, bf16[2,128,1024]{2,1,0:T(8,128)(2,1)S(1)}, u32[]{:S(2)}, u32[]{:S(2)}) collective-permute-start(bf16[2,128,1024]{2,1,0:T(8,128)(2,1)S(1)} %bitcast.115), channel_id=1, source_target_pairs={{0,1},{1,2},{2,3},{3,0},{4,5},{5,6},{6,7},{7,4},{8,9},{9,10},{10,1... | collective-permute-start | bytes 1572872 | tf_op jit(solution)/shard_map/ppermute | solution.py:954
  455.5 22.5 %collective-permute-start.26 = (bf16[256,1024]{1,0:T(8,128)(2,1)}, bf16[256,1024]{1,0:T(8,128)(2,1)}, u32[]{:S(2)}, u32[]{:S(2)}) collective-permute-start(bf16[256,1024]{1,0:T(8,128)(2,1)} %get-tuple-element.190), channel_id=1, source_target_pairs={{0,0},{1,4},{2,2},{3,6},{4,1},{5,5},{6,3},{7,7},{8,8},{9,12},{10,1... | collective-permute-start | bytes 1572872 | tf_op jit(solution)/shard_map/ppermute | solution.py:1114
  460.9 39.0 %collective-permute-start.28 = (bf16[256,1024]{1,0:T(8,128)(2,1)}, bf16[256,1024]{1,0:T(8,128)(2,1)}, u32[]{:S(2)}, u32[]{:S(2)}) collective-permute-start(bf16[256,1024]{1,0:T(8,128)(2,1)} %get-tuple-element.192), channel_id=1, source_target_pairs={{0,2},{1,6},{2,0},{3,4},{4,3},{5,7},{6,1},{7,5},{8,10},{9,14},{10,... | collective-permute-start | bytes 1572872 | tf_op jit(solution)/shard_map/ppermute | solution.py:1114
  462.6 53.8 %collective-permute-start.29 = (bf16[256,1024]{1,0:T(8,128)(2,1)}, bf16[256,1024]{1,0:T(8,128)(2,1)}, u32[]{:S(2)}, u32[]{:S(2)}) collective-permute-start(bf16[256,1024]{1,0:T(8,128)(2,1)} %get-tuple-element.193), channel_id=1, source_target_pairs={{0,3},{1,7},{2,1},{3,5},{4,2},{5,6},{6,0},{7,4},{8,11},{9,15},{10,... | collective-permute-start | bytes 1572872 | tf_op jit(solution)/shard_map/ppermute | solution.py:1114
  475.5 45.5 %collective-permute-start.35 = (bf16[2,128,1024]{2,1,0:T(8,128)(2,1)S(1)}, bf16[2,128,1024]{2,1,0:T(8,128)(2,1)S(1)}, u32[]{:S(2)}, u32[]{:S(2)}) collective-permute-start(bf16[2,128,1024]{2,1,0:T(8,128)(2,1)S(1)} %get-tuple-element.212), channel_id=1, source_target_pairs={{0,24},{1,25},{2,26},{3,27},{4,28},{5,29},{6,30},{7,31},{8,16},{9,... | collective-permute-start | bytes 1572872 | tf_op jit(solution)/shard_map/ppermute | solution.py:954
  478.0 43.0 %collective-permute-start.34 = (bf16[2,128,1024]{2,1,0:T(8,128)(2,1)S(1)}, bf16[2,128,1024]{2,1,0:T(8,128)(2,1)}, u32[]{:S(2)}, u32[]{:S(2)}) collective-permute-start(bf16[2,128,1024]{2,1,0:T(8,128)(2,1)S(1)} %get-tuple-element.211), channel_id=1, source_target_pairs={{0,16},{1,17},{2,18},{3,19},{4,20},{5,21},{6,22},{7,23},{8,24},{9,... | collective-permute-start | bytes 1572872 | tf_op jit(solution)/shard_map/ppermute | solution.py:954
  478.4 42.6 %collective-permute-start.33 = (bf16[2,128,1024]{2,1,0:T(8,128)(2,1)S(1)}, bf16[2,128,1024]{2,1,0:T(8,128)(2,1)}, u32[]{:S(2)}, u32[]{:S(2)}) collective-permute-start(bf16[2,128,1024]{2,1,0:T(8,128)(2,1)S(1)} %get-tuple-element.210), channel_id=1, source_target_pairs={{0,8},{1,9},{2,10},{3,11},{4,12},{5,13},{6,14},{7,15},{8,0},{9,1},... | collective-permute-start | bytes 1572872 | tf_op jit(solution)/shard_map/ppermute | solution.py:954
  480.0 41.0 %all-to-all-start.3 = ((f32[32,1,288]{2,1,0:T(1,128)}), f32[32,1,288]{2,1,0:T(1,128)S(1)}, u32[]{:S(2)}, u32[]{:S(2)}) async-start(f32[32,1,288]{2,1,0:T(1,128)} %all_to_all.31), calls=%async_computation.5 | async-start | bytes 98304 | tf_op jit(solution)/shard_map/all_to_all | solution.py:1100
  499.9 26.0 %collective-permute-start.32 = (bf16[128,1024]{1,0:T(8,128)(2,1)S(1)}, bf16[128,1024]{1,0:T(8,128)(2,1)}, u32[]{:S(2)}, u32[]{:S(2)}) collective-permute-start(bf16[128,1024]{1,0:T(8,128)(2,1)S(1)} %slice_bitcast_fusion.2), channel_id=1, source_target_pairs={{0,2},{1,3},{2,0},{3,1},{4,6},{5,7},{6,4},{7,5},{8,10},{9,11},{10,... | collective-permute-start | bytes 786440 | tf_op jit(solution)/shard_map/ppermute | solution.py:954
  (53 other events, 479.2 us)
Sparse Core Ops, SparseCore 0:
  11.0 187.1 all-gather.2
  258.6 70.2 reduce-scatter.2
  332.8 92.3 reduce-scatter.4
